TPU v7x, 128 devices: a whole 4x4x4 slice. The times are simulated.
128 devices in a mesh: comp: 4 (over y), lat: 4 (over z), lon: 8 (over x, core).
Axes of the slice: x: 4, y: 4, z: 4, core: 2. Of those that a mesh axis runs over, the one named last changes fastest.
Arguments:
- state: float32 [2048, 1024, 128], P(('comp', 'lat'), 'lon'), may hold values from -6 to 6
- land_mask: int32 [2048, 1024], P(('comp', 'lat'), 'lon'), may hold values 0 or 1
- intersection_list: int32 [2048, 8, 2, 3], P(('comp', 'lat'), 'lon'), may hold values from 0 to 127, as said below
- mix_atm: float32 [128, 128], replicated, may hold values from -0.5 to 0.5
- mix_ocn: float32 [128, 128], replicated, may hold values from -0.5 to 0.5
- flux_map: float32 [128, 8], replicated, may hold values from -0.5 to 0.5
- ocean_map: float32 [8, 128], replicated, may hold values from -2 to 2
- regrid_weights: bfloat16 [32, 128, 128], replicated, may hold values from -0.25 to 0.25
Outputs:
- state_out: float32 [2048, 1024, 128], P(('comp', 'lat'), 'lon')
- surface_out: float32 [2048, 1024], P(('comp', 'lat'), 'lon')
Inputs may be any that keep to these rules, and one draw needn't show every extreme that they name: `intersection_list`: entry 0 is an ocean tile lat * 8 + lon, entry 1 a row of that tile below 128, entry 2 a weight block below 32. With t the tile lat * 8 + lon of the list's own rows and r = min(4, 8), the entries of one tile name exactly the 2 r tiles (t + a * 8 + b - (r - 1) // 2) mod (4 * 8) for a in 0, 1 and b in 0 to r - 1, each by exactly 32 entries.
All inputs are finite; a program needn't handle non-finite values. No bound on the sum of `land_mask` on one device may be relied on, other than what follows from the above.
Results may differ from a plain program's by a relative error of at most 0.0012.
Values may be sent and summed in bfloat16 or wider, within the bound.
A program may use at most 192 MiB of HBM per device.

v0:
```python
import jax
import jax.numpy as jnp
from jax import lax
from jax.sharding import PartitionSpec as P

SMOOTHING = 0.2
PHYSICS = 0.5
HIGHEST = lax.Precision.HIGHEST


def with_halo(shard, sides, width, wrap):
    for axis, dim in sides:
        size, length = (lax.axis_size(axis), shard.shape[dim])
        up = [(i, (i + 1) % size) for i in range(size if wrap else size - 1)]
        down = [(j, i) for i, j in up]
        last = lax.slice_in_dim(shard, length - width, length, axis=dim)
        leading = lax.slice_in_dim(shard, 0, width, axis=dim)
        before = lax.ppermute(last, axis, up)
        after = lax.ppermute(leading, axis, down)
        shard = jnp.concatenate([before, shard, after], axis=dim)
    return shard


def from_behind(value, axis, steps):
    count = lax.axis_size(axis)
    pairs = [(source, (source + steps) % count) for source in range(count)]
    return lax.ppermute(value, axis, pairs)


def shortened(shard):
    return jax.tree.map(lambda a: a.astype(jnp.bfloat16) if a.dtype == jnp.float32 else a, shard)


def column_physics(values, mixing):
    return jnp.tanh(jnp.einsum("rck,kj->rcj", values, mixing, precision=HIGHEST))


def earlier_same(owners, usable):
    positions = jnp.arange(owners.shape[0], dtype=jnp.int32)
    before = (
        (owners[None, :] == owners[:, None])
        & (positions[None, :] < positions[:, None])
        & usable[None, :]
    )
    return jnp.sum(before.astype(jnp.int32), axis=1)


def pack_rows(blocks, owners, labels, usable, slots_each, owner_total):
    ranks = earlier_same(owners, usable)
    target_slot = owners * slots_each + ranks
    slot_ids = jnp.arange(owner_total * slots_each, dtype=jnp.int32)
    placing = (slot_ids[:, None] == target_slot[None, :]) & usable[None, :]
    packed = jnp.dot(
        placing.astype(jnp.bfloat16), blocks, preferred_element_type=jnp.float32
    ).astype(jnp.bfloat16)
    placed_labels = jnp.sum(jnp.where(placing, labels[None, :] + 1, 0), axis=1) - 1
    return (
        packed.reshape(owner_total, slots_each, blocks.shape[1]),
        placed_labels.reshape(owner_total, slots_each),
    )


def local(
    state, land_mask, intersection_list, mix_atm, mix_ocn, flux_map, ocean_map, regrid_weights
):
    tile_rows, block_len, levels = state.shape
    flux_count = flux_map.shape[1]
    weight_count = regrid_weights.shape[0]
    intersections = intersection_list.shape[2]
    comp_count = lax.axis_size("comp")
    lat_count = lax.axis_size("lat")
    lon_count = lax.axis_size("lon")
    tile_count = lat_count * lon_count
    reach = min(4, lon_count)
    neighbour_count = 2 * reach
    capacity = intersections * tile_rows // neighbour_count
    quarter = capacity // comp_count
    width = flux_count * block_len
    comp_index = lax.axis_index("comp")
    tile_index = lax.axis_index("lat") * lon_count + lax.axis_index("lon")
    band = comp_index * lat_count + lax.axis_index("lat")
    ocean_band = (comp_count - 1) * lat_count
    ocean_side = comp_index == comp_count - 1
    lower_valid = (band > 0) & ((band - 1 >= ocean_band) == (band >= ocean_band))
    upper_valid = (band < comp_count * lat_count - 1) & (
        (band + 1 >= ocean_band) == (band >= ocean_band)
    )
    sea_cells = land_mask == 1
    current = state
    flux_total = jnp.zeros((flux_count, tile_rows, block_len), jnp.float32)
    ocean_spread = None
    for substep in range(2):
        padded = with_halo(current.astype(jnp.bfloat16), ((("comp", "lat"), 0),), 1, False).astype(
            current.dtype
        )
        below = jnp.concatenate([jnp.where(lower_valid, padded[:1], 0.0), current[:-1]], axis=0)
        above = jnp.concatenate([current[1:], jnp.where(upper_valid, padded[-1:], 0.0)], axis=0)
        sides = with_halo(current, (("lon", 1),), 1, True)
        spread = below + above + sides[:, :-2] + sides[:, 2:] - 4.0 * current
        if substep == 0:
            ocean_spread = spread

        def advance(operands):
            values, spread_now, total = operands
            smooth = values + SMOOTHING * spread_now
            moved = smooth + PHYSICS * column_physics(smooth, mix_atm)
            return (moved, total + jnp.einsum("rck,kf->frc", moved, flux_map, precision=HIGHEST))

        def resting(operands):
            return (operands[0], operands[2])

        current, flux_total = lax.cond(ocean_side, resting, advance, (current, spread, flux_total))
    flux_sent = jnp.where(sea_cells[None], 0.5 * flux_total, 0.0).astype(jnp.bfloat16)
    entry_list = intersection_list.reshape(tile_rows * intersections, 3)
    owners = entry_list[:, 0]
    targets = entry_list[:, 1]
    weight_ids = entry_list[:, 2]
    labels = weight_ids * tile_rows + targets
    entry_blocks = jnp.repeat(flux_sent.transpose(1, 0, 2), intersections, axis=0).reshape(
        tile_rows * intersections, width
    )
    sending = jnp.broadcast_to(jnp.logical_not(ocean_side), owners.shape)
    offsets = [
        (n // reach * lon_count + n % reach - (reach - 1) // 2) % tile_count
        for n in range(neighbour_count)
    ]
    offset_table = jnp.array(offsets, jnp.int32)
    distance = (owners - tile_index + tile_count) % tile_count
    neighbour_ids = jnp.sum(
        jnp.where(
            distance[:, None] == offset_table[None, :],
            jnp.arange(neighbour_count, dtype=jnp.int32)[None, :],
            0,
        ),
        axis=1,
    )
    packed, packed_labels = pack_rows(
        entry_blocks, neighbour_ids, labels, sending, capacity, neighbour_count
    )
    moved_blocks = []
    moved_labels = []
    for neighbour in range(neighbour_count):
        if offsets[neighbour] == 0:
            one_blocks, one_labels = (packed[neighbour], packed_labels[neighbour])
        else:
            one_blocks, one_labels = from_behind(
                (packed[neighbour], packed_labels[neighbour]), ("lat", "lon"), offsets[neighbour]
            )
        moved_blocks.append(one_blocks)
        moved_labels.append(one_labels)
    stacked_blocks = jnp.stack(moved_blocks).reshape(neighbour_count, comp_count, quarter, width)
    stacked_labels = jnp.stack(moved_labels).reshape(neighbour_count, comp_count, quarter)
    arrived, arrived_labels = (
        lax.all_to_all(stacked_blocks, "comp", split_axis=1, concat_axis=1, tiled=True),
        lax.all_to_all(
            shortened(stacked_labels), "comp", split_axis=1, concat_axis=1, tiled=True
        ).astype(stacked_labels.dtype),
    )
    weights_wide = regrid_weights.astype(jnp.float32)
    label_ids = jnp.arange(weight_count * tile_rows, dtype=jnp.int32)
    flat_labels = arrived_labels.reshape(-1)
    selector = (flat_labels[:, None] == label_ids[None, :]).astype(jnp.bfloat16)
    binned = lax.dot_general(
        selector,
        arrived.reshape(flat_labels.shape[0], width),
        (((0,), (0,)), ((), ())),
        preferred_element_type=jnp.float32,
    )
    binned = binned.reshape(weight_count, tile_rows, flux_count, block_len)
    partial_forcing = jnp.einsum("wdfa,wab->fdb", binned, weights_wide, precision=HIGHEST)
    forcing = lax.psum(partial_forcing, "comp")

    def ocean_step(values):
        smooth = values + SMOOTHING * ocean_spread
        moved = (
            smooth
            + jnp.einsum("frc,fk->rck", forcing, ocean_map, precision=HIGHEST)
            + PHYSICS * column_physics(smooth, mix_ocn)
        )
        return jnp.where(sea_cells[:, :, None], moved, values)

    def unchanged(values):
        return values

    final_state = lax.cond(ocean_side, ocean_step, unchanged, current)
    surface = final_state[:, :, 0]
    everything = lax.all_gather(surface, ("comp", "lat", "lon"), axis=0, tiled=True)
    ocean_surface = everything[(comp_count - 1) * tile_count * tile_rows :]
    picked = jnp.take(ocean_surface, owners * tile_rows + targets, axis=0)
    images = jnp.einsum("eb,wab->ewa", picked, weights_wide, precision=HIGHEST)
    which_block = weight_ids[:, None] == jnp.arange(weight_count, dtype=jnp.int32)[None, :]
    chosen = jnp.sum(jnp.where(which_block[:, :, None], images, 0.0), axis=1)
    returned = chosen.reshape(tile_rows, intersections, block_len).sum(axis=1)
    surface_out = jnp.where(ocean_side, surface, jnp.where(sea_cells, returned, surface))
    return (final_state, surface_out)


def solution(mesh):
    placed = (
        P(("comp", "lat"), "lon", None),
        P(("comp", "lat"), "lon"),
        P(("comp", "lat"), "lon", None, None),
        P(),
        P(),
        P(),
        P(),
        P(),
    )
    return jax.shard_map(
        local,
        mesh=mesh,
        in_specs=placed,
        out_specs=(P(("comp", "lat"), "lon", None), P(("comp", "lat"), "lon")),
        check_vma=False,
    )
```

profile of v0, /device:TPU:1, one launch (start us, length us, event | category | flops | bytes accessed | tf_op | source)
XLA Modules:
  0.0 446.0 jit_solution(6722791696484953840)
XLA Ops:
  7.2 8.0 %copy.117 = f32[128,128,128]{2,1,0:T(8,128)} copy(f32[128,128,128]{2,1,0:T(8,128)} %param.15) | data formatting | bytes 16777216
  15.2 4.4 convert_element_type.30
  21.5 4.4 collective-permute-start
  33.3 10.9 %fusion.41 = (f32[127,128,128]{2,1,0:T(8,128)}, f32[127,128,128]{2,1,0:T(8,128)}) fusion(f32[128,128,128]{2,1,0:T(8,128)} %copy.117), kind=kLoop, calls=%fused_computation.103 | loop fusion | bytes 33292288 | tf_op jit(solution)/shard_map/slice | solution.py:97
  44.5 4.7 %collective-permute-done.9 = s32[32]{0:T(128)S(1)} collective-permute-done((s32[32]{0:T(128)S(1)}, s32[32]{0:T(128)S(1)}, u32[]{:S(2)}, u32[]{:S(2)}) %collective-permute-start.9) | collective-permute-done | bytes 160 | tf_op jit(solution)/shard_map/ppermute | solution.py:27
  49.3 5.6 %collective-permute-done.10 = s32[32]{0:T(128)S(1)} collective-permute-done((s32[32]{0:T(128)S(1)}, s32[32]{0:T(128)S(1)}, u32[]{:S(2)}, u32[]{:S(2)}) %collective-permute-start.10) | collective-permute-done | bytes 160 | tf_op jit(solution)/shard_map/ppermute | solution.py:27
  60.5 5.4 %collective-permute-done.12 = s32[32]{0:T(128)S(1)} collective-permute-done((s32[32]{0:T(128)S(1)}, s32[32]{0:T(128)S(1)}, u32[]{:S(2)}, u32[]{:S(2)}) %collective-permute-start.12) | collective-permute-done | bytes 160 | tf_op jit(solution)/shard_map/ppermute | solution.py:27
  66.0 5.2 %collective-permute-done.13 = s32[32]{0:T(128)S(1)} collective-permute-done((s32[32]{0:T(128)S(1)}, s32[32]{0:T(128)S(1)}, u32[]{:S(2)}, u32[]{:S(2)}) %collective-permute-start.13) | collective-permute-done | bytes 160 | tf_op jit(solution)/shard_map/ppermute | solution.py:27
  71.3 5.9 %collective-permute-done.14 = s32[32]{0:T(128)S(1)} collective-permute-done((s32[32]{0:T(128)S(1)}, s32[32]{0:T(128)S(1)}, u32[]{:S(2)}, u32[]{:S(2)}) %collective-permute-start.14) | collective-permute-done | bytes 160 | tf_op jit(solution)/shard_map/ppermute | solution.py:27
  77.4 18.3 %fusion.15 = f32[128,128,128]{2,1,0:T(8,128)} fusion(f32[128,1,128]{2,1,0:T(1,128)S(1)} %collective-permute-done.3, f32[128,128,128]{2,1,0:T(8,128)} %copy.117, f32[128,1,128]{2,1,0:T(1,128)S(1)} %collective-permute-done.2, f32[127,128,128]{2,1,0:T(8,128)} %get-tuple-element.139, f32[1,128,128]{2,1,0:T(8,128)S(1)} %get-tuple-element.145, ...), kind=kLoop, calls=%fused_computation.27 | loop fusion | flops 18874368 | bytes 33685504 | tf_op jit(solution)/shard_map/sub | solution.py:99
  95.7 27.4 %conditional.3 = (f32[128,128,128]{2,1,0:T(8,128)}, f32[8,128,128]{2,0,1:T(8,128)S(1)}) conditional(s32[]{:T(128)} %convert_element_type.29, (f32[128,128,128]{2,1,0:T(8,128)}, f32[128,128,128]{2,1,0:T(8,128)}, f32[128,128]{1,0:T(8,128)S(1)}, f32[128,8]{0,1:T(8,128)S(1)}) %tuple.90, f32[128,128,128]{2,1,0:T(8,128)} %copy.117), branch_computations={%region_0.1_spmd, %region_1.2_spmd} | conditional | flops 3435134976 | bytes 50925584 | solution.py:112
  99.3 14.4 %multiply_add_fusion = f32[128,128,128]{2,1,0:T(8,128)} fusion(f32[128,128,128]{2,1,0:T(8,128)S(1)} %copy.115, f32[128,128,128]{2,1,0:T(8,128)} %get-tuple-element.62, f32[128,128]{1,0:T(8,128)S(1)} %get-tuple-element.63), kind=kOutput, calls=%fused_computation.1 | convolution fusion | flops 3233808384 | bytes 25231360 | tf_op jit(solution)/shard_map/cond/branch_0_fun/rck,kj->rcj/dot_general | solution.py:35
  113.7 9.4 %convolution_bitcast_fusion = f32[8,128,128]{2,0,1:T(8,128)S(1)} fusion(f32[128,128,128]{2,1,0:T(8,128)} %multiply_add_fusion, f32[128,8]{0,1:T(8,128)S(1)} %get-tuple-element.64), kind=kOutput, calls=%fused_computation.3 | convolution fusion | flops 201326592 | bytes 8916992 | tf_op jit(solution)/shard_map/cond/branch_0_fun/rck,kf->frc/dot_general | solution.py:107
  123.1 4.4 convert_element_type.32
  127.5 6.7 %fusion.40 = (f32[127,128,128]{2,1,0:T(8,128)S(1)}, f32[127,128,128]{2,1,0:T(8,128)S(1)}) fusion(f32[128,128,128]{2,1,0:T(8,128)} %get-tuple-element.86), kind=kLoop, calls=%fused_computation.102 | loop fusion | bytes 33292288 | tf_op jit(solution)/shard_map/slice | solution.py:97
  134.3 3.9 collective-permute-start.4
  146.0 6.9 %pad_maximum_fusion.4 = (f32[128,128,128]{2,1,0:T(8,128)}, f32[128,128,128]{2,1,0:T(8,128)}) fusion(f32[127,128,128]{2,1,0:T(8,128)S(1)} %get-tuple-element.137, f32[1,128,128]{2,1,0:T(8,128)S(1)} %get-tuple-element.143, f32[1,128,128]{2,1,0:T(8,128)S(1)} %get-tuple-element.142, f32[127,128,128]{2,1,0:T(8,128)S(1)} %get-tuple-element.136), kind=kLoop, calls=%fused_computation.31 | loop fusion | flops 4194304 | bytes 33554432 | tf_op jit(solution)/shard_map/concatenate | solution.py:96
  152.8 12.6 %pad_maximum_fusion.1 = (f32[128,129,128]{2,1,0:T(8,128)}, f32[128,129,128]{2,1,0:T(8,128)}) fusion(f32[128,1,128]{2,1,0:T(1,128)} %collective-permute-done.7, f32[128,128,128]{2,1,0:T(8,128)} %get-tuple-element.86, f32[128,1,128]{2,1,0:T(1,128)} %collective-permute-done.6), kind=kLoop, calls=%fused_computation.24 | loop fusion | flops 4227072 | bytes 25427968 | tf_op jit(solution)/shard_map/concatenate | solution.py:20
  165.4 4.3 broadcast.111
  169.8 58.3 %conditional.4 = ((f32[128,128,128]{2,1,0:T(8,128)}, f32[8,128,128]{2,0,1:T(8,128)S(1)})) conditional(s32[]{:T(128)} %convert_element_type.29, (f32[128,128,128]{2,1,0:T(8,128)}, f32[128,128,128]{2,1,0:T(8,128)}, f32[128,129,128]{2,1,0:T(8,128)}, f32[128,129,128]{2,1,0:T(8,128)}, f32[128,128,128]{2,1,0:T(8,128)}, ...), branch_computations={%region_2.3_spmd, %region_3.4_spmd} | conditional | flops 3456237568 | bytes 135335968 | solution.py:112
  169.9 7.8 %copy.116 = f32[128,128,128]{2,1,0:T(8,128)} copy(f32[128,128,128]{2,1,0:T(8,128)} %get-tuple-element.65) | data formatting | bytes 16777216 | tf_op jit(solution)/shard_map/cond
  177.7 40.9 %multiply_add_fusion.3 = f32[128,128,128]{2,1,0:T(8,128)} fusion(f32[128,128,128]{2,1,0:T(8,128)} %copy.116, f32[128,128,128]{2,1,0:T(8,128)} %get-tuple-element.70, f32[128,129,128]{2,1,0:T(8,128)} %get-tuple-element.69, f32[128,129,128]{2,1,0:T(8,128)} %get-tuple-element.68, f32[128,128,128]{2,1,0:T(8,128)} %get-tuple-element.66, ...), kind=kOutput, calls=%fused_computation.7 | convolution fusion | flops 3254779904 | bytes 109117440 | tf_op jit(solution)/shard_map/cond/branch_0_fun/rck,kj->rcj/dot_general | solution.py:35
  218.6 9.4 %fusion.3 = f32[8,128,128]{2,0,1:T(8,128)S(1)} fusion(f32[8,128,128]{2,0,1:T(8,128)S(1)} %get-tuple-element.72, f32[128,128,128]{2,1,0:T(8,128)} %multiply_add_fusion.3, f32[128,8]{0,1:T(8,128)S(1)} %get-tuple-element.73), kind=kOutput, calls=%fused_computation.10 | convolution fusion | flops 201457664 | bytes 9441280 | tf_op jit(solution)/shard_map/cond/branch_0_fun/rck,kf->frc/dot_general | solution.py:107
  232.2 9.5 %all-to-all-start = ((s32[8,4,8]{2,0,1:T(8,128)}), s32[8,4,8]{2,0,1:T(8,128)S(1)}, u32[]{:S(2)}, u32[]{:S(2)}) async-start(s32[8,4,8]{2,0,1:T(8,128)} %copy.61), calls=%async_computation | async-start | bytes 32768 | tf_op jit(solution)/shard_map/all_to_all | solution.py:155
  246.3 3.8 collective-permute-done.17
  254.5 4.5 %all-to-all-start.1 = ((bf16[8,4,8,1024]{3,2,0,1:T(8,128)(2,1)}), bf16[8,4,8,1024]{3,2,0,1:T(8,128)(2,1)S(1)}, u32[]{:S(2)}, u32[]{:S(2)}) async-start(bf16[8,4,8,1024]{3,2,0,1:T(8,128)(2,1)} %bitcast_dynamic-update-slice_fusion), calls=%async_computation.1 | async-start | bytes 1048576 | tf_op jit(solution)/shard_map/all_to_all | solution.py:154
  259.5 6.4 %all-to-all-done.1 = bf16[8,4,8,1024]{3,2,0,1:T(8,128)(2,1)S(1)} async-done(((bf16[8,4,8,1024]{3,2,0,1:T(8,128)(2,1)}), bf16[8,4,8,1024]{3,2,0,1:T(8,128)(2,1)S(1)}, u32[]{:S(2)}, u32[]{:S(2)}) %all-to-all-start.1) | async-done | bytes 524320 | tf_op jit(solution)/shard_map/all_to_all | solution.py:154
  268.6 8.3 %convolution_bitcast_fusion.2 = f32[8,128,128]{2,1,0:T(8,128)} fusion(f32[32,128,8,128]{3,1,0,2:T(8,128)S(1)} %fusion.17, bf16[32,128,128]{2,1,0:T(8,128)(2,1)S(1)} %copy-done), kind=kOutput, calls=%fused_computation.41 | convolution fusion | flops 6442450944 | bytes 18350080 | tf_op jit(solution)/shard_map/wdfa,wab->fdb/dot_general | solution.py:170
  277.0 41.5 %all-reduce.2.cloned.1.call-done = f32[8,128,128]{2,1,0:T(8,128)} async-done(((f32[8,128,128]{2,1,0:T(8,128)}), f32[8,128,128]{2,1,0:T(8,128)}) %all-reduce.2.cloned.1.call-update) | async-done | bytes 524304 | tf_op jit(solution)/shard_map/psum | solution.py:171
  320.6 5.9 %copy.79 = f32[128,128,1]{1,0,2:T(8,128)} copy(f32[128,128,1]{2,1,0:T(8,128)} %bitcast.105) | data formatting | bytes 131072
  326.5 104.1 %all-gather.3.cloned.1.call-done = f32[16384,128,1]{1,0,2:T(8,128)} async-done(((f32[128,128,1]{1,0,2:T(8,128)}), f32[16384,128,1]{1,0,2:T(8,128)}) %all-gather.3.cloned.1.call-update) | async-done | bytes 8388624 | tf_op jit(solution)/shard_map/all_gather | solution.py:187
  433.1 5.0 %select_reduce_fusion = f32[256,128]{1,0:T(8,128)S(1)} fusion(bf16[32,128,128]{2,1,0:T(8,128)(2,1)S(1)} %copy-done, pred[256,32]{0,1:T(8,128)(4,1)S(1)} %iota_compare_fusion.2, f32[256,128]{1,0:T(8,128)S(1)} %gather_fusion, pred[256]{0:T(512)(128)(4,1)S(1)} %get-tuple-element.130), kind=kOutput, calls=%fused_computation.33 | convolution fusion | flops 1612709888 | bytes 1319168 | tf_op jit(solution)/shard_map/eb,wab->ewa/dot_general | solution.py:190
  (125 shorter events, 48.4 us)
Async XLA Ops:
  7.2 261.4 %copy-start = (bf16[32,128,128]{2,1,0:T(8,128)(2,1)S(1)}, bf16[32,128,128]{2,1,0:T(8,128)(2,1)}, u32[]{:S(2)}) copy-start(bf16[32,128,128]{2,1,0:T(8,128)(2,1)} %param.22) | copy-start | bytes 3145732
  21.5 55.8 %collective-permute-start = (bf16[1,128,128]{2,1,0:T(8,128)(2,1)S(1)}, bf16[1,128,128]{2,1,0:T(8,128)(2,1)S(1)}, u32[]{:S(2)}, u32[]{:S(2)}) collective-permute-start(bf16[1,128,128]{2,1,0:T(8,128)(2,1)S(1)} %get-tuple-element.148), channel_id=1, source_target_pairs={{0,8},{8,16},{16,24},{24,32},{32,40},{40,48},{48,56},{56,64},{64,7... | collective-permute-start | bytes 98312 | tf_op jit(solution)/shard_map/ppermute | solution.py:18
  25.9 51.5 %collective-permute-start.1 = (bf16[1,128,128]{2,1,0:T(8,128)(2,1)S(1)}, bf16[1,128,128]{2,1,0:T(8,128)(2,1)S(1)}, u32[]{:S(2)}, u32[]{:S(2)}) collective-permute-start(bf16[1,128,128]{2,1,0:T(8,128)(2,1)S(1)} %get-tuple-element.149), channel_id=1, source_target_pairs={{8,0},{16,8},{24,16},{32,24},{40,32},{48,40},{56,48},{64,56},{72,6... | collective-permute-start | bytes 98312 | tf_op jit(solution)/shard_map/ppermute | solution.py:19
  28.5 48.9 %collective-permute-start.2 = (f32[128,1,128]{2,1,0:T(1,128)S(1)}, f32[128,1,128]{2,1,0:T(1,128)S(1)}, u32[]{:S(2)}, u32[]{:S(2)}) collective-permute-start(f32[128,1,128]{2,1,0:T(1,128)S(1)} %get-tuple-element.140), channel_id=1, source_target_pairs={{0,1},{1,2},{2,3},{3,4},{4,5},{5,6},{6,7},{7,0},{8,9},{9,10},{10,1... | collective-permute-start | bytes 196616 | tf_op jit(solution)/shard_map/ppermute | solution.py:18
  30.6 46.8 %collective-permute-start.3 = (f32[128,1,128]{2,1,0:T(1,128)S(1)}, f32[128,1,128]{2,1,0:T(1,128)S(1)}, u32[]{:S(2)}, u32[]{:S(2)}) collective-permute-start(f32[128,1,128]{2,1,0:T(1,128)S(1)} %get-tuple-element.141), channel_id=1, source_target_pairs={{1,0},{2,1},{3,2},{4,3},{5,4},{6,5},{7,6},{0,7},{9,8},{10,9},{11,1... | collective-permute-start | bytes 196616 | tf_op jit(solution)/shard_map/ppermute | solution.py:19
  31.4 12.9 %collective-permute-start.8 = (s32[32]{0:T(128)S(1)}, s32[32]{0:T(128)S(1)}, u32[]{:S(2)}, u32[]{:S(2)}) collective-permute-start(s32[32]{0:T(128)S(1)} %get-tuple-element.167), channel_id=1, source_target_pairs={{0,31},{1,0},{2,1},{3,2},{4,3},{5,4},{6,5},{7,6},{8,7},{9,8},{10,9... | collective-permute-start | bytes 392 | tf_op jit(solution)/shard_map/ppermute | solution.py:27
  44.3 4.8 %collective-permute-start.9 = (s32[32]{0:T(128)S(1)}, s32[32]{0:T(128)S(1)}, u32[]{:S(2)}, u32[]{:S(2)}) collective-permute-start(s32[32]{0:T(128)S(1)} %get-tuple-element.165), channel_id=1, source_target_pairs={{0,1},{1,2},{2,3},{3,4},{4,5},{5,6},{6,7},{7,8},{8,9},{9,10},{10,1... | collective-permute-start | bytes 392 | tf_op jit(solution)/shard_map/ppermute | solution.py:27
  49.2 5.7 %collective-permute-start.10 = (s32[32]{0:T(128)S(1)}, s32[32]{0:T(128)S(1)}, u32[]{:S(2)}, u32[]{:S(2)}) collective-permute-start(s32[32]{0:T(128)S(1)} %get-tuple-element.164), channel_id=1, source_target_pairs={{0,2},{1,3},{2,4},{3,5},{4,6},{5,7},{6,8},{7,9},{8,10},{9,11},{10,... | collective-permute-start | bytes 392 | tf_op jit(solution)/shard_map/ppermute | solution.py:27
  54.9 5.1 %collective-permute-start.11 = (s32[32]{0:T(128)S(1)}, s32[32]{0:T(128)S(1)}, u32[]{:S(2)}, u32[]{:S(2)}) collective-permute-start(s32[32]{0:T(128)S(1)} %get-tuple-element.163), channel_id=1, source_target_pairs={{0,7},{1,8},{2,9},{3,10},{4,11},{5,12},{6,13},{7,14},{8,15},{9,16}... | collective-permute-start | bytes 392 | tf_op jit(solution)/shard_map/ppermute | solution.py:27
  60.0 6.0 %collective-permute-start.12 = (s32[32]{0:T(128)S(1)}, s32[32]{0:T(128)S(1)}, u32[]{:S(2)}, u32[]{:S(2)}) collective-permute-start(s32[32]{0:T(128)S(1)} %get-tuple-element.162), channel_id=1, source_target_pairs={{0,8},{1,9},{2,10},{3,11},{4,12},{5,13},{6,14},{7,15},{8,16},{9,17... | collective-permute-start | bytes 392 | tf_op jit(solution)/shard_map/ppermute | solution.py:27
  65.9 5.3 %collective-permute-start.13 = (s32[32]{0:T(128)S(1)}, s32[32]{0:T(128)S(1)}, u32[]{:S(2)}, u32[]{:S(2)}) collective-permute-start(s32[32]{0:T(128)S(1)} %get-tuple-element.161), channel_id=1, source_target_pairs={{0,9},{1,10},{2,11},{3,12},{4,13},{5,14},{6,15},{7,16},{8,17},{9,1... | collective-permute-start | bytes 392 | tf_op jit(solution)/shard_map/ppermute | solution.py:27
  71.2 6.0 %collective-permute-start.14 = (s32[32]{0:T(128)S(1)}, s32[32]{0:T(128)S(1)}, u32[]{:S(2)}, u32[]{:S(2)}) collective-permute-start(s32[32]{0:T(128)S(1)} %get-tuple-element.160), channel_id=1, source_target_pairs={{0,10},{1,11},{2,12},{3,13},{4,14},{5,15},{6,16},{7,17},{8,18},{9,... | collective-permute-start | bytes 392 | tf_op jit(solution)/shard_map/ppermute | solution.py:27
  77.4 18.3 %copy-start.5 = (f32[128,128]{1,0:T(8,128)S(1)}, f32[128,128]{1,0:T(8,128)}, u32[]{:S(2)}) copy-start(f32[128,128]{1,0:T(8,128)} %param.18) | copy-start | bytes 196612
  134.3 11.7 %collective-permute-start.4 = (bf16[1,128,128]{2,1,0:T(8,128)(2,1)S(1)}, bf16[1,128,128]{2,1,0:T(8,128)(2,1)S(1)}, u32[]{:S(2)}, u32[]{:S(2)}) collective-permute-start(bf16[1,128,128]{2,1,0:T(8,128)(2,1)S(1)} %get-tuple-element.146), channel_id=1, source_target_pairs={{0,8},{8,16},{16,24},{24,32},{32,40},{40,48},{48,56},{56,64},{64,7... | collective-permute-start | bytes 98312 | tf_op jit(solution)/shard_map/ppermute | solution.py:18
  138.1 7.8 %collective-permute-start.5 = (bf16[1,128,128]{2,1,0:T(8,128)(2,1)S(1)}, bf16[1,128,128]{2,1,0:T(8,128)(2,1)S(1)}, u32[]{:S(2)}, u32[]{:S(2)}) collective-permute-start(bf16[1,128,128]{2,1,0:T(8,128)(2,1)S(1)} %get-tuple-element.147), channel_id=1, source_target_pairs={{8,0},{16,8},{24,16},{32,24},{40,32},{48,40},{56,48},{64,56},{72,6... | collective-permute-start | bytes 98312 | tf_op jit(solution)/shard_map/ppermute | solution.py:19
  141.4 11.4 %collective-permute-start.6 = (f32[128,1,128]{2,1,0:T(1,128)}, f32[128,1,128]{2,1,0:T(1,128)}, u32[]{:S(2)}, u32[]{:S(2)}) collective-permute-start(f32[128,1,128]{2,1,0:T(1,128)} %get-tuple-element.135), channel_id=1, source_target_pairs={{0,1},{1,2},{2,3},{3,4},{4,5},{5,6},{6,7},{7,0},{8,9},{9,10},{10,1... | collective-permute-start | bytes 196616 | tf_op jit(solution)/shard_map/ppermute | solution.py:18
  144.0 8.8 %collective-permute-start.7 = (f32[128,1,128]{2,1,0:T(1,128)}, f32[128,1,128]{2,1,0:T(1,128)}, u32[]{:S(2)}, u32[]{:S(2)}) collective-permute-start(f32[128,1,128]{2,1,0:T(1,128)} %get-tuple-element.134), channel_id=1, source_target_pairs={{1,0},{2,1},{3,2},{4,3},{5,4},{6,5},{7,6},{0,7},{9,8},{10,9},{11,1... | collective-permute-start | bytes 196616 | tf_op jit(solution)/shard_map/ppermute | solution.py:19
  228.6 14.6 %collective-permute-start.15 = (bf16[32,1024]{1,0:T(8,128)(2,1)S(1)}, bf16[32,1024]{1,0:T(8,128)(2,1)S(1)}, u32[]{:S(2)}, u32[]{:S(2)}) collective-permute-start(bf16[32,1024]{1,0:T(8,128)(2,1)S(1)} %get-tuple-element.156), channel_id=1, source_target_pairs={{0,31},{1,0},{2,1},{3,2},{4,3},{5,4},{6,5},{7,6},{8,7},{9,8},{10,9... | collective-permute-start | bytes 196616 | tf_op jit(solution)/shard_map/ppermute | solution.py:27
  232.2 22.2 %all-to-all-start = ((s32[8,4,8]{2,0,1:T(8,128)}), s32[8,4,8]{2,0,1:T(8,128)S(1)}, u32[]{:S(2)}, u32[]{:S(2)}) async-start(s32[8,4,8]{2,0,1:T(8,128)} %copy.61), calls=%async_computation | async-start | bytes 32768 | tf_op jit(solution)/shard_map/all_to_all | solution.py:155
  241.8 3.8 collective-permute-start.16
  241.8 8.3 %collective-permute-start.17 = (bf16[32,1024]{1,0:T(8,128)(2,1)S(1)}, bf16[32,1024]{1,0:T(8,128)(2,1)S(1)}, u32[]{:S(2)}, u32[]{:S(2)}) collective-permute-start(bf16[32,1024]{1,0:T(8,128)(2,1)S(1)} %get-tuple-element.154), channel_id=1, source_target_pairs={{0,2},{1,3},{2,4},{3,5},{4,6},{5,7},{6,8},{7,9},{8,10},{9,11},{10,... | collective-permute-start | bytes 196616 | tf_op jit(solution)/shard_map/ppermute | solution.py:27
  241.8 8.9 %collective-permute-start.18 = (bf16[32,1024]{1,0:T(8,128)(2,1)S(1)}, bf16[32,1024]{1,0:T(8,128)(2,1)S(1)}, u32[]{:S(2)}, u32[]{:S(2)}) collective-permute-start(bf16[32,1024]{1,0:T(8,128)(2,1)S(1)} %get-tuple-element.153), channel_id=1, source_target_pairs={{0,7},{1,8},{2,9},{3,10},{4,11},{5,12},{6,13},{7,14},{8,15},{9,16}... | collective-permute-start | bytes 196616 | tf_op jit(solution)/shard_map/ppermute | solution.py:27
  243.2 8.1 %collective-permute-start.19 = (bf16[32,1024]{1,0:T(8,128)(2,1)S(1)}, bf16[32,1024]{1,0:T(8,128)(2,1)S(1)}, u32[]{:S(2)}, u32[]{:S(2)}) collective-permute-start(bf16[32,1024]{1,0:T(8,128)(2,1)S(1)} %get-tuple-element.152), channel_id=1, source_target_pairs={{0,8},{1,9},{2,10},{3,11},{4,12},{5,13},{6,14},{7,15},{8,16},{9,17... | collective-permute-start | bytes 196616 | tf_op jit(solution)/shard_map/ppermute | solution.py:27
  243.2 8.8 %collective-permute-start.20 = (bf16[32,1024]{1,0:T(8,128)(2,1)S(1)}, bf16[32,1024]{1,0:T(8,128)(2,1)S(1)}, u32[]{:S(2)}, u32[]{:S(2)}) collective-permute-start(bf16[32,1024]{1,0:T(8,128)(2,1)S(1)} %get-tuple-element.151), channel_id=1, source_target_pairs={{0,9},{1,10},{2,11},{3,12},{4,13},{5,14},{6,15},{7,16},{8,17},{9,1... | collective-permute-start | bytes 196616 | tf_op jit(solution)/shard_map/ppermute | solution.py:27
  245.6 8.2 %collective-permute-start.21 = (bf16[32,1024]{1,0:T(8,128)(2,1)S(1)}, bf16[32,1024]{1,0:T(8,128)(2,1)S(1)}, u32[]{:S(2)}, u32[]{:S(2)}) collective-permute-start(bf16[32,1024]{1,0:T(8,128)(2,1)S(1)} %get-tuple-element.150), channel_id=1, source_target_pairs={{0,10},{1,11},{2,12},{3,13},{4,14},{5,15},{6,16},{7,17},{8,18},{9,... | collective-permute-start | bytes 196616 | tf_op jit(solution)/shard_map/ppermute | solution.py:27
  254.5 11.5 %all-to-all-start.1 = ((bf16[8,4,8,1024]{3,2,0,1:T(8,128)(2,1)}), bf16[8,4,8,1024]{3,2,0,1:T(8,128)(2,1)S(1)}, u32[]{:S(2)}, u32[]{:S(2)}) async-start(bf16[8,4,8,1024]{3,2,0,1:T(8,128)(2,1)} %bitcast_dynamic-update-slice_fusion), calls=%async_computation.1 | async-start | bytes 1048576 | tf_op jit(solution)/shard_map/all_to_all | solution.py:154
  259.0 59.4 %all-reduce.2.cloned.1.call-start = ((), (), s32[]{:S(2)}) async-start(), calls=%async_computation.2 | async-start | bytes 1048576 | tf_op jit(solution)/shard_map/psum | solution.py:171
  268.6 49.9 %copy-start.7 = (f32[128,128]{1,0:T(8,128)S(1)}, f32[128,128]{1,0:T(8,128)}, u32[]{:S(2)}) copy-start(f32[128,128]{1,0:T(8,128)} %param.19) | copy-start | bytes 196612
  268.6 49.9 %copy-start.9 = (f32[8,128]{1,0:T(8,128)S(1)}, f32[8,128]{1,0:T(8,128)}, u32[]{:S(2)}) copy-start(f32[8,128]{1,0:T(8,128)} %param.21) | copy-start | bytes 12292
  276.9 153.7 %all-gather.3.cloned.1.call-start = ((), (), s32[]{:S(2)}) async-start(), calls=%async_computation.3 | async-start | bytes 8454144 | tf_op jit(solution)/shard_map/all_gather | solution.py:187
  320.6 117.7 %copy-start.4 = (s32[128,128]{1,0:T(8,128)S(1)}, s32[128,128]{1,0:T(8,128)}, u32[]{:S(2)}) copy-start(s32[128,128]{1,0:T(8,128)} %param.16) | copy-start | bytes 196612
  326.4 111.9 %copy-start.2 = (f32[128,128,1]{1,0,2:T(8,128)S(1)}, f32[128,128,1]{1,0,2:T(8,128)}, u32[]{:S(2)}) copy-start(f32[128,128,1]{1,0,2:T(8,128)} %copy.79) | copy-start | bytes 196612
  (6 other events, 68.6 us)
Sparse Core Ops, SparseCore 0:
  277.0 41.3 all-reduce.1
  326.6 104.0 all-gather.2
where the time goes:
time: 453 us; the launch traced here: 446 us
  waiting for transfers between devices  187 us (41%)
  matrix products  90.1 us (20%)
  local copies, waits for them, and re-layouts  61.9 us (14%)
  other arithmetic  47.9 us (11%)
  starting transfers between devices  42.3 us (9%)
  between operations  14.7 us (3%)
    all_gather x1, waiting for transfers between devices, local(): lax.all_gather(surface, ('comp', 'lat', 'lon'), axis=0, tiled=True)  104 us
    dot_general x2, matrix products, column_physics(): jnp.einsum('rck,kj->rcj', values, mixing, precision=HIGHEST)  55.3 us
    psum x1, waiting for transfers between devices, local(): forcing = lax.psum(partial_forcing, 'comp')  41.5 us
    ppermute x14, waiting for transfers between devices, from_behind(): return lax.ppermute(value, axis, pairs)  34.5 us
    unnamed x41, local copies, waits for them, and re-layouts  20.5 us
    dot_general x2, matrix products, advance(): jnp.einsum('rck,kf->frc', moved, flux_map, precision=HIGHEST)  18.8 us
    sub x1, other arithmetic, local(): spread = below + above + sides[:, :-2] + sides[:, 2:] - 4.0 * current  18.3 us
    slice x2, local copies, waits for them, and re-layouts, local(): current[1:]  17.7 us
  transfers between devices with their start and end apart: 26, of which 12 were waited for; matrix products, arithmetic and copies ran while one was open for 6% of the time, Pallas kernels for 0%

commit v1 on v0

--- a/solution.py
+++ b/solution.py
@@ -6,19 +6,6 @@
 SMOOTHING = 0.2
 PHYSICS = 0.5
 HIGHEST = lax.Precision.HIGHEST
-
-
-def with_halo(shard, sides, width, wrap):
-    for axis, dim in sides:
-        size, length = (lax.axis_size(axis), shard.shape[dim])
-        up = [(i, (i + 1) % size) for i in range(size if wrap else size - 1)]
-        down = [(j, i) for i, j in up]
-        last = lax.slice_in_dim(shard, length - width, length, axis=dim)
-        leading = lax.slice_in_dim(shard, 0, width, axis=dim)
-        before = lax.ppermute(last, axis, up)
-        after = lax.ppermute(leading, axis, down)
-        shard = jnp.concatenate([before, shard, after], axis=dim)
-    return shard
 
 
 def from_behind(value, axis, steps):
@@ -58,6 +45,40 @@
         packed.reshape(owner_total, slots_each, blocks.shape[1]),
         placed_labels.reshape(owner_total, slots_each),
     )
+
+
+def edge_rows(values, lower_valid, upper_valid):
+    bands = lax.axis_size("comp") * lax.axis_size("lat")
+    up = [(i, i + 1) for i in range(bands - 1)]
+    down = [(j, i) for i, j in up]
+    before = lax.ppermute(values[-1:], ("comp", "lat"), up)
+    after = lax.ppermute(values[:1], ("comp", "lat"), down)
+    return (jnp.where(lower_valid, before, 0.0), jnp.where(upper_valid, after, 0.0))
+
+
+def edge_columns(values):
+    size = lax.axis_size("lon")
+    up = [(i, (i + 1) % size) for i in range(size)]
+    down = [(j, i) for i, j in up]
+    before = lax.ppermute(values[:, -1:], "lon", up)
+    after = lax.ppermute(values[:, :1], "lon", down)
+    return before, after
+
+
+def laplace_local(values, lower_valid, upper_valid):
+    top, bottom = edge_rows(values, lower_valid, upper_valid)
+    left, right = edge_columns(values)
+    up = jnp.concatenate([top, values[:-1]], axis=0)
+    down = jnp.concatenate([values[1:], bottom], axis=0)
+    west = jnp.concatenate([left, values[:, :-1]], axis=1)
+    east = jnp.concatenate([values[:, 1:], right], axis=1)
+    return up + down + west + east - 4.0 * values
+
+
+def physics_step(values, spread, mixing):
+    smooth = values + SMOOTHING * spread
+    mixed = jnp.einsum("rck,kj->rcj", smooth, mixing, precision=lax.Precision.HIGH)
+    return smooth + PHYSICS * jnp.tanh(mixed)
 
 
 def local(
@@ -86,31 +107,26 @@
         (band + 1 >= ocean_band) == (band >= ocean_band)
     )
     sea_cells = land_mask == 1
-    current = state
-    flux_total = jnp.zeros((flux_count, tile_rows, block_len), jnp.float32)
-    ocean_spread = None
-    for substep in range(2):
-        padded = with_halo(current.astype(jnp.bfloat16), ((("comp", "lat"), 0),), 1, False).astype(
-            current.dtype
-        )
-        below = jnp.concatenate([jnp.where(lower_valid, padded[:1], 0.0), current[:-1]], axis=0)
-        above = jnp.concatenate([current[1:], jnp.where(upper_valid, padded[-1:], 0.0)], axis=0)
-        sides = with_halo(current, (("lon", 1),), 1, True)
-        spread = below + above + sides[:, :-2] + sides[:, 2:] - 4.0 * current
-        if substep == 0:
-            ocean_spread = spread
-
-        def advance(operands):
-            values, spread_now, total = operands
-            smooth = values + SMOOTHING * spread_now
-            moved = smooth + PHYSICS * column_physics(smooth, mix_atm)
-            return (moved, total + jnp.einsum("rck,kf->frc", moved, flux_map, precision=HIGHEST))
-
-        def resting(operands):
-            return (operands[0], operands[2])
-
-        current, flux_total = lax.cond(ocean_side, resting, advance, (current, spread, flux_total))
-    flux_sent = jnp.where(sea_cells[None], 0.5 * flux_total, 0.0).astype(jnp.bfloat16)
+
+    spread = laplace_local(state, lower_valid, upper_valid)
+    first = lax.cond(
+        ocean_side,
+        lambda v, s: physics_step(v, s, mix_ocn),
+        lambda v, s: physics_step(v, s, mix_atm),
+        state,
+        spread,
+    )
+    spread_next = laplace_local(first, lower_valid, upper_valid)
+
+    def atmosphere_second(values, spread_now):
+        moved = physics_step(values, spread_now, mix_atm)
+        total = jnp.einsum("rck,kf->frc", values + moved, flux_map, precision=HIGHEST)
+        return moved, jnp.where(sea_cells[None], 0.5 * total, 0.0).astype(jnp.bfloat16)
+
+    def ocean_second(values, spread_now):
+        return values, jnp.zeros((flux_count, tile_rows, block_len), jnp.bfloat16)
+
+    second, flux_sent = lax.cond(ocean_side, ocean_second, atmosphere_second, first, spread_next)
     entry_list = intersection_list.reshape(tile_rows * intersections, 3)
     owners = entry_list[:, 0]
     targets = entry_list[:, 1]
@@ -170,22 +186,14 @@
     partial_forcing = jnp.einsum("wdfa,wab->fdb", binned, weights_wide, precision=HIGHEST)
     forcing = lax.psum(partial_forcing, "comp")
 
-    def ocean_step(values):
-        smooth = values + SMOOTHING * ocean_spread
-        moved = (
-            smooth
-            + jnp.einsum("frc,fk->rck", forcing, ocean_map, precision=HIGHEST)
-            + PHYSICS * column_physics(smooth, mix_ocn)
-        )
-        return jnp.where(sea_cells[:, :, None], moved, values)
-
-    def unchanged(values):
-        return values
-
-    final_state = lax.cond(ocean_side, ocean_step, unchanged, current)
+    def ocean_final(values):
+        moved = values + jnp.einsum("frc,fk->rck", forcing, ocean_map, precision=HIGHEST)
+        return jnp.where(sea_cells[:, :, None], moved, state)
+
+    final_state = lax.cond(ocean_side, ocean_final, lambda values: values, second)
     surface = final_state[:, :, 0]
-    everything = lax.all_gather(surface, ("comp", "lat", "lon"), axis=0, tiled=True)
-    ocean_surface = everything[(comp_count - 1) * tile_count * tile_rows :]
+    ocean_only = lax.psum(jnp.where(ocean_side, surface, 0.0), "comp")
+    ocean_surface = lax.all_gather(ocean_only, ("lat", "lon"), axis=0, tiled=True)
     picked = jnp.take(ocean_surface, owners * tile_rows + targets, axis=0)
     images = jnp.einsum("eb,wab->ewa", picked, weights_wide, precision=HIGHEST)
     which_block = weight_ids[:, None] == jnp.arange(weight_count, dtype=jnp.int32)[None, :]

time: 453 us -> 423 us (0.934)
  matrix products: 90.1 us -> 72.6 us
  other arithmetic: 47.9 us -> 40.8 us
  waiting for transfers between devices: 187 us -> 181 us
    psum x0 -> x1, waiting for transfers between devices: none -> 62.6 us  [local(): ocean_only = lax.psum(jnp.where(ocean_side, surface, 0.0), 'comp')]
    all_gather x1, waiting for transfers between devices: 104 us -> 49.3 us  [local(): lax.all_gather(ocean_only, ('lat', 'lon'), axis=0, tiled=True)]
    slice x7 -> x8, local copies, waits for them, and re-layouts: 22.7 us -> 43.1 us  [the longest x2 21 us: laplace_local(): east = jnp.concatenate([values[:, 1:], right], axis=1)]
    dot_general x4 -> x3, matrix products: 74.1 us -> 56.7 us  [the longest x2 45.8 us: physics_step(): jnp.einsum('rck,kj->rcj', smooth, mixing, precision=lax.Precision.HIGH)]
    ppermute x14, waiting for transfers between devices: 34.5 us -> 20.7 us  [from_behind(): return lax.ppermute(value, axis, pairs)]
    cond x2 -> x0, local copies, waits for them, and re-layouts: 11.2 us -> none
    unnamed x41 -> x32, local copies, waits for them, and re-layouts: 20.5 us -> 10.6 us
    convert_element_type x2 -> x0, other arithmetic: 8.74 us -> none  [local(): current.astype(jnp.bfloat16)]
  transfers between devices with their start and end apart: 26 -> 27, of which waited for: 12 -> 10; matrix products, arithmetic and copies ran while one was open for 6% -> 12% of each run, Pallas kernels for 0% -> 0%
where the time goes in v1:
time: 423 us; the launch traced here: 415 us
  waiting for transfers between devices  181 us (43%)
  matrix products  72.6 us (17%)
  local copies, waits for them, and re-layouts  62.9 us (15%)
  starting transfers between devices  42 us (10%)
  other arithmetic  40.8 us (10%)
  between operations  14.4 us (3%)
    psum x1, waiting for transfers between devices, local(): ocean_only = lax.psum(jnp.where(ocean_side, surface, 0.0), 'comp')  62.6 us
    all_gather x1, waiting for transfers between devices, local(): lax.all_gather(ocean_only, ('lat', 'lon'), axis=0, tiled=True)  49.3 us
    dot_general x2, matrix products, physics_step(): jnp.einsum('rck,kj->rcj', smooth, mixing, precision=lax.Precision.HIGH)  45.8 us
    psum x1, waiting for transfers between devices, local(): forcing = lax.psum(partial_forcing, 'comp')  42.1 us
    slice x2, local copies, waits for them, and re-layouts, laplace_local(): east = jnp.concatenate([values[:, 1:], right], axis=1)  21 us
    ppermute x14, waiting for transfers between devices, from_behind(): return lax.ppermute(value, axis, pairs)  20.7 us
    slice x2, local copies, waits for them, and re-layouts, laplace_local(): down = jnp.concatenate([values[1:], bottom], axis=0)  17.7 us
    sub x1, other arithmetic, laplace_local(): return up + down + west + east - 4.0 * values  14.4 us
  transfers between devices with their start and end apart: 27, of which 10 were waited for; matrix products, arithmetic and copies ran while one was open for 12% of the time, Pallas kernels for 0%

profile of v1, /device:TPU:1, one launch (start us, length us, event | category | flops | bytes accessed | tf_op | source)
XLA Modules:
  0.0 414.7 jit_solution(8845678905374923356)
XLA Ops:
  9.5 5.0 %collective-permute-start = (f32[1,128,128]{2,1,0:T(8,128)S(1)}, f32[1,128,128]{2,1,0:T(8,128)S(1)}, u32[]{:S(2)}, u32[]{:S(2)}) collective-permute-start(f32[1,128,128]{2,1,0:T(8,128)S(1)} %get-tuple-element.139), channel_id=1, source_target_pairs={{0,8},{8,16},{16,24},{24,32},{32,40},{40,48},{48,56},{56,64},{64,7... | collective-permute-start | bytes 196616 | tf_op jit(solution)/shard_map/ppermute | solution.py:54
  21.9 13.2 %fusion.51 = (f32[128,127,128]{2,1,0:T(8,128)}, f32[128,127,128]{2,1,0:T(8,128)}) fusion(f32[128,128,128]{2,1,0:T(8,128)} %param.15), kind=kLoop, calls=%fused_computation.97 | loop fusion | bytes 33292288 | tf_op jit(solution)/shard_map/slice | solution.py:74
  35.1 6.6 %fusion.53 = (f32[127,128,128]{2,1,0:T(8,128)}, f32[127,128,128]{2,1,0:T(8,128)}) fusion(f32[128,128,128]{2,1,0:T(8,128)S(1)} %bitcast.96), kind=kLoop, calls=%fused_computation.99 | loop fusion | bytes 33292288 | tf_op jit(solution)/shard_map/slice | solution.py:72
  44.0 9.1 %collective-permute-done.10 = s32[32]{0:T(128)S(1)} collective-permute-done((s32[32]{0:T(128)S(1)}, s32[32]{0:T(128)S(1)}, u32[]{:S(2)}, u32[]{:S(2)}) %collective-permute-start.10) | collective-permute-done | bytes 160 | tf_op jit(solution)/shard_map/ppermute | solution.py:14
  53.3 3.3 collective-permute-done.12
  58.6 2.5 collective-permute-start.3
  62.9 14.4 %fusion.25 = f32[128,128,128]{2,1,0:T(8,128)S(1)} fusion(f32[127,128,128]{2,1,0:T(8,128)} %get-tuple-element.137, f32[1,128,128]{2,1,0:T(8,128)S(1)} %broadcast_select_fusion.3, f32[1,128,128]{2,1,0:T(8,128)S(1)} %broadcast_select_fusion.2, f32[127,128,128]{2,1,0:T(8,128)} %get-tuple-element.136, f32[128,127,128]{2,1,0:T(8,128)} %get-tuple-element.133, ...), kind=kLoop, calls=%fused_computation.26 | loop fusion | flops 18874368 | bytes 50331648 | tf_op jit(solution)/shard_map/sub | solution.py:75
  77.3 10.7 %conditional.3 = (f32[128,128,128]{2,1,0:T(8,128)}) conditional(s32[]{:T(128)} %convert_element_type.20, (f32[128,128,128]{2,1,0:T(8,128)S(1)}, f32[128,128,128]{2,1,0:T(8,128)}, f32[128,128]{1,0:T(8,128)S(1)}) %tuple.86, (f32[128,128,128]{2,1,0:T(8,128)S(1)}, f32[128,128,128]{2,1,0:T(8,128)}, f32[128,128]{1,0:T(8,128)S(1)}) %tuple.88), branch_computations={%region_0.1_spmd, %region_1.2_spmd} | conditional | flops 1623195648 | bytes 25231368 | solution.py:112
  77.3 10.2 %multiply_add_fusion = f32[128,128,128]{2,1,0:T(8,128)} fusion(f32[128,128,128]{2,1,0:T(8,128)} %get-tuple-element.60, f32[128,128,128]{2,1,0:T(8,128)S(1)} %get-tuple-element.61, f32[128,128]{1,0:T(8,128)S(1)} %get-tuple-element.62), kind=kOutput, calls=%fused_computation.1 | convolution fusion | flops 1623195648 | bytes 25231360 | tf_op jit(solution)/shard_map/cond/branch_0_fun/rck,kj->rcj/dot_general | solution.py:80
  88.0 7.8 %fusion.47 = (f32[128,127,128]{2,1,0:T(8,128)S(1)}, f32[128,127,128]{2,1,0:T(8,128)S(1)}) fusion(f32[128,128,128]{2,1,0:T(8,128)} %get-tuple-element.164), kind=kLoop, calls=%fused_computation.93 | loop fusion | bytes 33292288 | tf_op jit(solution)/shard_map/slice | solution.py:74
  96.6 11.1 %fusion.49 = (f32[127,128,128]{2,1,0:T(8,128)}, f32[127,128,128]{2,1,0:T(8,128)}) fusion(f32[128,128,128]{2,1,0:T(8,128)} %get-tuple-element.164), kind=kLoop, calls=%fused_computation.95 | loop fusion | bytes 33292288 | tf_op jit(solution)/shard_map/slice | solution.py:72
  110.3 3.6 collective-permute-start.7
  113.9 4.3 %collective-permute-start.4 = (f32[1,128,128]{2,1,0:T(8,128)S(1)}, f32[1,128,128]{2,1,0:T(8,128)S(1)}, u32[]{:S(2)}, u32[]{:S(2)}) collective-permute-start(f32[1,128,128]{2,1,0:T(8,128)S(1)} %get-tuple-element.131), channel_id=1, source_target_pairs={{0,8},{8,16},{16,24},{24,32},{32,40},{40,48},{48,56},{56,64},{64,7... | collective-permute-start | bytes 196616 | tf_op jit(solution)/shard_map/ppermute | solution.py:54
  118.2 7.7 %pad_maximum_fusion.1 = f32[128,128,128]{2,1,0:T(8,128)} fusion(f32[1,128,128]{2,1,0:T(8,128)S(1)} %broadcast_select_fusion, f32[127,128,128]{2,1,0:T(8,128)} %get-tuple-element.128), kind=kLoop, calls=%fused_computation.28 | loop fusion | flops 2097152 | bytes 16777216 | tf_op jit(solution)/shard_map/concatenate | solution.py:72
  126.0 7.8 %pad_maximum_fusion = f32[128,128,128]{2,1,0:T(8,128)} fusion(f32[127,128,128]{2,1,0:T(8,128)} %get-tuple-element.129, f32[1,128,128]{2,1,0:T(8,128)S(1)} %broadcast_select_fusion.1), kind=kLoop, calls=%fused_computation.27 | loop fusion | flops 2097152 | bytes 16777216 | tf_op jit(solution)/shard_map/concatenate | solution.py:71
  133.7 4.0 pad_maximum_fusion.3
  137.7 4.3 %pad_maximum_fusion.2 = f32[128,128,128]{2,1,0:T(8,128)} fusion(f32[128,127,128]{2,1,0:T(8,128)S(1)} %get-tuple-element.125, f32[128,1,128]{2,1,0:T(1,128)S(1)} %collective-permute-done.6), kind=kLoop, calls=%fused_computation.29 | loop fusion | flops 2097152 | bytes 16777216 | tf_op jit(solution)/shard_map/concatenate | solution.py:73
  142.0 4.3 %broadcast.122 = f32[128,128,128]{2,1,0:T(8,128)} broadcast(f32[]{:T(128)} %constant.79.clone.1), dimensions={} | broadcast | bytes 8388612 | tf_op jit(solution)/shard_map/broadcast.23
  146.4 46.5 %conditional.4 = (f32[128,128,128]{2,1,0:T(8,128)}, bf16[8,128,128]{2,0,1:T(8,128)(2,1)S(1)}) conditional(s32[]{:T(128)} %convert_element_type.20, (f32[128,128,128]{2,1,0:T(8,128)}, f32[128,128,128]{2,1,0:T(8,128)}, f32[128,128,128]{2,1,0:T(8,128)}, f32[128,128,128]{2,1,0:T(8,128)}, f32[128,128,128]{2,1,0:T(8,128)}, ...), branch_computations={%region_2.3_spmd, %region_3.4_spmd} | conditional | flops 1847984128 | bytes 75845648 | solution.py:129
  146.4 35.6 %multiply_add_fusion.6 = f32[128,128,128]{2,1,0:T(8,128)} fusion(f32[128,128,128]{2,1,0:T(8,128)} %get-tuple-element.66, f32[128,128,128]{2,1,0:T(8,128)} %get-tuple-element.71, f32[128,128,128]{2,1,0:T(8,128)} %get-tuple-element.70, f32[128,128,128]{2,1,0:T(8,128)} %get-tuple-element.69, f32[128,128,128]{2,1,0:T(8,128)} %get-tuple-element.67, ...), kind=kOutput, calls=%fused_computation.11 | convolution fusion | flops 1644167168 | bytes 58785792 | tf_op jit(solution)/shard_map/cond/branch_0_fun/rck,kj->rcj/dot_general | solution.py:80
  181.9 10.9 %fusion.15 = bf16[8,128,128]{2,0,1:T(8,128)(2,1)S(1)} fusion(f32[128,128,128]{2,1,0:T(8,128)} %get-tuple-element.66, f32[128,128,128]{2,1,0:T(8,128)} %multiply_add_fusion.6, pred[128,128]{1,0:T(8,128)(4,1)S(1)} %get-tuple-element.73, f32[128,8]{0,1:T(8,128)S(1)} %get-tuple-element.89), kind=kOutput, calls=%fused_computation.16 | convolution fusion | flops 203816960 | bytes 17059840 | tf_op jit(solution)/shard_map/cond/branch_0_fun/rck,kf->frc/dot_general | solution.py:123
  194.8 4.2 %all-to-all-start = ((s32[8,4,8]{2,0,1:T(8,128)}), s32[8,4,8]{2,0,1:T(8,128)S(1)}, u32[]{:S(2)}, u32[]{:S(2)}) async-start(s32[8,4,8]{2,0,1:T(8,128)} %copy.62), calls=%async_computation | async-start | bytes 32768 | tf_op jit(solution)/shard_map/all_to_all | solution.py:171
  200.2 3.0 collective-permute-start.18
  209.1 4.7 %collective-permute-done.17 = bf16[32,1024]{1,0:T(8,128)(2,1)S(1)} collective-permute-done((bf16[32,1024]{1,0:T(8,128)(2,1)S(1)}, bf16[32,1024]{1,0:T(8,128)(2,1)S(1)}, u32[]{:S(2)}, u32[]{:S(2)}) %collective-permute-start.17) | collective-permute-done | bytes 65568 | tf_op jit(solution)/shard_map/ppermute | solution.py:14
  217.3 4.5 %all-to-all-start.1 = ((bf16[8,4,8,1024]{3,2,0,1:T(8,128)(2,1)}), bf16[8,4,8,1024]{3,2,0,1:T(8,128)(2,1)S(1)}, u32[]{:S(2)}, u32[]{:S(2)}) async-start(bf16[8,4,8,1024]{3,2,0,1:T(8,128)(2,1)} %bitcast_dynamic-update-slice_fusion), calls=%async_computation.1 | async-start | bytes 1048576 | tf_op jit(solution)/shard_map/all_to_all | solution.py:170
  222.1 6.6 %all-to-all-done.1 = bf16[8,4,8,1024]{3,2,0,1:T(8,128)(2,1)S(1)} async-done(((bf16[8,4,8,1024]{3,2,0,1:T(8,128)(2,1)}), bf16[8,4,8,1024]{3,2,0,1:T(8,128)(2,1)S(1)}, u32[]{:S(2)}, u32[]{:S(2)}) %all-to-all-start.1) | async-done | bytes 524320 | tf_op jit(solution)/shard_map/all_to_all | solution.py:170
  231.4 8.3 %convolution_bitcast_fusion = f32[8,128,128]{2,1,0:T(8,128)} fusion(f32[32,128,8,128]{3,1,0,2:T(8,128)S(1)} %fusion.26, bf16[32,128,128]{2,1,0:T(8,128)(2,1)S(1)} %copy-done), kind=kOutput, calls=%fused_computation.38 | convolution fusion | flops 6442450944 | bytes 18350080 | tf_op jit(solution)/shard_map/wdfa,wab->fdb/dot_general | solution.py:186
  239.7 42.1 %all-reduce.3.cloned.1.call-done = f32[8,128,128]{2,1,0:T(8,128)} async-done(((f32[8,128,128]{2,1,0:T(8,128)}), f32[8,128,128]{2,1,0:T(8,128)}) %all-reduce.3.cloned.1.call-update) | async-done | bytes 524304 | tf_op jit(solution)/shard_map/psum | solution.py:187
  282.0 5.2 %copy.80 = f32[128,128,1]{1,0,2:T(8,128)S(1)} copy(f32[128,128,1]{2,1,0:T(8,128)} %bitcast.94) | data formatting | bytes 131072
  287.9 62.6 %all-reduce.5.cloned.1.call-done = f32[128,128]{1,0:T(8,128)} async-done(((f32[128,128]{1,0:T(8,128)}), f32[128,128]{1,0:T(8,128)}) %all-reduce.5.cloned.1.call-update) | async-done | bytes 65552 | tf_op jit(solution)/shard_map/psum | solution.py:195
  350.6 49.3 %all-gather.2.cloned.1.call-done = f32[4096,128]{1,0:T(8,128)} async-done(((f32[128,128]{1,0:T(8,128)}), f32[4096,128]{1,0:T(8,128)}) %all-gather.2.cloned.1.call-update) | async-done | bytes 2097168 | tf_op jit(solution)/shard_map/all_gather | solution.py:196
  402.2 5.0 %select_reduce_fusion = f32[256,128]{1,0:T(8,128)S(1)} fusion(bf16[32,128,128]{2,1,0:T(8,128)(2,1)S(1)} %copy-done, pred[256,32]{0,1:T(8,128)(4,1)S(1)} %iota_compare_fusion.2, f32[256,128]{1,0:T(8,128)S(1)} %gather_fusion, pred[256]{0:T(512)(128)(4,1)S(1)} %get-tuple-element.122), kind=kOutput, calls=%fused_computation.31 | convolution fusion | flops 1612709888 | bytes 1319168 | tf_op jit(solution)/shard_map/eb,wab->ewa/dot_general | solution.py:198
  (120 shorter events, 38.7 us)
Async XLA Ops:
  7.2 224.2 %copy-start = (bf16[32,128,128]{2,1,0:T(8,128)(2,1)S(1)}, bf16[32,128,128]{2,1,0:T(8,128)(2,1)}, u32[]{:S(2)}) copy-start(bf16[32,128,128]{2,1,0:T(8,128)(2,1)} %param.22) | copy-start | bytes 3145732
  8.2 54.6 %collective-permute-start.1 = (f32[1,128,128]{2,1,0:T(8,128)S(1)}, f32[1,128,128]{2,1,0:T(8,128)S(1)}, u32[]{:S(2)}, u32[]{:S(2)}) collective-permute-start(f32[1,128,128]{2,1,0:T(8,128)S(1)} %get-tuple-element.138), channel_id=1, source_target_pairs={{8,0},{16,8},{24,16},{32,24},{40,32},{48,40},{56,48},{64,56},{72,6... | collective-permute-start | bytes 196616 | tf_op jit(solution)/shard_map/ppermute | solution.py:55
  9.5 53.4 %collective-permute-start = (f32[1,128,128]{2,1,0:T(8,128)S(1)}, f32[1,128,128]{2,1,0:T(8,128)S(1)}, u32[]{:S(2)}, u32[]{:S(2)}) collective-permute-start(f32[1,128,128]{2,1,0:T(8,128)S(1)} %get-tuple-element.139), channel_id=1, source_target_pairs={{0,8},{8,16},{16,24},{24,32},{32,40},{40,48},{48,56},{56,64},{64,7... | collective-permute-start | bytes 196616 | tf_op jit(solution)/shard_map/ppermute | solution.py:54
  15.8 47.1 %collective-permute-start.2 = (f32[128,1,128]{2,1,0:T(1,128)S(1)}, f32[128,1,128]{2,1,0:T(1,128)S(1)}, u32[]{:S(2)}, u32[]{:S(2)}) collective-permute-start(f32[128,1,128]{2,1,0:T(1,128)S(1)} %get-tuple-element.135), channel_id=1, source_target_pairs={{0,1},{1,2},{2,3},{3,4},{4,5},{5,6},{6,7},{7,0},{8,9},{9,10},{10,1... | collective-permute-start | bytes 196616 | tf_op jit(solution)/shard_map/ppermute | solution.py:63
  20.1 21.7 %collective-permute-start.8 = (s32[32]{0:T(128)S(1)}, s32[32]{0:T(128)S(1)}, u32[]{:S(2)}, u32[]{:S(2)}) collective-permute-start(s32[32]{0:T(128)S(1)} %get-tuple-element.157), channel_id=1, source_target_pairs={{0,31},{1,0},{2,1},{3,2},{4,3},{5,4},{6,5},{7,6},{8,7},{9,8},{10,9... | collective-permute-start | bytes 392 | tf_op jit(solution)/shard_map/ppermute | solution.py:14
  20.1 14.9 %slice-start = ((s8[8388608]{0:T(1024)(128)(4,1)}), s8[4194304]{0:T(1024)(128)(4,1)S(1)}, s32[]{:S(2)}) async-start(s8[8388608]{0:T(1024)(128)(4,1)} %bitcast.95), calls=%async_computation.5 | async-start | bytes 8388608
  20.1 14.9 %slice-start.1 = ((s8[8388608]{0:T(1024)(128)(4,1)}), s8[4194304]{0:T(1024)(128)(4,1)S(1)}, s32[]{:S(2)}) async-start(s8[8388608]{0:T(1024)(128)(4,1)} %bitcast.95), calls=%async_computation.6 | async-start | bytes 8388608
  20.2 22.9 %collective-permute-start.9 = (s32[32]{0:T(128)S(1)}, s32[32]{0:T(128)S(1)}, u32[]{:S(2)}, u32[]{:S(2)}) collective-permute-start(s32[32]{0:T(128)S(1)} %get-tuple-element.155), channel_id=1, source_target_pairs={{0,1},{1,2},{2,3},{3,4},{4,5},{5,6},{6,7},{7,8},{8,9},{9,10},{10,1... | collective-permute-start | bytes 392 | tf_op jit(solution)/shard_map/ppermute | solution.py:14
  41.8 11.3 %collective-permute-start.10 = (s32[32]{0:T(128)S(1)}, s32[32]{0:T(128)S(1)}, u32[]{:S(2)}, u32[]{:S(2)}) collective-permute-start(s32[32]{0:T(128)S(1)} %get-tuple-element.154), channel_id=1, source_target_pairs={{0,2},{1,3},{2,4},{3,5},{4,6},{5,7},{6,8},{7,9},{8,10},{9,11},{10,... | collective-permute-start | bytes 392 | tf_op jit(solution)/shard_map/ppermute | solution.py:14
  43.1 10.1 %collective-permute-start.11 = (s32[32]{0:T(128)S(1)}, s32[32]{0:T(128)S(1)}, u32[]{:S(2)}, u32[]{:S(2)}) collective-permute-start(s32[32]{0:T(128)S(1)} %get-tuple-element.153), channel_id=1, source_target_pairs={{0,7},{1,8},{2,9},{3,10},{4,11},{5,12},{6,13},{7,14},{8,15},{9,16}... | collective-permute-start | bytes 392 | tf_op jit(solution)/shard_map/ppermute | solution.py:14
  53.1 3.6 collective-permute-start.12
  53.2 5.4 %collective-permute-start.13 = (s32[32]{0:T(128)S(1)}, s32[32]{0:T(128)S(1)}, u32[]{:S(2)}, u32[]{:S(2)}) collective-permute-start(s32[32]{0:T(128)S(1)} %get-tuple-element.151), channel_id=1, source_target_pairs={{0,9},{1,10},{2,11},{3,12},{4,13},{5,14},{6,15},{7,16},{8,17},{9,1... | collective-permute-start | bytes 392 | tf_op jit(solution)/shard_map/ppermute | solution.py:14
  56.7 6.0 %collective-permute-start.14 = (s32[32]{0:T(128)S(1)}, s32[32]{0:T(128)S(1)}, u32[]{:S(2)}, u32[]{:S(2)}) collective-permute-start(s32[32]{0:T(128)S(1)} %get-tuple-element.150), channel_id=1, source_target_pairs={{0,10},{1,11},{2,12},{3,13},{4,14},{5,15},{6,16},{7,17},{8,18},{9,... | collective-permute-start | bytes 392 | tf_op jit(solution)/shard_map/ppermute | solution.py:14
  58.6 4.3 %collective-permute-start.3 = (f32[128,1,128]{2,1,0:T(1,128)S(1)}, f32[128,1,128]{2,1,0:T(1,128)S(1)}, u32[]{:S(2)}, u32[]{:S(2)}) collective-permute-start(f32[128,1,128]{2,1,0:T(1,128)S(1)} %get-tuple-element.134), channel_id=1, source_target_pairs={{1,0},{2,1},{3,2},{4,3},{5,4},{6,5},{7,6},{0,7},{9,8},{10,9},{11,1... | collective-permute-start | bytes 196616 | tf_op jit(solution)/shard_map/ppermute | solution.py:64
  62.9 14.4 %copy-start.2 = (f32[128,128]{1,0:T(8,128)S(1)}, f32[128,128]{1,0:T(8,128)}, u32[]{:S(2)}) copy-start(f32[128,128]{1,0:T(8,128)} %param.18) | copy-start | bytes 196612
  107.7 10.4 %collective-permute-start.5 = (f32[1,128,128]{2,1,0:T(8,128)S(1)}, f32[1,128,128]{2,1,0:T(8,128)S(1)}, u32[]{:S(2)}, u32[]{:S(2)}) collective-permute-start(f32[1,128,128]{2,1,0:T(8,128)S(1)} %get-tuple-element.130), channel_id=1, source_target_pairs={{8,0},{16,8},{24,16},{32,24},{40,32},{48,40},{56,48},{64,56},{72,6... | collective-permute-start | bytes 196616 | tf_op jit(solution)/shard_map/ppermute | solution.py:55
  110.3 23.4 %collective-permute-start.7 = (f32[128,1,128]{2,1,0:T(1,128)S(1)}, f32[128,1,128]{2,1,0:T(1,128)S(1)}, u32[]{:S(2)}, u32[]{:S(2)}) collective-permute-start(f32[128,1,128]{2,1,0:T(1,128)S(1)} %get-tuple-element.126), channel_id=1, source_target_pairs={{1,0},{2,1},{3,2},{4,3},{5,4},{6,5},{7,6},{0,7},{9,8},{10,9},{11,1... | collective-permute-start | bytes 196616 | tf_op jit(solution)/shard_map/ppermute | solution.py:64
  113.9 23.8 %collective-permute-start.6 = (f32[128,1,128]{2,1,0:T(1,128)S(1)}, f32[128,1,128]{2,1,0:T(1,128)S(1)}, u32[]{:S(2)}, u32[]{:S(2)}) collective-permute-start(f32[128,1,128]{2,1,0:T(1,128)S(1)} %get-tuple-element.127), channel_id=1, source_target_pairs={{0,1},{1,2},{2,3},{3,4},{4,5},{5,6},{6,7},{7,0},{8,9},{9,10},{10,1... | collective-permute-start | bytes 196616 | tf_op jit(solution)/shard_map/ppermute | solution.py:63
  113.9 12.0 %collective-permute-start.4 = (f32[1,128,128]{2,1,0:T(8,128)S(1)}, f32[1,128,128]{2,1,0:T(8,128)S(1)}, u32[]{:S(2)}, u32[]{:S(2)}) collective-permute-start(f32[1,128,128]{2,1,0:T(8,128)S(1)} %get-tuple-element.131), channel_id=1, source_target_pairs={{0,8},{8,16},{16,24},{24,32},{32,40},{40,48},{48,56},{56,64},{64,7... | collective-permute-start | bytes 196616 | tf_op jit(solution)/shard_map/ppermute | solution.py:54
  193.3 9.9 %collective-permute-start.15 = (bf16[32,1024]{1,0:T(8,128)(2,1)S(1)}, bf16[32,1024]{1,0:T(8,128)(2,1)S(1)}, u32[]{:S(2)}, u32[]{:S(2)}) collective-permute-start(bf16[32,1024]{1,0:T(8,128)(2,1)S(1)} %get-tuple-element.146), channel_id=1, source_target_pairs={{0,31},{1,0},{2,1},{3,2},{4,3},{5,4},{6,5},{7,6},{8,7},{9,8},{10,9... | collective-permute-start | bytes 196616 | tf_op jit(solution)/shard_map/ppermute | solution.py:14
  194.8 22.5 %all-to-all-start = ((s32[8,4,8]{2,0,1:T(8,128)}), s32[8,4,8]{2,0,1:T(8,128)S(1)}, u32[]{:S(2)}, u32[]{:S(2)}) async-start(s32[8,4,8]{2,0,1:T(8,128)} %copy.62), calls=%async_computation | async-start | bytes 32768 | tf_op jit(solution)/shard_map/all_to_all | solution.py:171
  199.0 7.5 %collective-permute-start.16 = (bf16[32,1024]{1,0:T(8,128)(2,1)S(1)}, bf16[32,1024]{1,0:T(8,128)(2,1)S(1)}, u32[]{:S(2)}, u32[]{:S(2)}) collective-permute-start(bf16[32,1024]{1,0:T(8,128)(2,1)S(1)} %get-tuple-element.145), channel_id=1, source_target_pairs={{0,1},{1,2},{2,3},{3,4},{4,5},{5,6},{6,7},{7,8},{8,9},{9,10},{10,1... | collective-permute-start | bytes 196616 | tf_op jit(solution)/shard_map/ppermute | solution.py:14
  200.2 13.7 %collective-permute-start.17 = (bf16[32,1024]{1,0:T(8,128)(2,1)S(1)}, bf16[32,1024]{1,0:T(8,128)(2,1)S(1)}, u32[]{:S(2)}, u32[]{:S(2)}) collective-permute-start(bf16[32,1024]{1,0:T(8,128)(2,1)S(1)} %get-tuple-element.144), channel_id=1, source_target_pairs={{0,2},{1,3},{2,4},{3,5},{4,6},{5,7},{6,8},{7,9},{8,10},{9,11},{10,... | collective-permute-start | bytes 196616 | tf_op jit(solution)/shard_map/ppermute | solution.py:14
  200.2 14.3 %collective-permute-start.18 = (bf16[32,1024]{1,0:T(8,128)(2,1)S(1)}, bf16[32,1024]{1,0:T(8,128)(2,1)S(1)}, u32[]{:S(2)}, u32[]{:S(2)}) collective-permute-start(bf16[32,1024]{1,0:T(8,128)(2,1)S(1)} %get-tuple-element.143), channel_id=1, source_target_pairs={{0,7},{1,8},{2,9},{3,10},{4,11},{5,12},{6,13},{7,14},{8,15},{9,16}... | collective-permute-start | bytes 196616 | tf_op jit(solution)/shard_map/ppermute | solution.py:14
  203.2 11.9 %collective-permute-start.19 = (bf16[32,1024]{1,0:T(8,128)(2,1)S(1)}, bf16[32,1024]{1,0:T(8,128)(2,1)S(1)}, u32[]{:S(2)}, u32[]{:S(2)}) collective-permute-start(bf16[32,1024]{1,0:T(8,128)(2,1)S(1)} %get-tuple-element.142), channel_id=1, source_target_pairs={{0,8},{1,9},{2,10},{3,11},{4,12},{5,13},{6,14},{7,15},{8,16},{9,17... | collective-permute-start | bytes 196616 | tf_op jit(solution)/shard_map/ppermute | solution.py:14
  203.2 12.8 %collective-permute-start.20 = (bf16[32,1024]{1,0:T(8,128)(2,1)S(1)}, bf16[32,1024]{1,0:T(8,128)(2,1)S(1)}, u32[]{:S(2)}, u32[]{:S(2)}) collective-permute-start(bf16[32,1024]{1,0:T(8,128)(2,1)S(1)} %get-tuple-element.141), channel_id=1, source_target_pairs={{0,9},{1,10},{2,11},{3,12},{4,13},{5,14},{6,15},{7,16},{8,17},{9,1... | collective-permute-start | bytes 196616 | tf_op jit(solution)/shard_map/ppermute | solution.py:14
  206.5 10.2 %collective-permute-start.21 = (bf16[32,1024]{1,0:T(8,128)(2,1)S(1)}, bf16[32,1024]{1,0:T(8,128)(2,1)S(1)}, u32[]{:S(2)}, u32[]{:S(2)}) collective-permute-start(bf16[32,1024]{1,0:T(8,128)(2,1)S(1)} %get-tuple-element.140), channel_id=1, source_target_pairs={{0,10},{1,11},{2,12},{3,13},{4,14},{5,15},{6,16},{7,17},{8,18},{9,... | collective-permute-start | bytes 196616 | tf_op jit(solution)/shard_map/ppermute | solution.py:14
  217.3 11.5 %all-to-all-start.1 = ((bf16[8,4,8,1024]{3,2,0,1:T(8,128)(2,1)}), bf16[8,4,8,1024]{3,2,0,1:T(8,128)(2,1)S(1)}, u32[]{:S(2)}, u32[]{:S(2)}) async-start(bf16[8,4,8,1024]{3,2,0,1:T(8,128)(2,1)} %bitcast_dynamic-update-slice_fusion), calls=%async_computation.1 | async-start | bytes 1048576 | tf_op jit(solution)/shard_map/all_to_all | solution.py:170
  221.8 60.0 %all-reduce.3.cloned.1.call-start = ((), (), s32[]{:S(2)}) async-start(), calls=%async_computation.2 | async-start | bytes 1048576 | tf_op jit(solution)/shard_map/psum | solution.py:187
  231.3 50.5 %copy-start.4 = (f32[8,128]{1,0:T(8,128)S(1)}, f32[8,128]{1,0:T(8,128)}, u32[]{:S(2)}) copy-start(f32[8,128]{1,0:T(8,128)} %param.21) | copy-start | bytes 12292
  239.7 110.8 %all-reduce.5.cloned.1.call-start = ((), (), s32[]{:S(2)}) async-start(), calls=%async_computation.3 | async-start | bytes 131072 | tf_op jit(solution)/shard_map/psum | solution.py:195
  287.9 112.0 %all-gather.2.cloned.1.call-start = ((), (), s32[]{:S(2)}) async-start(), calls=%async_computation.4 | async-start | bytes 2162688 | tf_op jit(solution)/shard_map/all_gather | solution.py:196
  (3 other events, 25.3 us)
Sparse Core Ops, SparseCore 0:
  239.8 41.9 all-reduce.2
  288.0 62.4 all-reduce.4
  353.1 46.7 all-gather.1

commit v2 on v1

--- a/solution.py
+++ b/solution.py
@@ -1,11 +1,91 @@
 import jax
 import jax.numpy as jnp
 from jax import lax
+from jax.experimental import pallas as pl
+from jax.experimental.pallas import tpu as pltpu
 from jax.sharding import PartitionSpec as P
+import functools
 
 SMOOTHING = 0.2
 PHYSICS = 0.5
 HIGHEST = lax.Precision.HIGHEST
+ROW_BLOCK = 8
+
+
+def split_bf16(values):
+    high = values.astype(jnp.bfloat16)
+    low = (values - high.astype(jnp.float32)).astype(jnp.bfloat16)
+    return high, low
+
+
+def three_pass(lhs, rhs, dims):
+    lhs_hi, lhs_lo = split_bf16(lhs)
+    rhs_hi, rhs_lo = split_bf16(rhs)
+
+    def one(a, b):
+        return lax.dot_general(a, b, (dims, ((), ())), preferred_element_type=jnp.float32)
+
+    return one(lhs_hi, rhs_hi) + (one(lhs_hi, rhs_lo) + one(lhs_lo, rhs_hi))
+
+
+def substep_kernel(with_flux, x_ref, top_ref, bottom_ref, west_ref, east_ref, mix_ref, *rest):
+    if with_flux:
+        fluxes_ref, out_ref, flux_out_ref = rest
+    else:
+        (out_ref,) = rest
+    rows, cols, levels = x_ref.shape
+    centre = x_ref[...]
+    up = jnp.concatenate([top_ref[...], centre[:-1]], axis=0)
+    down = jnp.concatenate([centre[1:], bottom_ref[...]], axis=0)
+    column = lax.broadcasted_iota(jnp.int32, centre.shape, 1)
+    west = jnp.where(column == 0, west_ref[...], pltpu.roll(centre, 1, 1))
+    east = jnp.where(column == cols - 1, east_ref[...], pltpu.roll(centre, cols - 1, 1))
+    smooth = centre + SMOOTHING * (up + down + west + east - 4.0 * centre)
+    flat = smooth.reshape(rows * cols, levels)
+    mixed = three_pass(flat, mix_ref[...], ((1,), (0,)))
+    moved = flat + PHYSICS * jnp.tanh(mixed)
+    out_ref[...] = moved.reshape(rows, cols, levels)
+    if with_flux:
+        total = centre.reshape(rows * cols, levels) + moved
+        flux_out_ref[...] = three_pass(fluxes_ref[...], total, ((1,), (1,)))
+
+
+def substep(values, top, bottom, west, east, mixing, fluxes_t=None):
+    rows, cols, levels = values.shape
+    blocks = rows // ROW_BLOCK
+    top_rows = jnp.concatenate([top, values[ROW_BLOCK - 1 : rows - 1 : ROW_BLOCK]], axis=0)
+    bottom_rows = jnp.concatenate([values[ROW_BLOCK:rows:ROW_BLOCK], bottom], axis=0)
+    with_flux = fluxes_t is not None
+    in_specs = [
+        pl.BlockSpec((ROW_BLOCK, cols, levels), lambda i: (i, 0, 0)),
+        pl.BlockSpec((1, cols, levels), lambda i: (i, 0, 0)),
+        pl.BlockSpec((1, cols, levels), lambda i: (i, 0, 0)),
+        pl.BlockSpec((ROW_BLOCK, 1, levels), lambda i: (i, 0, 0)),
+        pl.BlockSpec((ROW_BLOCK, 1, levels), lambda i: (i, 0, 0)),
+        pl.BlockSpec((levels, levels), lambda i: (0, 0)),
+    ]
+    operands = [values, top_rows, bottom_rows, west, east, mixing]
+    out_shape = [jax.ShapeDtypeStruct(values.shape, jnp.float32)]
+    out_specs = [pl.BlockSpec((ROW_BLOCK, cols, levels), lambda i: (i, 0, 0))]
+    if with_flux:
+        flux_count = fluxes_t.shape[0]
+        in_specs.append(pl.BlockSpec((flux_count, levels), lambda i: (0, 0)))
+        operands.append(fluxes_t)
+        out_shape.append(jax.ShapeDtypeStruct((flux_count, rows * cols), jnp.float32))
+        out_specs.append(pl.BlockSpec((flux_count, ROW_BLOCK * cols), lambda i: (0, i)))
+    cells = rows * cols
+    flops = 6 * cells * levels * levels + (6 * cells * levels * 8 if with_flux else 0)
+    result = pl.pallas_call(
+        functools.partial(substep_kernel, with_flux),
+        grid=(blocks,),
+        in_specs=in_specs,
+        out_specs=out_specs,
+        out_shape=out_shape,
+        cost_estimate=pl.CostEstimate(
+            flops=flops, transcendentals=cells * levels, bytes_accessed=8 * cells * levels
+        ),
+    )(*operands)
+    return result
 
 
 def from_behind(value, axis, steps):
@@ -63,22 +143,6 @@
     before = lax.ppermute(values[:, -1:], "lon", up)
     after = lax.ppermute(values[:, :1], "lon", down)
     return before, after
-
-
-def laplace_local(values, lower_valid, upper_valid):
-    top, bottom = edge_rows(values, lower_valid, upper_valid)
-    left, right = edge_columns(values)
-    up = jnp.concatenate([top, values[:-1]], axis=0)
-    down = jnp.concatenate([values[1:], bottom], axis=0)
-    west = jnp.concatenate([left, values[:, :-1]], axis=1)
-    east = jnp.concatenate([values[:, 1:], right], axis=1)
-    return up + down + west + east - 4.0 * values
-
-
-def physics_step(values, spread, mixing):
-    smooth = values + SMOOTHING * spread
-    mixed = jnp.einsum("rck,kj->rcj", smooth, mixing, precision=lax.Precision.HIGH)
-    return smooth + PHYSICS * jnp.tanh(mixed)
 
 
 def local(
@@ -108,25 +172,24 @@
     )
     sea_cells = land_mask == 1
 
-    spread = laplace_local(state, lower_valid, upper_valid)
-    first = lax.cond(
-        ocean_side,
-        lambda v, s: physics_step(v, s, mix_ocn),
-        lambda v, s: physics_step(v, s, mix_atm),
-        state,
-        spread,
-    )
-    spread_next = laplace_local(first, lower_valid, upper_valid)
-
-    def atmosphere_second(values, spread_now):
-        moved = physics_step(values, spread_now, mix_atm)
-        total = jnp.einsum("rck,kf->frc", values + moved, flux_map, precision=HIGHEST)
+    top, bottom = edge_rows(state, lower_valid, upper_valid)
+    west, east = edge_columns(state)
+    mixing = jnp.where(ocean_side, mix_ocn, mix_atm)
+    (first,) = substep(state, top, bottom, west, east, mixing)
+    top, bottom = edge_rows(first, lower_valid, upper_valid)
+    west, east = edge_columns(first)
+
+    def atmosphere_second(values, top, bottom, west, east):
+        moved, total = substep(values, top, bottom, west, east, mix_atm, flux_map.T)
+        total = total.reshape(flux_count, tile_rows, block_len)
         return moved, jnp.where(sea_cells[None], 0.5 * total, 0.0).astype(jnp.bfloat16)
 
-    def ocean_second(values, spread_now):
+    def ocean_second(values, top, bottom, west, east):
         return values, jnp.zeros((flux_count, tile_rows, block_len), jnp.bfloat16)
 
-    second, flux_sent = lax.cond(ocean_side, ocean_second, atmosphere_second, first, spread_next)
+    second, flux_sent = lax.cond(
+        ocean_side, ocean_second, atmosphere_second, first, top, bottom, west, east
+    )
     entry_list = intersection_list.reshape(tile_rows * intersections, 3)
     owners = entry_list[:, 0]
     targets = entry_list[:, 1]

time: 423 us -> 335 us (0.79)
  the two profiles are of different devices: /device:TPU:1 before, /device:TPU:25 now
where the time goes in v2:
time: 335 us; the launch traced here: 333 us
  waiting for transfers between devices  155 us (46%)
  starting transfers between devices  74.7 us (22%)
  matrix products  34.3 us (10%)
  local copies, waits for them, and re-layouts  31.9 us (10%)
  Pallas kernels  15.6 us (5%)
  between operations  14.2 us (4%)
  other arithmetic  7.08 us (2%)
    all_gather x1, waiting for transfers between devices, local(): lax.all_gather(ocean_only, ('lat', 'lon'), axis=0, tiled=True)  50.3 us
    psum x1, waiting for transfers between devices, local(): forcing = lax.psum(partial_forcing, 'comp')  42.2 us
    psum x1, waiting for transfers between devices, local(): ocean_only = lax.psum(jnp.where(ocean_side, surface, 0.0), 'comp')  40.3 us
    all_to_all x1, starting transfers between devices, local(): lax.all_to_all(shortened(stacked_labels), 'comp', split_axis=1, concat_ax...  36.2 us
    dot_general x1, matrix products, ocean_final(): jnp.einsum('frc,fk->rck', forcing, ocean_map, precision=HIGHEST)  18.3 us
    pallas_call x1, Pallas kernels, substep(): pl.pallas_call(functools.partial(substep_kernel, with_flux), grid=(blocks...  15.6 us
    unnamed x52, local copies, waits for them, and re-layouts  14.1 us
    ppermute x2, starting transfers between devices, edge_rows(): after = lax.ppermute(values[:1], ('comp', 'lat'), down)  14 us
  transfers between devices with their start and end apart: 27, of which 13 were waited for; matrix products, arithmetic and copies ran while one was open for 6% of the time, Pallas kernels for 0%

profile of v2, /device:TPU:25, one launch (start us, length us, event | category | flops | bytes accessed | tf_op | source)
XLA Modules:
  0.0 332.7 jit_solution(12359915198318932023)
XLA Ops:
  8.2 5.8 %collective-permute-start.1 = (f32[1,128,128]{2,1,0:T(8,128)S(1)}, f32[1,128,128]{2,1,0:T(8,128)S(1)}, u32[]{:S(2)}, u32[]{:S(2)}) collective-permute-start(f32[1,128,128]{2,1,0:T(8,128)S(1)} %get-tuple-element.139), channel_id=1, source_target_pairs={{8,0},{16,8},{24,16},{32,24},{40,32},{48,40},{56,48},{64,56},{72,6... | collective-permute-start | bytes 196616 | tf_op jit(solution)/shard_map/ppermute | solution.py:135
  14.0 1.9 collective-permute-start
  17.2 2.1 collective-permute-start.2
  22.0 1.7 collective-permute-start.9
  23.8 1.6 fusion.29
  26.4 1.5 broadcast_select_fusion.2.mix_ref
  30.1 3.5 %collective-permute-done.10 = s32[32]{0:T(128)S(1)} collective-permute-done((s32[32]{0:T(128)S(1)}, s32[32]{0:T(128)S(1)}, u32[]{:S(2)}, u32[]{:S(2)}) %collective-permute-start.10) | collective-permute-done | bytes 160 | tf_op jit(solution)/shard_map/ppermute | solution.py:94
  34.4 2.8 collective-permute-done.12
  39.0 3.3 %collective-permute-start.3 = (f32[128,1,128]{2,1,0:T(1,128)S(1)}, f32[128,1,128]{2,1,0:T(1,128)S(1)}, u32[]{:S(2)}, u32[]{:S(2)}) collective-permute-start(f32[128,1,128]{2,1,0:T(1,128)S(1)} %get-tuple-element.135), channel_id=1, source_target_pairs={{1,0},{2,1},{3,2},{4,3},{5,4},{6,5},{7,6},{0,7},{9,8},{10,9},{11,1... | collective-permute-start | bytes 196616 | tf_op jit(solution)/shard_map/ppermute | solution.py:144
  49.6 15.6 %shard_map.107 = f32[128,128,128]{2,1,0:T(8,128)} custom-call(f32[128,128,128]{2,1,0:T(8,128)} %x_ref.1, f32[16,128,128]{2,1,0:T(8,128)} %pad_maximum_fusion.2.top_ref, f32[16,128,128]{2,1,0:T(8,128)} %pad_maximum_fusion.3.bottom_ref, f32[128,1,128]{2,1,0:T(1,128)} %copy-done.4, f32[128,1,128]{2,1,0:T(1,128)} %copy-done.5, ...), custom_call_target="tpu_custom_call" | custom-call | flops 1610612736 | bytes 16777216 | tf_op jit(solution)/shard_map/pallas_call | solution.py:78
  67.3 1.9 collective-permute-start.4
  69.3 8.2 %collective-permute-start.5 = (f32[1,128,128]{2,1,0:T(8,128)S(1)}, f32[1,128,128]{2,1,0:T(8,128)S(1)}, u32[]{:S(2)}, u32[]{:S(2)}) collective-permute-start(f32[1,128,128]{2,1,0:T(8,128)S(1)} %get-tuple-element.131), channel_id=1, source_target_pairs={{8,0},{16,8},{24,16},{32,24},{40,32},{48,40},{56,48},{64,56},{72,6... | collective-permute-start | bytes 196616 | tf_op jit(solution)/shard_map/ppermute | solution.py:135
  78.8 2.4 collective-permute-done.7
  82.2 1.7 collective-permute-start.15
  84.5 36.2 %all-to-all-start = ((s32[8,4,8]{2,0,1:T(8,128)}), s32[8,4,8]{2,0,1:T(8,128)S(1)}, u32[]{:S(2)}, u32[]{:S(2)}) async-start(s32[8,4,8]{2,0,1:T(8,128)} %copy.62), calls=%async_computation | async-start | bytes 32768 | tf_op jit(solution)/shard_map/all_to_all | solution.py:234
  120.7 4.6 %collective-permute-start.18 = (bf16[32,1024]{1,0:T(8,128)(2,1)S(1)}, bf16[32,1024]{1,0:T(8,128)(2,1)S(1)}, u32[]{:S(2)}, u32[]{:S(2)}) collective-permute-start(bf16[32,1024]{1,0:T(8,128)(2,1)S(1)} %get-tuple-element.144), channel_id=1, source_target_pairs={{0,7},{1,8},{2,9},{3,10},{4,11},{5,12},{6,13},{7,14},{8,15},{9,16}... | collective-permute-start | bytes 196616 | tf_op jit(solution)/shard_map/ppermute | solution.py:94
  127.6 2.8 collective-permute-done.17
  132.4 1.5 collective-permute-done.20
  134.5 1.5 collective-permute-done.21
  136.6 4.2 %all-to-all-start.1 = ((bf16[8,4,8,1024]{3,2,0,1:T(8,128)(2,1)}), bf16[8,4,8,1024]{3,2,0,1:T(8,128)(2,1)S(1)}, u32[]{:S(2)}, u32[]{:S(2)}) async-start(bf16[8,4,8,1024]{3,2,0,1:T(8,128)(2,1)} %bitcast_dynamic-update-slice_fusion), calls=%async_computation.1 | async-start | bytes 1048576 | tf_op jit(solution)/shard_map/all_to_all | solution.py:233
  141.0 5.5 %all-to-all-done.1 = bf16[8,4,8,1024]{3,2,0,1:T(8,128)(2,1)S(1)} async-done(((bf16[8,4,8,1024]{3,2,0,1:T(8,128)(2,1)}), bf16[8,4,8,1024]{3,2,0,1:T(8,128)(2,1)S(1)}, u32[]{:S(2)}, u32[]{:S(2)}) %all-to-all-start.1) | async-done | bytes 524320 | tf_op jit(solution)/shard_map/all_to_all | solution.py:233
  146.7 2.4 fusion.3
  149.1 8.3 %convolution_bitcast_fusion = f32[8,128,128]{2,1,0:T(8,128)} fusion(f32[32,128,8,128]{3,1,0,2:T(8,128)S(1)} %fusion.3, bf16[32,128,128]{2,1,0:T(8,128)(2,1)S(1)} %copy-done), kind=kOutput, calls=%fused_computation.15 | convolution fusion | flops 6442450944 | bytes 18350080 | tf_op jit(solution)/shard_map/wdfa,wab->fdb/dot_general | solution.py:249
  157.5 42.2 %all-reduce.3.cloned.1.call-done = f32[8,128,128]{2,1,0:T(8,128)} async-done(((f32[8,128,128]{2,1,0:T(8,128)}), f32[8,128,128]{2,1,0:T(8,128)}) %all-reduce.3.cloned.1.call-update) | async-done | bytes 524304 | tf_op jit(solution)/shard_map/psum | solution.py:250
  199.7 21.7 %conditional.3 = (f32[128,128,128]{2,1,0:T(8,128)}) conditional(s32[]{:T(128)} %convert_element_type.16, f32[128,128,128]{2,1,0:T(8,128)} %get-tuple-element.56, (pred[128,128]{1,0:T(8,128)(4,1)S(1)}, f32[8,128,128]{2,1,0:T(8,128)}, f32[8,128]{1,0:T(8,128)S(1)}, f32[128,128,128]{2,1,0:T(8,128)}, f32[128,128,128]{2,1,0:T(8,128)}) %tuple.80), branch_computations={%region_6.7_spmd, %region_7.8_spmd} | conditional | flops 205520896 | bytes 42487816 | solution.py:256
  199.7 18.3 %add_select_fusion = f32[128,128,128]{2,1,0:T(8,128)S(1)} fusion(f32[128,128,128]{2,1,0:T(8,128)} %get-tuple-element.51, f32[128,128,128]{2,1,0:T(8,128)} %get-tuple-element.48, pred[128,128]{1,0:T(8,128)(4,1)S(1)} %get-tuple-element.47, f32[8,128,128]{2,1,0:T(8,128)} %get-tuple-element.119, f32[8,128]{1,0:T(8,128)S(1)} %get-tuple-element.67), kind=kOutput, calls=%fused_computation.1 | convolution fusion | flops 205520896 | bytes 25710592 | tf_op jit(solution)/shard_map/cond/branch_1_fun/frc,fk->rck/dot_general | solution.py:253
  217.9 3.4 %copy.108 = f32[128,128,128]{2,1,0:T(8,128)} copy(f32[128,128,128]{2,1,0:T(8,128)S(1)} %add_select_fusion) | data formatting | bytes 16777216 | tf_op jit(solution)/shard_map/cond
  221.4 5.2 %copy.80 = f32[128,128,1]{1,0,2:T(8,128)S(1)} copy(f32[128,128,1]{2,1,0:T(8,128)} %bitcast.86) | data formatting | bytes 131072
  227.3 40.3 %all-reduce.5.cloned.1.call-done = f32[128,128]{1,0:T(8,128)} async-done(((f32[128,128]{1,0:T(8,128)}), f32[128,128]{1,0:T(8,128)}) %all-reduce.5.cloned.1.call-update) | async-done | bytes 65552 | tf_op jit(solution)/shard_map/psum | solution.py:258
  267.7 50.3 %all-gather.2.cloned.1.call-done = f32[4096,128]{1,0:T(8,128)} async-done(((f32[128,128]{1,0:T(8,128)}), f32[4096,128]{1,0:T(8,128)}) %all-gather.2.cloned.1.call-update) | async-done | bytes 2097168 | tf_op jit(solution)/shard_map/all_gather | solution.py:259
  318.0 2.3 gather_fusion
  320.3 5.0 %select_reduce_fusion = f32[256,128]{1,0:T(8,128)S(1)} fusion(bf16[32,128,128]{2,1,0:T(8,128)(2,1)S(1)} %copy-done, pred[256,32]{0,1:T(8,128)(4,1)S(1)} %iota_compare_fusion.2, f32[256,128]{1,0:T(8,128)S(1)} %gather_fusion, pred[256]{0:T(512)(128)(4,1)S(1)} %get-tuple-element.123), kind=kOutput, calls=%fused_computation.8 | convolution fusion | flops 1612709888 | bytes 1319168 | tf_op jit(solution)/shard_map/eb,wab->ewa/dot_general | solution.py:261
  (134 shorter events, 30.5 us)
Async XLA Ops:
  7.2 141.9 %copy-start = (bf16[32,128,128]{2,1,0:T(8,128)(2,1)S(1)}, bf16[32,128,128]{2,1,0:T(8,128)(2,1)}, u32[]{:S(2)}) copy-start(bf16[32,128,128]{2,1,0:T(8,128)(2,1)} %param.20) | copy-start | bytes 3145732
  8.2 38.0 %collective-permute-start.1 = (f32[1,128,128]{2,1,0:T(8,128)S(1)}, f32[1,128,128]{2,1,0:T(8,128)S(1)}, u32[]{:S(2)}, u32[]{:S(2)}) collective-permute-start(f32[1,128,128]{2,1,0:T(8,128)S(1)} %get-tuple-element.139), channel_id=1, source_target_pairs={{8,0},{16,8},{24,16},{32,24},{40,32},{48,40},{56,48},{64,56},{72,6... | collective-permute-start | bytes 196616 | tf_op jit(solution)/shard_map/ppermute | solution.py:135
  14.0 33.2 %collective-permute-start = (f32[1,128,128]{2,1,0:T(8,128)S(1)}, f32[1,128,128]{2,1,0:T(8,128)S(1)}, u32[]{:S(2)}, u32[]{:S(2)}) collective-permute-start(f32[1,128,128]{2,1,0:T(8,128)S(1)} %get-tuple-element.140), channel_id=1, source_target_pairs={{0,8},{8,16},{16,24},{24,32},{32,40},{40,48},{48,56},{56,64},{64,7... | collective-permute-start | bytes 196616 | tf_op jit(solution)/shard_map/ppermute | solution.py:134
  17.2 31.1 %collective-permute-start.2 = (f32[128,1,128]{2,1,0:T(1,128)S(1)}, f32[128,1,128]{2,1,0:T(1,128)S(1)}, u32[]{:S(2)}, u32[]{:S(2)}) collective-permute-start(f32[128,1,128]{2,1,0:T(1,128)S(1)} %get-tuple-element.136), channel_id=1, source_target_pairs={{0,1},{1,2},{2,3},{3,4},{4,5},{5,6},{6,7},{7,0},{8,9},{9,10},{10,1... | collective-permute-start | bytes 196616 | tf_op jit(solution)/shard_map/ppermute | solution.py:143
  22.0 5.8 %collective-permute-start.8 = (s32[32]{0:T(128)S(1)}, s32[32]{0:T(128)S(1)}, u32[]{:S(2)}, u32[]{:S(2)}) collective-permute-start(s32[32]{0:T(128)S(1)} %get-tuple-element.158), channel_id=1, source_target_pairs={{0,31},{1,0},{2,1},{3,2},{4,3},{5,4},{6,5},{7,6},{8,7},{9,8},{10,9... | collective-permute-start | bytes 392 | tf_op jit(solution)/shard_map/ppermute | solution.py:94
  22.0 7.1 %collective-permute-start.9 = (s32[32]{0:T(128)S(1)}, s32[32]{0:T(128)S(1)}, u32[]{:S(2)}, u32[]{:S(2)}) collective-permute-start(s32[32]{0:T(128)S(1)} %get-tuple-element.156), channel_id=1, source_target_pairs={{0,1},{1,2},{2,3},{3,4},{4,5},{5,6},{6,7},{7,8},{8,9},{9,10},{10,1... | collective-permute-start | bytes 392 | tf_op jit(solution)/shard_map/ppermute | solution.py:94
  27.9 5.7 %collective-permute-start.10 = (s32[32]{0:T(128)S(1)}, s32[32]{0:T(128)S(1)}, u32[]{:S(2)}, u32[]{:S(2)}) collective-permute-start(s32[32]{0:T(128)S(1)} %get-tuple-element.155), channel_id=1, source_target_pairs={{0,2},{1,3},{2,4},{3,5},{4,6},{5,7},{6,8},{7,9},{8,10},{9,11},{10,... | collective-permute-start | bytes 392 | tf_op jit(solution)/shard_map/ppermute | solution.py:94
  29.2 5.1 %collective-permute-start.11 = (s32[32]{0:T(128)S(1)}, s32[32]{0:T(128)S(1)}, u32[]{:S(2)}, u32[]{:S(2)}) collective-permute-start(s32[32]{0:T(128)S(1)} %get-tuple-element.154), channel_id=1, source_target_pairs={{0,7},{1,8},{2,9},{3,10},{4,11},{5,12},{6,13},{7,14},{8,15},{9,16}... | collective-permute-start | bytes 392 | tf_op jit(solution)/shard_map/ppermute | solution.py:94
  33.6 3.6 %collective-permute-start.12 = (s32[32]{0:T(128)S(1)}, s32[32]{0:T(128)S(1)}, u32[]{:S(2)}, u32[]{:S(2)}) collective-permute-start(s32[32]{0:T(128)S(1)} %get-tuple-element.153), channel_id=1, source_target_pairs={{0,8},{1,9},{2,10},{3,11},{4,12},{5,13},{6,14},{7,15},{8,16},{9,17... | collective-permute-start | bytes 392 | tf_op jit(solution)/shard_map/ppermute | solution.py:94
  34.3 4.2 %collective-permute-start.13 = (s32[32]{0:T(128)S(1)}, s32[32]{0:T(128)S(1)}, u32[]{:S(2)}, u32[]{:S(2)}) collective-permute-start(s32[32]{0:T(128)S(1)} %get-tuple-element.152), channel_id=1, source_target_pairs={{0,9},{1,10},{2,11},{3,12},{4,13},{5,14},{6,15},{7,16},{8,17},{9,1... | collective-permute-start | bytes 392 | tf_op jit(solution)/shard_map/ppermute | solution.py:94
  37.2 6.5 %collective-permute-start.14 = (s32[32]{0:T(128)}, s32[32]{0:T(128)}, u32[]{:S(2)}, u32[]{:S(2)}) collective-permute-start(s32[32]{0:T(128)} %get-tuple-element.151), channel_id=1, source_target_pairs={{0,10},{1,11},{2,12},{3,13},{4,14},{5,15},{6,16},{7,17},{8,18},{9,... | collective-permute-start | bytes 392 | tf_op jit(solution)/shard_map/ppermute | solution.py:94
  39.0 9.3 %collective-permute-start.3 = (f32[128,1,128]{2,1,0:T(1,128)S(1)}, f32[128,1,128]{2,1,0:T(1,128)S(1)}, u32[]{:S(2)}, u32[]{:S(2)}) collective-permute-start(f32[128,1,128]{2,1,0:T(1,128)S(1)} %get-tuple-element.135), channel_id=1, source_target_pairs={{1,0},{2,1},{3,2},{4,3},{5,4},{6,5},{7,6},{0,7},{9,8},{10,9},{11,1... | collective-permute-start | bytes 196616 | tf_op jit(solution)/shard_map/ppermute | solution.py:144
  67.3 10.6 %collective-permute-start.4 = (f32[1,128,128]{2,1,0:T(8,128)S(1)}, f32[1,128,128]{2,1,0:T(8,128)S(1)}, u32[]{:S(2)}, u32[]{:S(2)}) collective-permute-start(f32[1,128,128]{2,1,0:T(8,128)S(1)} %get-tuple-element.132), channel_id=1, source_target_pairs={{0,8},{8,16},{16,24},{24,32},{32,40},{40,48},{48,56},{56,64},{64,7... | collective-permute-start | bytes 196616 | tf_op jit(solution)/shard_map/ppermute | solution.py:134
  69.3 9.5 %collective-permute-start.5 = (f32[1,128,128]{2,1,0:T(8,128)S(1)}, f32[1,128,128]{2,1,0:T(8,128)S(1)}, u32[]{:S(2)}, u32[]{:S(2)}) collective-permute-start(f32[1,128,128]{2,1,0:T(8,128)S(1)} %get-tuple-element.131), channel_id=1, source_target_pairs={{8,0},{16,8},{24,16},{32,24},{40,32},{48,40},{56,48},{64,56},{72,6... | collective-permute-start | bytes 196616 | tf_op jit(solution)/shard_map/ppermute | solution.py:135
  77.5 1.3 collective-permute-start.6
  77.5 3.7 %collective-permute-start.7 = (f32[128,1,128]{2,1,0:T(1,128)S(1)}, f32[128,1,128]{2,1,0:T(1,128)S(1)}, u32[]{:S(2)}, u32[]{:S(2)}) collective-permute-start(f32[128,1,128]{2,1,0:T(1,128)S(1)} %get-tuple-element.133), channel_id=1, source_target_pairs={{1,0},{2,1},{3,2},{4,3},{5,4},{6,5},{7,6},{0,7},{9,8},{10,9},{11,1... | collective-permute-start | bytes 196616 | tf_op jit(solution)/shard_map/ppermute | solution.py:144
  82.2 43.1 %collective-permute-start.15 = (bf16[32,1024]{1,0:T(8,128)(2,1)S(1)}, bf16[32,1024]{1,0:T(8,128)(2,1)S(1)}, u32[]{:S(2)}, u32[]{:S(2)}) collective-permute-start(bf16[32,1024]{1,0:T(8,128)(2,1)S(1)} %get-tuple-element.147), channel_id=1, source_target_pairs={{0,31},{1,0},{2,1},{3,2},{4,3},{5,4},{6,5},{7,6},{8,7},{9,8},{10,9... | collective-permute-start | bytes 196616 | tf_op jit(solution)/shard_map/ppermute | solution.py:94
  84.5 52.1 %all-to-all-start = ((s32[8,4,8]{2,0,1:T(8,128)}), s32[8,4,8]{2,0,1:T(8,128)S(1)}, u32[]{:S(2)}, u32[]{:S(2)}) async-start(s32[8,4,8]{2,0,1:T(8,128)} %copy.62), calls=%async_computation | async-start | bytes 32768 | tf_op jit(solution)/shard_map/all_to_all | solution.py:234
  120.7 5.9 %collective-permute-start.16 = (bf16[32,1024]{1,0:T(8,128)(2,1)S(1)}, bf16[32,1024]{1,0:T(8,128)(2,1)S(1)}, u32[]{:S(2)}, u32[]{:S(2)}) collective-permute-start(bf16[32,1024]{1,0:T(8,128)(2,1)S(1)} %get-tuple-element.146), channel_id=1, source_target_pairs={{0,1},{1,2},{2,3},{3,4},{4,5},{5,6},{6,7},{7,8},{8,9},{9,10},{10,1... | collective-permute-start | bytes 196616 | tf_op jit(solution)/shard_map/ppermute | solution.py:94
  120.7 9.7 %collective-permute-start.17 = (bf16[32,1024]{1,0:T(8,128)(2,1)S(1)}, bf16[32,1024]{1,0:T(8,128)(2,1)S(1)}, u32[]{:S(2)}, u32[]{:S(2)}) collective-permute-start(bf16[32,1024]{1,0:T(8,128)(2,1)S(1)} %get-tuple-element.145), channel_id=1, source_target_pairs={{0,2},{1,3},{2,4},{3,5},{4,6},{5,7},{6,8},{7,9},{8,10},{9,11},{10,... | collective-permute-start | bytes 196616 | tf_op jit(solution)/shard_map/ppermute | solution.py:94
  120.7 10.3 %collective-permute-start.18 = (bf16[32,1024]{1,0:T(8,128)(2,1)S(1)}, bf16[32,1024]{1,0:T(8,128)(2,1)S(1)}, u32[]{:S(2)}, u32[]{:S(2)}) collective-permute-start(bf16[32,1024]{1,0:T(8,128)(2,1)S(1)} %get-tuple-element.144), channel_id=1, source_target_pairs={{0,7},{1,8},{2,9},{3,10},{4,11},{5,12},{6,13},{7,14},{8,15},{9,16}... | collective-permute-start | bytes 196616 | tf_op jit(solution)/shard_map/ppermute | solution.py:94
  125.3 6.4 %collective-permute-start.19 = (bf16[32,1024]{1,0:T(8,128)(2,1)S(1)}, bf16[32,1024]{1,0:T(8,128)(2,1)S(1)}, u32[]{:S(2)}, u32[]{:S(2)}) collective-permute-start(bf16[32,1024]{1,0:T(8,128)(2,1)S(1)} %get-tuple-element.143), channel_id=1, source_target_pairs={{0,8},{1,9},{2,10},{3,11},{4,12},{5,13},{6,14},{7,15},{8,16},{9,17... | collective-permute-start | bytes 196616 | tf_op jit(solution)/shard_map/ppermute | solution.py:94
  125.3 8.6 %collective-permute-start.20 = (bf16[32,1024]{1,0:T(8,128)(2,1)S(1)}, bf16[32,1024]{1,0:T(8,128)(2,1)S(1)}, u32[]{:S(2)}, u32[]{:S(2)}) collective-permute-start(bf16[32,1024]{1,0:T(8,128)(2,1)S(1)} %get-tuple-element.142), channel_id=1, source_target_pairs={{0,9},{1,10},{2,11},{3,12},{4,13},{5,14},{6,15},{7,16},{8,17},{9,1... | collective-permute-start | bytes 196616 | tf_op jit(solution)/shard_map/ppermute | solution.py:94
  126.6 9.4 %collective-permute-start.21 = (bf16[32,1024]{1,0:T(8,128)(2,1)S(1)}, bf16[32,1024]{1,0:T(8,128)(2,1)S(1)}, u32[]{:S(2)}, u32[]{:S(2)}) collective-permute-start(bf16[32,1024]{1,0:T(8,128)(2,1)S(1)} %get-tuple-element.141), channel_id=1, source_target_pairs={{0,10},{1,11},{2,12},{3,13},{4,14},{5,15},{6,16},{7,17},{8,18},{9,... | collective-permute-start | bytes 196616 | tf_op jit(solution)/shard_map/ppermute | solution.py:94
  136.6 9.8 %all-to-all-start.1 = ((bf16[8,4,8,1024]{3,2,0,1:T(8,128)(2,1)}), bf16[8,4,8,1024]{3,2,0,1:T(8,128)(2,1)S(1)}, u32[]{:S(2)}, u32[]{:S(2)}) async-start(bf16[8,4,8,1024]{3,2,0,1:T(8,128)(2,1)} %bitcast_dynamic-update-slice_fusion), calls=%async_computation.1 | async-start | bytes 1048576 | tf_op jit(solution)/shard_map/all_to_all | solution.py:233
  140.8 58.8 %all-reduce.3.cloned.1.call-start = ((), (), s32[]{:S(2)}) async-start(), calls=%async_computation.2 | async-start | bytes 1048576 | tf_op jit(solution)/shard_map/psum | solution.py:250
  149.1 50.6 %copy-start.17 = (f32[8,128]{1,0:T(8,128)S(1)}, f32[8,128]{1,0:T(8,128)}, u32[]{:S(2)}) copy-start(f32[8,128]{1,0:T(8,128)} %param.19) | copy-start | bytes 12292
  157.4 110.2 %all-reduce.5.cloned.1.call-start = ((), (), s32[]{:S(2)}) async-start(), calls=%async_computation.3 | async-start | bytes 131072 | tf_op jit(solution)/shard_map/psum | solution.py:258
  221.3 46.3 %copy-start.7 = (s32[256,3]{0,1:T(4,128)S(1)}, s32[256,3]{0,1:T(4,128)}, u32[]{:S(2)}) copy-start(s32[256,3]{0,1:T(4,128)} %copy-done.6) | copy-start | bytes 9220
  221.4 46.3 %copy-start.13 = (s32[256,1]{0,1:T(1,128)S(1)}, s32[256,1]{0,1:T(1,128)}, u32[]{:S(2)}) copy-start(s32[256,1]{0,1:T(1,128)} %copy-done.12) | copy-start | bytes 3076
  221.4 104.2 %copy-start.3 = (s32[128,128]{1,0:T(8,128)S(1)}, s32[128,128]{1,0:T(8,128)}, u32[]{:S(2)}) copy-start(s32[128,128]{1,0:T(8,128)} %param.14) | copy-start | bytes 196612
  227.3 90.7 %all-gather.2.cloned.1.call-start = ((), (), s32[]{:S(2)}) async-start(), calls=%async_computation.4 | async-start | bytes 2162688 | tf_op jit(solution)/shard_map/all_gather | solution.py:259
  (13 other events, 144.6 us)
Sparse Core Ops, SparseCore 0:
  157.5 42.0 all-reduce.2
  227.4 40.1 all-reduce.4
  270.1 47.8 all-gather.1

commit v3 on v2

--- a/solution.py
+++ b/solution.py
@@ -88,16 +88,6 @@
     return result
 
 
-def from_behind(value, axis, steps):
-    count = lax.axis_size(axis)
-    pairs = [(source, (source + steps) % count) for source in range(count)]
-    return lax.ppermute(value, axis, pairs)
-
-
-def shortened(shard):
-    return jax.tree.map(lambda a: a.astype(jnp.bfloat16) if a.dtype == jnp.float32 else a, shard)
-
-
 def column_physics(values, mixing):
     return jnp.tanh(jnp.einsum("rck,kj->rcj", values, mixing, precision=HIGHEST))
 
@@ -143,6 +133,155 @@
     before = lax.ppermute(values[:, -1:], "lon", up)
     after = lax.ppermute(values[:, :1], "lon", down)
     return before, after
+
+
+MESH_IDS = pl.DeviceIdType.MESH
+
+
+def tile_device(comp, tile, lon_total):
+    return (comp, tile // lon_total, tile % lon_total)
+
+
+def gather_kernel(offsets, shape, send_ref, out_ref, land, send_sems, recv_sems):
+    comp_total, lat_total, lon_total = shape
+    comp = lax.axis_index("comp")
+    tiles = lat_total * lon_total
+    tile = lax.axis_index("lat") * lon_total + lax.axis_index("lon")
+    ocean = comp_total - 1
+    count = len(offsets)
+    barrier = pltpu.get_barrier_semaphore()
+
+    @pl.when(comp != ocean)
+    def _():
+        for off in offsets:
+            target = tile_device(ocean, (tile + off) % tiles, lon_total)
+            pl.semaphore_signal(barrier, 1, device_id=target, device_id_type=MESH_IDS)
+        pl.semaphore_wait(barrier, count)
+        copies = []
+        for k, off in enumerate(offsets):
+            target = tile_device(ocean, (tile + off) % tiles, lon_total)
+            copy = pltpu.make_async_remote_copy(
+                src_ref=send_ref.at[k],
+                dst_ref=land.at[comp * count + k],
+                send_sem=send_sems.at[k],
+                recv_sem=recv_sems.at[comp * count + k],
+                device_id=target,
+                device_id_type=MESH_IDS,
+            )
+            copy.start()
+            copies.append(copy)
+        for copy in copies:
+            copy.wait_send()
+        out_ref[...] = jnp.zeros_like(out_ref)
+
+    @pl.when(comp == ocean)
+    def _():
+        for source_comp in range(ocean):
+            for off in offsets:
+                source = tile_device(source_comp, (tile + tiles - off) % tiles, lon_total)
+                pl.semaphore_signal(barrier, 1, device_id=source, device_id_type=MESH_IDS)
+        pl.semaphore_wait(barrier, count * ocean)
+        for source_comp in range(ocean):
+            for k, off in enumerate(offsets):
+                source = tile_device(source_comp, (tile + tiles - off) % tiles, lon_total)
+                slot = source_comp * count + k
+                pltpu.make_async_remote_copy(
+                    src_ref=send_ref.at[k],
+                    dst_ref=land.at[slot],
+                    send_sem=send_sems.at[k],
+                    recv_sem=recv_sems.at[slot],
+                    device_id=source,
+                    device_id_type=MESH_IDS,
+                ).wait_recv()
+        out_ref[...] = land[...]
+
+
+def gather_to_ocean(blocks, offsets, shape):
+    count = len(offsets)
+    senders = (shape[0] - 1) * count
+    slot_shape = blocks.shape[1:]
+    return pl.pallas_call(
+        functools.partial(gather_kernel, tuple(offsets), tuple(shape)),
+        out_shape=jax.ShapeDtypeStruct((senders,) + slot_shape, blocks.dtype),
+        in_specs=[pl.BlockSpec(memory_space=pltpu.VMEM)],
+        out_specs=pl.BlockSpec(memory_space=pltpu.VMEM),
+        scratch_shapes=[
+            pltpu.VMEM((senders,) + slot_shape, blocks.dtype),
+            pltpu.SemaphoreType.DMA((count,)),
+            pltpu.SemaphoreType.DMA((senders,)),
+        ],
+        compiler_params=pltpu.CompilerParams(collective_id=0, has_side_effects=True),
+    )(blocks)
+
+
+def spread_kernel(offsets, shape, surface_ref, out_ref, land, send_sems, recv_sems):
+    comp_total, lat_total, lon_total = shape
+    comp = lax.axis_index("comp")
+    tiles = lat_total * lon_total
+    tile = lax.axis_index("lat") * lon_total + lax.axis_index("lon")
+    ocean = comp_total - 1
+    count = len(offsets)
+    barrier = pltpu.get_barrier_semaphore()
+
+    @pl.when(comp == ocean)
+    def _():
+        for target_comp in range(ocean):
+            for off in offsets:
+                target = tile_device(target_comp, (tile + tiles - off) % tiles, lon_total)
+                pl.semaphore_signal(barrier, 1, device_id=target, device_id_type=MESH_IDS)
+        pl.semaphore_wait(barrier, count * ocean)
+        copies = []
+        for target_comp in range(ocean):
+            for k, off in enumerate(offsets):
+                target = tile_device(target_comp, (tile + tiles - off) % tiles, lon_total)
+                copy = pltpu.make_async_remote_copy(
+                    src_ref=surface_ref,
+                    dst_ref=land.at[k],
+                    send_sem=send_sems.at[target_comp * count + k],
+                    recv_sem=recv_sems.at[k],
+                    device_id=target,
+                    device_id_type=MESH_IDS,
+                )
+                copy.start()
+                copies.append(copy)
+        for copy in copies:
+            copy.wait_send()
+        out_ref[...] = jnp.zeros_like(out_ref)
+
+    @pl.when(comp != ocean)
+    def _():
+        for off in offsets:
+            source = tile_device(ocean, (tile + off) % tiles, lon_total)
+            pl.semaphore_signal(barrier, 1, device_id=source, device_id_type=MESH_IDS)
+        pl.semaphore_wait(barrier, count)
+        for k, off in enumerate(offsets):
+            source = tile_device(ocean, (tile + off) % tiles, lon_total)
+            pltpu.make_async_remote_copy(
+                src_ref=surface_ref,
+                dst_ref=land.at[k],
+                send_sem=send_sems.at[k],
+                recv_sem=recv_sems.at[k],
+                device_id=source,
+                device_id_type=MESH_IDS,
+            ).wait_recv()
+        out_ref[...] = land[...]
+
+
+def spread_from_ocean(surface, offsets, shape):
+    count = len(offsets)
+    senders = (shape[0] - 1) * count
+    return pl.pallas_call(
+        functools.partial(spread_kernel, tuple(offsets), tuple(shape)),
+        out_shape=jax.ShapeDtypeStruct((count,) + surface.shape, surface.dtype),
+        in_specs=[pl.BlockSpec(memory_space=pltpu.VMEM)],
+        out_specs=pl.BlockSpec(memory_space=pltpu.VMEM),
+        scratch_shapes=[
+            pltpu.VMEM((count,) + surface.shape, surface.dtype),
+            pltpu.SemaphoreType.DMA((senders,)),
+            pltpu.SemaphoreType.DMA((count,)),
+        ],
+        compiler_params=pltpu.CompilerParams(collective_id=1, has_side_effects=True),
+    )(surface)
 
 
 def local(
@@ -159,7 +298,6 @@
     reach = min(4, lon_count)
     neighbour_count = 2 * reach
     capacity = intersections * tile_rows // neighbour_count
-    quarter = capacity // comp_count
     width = flux_count * block_len
     comp_index = lax.axis_index("comp")
     tile_index = lax.axis_index("lat") * lon_count + lax.axis_index("lon")
@@ -198,6 +336,11 @@
     entry_blocks = jnp.repeat(flux_sent.transpose(1, 0, 2), intersections, axis=0).reshape(
         tile_rows * intersections, width
     )
+    lane = jnp.arange(128, dtype=jnp.int32)[None, :]
+    label_lanes = jnp.where(
+        lane == 0, weight_ids[:, None], jnp.where(lane == 1, targets[:, None], 0)
+    ).astype(jnp.bfloat16)
+    entry_blocks = jnp.concatenate([entry_blocks, label_lanes], axis=1)
     sending = jnp.broadcast_to(jnp.logical_not(ocean_side), owners.shape)
     offsets = [
         (n // reach * lon_count + n % reach - (reach - 1) // 2) % tile_count
@@ -213,51 +356,40 @@
         ),
         axis=1,
     )
-    packed, packed_labels = pack_rows(
-        entry_blocks, neighbour_ids, labels, sending, capacity, neighbour_count
-    )
-    moved_blocks = []
-    moved_labels = []
-    for neighbour in range(neighbour_count):
-        if offsets[neighbour] == 0:
-            one_blocks, one_labels = (packed[neighbour], packed_labels[neighbour])
-        else:
-            one_blocks, one_labels = from_behind(
-                (packed[neighbour], packed_labels[neighbour]), ("lat", "lon"), offsets[neighbour]
-            )
-        moved_blocks.append(one_blocks)
-        moved_labels.append(one_labels)
-    stacked_blocks = jnp.stack(moved_blocks).reshape(neighbour_count, comp_count, quarter, width)
-    stacked_labels = jnp.stack(moved_labels).reshape(neighbour_count, comp_count, quarter)
-    arrived, arrived_labels = (
-        lax.all_to_all(stacked_blocks, "comp", split_axis=1, concat_axis=1, tiled=True),
-        lax.all_to_all(
-            shortened(stacked_labels), "comp", split_axis=1, concat_axis=1, tiled=True
-        ).astype(stacked_labels.dtype),
-    )
-    weights_wide = regrid_weights.astype(jnp.float32)
-    label_ids = jnp.arange(weight_count * tile_rows, dtype=jnp.int32)
-    flat_labels = arrived_labels.reshape(-1)
-    selector = (flat_labels[:, None] == label_ids[None, :]).astype(jnp.bfloat16)
-    binned = lax.dot_general(
-        selector,
-        arrived.reshape(flat_labels.shape[0], width),
-        (((0,), (0,)), ((), ())),
-        preferred_element_type=jnp.float32,
-    )
-    binned = binned.reshape(weight_count, tile_rows, flux_count, block_len)
-    partial_forcing = jnp.einsum("wdfa,wab->fdb", binned, weights_wide, precision=HIGHEST)
-    forcing = lax.psum(partial_forcing, "comp")
-
-    def ocean_final(values):
+    packed, _ = pack_rows(entry_blocks, neighbour_ids, labels, sending, capacity, neighbour_count)
+    mesh_shape = (comp_count, lat_count, lon_count)
+    arrived = gather_to_ocean(packed, offsets, mesh_shape)
+    weights_low = regrid_weights
+
+    def ocean_final(values, arrived):
+        flat = arrived.reshape(-1, width + 128)
+        fluxes = flat[:, :width]
+        arrived_labels = flat[:, width].astype(jnp.int32) * tile_rows + flat[:, width + 1].astype(
+            jnp.int32
+        )
+        label_ids = jnp.arange(weight_count * tile_rows, dtype=jnp.int32)
+        selector = (arrived_labels[:, None] == label_ids[None, :]).astype(jnp.bfloat16)
+        binned = lax.dot_general(
+            selector, fluxes, (((0,), (0,)), ((), ())), preferred_element_type=jnp.float32
+        )
+        binned = binned.reshape(weight_count, tile_rows, flux_count, block_len)
+        binned_hi = binned.astype(jnp.bfloat16)
+        binned_lo = (binned - binned_hi.astype(jnp.float32)).astype(jnp.bfloat16)
+        forcing = jnp.einsum(
+            "wdfa,wab->fdb", binned_hi, weights_low, preferred_element_type=jnp.float32
+        ) + jnp.einsum("wdfa,wab->fdb", binned_lo, weights_low, preferred_element_type=jnp.float32)
         moved = values + jnp.einsum("frc,fk->rck", forcing, ocean_map, precision=HIGHEST)
         return jnp.where(sea_cells[:, :, None], moved, state)
 
-    final_state = lax.cond(ocean_side, ocean_final, lambda values: values, second)
+    final_state = lax.cond(ocean_side, ocean_final, lambda values, arrived: values, second, arrived)
     surface = final_state[:, :, 0]
-    ocean_only = lax.psum(jnp.where(ocean_side, surface, 0.0), "comp")
-    ocean_surface = lax.all_gather(ocean_only, ("lat", "lon"), axis=0, tiled=True)
-    picked = jnp.take(ocean_surface, owners * tile_rows + targets, axis=0)
+    around = spread_from_ocean(surface, offsets, mesh_shape)
+    picked = jnp.take(
+        around.reshape(neighbour_count * tile_rows, block_len),
+        neighbour_ids * tile_rows + targets,
+        axis=0,
+    )
+    weights_wide = regrid_weights.astype(jnp.float32)
     images = jnp.einsum("eb,wab->ewa", picked, weights_wide, precision=HIGHEST)
     which_block = weight_ids[:, None] == jnp.arange(weight_count, dtype=jnp.int32)[None, :]
     chosen = jnp.sum(jnp.where(which_block[:, :, None], images, 0.0), axis=1)

time: 335 us -> 202 us (0.60)
  waiting for transfers between devices: 155 us -> 3.84 us
  Pallas kernels: 15.6 us -> 100 us
  starting transfers between devices: 74.7 us -> 19.7 us
  between operations: 14.2 us -> 0.95 us
  matrix products: 34.3 us -> 39.3 us
    pallas_call x0 -> x2, Pallas kernels: none -> 84.6 us  [the longest x1 59.8 us: gather_to_ocean(): pl.pallas_call(functools.partial(gather_kernel, tuple(offsets), tuple(sha...]
    psum x2 -> x0, waiting for transfers between devices: 82.5 us -> none  [the longest x1 42.2 us: local(): forcing = lax.psum(partial_forcing, 'comp')]
    all_gather x1 -> x0, waiting for transfers between devices: 50.3 us -> none  [local(): lax.all_gather(ocean_only, ('lat', 'lon'), axis=0, tiled=True)]
    all_to_all x2 -> x0, starting transfers between devices: 40.4 us -> none  [the longest x1 36.2 us: local(): lax.all_to_all(shortened(stacked_labels), 'comp', split_axis=1, concat_ax...]
    ppermute x14 -> x0, waiting for transfers between devices: 13.4 us -> none  [from_behind(): return lax.ppermute(value, axis, pairs)]
    ppermute x14 -> x0, starting transfers between devices: 10.4 us -> none  [from_behind(): return lax.ppermute(value, axis, pairs)]
    cond x1 -> x2, local copies, waits for them, and re-layouts: 3.4 us -> 12.8 us
    unnamed x52 -> x17, local copies, waits for them, and re-layouts: 14.1 us -> 8.02 us
  transfers between devices with their start and end apart: 27 -> 8, of which waited for: 13 -> 2; matrix products, arithmetic and copies ran while one was open for 6% -> 5% of each run, Pallas kernels for 0% -> 0%
where the time goes in v3:
time: 202 us; the launch traced here: 200 us
  Pallas kernels  100 us (50%)
  matrix products  39.3 us (19%)
  local copies, waits for them, and re-layouts  28.9 us (14%)
  starting transfers between devices  19.7 us (10%)
  other arithmetic  7.49 us (4%)
  waiting for transfers between devices  3.84 us (2%)
    pallas_call x1, Pallas kernels, gather_to_ocean(): pl.pallas_call(functools.partial(gather_kernel, tuple(offsets), tuple(sha...  59.8 us
    pallas_call x1, Pallas kernels, spread_from_ocean(): pl.pallas_call(functools.partial(spread_kernel, tuple(offsets), tuple(sha...  24.8 us
    dot_general x1, matrix products, ocean_final(): jnp.einsum('frc,fk->rck', forcing, ocean_map, precision=HIGHEST)  17.9 us
    pallas_call x1, Pallas kernels, substep(): pl.pallas_call(functools.partial(substep_kernel, with_flux), grid=(blocks...  15.6 us
    cond x2, local copies, waits for them, and re-layouts  12.8 us
    ppermute x2, starting transfers between devices, edge_rows(): after = lax.ppermute(values[:1], ('comp', 'lat'), down)  11.6 us
    dot_general x1, matrix products, ocean_final(): lax.dot_general(selector, fluxes, (((0,), (0,)), ((), ())), preferred_ele...  10.5 us
    unnamed x17, local copies, waits for them, and re-layouts  8.02 us
  transfers between devices with their start and end apart: 8, of which 2 were waited for; matrix products, arithmetic and copies ran while one was open for 5% of the time, Pallas kernels for 0%

profile of v3, /device:TPU:25, one launch (start us, length us, event | category | flops | bytes accessed | tf_op | source)
XLA Modules:
  0.0 200.4 jit_solution(14605965039842339974)
XLA Ops:
  0.6 0.9 fusion.42
  1.5 5.8 %collective-permute-start.1 = (f32[1,128,128]{2,1,0:T(8,128)S(1)}, f32[1,128,128]{2,1,0:T(8,128)S(1)}, u32[]{:S(2)}, u32[]{:S(2)}) collective-permute-start(f32[1,128,128]{2,1,0:T(8,128)S(1)} %get-tuple-element.118), channel_id=1, source_target_pairs={{8,0},{16,8},{24,16},{32,24},{40,32},{48,40},{56,48},{64,56},{72,6... | collective-permute-start | bytes 196616 | tf_op jit(solution)/shard_map/ppermute | solution.py:125
  7.4 1.9 collective-permute-start
  9.3 1.3 fusion.40
  10.6 2.1 %collective-permute-start.2 = (f32[128,1,128]{2,1,0:T(1,128)S(1)}, f32[128,1,128]{2,1,0:T(1,128)S(1)}, u32[]{:S(2)}, u32[]{:S(2)}) collective-permute-start(f32[128,1,128]{2,1,0:T(1,128)S(1)} %get-tuple-element.115), channel_id=1, source_target_pairs={{0,1},{1,2},{2,3},{3,4},{4,5},{5,6},{6,7},{7,0},{8,9},{9,10},{10,1... | collective-permute-start | bytes 196616 | tf_op jit(solution)/shard_map/ppermute | solution.py:133
  12.7 1.6 fusion.41
  14.3 0.9 broadcast_compare_fusion
  17.1 1.5 broadcast_select_fusion.2.mix_ref
  18.8 1.1 pad_maximum_fusion.3.bottom_ref
  19.9 1.1 pad_maximum_fusion.2.top_ref
  22.2 15.6 %shard_map.107 = f32[128,128,128]{2,1,0:T(8,128)} custom-call(f32[128,128,128]{2,1,0:T(8,128)} %x_ref.1, f32[16,128,128]{2,1,0:T(8,128)} %pad_maximum_fusion.2.top_ref, f32[16,128,128]{2,1,0:T(8,128)} %pad_maximum_fusion.3.bottom_ref, f32[128,1,128]{2,1,0:T(1,128)} %copy-done.4, f32[128,1,128]{2,1,0:T(1,128)} %copy-done.5, ...), custom_call_target="tpu_custom_call" | custom-call | flops 1610612736 | bytes 16777216 | tf_op jit(solution)/shard_map/pallas_call | solution.py:78
  37.8 0.9 fusion.38
  38.7 1.3 fusion.39
  40.0 1.9 collective-permute-start.4
  41.9 5.8 %collective-permute-start.5 = (f32[1,128,128]{2,1,0:T(8,128)S(1)}, f32[1,128,128]{2,1,0:T(8,128)S(1)}, u32[]{:S(2)}, u32[]{:S(2)}) collective-permute-start(f32[1,128,128]{2,1,0:T(8,128)S(1)} %get-tuple-element.110), channel_id=1, source_target_pairs={{8,0},{16,8},{24,16},{32,24},{40,32},{48,40},{56,48},{64,56},{72,6... | collective-permute-start | bytes 196616 | tf_op jit(solution)/shard_map/ppermute | solution.py:125
  47.7 2.0 %collective-permute-start.6 = (f32[128,1,128]{2,1,0:T(1,128)S(1)}, f32[128,1,128]{2,1,0:T(1,128)S(1)}, u32[]{:S(2)}, u32[]{:S(2)}) collective-permute-start(f32[128,1,128]{2,1,0:T(1,128)S(1)} %get-tuple-element.113), channel_id=1, source_target_pairs={{0,1},{1,2},{2,3},{3,4},{4,5},{5,6},{6,7},{7,0},{8,9},{9,10},{10,1... | collective-permute-start | bytes 196616 | tf_op jit(solution)/shard_map/ppermute | solution.py:133
  49.9 1.2 collective-permute-done.6
  51.1 2.7 %collective-permute-done.7 = f32[128,1,128]{2,1,0:T(1,128)S(1)} collective-permute-done((f32[128,1,128]{2,1,0:T(1,128)S(1)}, f32[128,1,128]{2,1,0:T(1,128)S(1)}, u32[]{:S(2)}, u32[]{:S(2)}) %collective-permute-start.7) | collective-permute-done | bytes 65568 | tf_op jit(solution)/shard_map/ppermute | solution.py:134
  54.0 1.2 convolution_convert_fusion
  55.2 59.8 %shard_map.108 = bf16[24,32,1152]{2,1,0:T(8,128)(2,1)S(1)} custom-call(bf16[8,32,1152]{2,1,0:T(8,128)(2,1)} %bitcast.97), custom_call_target="tpu_custom_call" | custom-call | tf_op jit(solution)/shard_map/pallas_call | solution.py:203
  115.0 46.3 %conditional.3 = (f32[128,128,128]{2,1,0:T(8,128)}) conditional(s32[]{:T(128)} %convert_element_type.36, f32[128,128,128]{2,1,0:T(8,128)} %get-tuple-element.59, (pred[128,128]{1,0:T(8,128)(4,1)S(1)}, bf16[24,32,1152]{2,1,0:T(8,128)(2,1)S(1)}, bf16[32,128,128]{2,1,0:T(8,128)(2,1)S(1)}, f32[8,128]{1,0:T(8,128)S(1)}, f32[128,128,128]{2,1,0:T(8,128)}, ...), branch_computations={%region_4.5_spmd, %region_5.6_spmd} | conditional | flops 8815512576 | bytes 131627016 | solution.py:384
  115.3 10.5 %fusion.3 = f32[512,8,8,128]{3,1,2,0:T(8,128)} fusion(s32[768]{0:T(1024)S(1)} %add_reduce_fusion, bf16[768,1152]{1,0:T(8,128)(2,1)S(1)} %bitcast.93), kind=kOutput, calls=%fused_computation.10 | convolution fusion | flops 6445596672 | bytes 18354176 | tf_op jit(solution)/shard_map/cond/branch_1_fun/dot_general | solution.py:372
  125.8 9.4 %copy.28 = f32[512,8,8,128]{3,2,1,0:T(8,128)S(1)} copy(f32[512,8,8,128]{3,1,2,0:T(8,128)} %fusion.3) | data formatting | bytes 33554432 | tf_op jit(solution)/shard_map/cond
  135.2 2.4 %fusion.10 = f32[128,8,128]{2,1,0:T(8,128)S(1)} fusion(bf16[32,128,128]{2,1,0:T(8,128)(2,1)S(1)} %get-tuple-element.52, f32[32,128,8,128]{3,2,1,0:T(8,128)S(1)} %bitcast.88), kind=kOutput, calls=%fused_computation.17 | convolution fusion | flops 1090519040 | bytes 18350080 | tf_op jit(solution)/shard_map/cond/branch_1_fun/wdfa,wab->fdb/dot_general | solution.py:380
  137.6 2.4 %fusion.14 = f32[8,128,128]{2,0,1:T(8,128)S(1)} fusion(f32[128,8,128]{2,1,0:T(8,128)S(1)} %fusion.10, bf16[32,128,128]{2,1,0:T(8,128)(2,1)S(1)} %get-tuple-element.52, f32[32,128,8,128]{3,2,1,0:T(8,128)S(1)} %bitcast.89), kind=kOutput, calls=%fused_computation.19 | convolution fusion | flops 1073872896 | bytes 18874368 | tf_op jit(solution)/shard_map/cond/branch_1_fun/wdfa,wab->fdb/dot_general | solution.py:378
  140.0 17.9 %add_select_fusion = f32[128,128,128]{2,1,0:T(8,128)S(1)} fusion(f32[128,128,128]{2,1,0:T(8,128)} %get-tuple-element.54, f32[128,128,128]{2,1,0:T(8,128)} %get-tuple-element.50, pred[128,128]{1,0:T(8,128)(4,1)S(1)} %get-tuple-element.49, f32[8,128,128]{2,0,1:T(8,128)S(1)} %fusion.14, f32[8,128]{1,0:T(8,128)S(1)} %get-tuple-element.70), kind=kOutput, calls=%fused_computation.12 | convolution fusion | flops 205520896 | bytes 25710592 | tf_op jit(solution)/shard_map/cond/branch_1_fun/frc,fk->rck/dot_general | solution.py:381
  157.9 3.4 %copy.37 = f32[128,128,128]{2,1,0:T(8,128)} copy(f32[128,128,128]{2,1,0:T(8,128)S(1)} %add_select_fusion) | data formatting | bytes 16777216 | tf_op jit(solution)/shard_map/cond
  161.3 5.9 %copy.27 = f32[128,128,1]{1,0,2:T(8,128)} copy(f32[128,128,1]{2,1,0:T(8,128)} %bitcast.90) | data formatting | bytes 131072
  167.1 24.8 %shard_map.109 = f32[8,128,128]{2,1,0:T(8,128)} custom-call(f32[128,128]{1,0:T(8,128)} %bitcast.96), custom_call_target="tpu_custom_call" | custom-call | tf_op jit(solution)/shard_map/pallas_call | solution.py:273
  192.0 1.8 gather_fusion
  193.7 5.0 %select_reduce_fusion = f32[256,128]{1,0:T(8,128)S(1)} fusion(bf16[32,128,128]{2,1,0:T(8,128)(2,1)S(1)} %copy-done.1, pred[256,32]{0,1:T(8,128)(4,1)S(1)} %iota_compare_fusion.6, f32[256,128]{1,0:T(8,128)S(1)} %gather_fusion, pred[256]{0:T(512)(128)(4,1)S(1)} %get-tuple-element.102), kind=kOutput, calls=%fused_computation.24 | convolution fusion | flops 1612709888 | bytes 1319168 | tf_op jit(solution)/shard_map/eb,wab->ewa/dot_general | solution.py:393
  198.9 1.5 select_select_fusion
  (44 shorter events, 4.2 us)
Async XLA Ops:
  1.5 17.3 %collective-permute-start.1 = (f32[1,128,128]{2,1,0:T(8,128)S(1)}, f32[1,128,128]{2,1,0:T(8,128)S(1)}, u32[]{:S(2)}, u32[]{:S(2)}) collective-permute-start(f32[1,128,128]{2,1,0:T(8,128)S(1)} %get-tuple-element.118), channel_id=1, source_target_pairs={{8,0},{16,8},{24,16},{32,24},{40,32},{48,40},{56,48},{64,56},{72,6... | collective-permute-start | bytes 196616 | tf_op jit(solution)/shard_map/ppermute | solution.py:125
  7.4 12.5 %collective-permute-start = (f32[1,128,128]{2,1,0:T(8,128)S(1)}, f32[1,128,128]{2,1,0:T(8,128)S(1)}, u32[]{:S(2)}, u32[]{:S(2)}) collective-permute-start(f32[1,128,128]{2,1,0:T(8,128)S(1)} %get-tuple-element.119), channel_id=1, source_target_pairs={{0,8},{8,16},{16,24},{24,32},{32,40},{40,48},{48,56},{56,64},{64,7... | collective-permute-start | bytes 196616 | tf_op jit(solution)/shard_map/ppermute | solution.py:124
  10.6 10.4 %collective-permute-start.2 = (f32[128,1,128]{2,1,0:T(1,128)S(1)}, f32[128,1,128]{2,1,0:T(1,128)S(1)}, u32[]{:S(2)}, u32[]{:S(2)}) collective-permute-start(f32[128,1,128]{2,1,0:T(1,128)S(1)} %get-tuple-element.115), channel_id=1, source_target_pairs={{0,1},{1,2},{2,3},{3,4},{4,5},{5,6},{6,7},{7,0},{8,9},{9,10},{10,1... | collective-permute-start | bytes 196616 | tf_op jit(solution)/shard_map/ppermute | solution.py:133
  12.7 8.3 %collective-permute-start.3 = (f32[128,1,128]{2,1,0:T(1,128)S(1)}, f32[128,1,128]{2,1,0:T(1,128)S(1)}, u32[]{:S(2)}, u32[]{:S(2)}) collective-permute-start(f32[128,1,128]{2,1,0:T(1,128)S(1)} %get-tuple-element.114), channel_id=1, source_target_pairs={{1,0},{2,1},{3,2},{4,3},{5,4},{6,5},{7,6},{0,7},{9,8},{10,9},{11,1... | collective-permute-start | bytes 196616 | tf_op jit(solution)/shard_map/ppermute | solution.py:134
  21.0 32.8 %copy-start.2 = (f32[128,128]{1,0:T(8,128)S(1)}, f32[128,128]{1,0:T(8,128)}, u32[]{:S(2)}) copy-start(f32[128,128]{1,0:T(8,128)} %param.16) | copy-start | bytes 196612
  21.0 32.8 %copy-start.6 = (f32[128,8]{0,1:T(8,128)S(1)}, f32[128,8]{0,1:T(8,128)}, u32[]{:S(2)}) copy-start(f32[128,8]{0,1:T(8,128)} %param.18) | copy-start | bytes 12292
  21.0 0.6 copy-start.4
  21.6 0.6 copy-start.5
  40.0 9.9 %collective-permute-start.4 = (f32[1,128,128]{2,1,0:T(8,128)S(1)}, f32[1,128,128]{2,1,0:T(8,128)S(1)}, u32[]{:S(2)}, u32[]{:S(2)}) collective-permute-start(f32[1,128,128]{2,1,0:T(8,128)S(1)} %get-tuple-element.111), channel_id=1, source_target_pairs={{0,8},{8,16},{16,24},{24,32},{32,40},{40,48},{48,56},{56,64},{64,7... | collective-permute-start | bytes 196616 | tf_op jit(solution)/shard_map/ppermute | solution.py:124
  41.9 7.9 %collective-permute-start.5 = (f32[1,128,128]{2,1,0:T(8,128)S(1)}, f32[1,128,128]{2,1,0:T(8,128)S(1)}, u32[]{:S(2)}, u32[]{:S(2)}) collective-permute-start(f32[1,128,128]{2,1,0:T(8,128)S(1)} %get-tuple-element.110), channel_id=1, source_target_pairs={{8,0},{16,8},{24,16},{32,24},{40,32},{48,40},{56,48},{64,56},{72,6... | collective-permute-start | bytes 196616 | tf_op jit(solution)/shard_map/ppermute | solution.py:125
  47.7 3.4 %collective-permute-start.6 = (f32[128,1,128]{2,1,0:T(1,128)S(1)}, f32[128,1,128]{2,1,0:T(1,128)S(1)}, u32[]{:S(2)}, u32[]{:S(2)}) collective-permute-start(f32[128,1,128]{2,1,0:T(1,128)S(1)} %get-tuple-element.113), channel_id=1, source_target_pairs={{0,1},{1,2},{2,3},{3,4},{4,5},{5,6},{6,7},{7,0},{8,9},{9,10},{10,1... | collective-permute-start | bytes 196616 | tf_op jit(solution)/shard_map/ppermute | solution.py:133
  49.7 4.0 %collective-permute-start.7 = (f32[128,1,128]{2,1,0:T(1,128)S(1)}, f32[128,1,128]{2,1,0:T(1,128)S(1)}, u32[]{:S(2)}, u32[]{:S(2)}) collective-permute-start(f32[128,1,128]{2,1,0:T(1,128)S(1)} %get-tuple-element.112), channel_id=1, source_target_pairs={{1,0},{2,1},{3,2},{4,3},{5,4},{6,5},{7,6},{0,7},{9,8},{10,9},{11,1... | collective-permute-start | bytes 196616 | tf_op jit(solution)/shard_map/ppermute | solution.py:134
  53.8 61.2 %copy-start.1 = (bf16[32,128,128]{2,1,0:T(8,128)(2,1)S(1)}, bf16[32,128,128]{2,1,0:T(8,128)(2,1)}, u32[]{:S(2)}) copy-start(bf16[32,128,128]{2,1,0:T(8,128)(2,1)} %param.20) | copy-start | bytes 3145732
  53.8 61.2 %copy-start.7 = (f32[8,128]{1,0:T(8,128)S(1)}, f32[8,128]{1,0:T(8,128)}, u32[]{:S(2)}) copy-start(f32[8,128]{1,0:T(8,128)} %param.19) | copy-start | bytes 12292
  161.3 37.6 %copy-start.3 = (s32[128,128]{1,0:T(8,128)S(1)}, s32[128,128]{1,0:T(8,128)}, u32[]{:S(2)}) copy-start(s32[128,128]{1,0:T(8,128)} %param.14) | copy-start | bytes 196612

commit v4 on v3

--- a/solution.py
+++ b/solution.py
@@ -114,6 +114,7 @@
     return (
         packed.reshape(owner_total, slots_each, blocks.shape[1]),
         placed_labels.reshape(owner_total, slots_each),
+        target_slot,
     )
 
 
@@ -235,7 +236,7 @@
             for k, off in enumerate(offsets):
                 target = tile_device(target_comp, (tile + tiles - off) % tiles, lon_total)
                 copy = pltpu.make_async_remote_copy(
-                    src_ref=surface_ref,
+                    src_ref=surface_ref.at[target_comp * count + k],
                     dst_ref=land.at[k],
                     send_sem=send_sems.at[target_comp * count + k],
                     recv_sem=recv_sems.at[k],
@@ -257,7 +258,7 @@
         for k, off in enumerate(offsets):
             source = tile_device(ocean, (tile + off) % tiles, lon_total)
             pltpu.make_async_remote_copy(
-                src_ref=surface_ref,
+                src_ref=surface_ref.at[k],
                 dst_ref=land.at[k],
                 send_sem=send_sems.at[k],
                 recv_sem=recv_sems.at[k],
@@ -267,21 +268,22 @@
         out_ref[...] = land[...]
 
 
-def spread_from_ocean(surface, offsets, shape):
+def spread_from_ocean(replies, offsets, shape):
     count = len(offsets)
     senders = (shape[0] - 1) * count
+    slot_shape = replies.shape[1:]
     return pl.pallas_call(
         functools.partial(spread_kernel, tuple(offsets), tuple(shape)),
-        out_shape=jax.ShapeDtypeStruct((count,) + surface.shape, surface.dtype),
+        out_shape=jax.ShapeDtypeStruct((count,) + slot_shape, replies.dtype),
         in_specs=[pl.BlockSpec(memory_space=pltpu.VMEM)],
         out_specs=pl.BlockSpec(memory_space=pltpu.VMEM),
         scratch_shapes=[
-            pltpu.VMEM((count,) + surface.shape, surface.dtype),
+            pltpu.VMEM((count,) + slot_shape, replies.dtype),
             pltpu.SemaphoreType.DMA((senders,)),
             pltpu.SemaphoreType.DMA((count,)),
         ],
         compiler_params=pltpu.CompilerParams(collective_id=1, has_side_effects=True),
-    )(surface)
+    )(replies)
 
 
 def local(
@@ -356,12 +358,14 @@
         ),
         axis=1,
     )
-    packed, _ = pack_rows(entry_blocks, neighbour_ids, labels, sending, capacity, neighbour_count)
+    packed, _, entry_slots = pack_rows(entry_blocks, neighbour_ids, labels, sending, capacity, neighbour_count)
     mesh_shape = (comp_count, lat_count, lon_count)
     arrived = gather_to_ocean(packed, offsets, mesh_shape)
     weights_low = regrid_weights
-
-    def ocean_final(values, arrived):
+    weights_wide = regrid_weights.astype(jnp.float32)
+    senders = (comp_count - 1) * neighbour_count
+
+    def ocean_reply(values, arrived):
         flat = arrived.reshape(-1, width + 128)
         fluxes = flat[:, :width]
         arrived_labels = flat[:, width].astype(jnp.int32) * tile_rows + flat[:, width + 1].astype(
@@ -373,27 +377,40 @@
             selector, fluxes, (((0,), (0,)), ((), ())), preferred_element_type=jnp.float32
         )
         binned = binned.reshape(weight_count, tile_rows, flux_count, block_len)
-        binned_hi = binned.astype(jnp.bfloat16)
-        binned_lo = (binned - binned_hi.astype(jnp.float32)).astype(jnp.bfloat16)
+        binned_hi = lax.reduce_precision(binned, exponent_bits=8, mantissa_bits=7)
+        binned_lo = (binned - binned_hi).astype(jnp.bfloat16)
         forcing = jnp.einsum(
-            "wdfa,wab->fdb", binned_hi, weights_low, preferred_element_type=jnp.float32
+            "wdfa,wab->fdb",
+            binned_hi.astype(jnp.bfloat16),
+            weights_low,
+            preferred_element_type=jnp.float32,
         ) + jnp.einsum("wdfa,wab->fdb", binned_lo, weights_low, preferred_element_type=jnp.float32)
+        lifted = jnp.sum(forcing * ocean_map[:, 0][:, None, None], axis=0)
+        top_level = jnp.where(sea_cells, values[:, :, 0] + lifted, state[:, :, 0])
+        table = jnp.einsum("db,wab->wda", top_level, weights_wide, precision=HIGHEST)
+        replies = jnp.take(table.reshape(weight_count * tile_rows, block_len), arrived_labels, axis=0)
+        return forcing, replies.reshape(senders, capacity, block_len)
+
+    def atmosphere_reply(values, arrived):
+        return (
+            jnp.zeros((flux_count, tile_rows, block_len), jnp.float32),
+            jnp.zeros((senders, capacity, block_len), jnp.float32),
+        )
+
+    forcing, replies = lax.cond(ocean_side, ocean_reply, atmosphere_reply, first, arrived)
+    answers = spread_from_ocean(replies, offsets, mesh_shape)
+    per_entry = jnp.take(
+        answers.reshape(neighbour_count * capacity, block_len), entry_slots, axis=0
+    )
+    returned = per_entry.reshape(tile_rows, intersections, block_len).sum(axis=1)
+    first, forcing, answers = lax.optimization_barrier((first, forcing, answers))
+
+    def ocean_final(values, forcing):
         moved = values + jnp.einsum("frc,fk->rck", forcing, ocean_map, precision=HIGHEST)
         return jnp.where(sea_cells[:, :, None], moved, state)
 
-    final_state = lax.cond(ocean_side, ocean_final, lambda values, arrived: values, second, arrived)
+    final_state = lax.cond(ocean_side, ocean_final, lambda values, forcing: second, first, forcing)
     surface = final_state[:, :, 0]
-    around = spread_from_ocean(surface, offsets, mesh_shape)
-    picked = jnp.take(
-        around.reshape(neighbour_count * tile_rows, block_len),
-        neighbour_ids * tile_rows + targets,
-        axis=0,
-    )
-    weights_wide = regrid_weights.astype(jnp.float32)
-    images = jnp.einsum("eb,wab->ewa", picked, weights_wide, precision=HIGHEST)
-    which_block = weight_ids[:, None] == jnp.arange(weight_count, dtype=jnp.int32)[None, :]
-    chosen = jnp.sum(jnp.where(which_block[:, :, None], images, 0.0), axis=1)
-    returned = chosen.reshape(tile_rows, intersections, block_len).sum(axis=1)
     surface_out = jnp.where(ocean_side, surface, jnp.where(sea_cells, returned, surface))
     return (final_state, surface_out)
 

time: 202 us -> 212 us (1.050)
  Pallas kernels: 100 us -> 68.3 us
  local copies, waits for them, and re-layouts: 28.9 us -> 57.7 us
  matrix products: 39.3 us -> 48.1 us
  other arithmetic: 7.49 us -> 12.4 us
    pallas_call x1, Pallas kernels: 24.8 us -> 6.07 us  [spread_from_ocean(): pl.pallas_call(functools.partial(spread_kernel, tuple(offsets), tuple(sha...]
    another operation x1 -> x4, local copies, waits for them, and re-layouts: 0.04 us -> 18.8 us
    pallas_call x1, Pallas kernels: 59.8 us -> 46.6 us  [gather_to_ocean(): pl.pallas_call(functools.partial(gather_kernel, tuple(offsets), tuple(sha...]
    cond x2 -> x7, local copies, waits for them, and re-layouts: 12.8 us -> 22.6 us
    dot_general x4, matrix products: 20.2 us -> 28.6 us  [the longest x1 10.6 us: ocean_reply(): jnp.einsum('wdfa,wab->fdb', binned_hi.astype(jnp.bfloat16), weights_low,...]
    convert_element_type x0 -> x1, other arithmetic: none -> 2.86 us  [local(): weights_wide = regrid_weights.astype(jnp.float32)]
    unnamed x17 -> x25, local copies, waits for them, and re-layouts: 8.02 us -> 7.43 us
  transfers between devices with their start and end apart: 8 -> 8, of which waited for: 2 -> 2; matrix products, arithmetic and copies ran while one was open for 5% -> 6% of each run, Pallas kernels for 0% -> 0%
where the time goes in v4:
time: 212 us; the launch traced here: 211 us
  Pallas kernels  68.3 us (32%)
  local copies, waits for them, and re-layouts  57.7 us (27%)
  matrix products  48.1 us (23%)
  starting transfers between devices  19.7 us (9%)
  other arithmetic  12.4 us (6%)
  waiting for transfers between devices  3.26 us (2%)
    pallas_call x1, Pallas kernels, gather_to_ocean(): pl.pallas_call(functools.partial(gather_kernel, tuple(offsets), tuple(sha...  46.6 us
    cond x7, local copies, waits for them, and re-layouts  22.6 us
    another operation x4, local copies, waits for them, and re-layouts  18.8 us
    dot_general x1, matrix products, ocean_final(): jnp.einsum('frc,fk->rck', forcing, ocean_map, precision=HIGHEST)  18.3 us
    pallas_call x1, Pallas kernels, substep(): pl.pallas_call(functools.partial(substep_kernel, with_flux), grid=(blocks...  15.6 us
    ppermute x2, starting transfers between devices, edge_rows(): after = lax.ppermute(values[:1], ('comp', 'lat'), down)  11.6 us
    dot_general x1, matrix products, ocean_reply(): jnp.einsum('wdfa,wab->fdb', binned_hi.astype(jnp.bfloat16), weights_low,...  10.6 us
    dot_general x1, matrix products, ocean_reply(): lax.dot_general(selector, fluxes, (((0,), (0,)), ((), ())), preferred_ele...  10.3 us
  transfers between devices with their start and end apart: 8, of which 2 were waited for; matrix products, arithmetic and copies ran while one was open for 6% of the time, Pallas kernels for 0%

profile of v4, /device:TPU:25, one launch (start us, length us, event | category | flops | bytes accessed | tf_op | source)
XLA Modules:
  0.0 210.7 jit_solution(16007807857197915135)
XLA Ops:
  1.5 5.8 %collective-permute-start.1 = (f32[1,128,128]{2,1,0:T(8,128)S(1)}, f32[1,128,128]{2,1,0:T(8,128)S(1)}, u32[]{:S(2)}, u32[]{:S(2)}) collective-permute-start(f32[1,128,128]{2,1,0:T(8,128)S(1)} %get-tuple-element.186), channel_id=1, source_target_pairs={{8,0},{16,8},{24,16},{32,24},{40,32},{48,40},{56,48},{64,56},{72,6... | collective-permute-start | bytes 196616 | tf_op jit(solution)/shard_map/ppermute | solution.py:126
  7.4 1.9 collective-permute-start
  9.3 1.3 fusion.43
  10.6 2.1 collective-permute-start.2
  12.7 1.6 fusion.44
  17.9 1.5 broadcast_select_fusion.3.mix_ref
  19.5 2.9 %convert_element_type.44 = f32[32,128,128]{2,1,0:T(8,128)} convert(bf16[32,128,128]{2,1,0:T(8,128)(2,1)} %param.22) | non-fusion elementwise | flops 524288 | bytes 3145728 | tf_op jit(solution)/shard_map/convert_element_type | solution.py:365
  25.8 15.6 %shard_map.106 = f32[128,128,128]{2,1,0:T(8,128)} custom-call(f32[128,128,128]{2,1,0:T(8,128)} %x_ref.1, f32[16,128,128]{2,1,0:T(8,128)} %pad_maximum_fusion.2.top_ref, f32[16,128,128]{2,1,0:T(8,128)} %pad_maximum_fusion.3.bottom_ref, f32[128,1,128]{2,1,0:T(1,128)} %copy-done.6, f32[128,1,128]{2,1,0:T(1,128)} %copy-done.7, ...), custom_call_target="tpu_custom_call" | custom-call | flops 1610612736 | bytes 16777216 | tf_op jit(solution)/shard_map/pallas_call | solution.py:78
  42.3 1.3 fusion.42
  43.6 1.9 collective-permute-start.4
  45.5 5.8 %collective-permute-start.5 = (f32[1,128,128]{2,1,0:T(8,128)S(1)}, f32[1,128,128]{2,1,0:T(8,128)S(1)}, u32[]{:S(2)}, u32[]{:S(2)}) collective-permute-start(f32[1,128,128]{2,1,0:T(8,128)S(1)} %get-tuple-element.178), channel_id=1, source_target_pairs={{8,0},{16,8},{24,16},{32,24},{40,32},{48,40},{56,48},{64,56},{72,6... | collective-permute-start | bytes 196616 | tf_op jit(solution)/shard_map/ppermute | solution.py:126
  51.3 2.0 collective-permute-start.6
  54.7 2.7 %collective-permute-done.7 = f32[128,1,128]{2,1,0:T(1,128)S(1)} collective-permute-done((f32[128,1,128]{2,1,0:T(1,128)S(1)}, f32[128,1,128]{2,1,0:T(1,128)S(1)}, u32[]{:S(2)}, u32[]{:S(2)}) %collective-permute-start.7) | collective-permute-done | bytes 65568 | tf_op jit(solution)/shard_map/ppermute | solution.py:135
  57.4 8.0 %conditional.3 = (f32[128,128,128]{2,1,0:T(8,128)}, bf16[8,128,128]{2,0,1:T(8,128)(2,1)S(1)}) conditional(s32[]{:T(128)} %convert_element_type.40, (f32[128,128,128]{2,1,0:T(8,128)}, pred[1,128,128]{2,1,0:T(8,128)(4,1)S(1)}, pred[1,128,128]{2,1,0:T(8,128)(4,1)S(1)}, f32[128,8]{0,1:T(8,128)S(1)}, f32[128,1,128]{2,1,0:T(1,128)S(1)}, ...), branch_computations={%region_0.1_spmd.clone, %region_1.2_spmd} | conditional | flops 1712226304 | bytes 26066960 | solution.py:330
  57.4 8.0 %copy.70 = f32[128,128,128]{2,1,0:T(8,128)} copy(f32[128,128,128]{2,1,0:T(8,128)} %param.1) | data formatting | bytes 16777216 | tf_op jit(solution)/shard_map/cond
  66.8 46.6 %shard_map.107 = bf16[24,32,1152]{2,1,0:T(8,128)(2,1)S(1)} custom-call(bf16[8,32,1152]{2,1,0:T(8,128)(2,1)} %bitcast.90), custom_call_target="tpu_custom_call" | custom-call | tf_op jit(solution)/shard_map/pallas_call | solution.py:204
  113.4 62.5 %conditional.4 = (f32[8,128,128]{2,1,0:T(8,128)}, f32[24,32,128]{2,1,0:T(8,128)S(1)}) conditional(s32[]{:T(128)} %convert_element_type.40, () %tuple.42, (bf16[24,32,1152]{2,1,0:T(8,128)(2,1)S(1)}, bf16[32,128,128]{2,1,0:T(8,128)(2,1)S(1)}, f32[128,128,128]{2,1,0:T(8,128)}, f32[8,128]{1,0:T(8,128)S(1)}, f32[128,128,128]{2,1,0:T(8,128)}, ...), branch_computations={%region_4.5_spmd, %region_5.7_spmd} | conditional | flops 9419880448 | bytes 202953904 | solution.py:400
  113.8 10.3 %fusion.5 = f32[512,8,8,128]{3,1,2,0:T(8,128)} fusion(s32[768]{0:T(1024)S(1)} %get-tuple-element.169, bf16[768,1152]{1,0:T(8,128)(2,1)S(1)} %bitcast.85), kind=kOutput, calls=%fused_computation.14 | convolution fusion | flops 6445596672 | bytes 18354176 | tf_op jit(solution)/shard_map/cond/branch_1_fun/dot_general | solution.py:376
  124.2 9.6 %copy.48 = f32[512,8,8,128]{3,2,1,0:T(8,128)S(1)} copy(f32[512,8,8,128]{3,1,2,0:T(8,128)} %fusion.5) | data formatting | bytes 33554432 | tf_op jit(solution)/shard_map/cond
  133.8 4.1 %fusion.11 = f32[128,8,128]{2,0,1:T(8,128)S(1)} fusion(f32[32,128,8,128]{3,2,1,0:T(8,128)S(1)} %bitcast.79, bf16[32,128,128]{2,1,0:T(8,128)(2,1)S(1)} %get-tuple-element.62), kind=kOutput, calls=%fused_computation.19 | convolution fusion | flops 1086324736 | bytes 18350080 | tf_op jit(solution)/shard_map/cond/branch_1_fun/wdfa,wab->fdb/dot_general | solution.py:387
  137.8 1.7 copy-done
  139.6 10.6 %multiply_reduce_fusion = (f32[128,128]{1,0:T(8,128)S(1)}, f32[8,128,128]{2,1,0:T(8,128)}) fusion(f32[8]{0:T(128)S(1)} %slice_bitcast_fusion.2, f32[128,8,128]{2,0,1:T(8,128)S(1)} %fusion.11, bf16[32,128,128]{2,1,0:T(8,128)(2,1)S(1)} %get-tuple-element.62, f32[32,128,8,128]{3,2,1,0:T(8,128)} %bitcast.80), kind=kOutput, calls=%fused_computation.26 | convolution fusion | flops 1082507264 | bytes 18939936 | tf_op jit(solution)/shard_map/cond/branch_1_fun/wdfa,wab->fdb/dot_general | solution.py:382
  150.2 9.3 %copy.40 = f32[128,128,128]{1,0,2:T(8,128)} copy(f32[128,128,128]{2,1,0:T(8,128)} %get-tuple-element.158) | data formatting | bytes 16777216 | tf_op jit(solution)/shard_map
  159.5 9.3 %copy.42 = f32[128,128,128]{1,0,2:T(8,128)} copy(f32[128,128,128]{2,1,0:T(8,128)} %get-tuple-element.160) | data formatting | bytes 16777216 | tf_op jit(solution)/shard_map
  168.8 3.6 %fusion.23 = f32[128,32,128]{2,0,1:T(8,128)S(1)} fusion(f32[32,128,128]{2,1,0:T(8,128)} %get-tuple-element.67, pred[128,128]{1,0:T(32,128)(4,1)S(1)} %get-tuple-element.63, f32[128,128,128]{1,0,2:T(8,128)} %copy.42, f32[128,128]{1,0:T(8,128)S(1)} %get-tuple-element.176, f32[128,128,128]{1,0,2:T(8,128)} %copy.40), kind=kOutput, calls=%fused_computation.35 | convolution fusion | flops 805339136 | bytes 4407296 | tf_op jit(solution)/shard_map/cond/branch_1_fun/db,wab->wda/dot_general | solution.py:390
  172.4 1.6 gather_fusion
  174.0 1.4 and_reduce_fusion
  175.9 6.1 %shard_map.108 = f32[8,32,128]{2,1,0:T(8,128)} custom-call(f32[24,32,128]{2,1,0:T(8,128)S(1)} %get-tuple-element.84.surface_ref), custom_call_target="tpu_custom_call" | custom-call | tf_op jit(solution)/shard_map/pallas_call | solution.py:275
  181.9 21.7 %conditional.5 = (f32[128,128,128]{2,1,0:T(8,128)}) conditional(s32[]{:T(128)} %convert_element_type.40, f32[128,128,128]{2,1,0:T(8,128)} %get-tuple-element.81, (pred[128,128]{1,0:T(32,128)(4,1)S(1)}, f32[8,128,128]{2,1,0:T(8,128)}, f32[8,128]{1,0:T(8,128)}, f32[128,128,128]{2,1,0:T(8,128)}, f32[128,128,128]{2,1,0:T(8,128)}) %tuple.45), branch_computations={%region_7.8_spmd, %region_8.9_spmd} | conditional | flops 205520896 | bytes 42487816 | solution.py:412
  182.0 18.3 %add_select_fusion = f32[128,128,128]{2,1,0:T(8,128)S(1)} fusion(f32[128,128,128]{2,1,0:T(8,128)} %get-tuple-element.72, f32[128,128,128]{2,1,0:T(8,128)} %get-tuple-element.69, pred[128,128]{1,0:T(8,128)(4,1)S(1)} %bitcast.94, f32[8,128,128]{2,1,0:T(8,128)} %get-tuple-element.164, f32[8,128]{1,0:T(8,128)} %get-tuple-element.71), kind=kOutput, calls=%fused_computation.2 | convolution fusion | flops 205520896 | bytes 25710592 | tf_op jit(solution)/shard_map/cond/branch_1_fun/frc,fk->rck/dot_general | solution.py:409
  200.3 3.4 %copy.77 = f32[128,128,128]{2,1,0:T(8,128)} copy(f32[128,128,128]{2,1,0:T(8,128)S(1)} %add_select_fusion) | data formatting | bytes 16777216 | tf_op jit(solution)/shard_map/cond
  203.7 5.2 %copy.47 = f32[128,128,1]{1,0,2:T(8,128)S(1)} copy(f32[128,128,1]{2,1,0:T(8,128)} %bitcast.83) | data formatting | bytes 131072
  (69 shorter events, 14.1 us)
Async XLA Ops:
  1.5 20.9 %collective-permute-start.1 = (f32[1,128,128]{2,1,0:T(8,128)S(1)}, f32[1,128,128]{2,1,0:T(8,128)S(1)}, u32[]{:S(2)}, u32[]{:S(2)}) collective-permute-start(f32[1,128,128]{2,1,0:T(8,128)S(1)} %get-tuple-element.186), channel_id=1, source_target_pairs={{8,0},{16,8},{24,16},{32,24},{40,32},{48,40},{56,48},{64,56},{72,6... | collective-permute-start | bytes 196616 | tf_op jit(solution)/shard_map/ppermute | solution.py:126
  7.4 16.1 %collective-permute-start = (f32[1,128,128]{2,1,0:T(8,128)S(1)}, f32[1,128,128]{2,1,0:T(8,128)S(1)}, u32[]{:S(2)}, u32[]{:S(2)}) collective-permute-start(f32[1,128,128]{2,1,0:T(8,128)S(1)} %get-tuple-element.187), channel_id=1, source_target_pairs={{0,8},{8,16},{16,24},{24,32},{32,40},{40,48},{48,56},{56,64},{64,7... | collective-permute-start | bytes 196616 | tf_op jit(solution)/shard_map/ppermute | solution.py:125
  10.6 13.9 %collective-permute-start.2 = (f32[128,1,128]{2,1,0:T(1,128)S(1)}, f32[128,1,128]{2,1,0:T(1,128)S(1)}, u32[]{:S(2)}, u32[]{:S(2)}) collective-permute-start(f32[128,1,128]{2,1,0:T(1,128)S(1)} %get-tuple-element.183), channel_id=1, source_target_pairs={{0,1},{1,2},{2,3},{3,4},{4,5},{5,6},{6,7},{7,0},{8,9},{9,10},{10,1... | collective-permute-start | bytes 196616 | tf_op jit(solution)/shard_map/ppermute | solution.py:134
  12.7 11.9 %collective-permute-start.3 = (f32[128,1,128]{2,1,0:T(1,128)S(1)}, f32[128,1,128]{2,1,0:T(1,128)S(1)}, u32[]{:S(2)}, u32[]{:S(2)}) collective-permute-start(f32[128,1,128]{2,1,0:T(1,128)S(1)} %get-tuple-element.182), channel_id=1, source_target_pairs={{1,0},{2,1},{3,2},{4,3},{5,4},{6,5},{7,6},{0,7},{9,8},{10,9},{11,1... | collective-permute-start | bytes 196616 | tf_op jit(solution)/shard_map/ppermute | solution.py:135
  17.1 24.3 %copy-start.10 = (s32[256]{0:T(256)}, s32[256]{0:T(256)S(1)}, u32[]{:S(2)}) copy-start(s32[256]{0:T(256)S(1)} %multiply_add_fusion) | copy-start | bytes 3076
  24.5 32.8 %copy-start.4 = (f32[128,128]{1,0:T(8,128)S(1)}, f32[128,128]{1,0:T(8,128)}, u32[]{:S(2)}) copy-start(f32[128,128]{1,0:T(8,128)} %param.18) | copy-start | bytes 196612
  24.5 32.8 %copy-start.12 = (f32[128,8]{0,1:T(8,128)S(1)}, f32[128,8]{0,1:T(8,128)}, u32[]{:S(2)}) copy-start(f32[128,8]{0,1:T(8,128)} %param.20) | copy-start | bytes 12292
  24.5 0.6 copy-start.6
  25.2 0.6 copy-start.7
  43.6 10.5 %collective-permute-start.4 = (f32[1,128,128]{2,1,0:T(8,128)S(1)}, f32[1,128,128]{2,1,0:T(8,128)S(1)}, u32[]{:S(2)}, u32[]{:S(2)}) collective-permute-start(f32[1,128,128]{2,1,0:T(8,128)S(1)} %get-tuple-element.179), channel_id=1, source_target_pairs={{0,8},{8,16},{16,24},{24,32},{32,40},{40,48},{48,56},{56,64},{64,7... | collective-permute-start | bytes 196616 | tf_op jit(solution)/shard_map/ppermute | solution.py:125
  45.5 8.5 %collective-permute-start.5 = (f32[1,128,128]{2,1,0:T(8,128)S(1)}, f32[1,128,128]{2,1,0:T(8,128)S(1)}, u32[]{:S(2)}, u32[]{:S(2)}) collective-permute-start(f32[1,128,128]{2,1,0:T(8,128)S(1)} %get-tuple-element.178), channel_id=1, source_target_pairs={{8,0},{16,8},{24,16},{32,24},{40,32},{48,40},{56,48},{64,56},{72,6... | collective-permute-start | bytes 196616 | tf_op jit(solution)/shard_map/ppermute | solution.py:126
  51.3 3.4 %collective-permute-start.6 = (f32[128,1,128]{2,1,0:T(1,128)S(1)}, f32[128,1,128]{2,1,0:T(1,128)S(1)}, u32[]{:S(2)}, u32[]{:S(2)}) collective-permute-start(f32[128,1,128]{2,1,0:T(1,128)S(1)} %get-tuple-element.181), channel_id=1, source_target_pairs={{0,1},{1,2},{2,3},{3,4},{4,5},{5,6},{6,7},{7,0},{8,9},{9,10},{10,1... | collective-permute-start | bytes 196616 | tf_op jit(solution)/shard_map/ppermute | solution.py:134
  53.3 4.0 %collective-permute-start.7 = (f32[128,1,128]{2,1,0:T(1,128)S(1)}, f32[128,1,128]{2,1,0:T(1,128)S(1)}, u32[]{:S(2)}, u32[]{:S(2)}) collective-permute-start(f32[128,1,128]{2,1,0:T(1,128)S(1)} %get-tuple-element.180), channel_id=1, source_target_pairs={{1,0},{2,1},{3,2},{4,3},{5,4},{6,5},{7,6},{0,7},{9,8},{10,9},{11,1... | collective-permute-start | bytes 196616 | tf_op jit(solution)/shard_map/ppermute | solution.py:135
  57.4 8.2 %copy-start.11 = (s32[256]{0:T(256)S(1)}, s32[256]{0:T(256)}, u32[]{:S(2)}) copy-start(s32[256]{0:T(256)} %copy-done.10) | copy-start | bytes 3076
  57.4 56.0 %copy-start.2 = (bf16[32,128,128]{2,1,0:T(8,128)(2,1)S(1)}, bf16[32,128,128]{2,1,0:T(8,128)(2,1)}, u32[]{:S(2)}) copy-start(bf16[32,128,128]{2,1,0:T(8,128)(2,1)} %param.22) | copy-start | bytes 3145732
  57.4 56.0 %copy-start.9 = (f32[8,128]{1,0:T(8,128)S(1)}, f32[8,128]{1,0:T(8,128)}, u32[]{:S(2)}) copy-start(f32[8,128]{1,0:T(8,128)} %param.21) | copy-start | bytes 12292
  113.4 10.7 %copy-start.3 = (bf16[24,32,1152]{2,1,0:T(8,128)(2,1)}, bf16[24,32,1152]{2,1,0:T(8,128)(2,1)S(1)}, u32[]{:S(2)}) copy-start(bf16[24,32,1152]{2,1,0:T(8,128)(2,1)S(1)} %get-tuple-element.61) | copy-start | bytes 5308420 | tf_op jit(solution)/shard_map/cond
  133.8 5.7 %copy-start = (f32[512,8,8,128]{3,2,1,0:T(8,128)}, f32[512,8,8,128]{3,2,1,0:T(8,128)S(1)}, u32[]{:S(2)}) copy-start(f32[512,8,8,128]{3,2,1,0:T(8,128)S(1)} %copy.48) | copy-start | bytes 50331652 | tf_op jit(solution)/shard_map/cond
  203.7 5.3 %copy-start.1 = (f32[8,32,128]{2,1,0:T(8,128)S(1)}, f32[8,32,128]{2,1,0:T(8,128)}, u32[]{:S(2)}) copy-start(f32[8,32,128]{2,1,0:T(8,128)} %shard_map.108) | copy-start | bytes 393220
  203.7 6.1 %copy-start.8 = (pred[128,2]{1,0:T(8,128)(4,1)S(1)}, pred[128,2]{1,0:T(8,128)(4,1)}, u32[]{:S(2)}) copy-start(pred[128,2]{1,0:T(8,128)(4,1)} %compare_and_fusion) | copy-start | bytes 772
  203.7 6.4 %copy-start.5 = (s32[128,128]{1,0:T(8,128)S(1)}, s32[128,128]{1,0:T(8,128)}, u32[]{:S(2)}) copy-start(s32[128,128]{1,0:T(8,128)} %param.16) | copy-start | bytes 196612

commit v5 on v4

--- a/solution.py
+++ b/solution.py
@@ -28,11 +28,25 @@
     return one(lhs_hi, rhs_hi) + (one(lhs_hi, rhs_lo) + one(lhs_lo, rhs_hi))
 
 
+def exact_rows(picker, values):
+    high = values.astype(jnp.bfloat16)
+    rest = values - high.astype(jnp.float32)
+    middle = rest.astype(jnp.bfloat16)
+    low = (rest - middle.astype(jnp.float32)).astype(jnp.bfloat16)
+
+    def one(piece):
+        return lax.dot_general(
+            picker, piece, (((1,), (1,)), ((), ())), preferred_element_type=jnp.float32
+        )
+
+    return one(high) + one(middle) + one(low)
+
+
 def substep_kernel(with_flux, x_ref, top_ref, bottom_ref, west_ref, east_ref, mix_ref, *rest):
     if with_flux:
-        fluxes_ref, out_ref, flux_out_ref = rest
+        fluxes_ref, out_ref, planes_ref, flux_out_ref = rest
     else:
-        (out_ref,) = rest
+        out_ref, planes_ref = rest
     rows, cols, levels = x_ref.shape
     centre = x_ref[...]
     up = jnp.concatenate([top_ref[...], centre[:-1]], axis=0)
@@ -45,6 +59,13 @@
     mixed = three_pass(flat, mix_ref[...], ((1,), (0,)))
     moved = flat + PHYSICS * jnp.tanh(mixed)
     out_ref[...] = moved.reshape(rows, cols, levels)
+    plane_row = lax.broadcasted_iota(jnp.int32, (8, levels), 0)
+    plane_lane = lax.broadcasted_iota(jnp.int32, (8, levels), 1)
+    pick_out = ((plane_row == 0) & (plane_lane == 0)).astype(jnp.bfloat16)
+    pick_in = ((plane_row == 1) & (plane_lane == 0)).astype(jnp.bfloat16)
+    planes_ref[...] = exact_rows(pick_out, moved) + exact_rows(
+        pick_in, centre.reshape(rows * cols, levels)
+    )
     if with_flux:
         total = centre.reshape(rows * cols, levels) + moved
         flux_out_ref[...] = three_pass(fluxes_ref[...], total, ((1,), (1,)))
@@ -65,8 +86,14 @@
         pl.BlockSpec((levels, levels), lambda i: (0, 0)),
     ]
     operands = [values, top_rows, bottom_rows, west, east, mixing]
-    out_shape = [jax.ShapeDtypeStruct(values.shape, jnp.float32)]
-    out_specs = [pl.BlockSpec((ROW_BLOCK, cols, levels), lambda i: (i, 0, 0))]
+    out_shape = [
+        jax.ShapeDtypeStruct(values.shape, jnp.float32),
+        jax.ShapeDtypeStruct((8, rows * cols), jnp.float32),
+    ]
+    out_specs = [
+        pl.BlockSpec((ROW_BLOCK, cols, levels), lambda i: (i, 0, 0)),
+        pl.BlockSpec((8, ROW_BLOCK * cols), lambda i: (0, i)),
+    ]
     if with_flux:
         flux_count = fluxes_t.shape[0]
         in_specs.append(pl.BlockSpec((flux_count, levels), lambda i: (0, 0)))
@@ -315,19 +342,26 @@
     top, bottom = edge_rows(state, lower_valid, upper_valid)
     west, east = edge_columns(state)
     mixing = jnp.where(ocean_side, mix_ocn, mix_atm)
-    (first,) = substep(state, top, bottom, west, east, mixing)
+    first, first_planes = substep(state, top, bottom, west, east, mixing)
+    first_top = first_planes[0].reshape(tile_rows, block_len)
+    state_top = first_planes[1].reshape(tile_rows, block_len)
     top, bottom = edge_rows(first, lower_valid, upper_valid)
     west, east = edge_columns(first)
 
     def atmosphere_second(values, top, bottom, west, east):
-        moved, total = substep(values, top, bottom, west, east, mix_atm, flux_map.T)
+        moved, planes, total = substep(values, top, bottom, west, east, mix_atm, flux_map.T)
         total = total.reshape(flux_count, tile_rows, block_len)
-        return moved, jnp.where(sea_cells[None], 0.5 * total, 0.0).astype(jnp.bfloat16)
+        sent = jnp.where(sea_cells[None], 0.5 * total, 0.0).astype(jnp.bfloat16)
+        return moved, planes[0].reshape(tile_rows, block_len), sent
 
     def ocean_second(values, top, bottom, west, east):
-        return values, jnp.zeros((flux_count, tile_rows, block_len), jnp.bfloat16)
-
-    second, flux_sent = lax.cond(
+        return (
+            values,
+            jnp.zeros((tile_rows, block_len), jnp.float32),
+            jnp.zeros((flux_count, tile_rows, block_len), jnp.bfloat16),
+        )
+
+    second, second_top, flux_sent = lax.cond(
         ocean_side, ocean_second, atmosphere_second, first, top, bottom, west, east
     )
     entry_list = intersection_list.reshape(tile_rows * intersections, 3)
@@ -365,7 +399,7 @@
     weights_wide = regrid_weights.astype(jnp.float32)
     senders = (comp_count - 1) * neighbour_count
 
-    def ocean_reply(values, arrived):
+    def ocean_reply(values_top, arrived):
         flat = arrived.reshape(-1, width + 128)
         fluxes = flat[:, :width]
         arrived_labels = flat[:, width].astype(jnp.int32) * tile_rows + flat[:, width + 1].astype(
@@ -386,18 +420,21 @@
             preferred_element_type=jnp.float32,
         ) + jnp.einsum("wdfa,wab->fdb", binned_lo, weights_low, preferred_element_type=jnp.float32)
         lifted = jnp.sum(forcing * ocean_map[:, 0][:, None, None], axis=0)
-        top_level = jnp.where(sea_cells, values[:, :, 0] + lifted, state[:, :, 0])
+        top_level = jnp.where(sea_cells, values_top + lifted, state_top)
         table = jnp.einsum("db,wab->wda", top_level, weights_wide, precision=HIGHEST)
         replies = jnp.take(table.reshape(weight_count * tile_rows, block_len), arrived_labels, axis=0)
-        return forcing, replies.reshape(senders, capacity, block_len)
-
-    def atmosphere_reply(values, arrived):
+        return forcing, replies.reshape(senders, capacity, block_len), top_level
+
+    def atmosphere_reply(values_top, arrived):
         return (
             jnp.zeros((flux_count, tile_rows, block_len), jnp.float32),
             jnp.zeros((senders, capacity, block_len), jnp.float32),
+            values_top,
         )
 
-    forcing, replies = lax.cond(ocean_side, ocean_reply, atmosphere_reply, first, arrived)
+    forcing, replies, ocean_top = lax.cond(
+        ocean_side, ocean_reply, atmosphere_reply, first_top, arrived
+    )
     answers = spread_from_ocean(replies, offsets, mesh_shape)
     per_entry = jnp.take(
         answers.reshape(neighbour_count * capacity, block_len), entry_slots, axis=0
@@ -410,8 +447,7 @@
         return jnp.where(sea_cells[:, :, None], moved, state)
 
     final_state = lax.cond(ocean_side, ocean_final, lambda values, forcing: second, first, forcing)
-    surface = final_state[:, :, 0]
-    surface_out = jnp.where(ocean_side, surface, jnp.where(sea_cells, returned, surface))
+    surface_out = jnp.where(ocean_side, ocean_top, jnp.where(sea_cells, returned, second_top))
     return (final_state, surface_out)
 
 

time: 212 us -> 208 us (0.981)
  local copies, waits for them, and re-layouts: 57.7 us -> 36.7 us
  Pallas kernels: 68.3 us -> 83.3 us
  other arithmetic: 12.4 us -> 15.5 us
    another operation x4 -> x3, local copies, waits for them, and re-layouts: 18.8 us -> 0.14 us
    pallas_call x1, Pallas kernels: 46.6 us -> 54.2 us  [gather_to_ocean(): pl.pallas_call(functools.partial(gather_kernel, tuple(offsets), tuple(sha...]
    pallas_call x1, Pallas kernels: 15.6 us -> 23 us  [substep(): pl.pallas_call(functools.partial(substep_kernel, with_flux), grid=(blocks...]
    unnamed x25 -> x22, local copies, waits for them, and re-layouts: 7.43 us -> 2.19 us
    select_n x1 -> x2, other arithmetic: 0.65 us -> 2.97 us  [the longest x1 1.49 us: ocean_reply(): top_level = jnp.where(sea_cells, values_top + lifted, state_top)]
    cond x7 -> x9, local copies, waits for them, and re-layouts: 22.6 us -> 22.6 us
  transfers between devices with their start and end apart: 8 -> 8, of which waited for: 2 -> 1; matrix products, arithmetic and copies ran while one was open for 6% -> 7% of each run, Pallas kernels for 0% -> 0%
where the time goes in v5:
time: 208 us; the launch traced here: 207 us
  Pallas kernels  83.3 us (40%)
  matrix products  47.5 us (23%)
  local copies, waits for them, and re-layouts  36.7 us (18%)
  starting transfers between devices  19.7 us (9%)
  other arithmetic  15.5 us (7%)
  waiting for transfers between devices  2.6 us (1%)
    pallas_call x1, Pallas kernels, gather_to_ocean(): pl.pallas_call(functools.partial(gather_kernel, tuple(offsets), tuple(sha...  54.2 us
    pallas_call x1, Pallas kernels, substep(): pl.pallas_call(functools.partial(substep_kernel, with_flux), grid=(blocks...  23 us
    cond x9, local copies, waits for them, and re-layouts  22.6 us
    dot_general x1, matrix products, ocean_final(): jnp.einsum('frc,fk->rck', forcing, ocean_map, precision=HIGHEST)  18.3 us
    ppermute x2, starting transfers between devices, edge_rows(): after = lax.ppermute(values[:1], ('comp', 'lat'), down)  11.6 us
    dot_general x1, matrix products, ocean_reply(): jnp.einsum('wdfa,wab->fdb', binned_hi.astype(jnp.bfloat16), weights_low,...  10.8 us
    dot_general x1, matrix products, ocean_reply(): lax.dot_general(selector, fluxes, (((0,), (0,)), ((), ())), preferred_ele...  10.3 us
    pallas_call x1, Pallas kernels, spread_from_ocean(): pl.pallas_call(functools.partial(spread_kernel, tuple(offsets), tuple(sha...  6.08 us
  transfers between devices with their start and end apart: 8, of which 1 were waited for; matrix products, arithmetic and copies ran while one was open for 7% of the time, Pallas kernels for 0%

profile of v5, /device:TPU:25, one launch (start us, length us, event | category | flops | bytes accessed | tf_op | source)
XLA Modules:
  0.0 206.7 jit_solution(10142141169432927138)
XLA Ops:
  1.5 5.8 %collective-permute-start.1 = (f32[1,128,128]{2,1,0:T(8,128)S(1)}, f32[1,128,128]{2,1,0:T(8,128)S(1)}, u32[]{:S(2)}, u32[]{:S(2)}) collective-permute-start(f32[1,128,128]{2,1,0:T(8,128)S(1)} %get-tuple-element.193), channel_id=1, source_target_pairs={{8,0},{16,8},{24,16},{32,24},{40,32},{48,40},{56,48},{64,56},{72,6... | collective-permute-start | bytes 196616 | tf_op jit(solution)/shard_map/ppermute | solution.py:153
  7.4 1.9 collective-permute-start
  9.3 1.3 fusion.39
  10.6 2.1 collective-permute-start.2
  12.7 1.6 fusion.40
  17.9 1.5 broadcast_select_fusion.3.mix_ref
  19.6 2.9 %convert_element_type.44 = f32[32,128,128]{2,1,0:T(8,128)} convert(bf16[32,128,128]{2,1,0:T(8,128)(2,1)} %param.22) | non-fusion elementwise | flops 524288 | bytes 3145728 | tf_op jit(solution)/shard_map/convert_element_type | solution.py:399
  25.8 23.0 %shard_map.106 = (f32[128,128,128]{2,1,0:T(8,128)}, f32[8,16384]{1,0:T(8,128)S(1)}) custom-call(f32[128,128,128]{2,1,0:T(8,128)} %x_ref.1, f32[16,128,128]{2,1,0:T(8,128)} %pad_maximum_fusion.2.top_ref, f32[16,128,128]{2,1,0:T(8,128)} %pad_maximum_fusion.3.bottom_ref, f32[128,1,128]{2,1,0:T(1,128)} %copy-done.8, f32[128,1,128]{2,1,0:T(1,128)} %copy-done.9, ...), custom_call_target="tpu_custom_call" | custom-call | flops 1610612736 | bytes 16777216 | tf_op jit(solution)/shard_map/pallas_call | solution.py:105
  49.8 1.3 fusion.38
  51.1 1.9 collective-permute-start.4
  53.1 5.8 %collective-permute-start.5 = (f32[1,128,128]{2,1,0:T(8,128)S(1)}, f32[1,128,128]{2,1,0:T(8,128)S(1)}, u32[]{:S(2)}, u32[]{:S(2)}) collective-permute-start(f32[1,128,128]{2,1,0:T(8,128)S(1)} %get-tuple-element.185), channel_id=1, source_target_pairs={{8,0},{16,8},{24,16},{32,24},{40,32},{48,40},{56,48},{64,56},{72,6... | collective-permute-start | bytes 196616 | tf_op jit(solution)/shard_map/ppermute | solution.py:153
  58.8 2.0 collective-permute-start.6
  62.3 2.6 %collective-permute-done.7 = f32[128,1,128]{2,1,0:T(1,128)S(1)} collective-permute-done((f32[128,1,128]{2,1,0:T(1,128)S(1)}, f32[128,1,128]{2,1,0:T(1,128)S(1)}, u32[]{:S(2)}, u32[]{:S(2)}) %collective-permute-start.7) | collective-permute-done | bytes 65568 | tf_op jit(solution)/shard_map/ppermute | solution.py:162
  65.0 8.0 %conditional.3 = (f32[128,128,128]{2,1,0:T(8,128)}, f32[128,128]{1,0:T(8,128)S(1)}, bf16[8,128,128]{2,0,1:T(8,128)(2,1)S(1)}) conditional(s32[]{:T(128)} %convert_element_type.40, (f32[128,128,128]{2,1,0:T(8,128)}, pred[1,128,128]{2,1,0:T(8,128)(4,1)S(1)}, pred[1,128,128]{2,1,0:T(8,128)(4,1)S(1)}, f32[128,8]{0,1:T(8,128)S(1)}, ...), branch_computations={%region_0.1_spmd.clone, %region_1.2_spmd} | conditional | flops 1712226304 | bytes 26198040 | solution.py:364
  65.0 8.0 %copy.58 = f32[128,128,128]{2,1,0:T(8,128)} copy(f32[128,128,128]{2,1,0:T(8,128)} %param.1) | data formatting | bytes 16777216 | tf_op jit(solution)/shard_map/cond
  74.4 54.2 %shard_map.107 = bf16[24,32,1152]{2,1,0:T(8,128)(2,1)S(1)} custom-call(bf16[8,32,1152]{2,1,0:T(8,128)(2,1)} %bitcast.73), custom_call_target="tpu_custom_call" | custom-call | tf_op jit(solution)/shard_map/pallas_call | solution.py:231
  128.6 46.1 %conditional.4 = (f32[8,128,128]{2,1,0:T(8,128)}, f32[24,32,128]{2,1,0:T(8,128)S(1)}, f32[128,128]{1,0:T(8,128)}) conditional(s32[]{:T(128)} %convert_element_type.40, f32[128,128]{1,0:T(8,128)} %bitcast.14, (bf16[24,32,1152]{2,1,0:T(8,128)(2,1)S(1)}, bf16[32,128,128]{2,1,0:T(8,128)(2,1)S(1)}, f32[8,128]{1,0:T(8,128)S(1)}, f32[128,128]{1,0:T(8,128)}, ...), branch_computations={%region_4.5_spmd, %region_5.7_spmd} | conditional | flops 9419880448 | bytes 178050272 | solution.py:435
  129.2 10.3 %fusion.5 = f32[512,8,8,128]{3,1,2,0:T(8,128)} fusion(s32[768]{0:T(1024)S(1)} %get-tuple-element.176, bf16[768,1152]{1,0:T(8,128)(2,1)S(1)} %bitcast.68), kind=kOutput, calls=%fused_computation.14 | convolution fusion | flops 6445596672 | bytes 18354176 | tf_op jit(solution)/shard_map/cond/branch_1_fun/dot_general | solution.py:410
  139.5 9.6 %copy.35 = f32[512,8,8,128]{3,2,1,0:T(8,128)S(1)} copy(f32[512,8,8,128]{3,1,2,0:T(8,128)} %fusion.5) | data formatting | bytes 33554432 | tf_op jit(solution)/shard_map/cond
  149.1 4.1 %fusion.11 = f32[128,8,128]{2,0,1:T(8,128)S(1)} fusion(f32[32,128,8,128]{3,2,1,0:T(8,128)S(1)} %bitcast.63, bf16[32,128,128]{2,1,0:T(8,128)(2,1)S(1)} %get-tuple-element.60), kind=kOutput, calls=%fused_computation.19 | convolution fusion | flops 1086324736 | bytes 18350080 | tf_op jit(solution)/shard_map/cond/branch_1_fun/wdfa,wab->fdb/dot_general | solution.py:421
  153.2 1.6 copy-done
  155.0 10.8 %multiply_reduce_fusion = (f32[128,128]{1,0:T(8,128)S(1)}, f32[8,128,128]{2,1,0:T(8,128)}) fusion(f32[8]{0:T(128)S(1)} %slice_bitcast_fusion, f32[128,8,128]{2,0,1:T(8,128)S(1)} %fusion.11, bf16[32,128,128]{2,1,0:T(8,128)(2,1)S(1)} %get-tuple-element.60, f32[32,128,8,128]{3,2,1,0:T(8,128)} %bitcast.64), kind=kOutput, calls=%fused_computation.26 | convolution fusion | flops 1082507264 | bytes 18939936 | tf_op jit(solution)/shard_map/cond/branch_1_fun/wdfa,wab->fdb/dot_general | solution.py:416
  166.8 1.5 add_select_fusion.1
  168.3 2.8 %fusion.21 = f32[128,32,128]{2,0,1:T(8,128)S(1)} fusion(f32[32,128,128]{2,1,0:T(8,128)S(1)} %copy-done.2, f32[128,128]{1,0:T(8,128)} %add_select_fusion.1), kind=kOutput, calls=%fused_computation.32 | convolution fusion | flops 805306368 | bytes 4259840 | tf_op jit(solution)/shard_map/cond/branch_1_fun/db,wab->wda/dot_general | solution.py:424
  171.2 1.6 gather_fusion
  172.7 1.4 and_reduce_fusion
  174.6 6.1 %shard_map.108 = f32[8,32,128]{2,1,0:T(8,128)} custom-call(f32[24,32,128]{2,1,0:T(8,128)S(1)} %get-tuple-element.88.surface_ref), custom_call_target="tpu_custom_call" | custom-call | tf_op jit(solution)/shard_map/pallas_call | solution.py:302
  180.7 1.8 gather_fusion.1
  183.5 21.8 %conditional.5 = (f32[128,128,128]{2,1,0:T(8,128)}) conditional(s32[]{:T(128)} %convert_element_type.40, f32[128,128,128]{2,1,0:T(8,128)} %get-tuple-element.84, (pred[128,128]{1,0:T(8,128)(4,1)S(1)}, f32[8,128,128]{2,1,0:T(8,128)}, f32[8,128]{1,0:T(8,128)}, f32[128,128,128]{2,1,0:T(8,128)}, f32[128,128,128]{2,1,0:T(8,128)}) %tuple.34), branch_computations={%region_7.8_spmd, %region_8.9_spmd} | conditional | flops 205520896 | bytes 42487816 | solution.py:449
  183.5 18.3 %add_select_fusion = f32[128,128,128]{2,1,0:T(8,128)S(1)} fusion(f32[128,128,128]{2,1,0:T(8,128)} %get-tuple-element.70, f32[128,128,128]{2,1,0:T(8,128)} %get-tuple-element.67, pred[128,128]{1,0:T(8,128)(4,1)S(1)} %get-tuple-element.66, f32[8,128,128]{2,1,0:T(8,128)} %get-tuple-element.171, f32[8,128]{1,0:T(8,128)} %get-tuple-element.69), kind=kOutput, calls=%fused_computation.2 | convolution fusion | flops 205520896 | bytes 25710592 | tf_op jit(solution)/shard_map/cond/branch_1_fun/frc,fk->rck/dot_general | solution.py:446
  201.8 3.4 %copy.68 = f32[128,128,128]{2,1,0:T(8,128)} copy(f32[128,128,128]{2,1,0:T(8,128)S(1)} %add_select_fusion) | data formatting | bytes 16777216 | tf_op jit(solution)/shard_map/cond
  205.2 1.5 select_select_fusion
  (70 shorter events, 14.6 us)
Async XLA Ops:
  1.5 20.9 %collective-permute-start.1 = (f32[1,128,128]{2,1,0:T(8,128)S(1)}, f32[1,128,128]{2,1,0:T(8,128)S(1)}, u32[]{:S(2)}, u32[]{:S(2)}) collective-permute-start(f32[1,128,128]{2,1,0:T(8,128)S(1)} %get-tuple-element.193), channel_id=1, source_target_pairs={{8,0},{16,8},{24,16},{32,24},{40,32},{48,40},{56,48},{64,56},{72,6... | collective-permute-start | bytes 196616 | tf_op jit(solution)/shard_map/ppermute | solution.py:153
  7.4 16.1 %collective-permute-start = (f32[1,128,128]{2,1,0:T(8,128)S(1)}, f32[1,128,128]{2,1,0:T(8,128)S(1)}, u32[]{:S(2)}, u32[]{:S(2)}) collective-permute-start(f32[1,128,128]{2,1,0:T(8,128)S(1)} %get-tuple-element.194), channel_id=1, source_target_pairs={{0,8},{8,16},{16,24},{24,32},{32,40},{40,48},{48,56},{56,64},{64,7... | collective-permute-start | bytes 196616 | tf_op jit(solution)/shard_map/ppermute | solution.py:152
  10.6 14.0 %collective-permute-start.2 = (f32[128,1,128]{2,1,0:T(1,128)S(1)}, f32[128,1,128]{2,1,0:T(1,128)S(1)}, u32[]{:S(2)}, u32[]{:S(2)}) collective-permute-start(f32[128,1,128]{2,1,0:T(1,128)S(1)} %get-tuple-element.190), channel_id=1, source_target_pairs={{0,1},{1,2},{2,3},{3,4},{4,5},{5,6},{6,7},{7,0},{8,9},{9,10},{10,1... | collective-permute-start | bytes 196616 | tf_op jit(solution)/shard_map/ppermute | solution.py:161
  12.7 11.9 %collective-permute-start.3 = (f32[128,1,128]{2,1,0:T(1,128)S(1)}, f32[128,1,128]{2,1,0:T(1,128)S(1)}, u32[]{:S(2)}, u32[]{:S(2)}) collective-permute-start(f32[128,1,128]{2,1,0:T(1,128)S(1)} %get-tuple-element.189), channel_id=1, source_target_pairs={{1,0},{2,1},{3,2},{4,3},{5,4},{6,5},{7,6},{0,7},{9,8},{10,9},{11,1... | collective-permute-start | bytes 196616 | tf_op jit(solution)/shard_map/ppermute | solution.py:162
  22.4 42.5 %copy-start.4 = (f32[128,128]{1,0:T(8,128)S(1)}, f32[128,128]{1,0:T(8,128)}, u32[]{:S(2)}) copy-start(f32[128,128]{1,0:T(8,128)} %param.18) | copy-start | bytes 196612
  22.4 42.5 %copy-start.12 = (f32[128,8]{0,1:T(8,128)S(1)}, f32[128,8]{0,1:T(8,128)}, u32[]{:S(2)}) copy-start(f32[128,8]{0,1:T(8,128)} %param.20) | copy-start | bytes 12292
  24.6 0.6 copy-start.8
  25.2 0.6 copy-start.9
  48.8 16.1 %copy-start.10 = (f32[8,16384]{1,0:T(8,128)}, f32[8,16384]{1,0:T(8,128)S(1)}, u32[]{:S(2)}) copy-start(f32[8,16384]{1,0:T(8,128)S(1)} %get-tuple-element.85) | copy-start | bytes 1572868
  51.1 11.1 %collective-permute-start.4 = (f32[1,128,128]{2,1,0:T(8,128)S(1)}, f32[1,128,128]{2,1,0:T(8,128)S(1)}, u32[]{:S(2)}, u32[]{:S(2)}) collective-permute-start(f32[1,128,128]{2,1,0:T(8,128)S(1)} %get-tuple-element.186), channel_id=1, source_target_pairs={{0,8},{8,16},{16,24},{24,32},{32,40},{40,48},{48,56},{56,64},{64,7... | collective-permute-start | bytes 196616 | tf_op jit(solution)/shard_map/ppermute | solution.py:152
  53.1 9.2 %collective-permute-start.5 = (f32[1,128,128]{2,1,0:T(8,128)S(1)}, f32[1,128,128]{2,1,0:T(8,128)S(1)}, u32[]{:S(2)}, u32[]{:S(2)}) collective-permute-start(f32[1,128,128]{2,1,0:T(8,128)S(1)} %get-tuple-element.185), channel_id=1, source_target_pairs={{8,0},{16,8},{24,16},{32,24},{40,32},{48,40},{56,48},{64,56},{72,6... | collective-permute-start | bytes 196616 | tf_op jit(solution)/shard_map/ppermute | solution.py:153
  58.8 3.4 %collective-permute-start.6 = (f32[128,1,128]{2,1,0:T(1,128)S(1)}, f32[128,1,128]{2,1,0:T(1,128)S(1)}, u32[]{:S(2)}, u32[]{:S(2)}) collective-permute-start(f32[128,1,128]{2,1,0:T(1,128)S(1)} %get-tuple-element.188), channel_id=1, source_target_pairs={{0,1},{1,2},{2,3},{3,4},{4,5},{5,6},{6,7},{7,0},{8,9},{9,10},{10,1... | collective-permute-start | bytes 196616 | tf_op jit(solution)/shard_map/ppermute | solution.py:161
  60.9 4.0 %collective-permute-start.7 = (f32[128,1,128]{2,1,0:T(1,128)S(1)}, f32[128,1,128]{2,1,0:T(1,128)S(1)}, u32[]{:S(2)}, u32[]{:S(2)}) collective-permute-start(f32[128,1,128]{2,1,0:T(1,128)S(1)} %get-tuple-element.187), channel_id=1, source_target_pairs={{1,0},{2,1},{3,2},{4,3},{5,4},{6,5},{7,6},{0,7},{9,8},{10,9},{11,1... | collective-permute-start | bytes 196616 | tf_op jit(solution)/shard_map/ppermute | solution.py:162
  64.9 63.6 %copy-start.1 = (bf16[32,128,128]{2,1,0:T(8,128)(2,1)S(1)}, bf16[32,128,128]{2,1,0:T(8,128)(2,1)}, u32[]{:S(2)}) copy-start(bf16[32,128,128]{2,1,0:T(8,128)(2,1)} %param.22) | copy-start | bytes 3145732
  64.9 63.6 %copy-start.11 = (f32[8,128]{1,0:T(8,128)S(1)}, f32[8,128]{1,0:T(8,128)}, u32[]{:S(2)}) copy-start(f32[8,128]{1,0:T(8,128)} %param.21) | copy-start | bytes 12292
  73.0 55.6 %copy-start.6 = (f32[128,128]{1,0:T(8,128)}, f32[128,128]{1,0:T(8,128)S(1)}, u32[]{:S(2)}) copy-start(f32[128,128]{1,0:T(8,128)S(1)} %get-tuple-element.92) | copy-start | bytes 196612
  128.8 10.7 %copy-start.3 = (bf16[24,32,1152]{2,1,0:T(8,128)(2,1)}, bf16[24,32,1152]{2,1,0:T(8,128)(2,1)S(1)}, u32[]{:S(2)}) copy-start(bf16[24,32,1152]{2,1,0:T(8,128)(2,1)S(1)} %get-tuple-element.59) | copy-start | bytes 5308420 | tf_op jit(solution)/shard_map/cond
  149.1 5.7 %copy-start = (f32[512,8,8,128]{3,2,1,0:T(8,128)}, f32[512,8,8,128]{3,2,1,0:T(8,128)S(1)}, u32[]{:S(2)}) copy-start(f32[512,8,8,128]{3,2,1,0:T(8,128)S(1)} %copy.35) | copy-start | bytes 50331652 | tf_op jit(solution)/shard_map/cond
  155.0 13.4 %copy-start.2 = (f32[32,128,128]{2,1,0:T(8,128)S(1)}, f32[32,128,128]{2,1,0:T(8,128)}, u32[]{:S(2)}) copy-start(f32[32,128,128]{2,1,0:T(8,128)} %get-tuple-element.65) | copy-start | bytes 6291460 | tf_op jit(solution)/shard_map/cond
  183.5 21.8 %copy-start.5 = (s32[128,128]{1,0:T(8,128)S(1)}, s32[128,128]{1,0:T(8,128)}, u32[]{:S(2)}) copy-start(s32[128,128]{1,0:T(8,128)} %param.16) | copy-start | bytes 196612
  183.5 21.8 %copy-start.7 = (f32[128,128]{1,0:T(8,128)S(1)}, f32[128,128]{1,0:T(8,128)}, u32[]{:S(2)}) copy-start(f32[128,128]{1,0:T(8,128)} %copy-done.6) | copy-start | bytes 196612

commit v6 on v5

--- a/solution.py
+++ b/solution.py
@@ -42,9 +42,9 @@
     return one(high) + one(middle) + one(low)
 
 
-def substep_kernel(with_flux, x_ref, top_ref, bottom_ref, west_ref, east_ref, mix_ref, *rest):
+def substep_kernel(with_flux, comp_total, x_ref, top_ref, bottom_ref, west_ref, east_ref, mix_ref, *rest):
     if with_flux:
-        fluxes_ref, out_ref, planes_ref, flux_out_ref = rest
+        fluxes_ref, out_ref, flux_out_ref = rest
     else:
         out_ref, planes_ref = rest
     rows, cols, levels = x_ref.shape
@@ -59,19 +59,29 @@
     mixed = three_pass(flat, mix_ref[...], ((1,), (0,)))
     moved = flat + PHYSICS * jnp.tanh(mixed)
     out_ref[...] = moved.reshape(rows, cols, levels)
-    plane_row = lax.broadcasted_iota(jnp.int32, (8, levels), 0)
-    plane_lane = lax.broadcasted_iota(jnp.int32, (8, levels), 1)
-    pick_out = ((plane_row == 0) & (plane_lane == 0)).astype(jnp.bfloat16)
-    pick_in = ((plane_row == 1) & (plane_lane == 0)).astype(jnp.bfloat16)
-    planes_ref[...] = exact_rows(pick_out, moved) + exact_rows(
-        pick_in, centre.reshape(rows * cols, levels)
-    )
-    if with_flux:
+    if not with_flux:
+        ocean = lax.axis_index("comp") == comp_total - 1
+
+        @pl.when(ocean)
+        def _():
+            plane_row = lax.broadcasted_iota(jnp.int32, (8, levels), 0)
+            plane_lane = lax.broadcasted_iota(jnp.int32, (8, levels), 1)
+            pick_out = ((plane_row == 0) & (plane_lane == 0)).astype(jnp.bfloat16)
+            pick_in = ((plane_row == 1) & (plane_lane == 0)).astype(jnp.bfloat16)
+            planes_ref[...] = exact_rows(pick_out, moved) + exact_rows(
+                pick_in, centre.reshape(rows * cols, levels)
+            )
+
+        @pl.when(jnp.logical_not(ocean))
+        def _():
+            planes_ref[...] = jnp.zeros_like(planes_ref)
+
+    else:
         total = centre.reshape(rows * cols, levels) + moved
         flux_out_ref[...] = three_pass(fluxes_ref[...], total, ((1,), (1,)))
 
 
-def substep(values, top, bottom, west, east, mixing, fluxes_t=None):
+def substep(values, top, bottom, west, east, mixing, comp_total, fluxes_t=None):
     rows, cols, levels = values.shape
     blocks = rows // ROW_BLOCK
     top_rows = jnp.concatenate([top, values[ROW_BLOCK - 1 : rows - 1 : ROW_BLOCK]], axis=0)
@@ -86,14 +96,11 @@
         pl.BlockSpec((levels, levels), lambda i: (0, 0)),
     ]
     operands = [values, top_rows, bottom_rows, west, east, mixing]
-    out_shape = [
-        jax.ShapeDtypeStruct(values.shape, jnp.float32),
-        jax.ShapeDtypeStruct((8, rows * cols), jnp.float32),
-    ]
-    out_specs = [
-        pl.BlockSpec((ROW_BLOCK, cols, levels), lambda i: (i, 0, 0)),
-        pl.BlockSpec((8, ROW_BLOCK * cols), lambda i: (0, i)),
-    ]
+    out_shape = [jax.ShapeDtypeStruct(values.shape, jnp.float32)]
+    out_specs = [pl.BlockSpec((ROW_BLOCK, cols, levels), lambda i: (i, 0, 0))]
+    if not with_flux:
+        out_shape.append(jax.ShapeDtypeStruct((8, rows * cols), jnp.float32))
+        out_specs.append(pl.BlockSpec((8, ROW_BLOCK * cols), lambda i: (0, i)))
     if with_flux:
         flux_count = fluxes_t.shape[0]
         in_specs.append(pl.BlockSpec((flux_count, levels), lambda i: (0, 0)))
@@ -103,7 +110,7 @@
     cells = rows * cols
     flops = 6 * cells * levels * levels + (6 * cells * levels * 8 if with_flux else 0)
     result = pl.pallas_call(
-        functools.partial(substep_kernel, with_flux),
+        functools.partial(substep_kernel, with_flux, comp_total),
         grid=(blocks,),
         in_specs=in_specs,
         out_specs=out_specs,
@@ -313,6 +320,51 @@
     )(replies)
 
 
+def regrid_kernel(weight_ids_ref, rows_ref, fluxes_ref, weights_ref, out_ref):
+    flux_count, tile_rows, block_len = out_ref.shape
+    entries = fluxes_ref.shape[0]
+    weight_count = weights_ref.shape[0]
+    out_ref[...] = jnp.zeros_like(out_ref)
+    row_ids = lax.broadcasted_iota(jnp.int32, (tile_rows, entries), 0)
+    row_hits = row_ids == rows_ref[...]
+
+    def one_weight(w, carry):
+        picker = (row_hits & (weight_ids_ref[...] == w)).astype(jnp.bfloat16)
+        weight = weights_ref[w]
+        for f in range(flux_count):
+            binned = jnp.dot(
+                picker,
+                fluxes_ref[:, f * block_len : (f + 1) * block_len],
+                preferred_element_type=jnp.float32,
+            )
+            high = binned.astype(jnp.bfloat16)
+            low = (binned - high.astype(jnp.float32)).astype(jnp.bfloat16)
+            out_ref[f] += jnp.dot(high, weight, preferred_element_type=jnp.float32) + jnp.dot(
+                low, weight, preferred_element_type=jnp.float32
+            )
+        return carry
+
+    lax.fori_loop(0, weight_count, one_weight, 0)
+
+
+def regrid_arrivals(weight_ids, rows, fluxes, weights, flux_count):
+    entries, width = fluxes.shape
+    weight_count, block_len, _ = weights.shape
+    tile_rows = block_len
+    cells = flux_count * tile_rows * block_len
+    return pl.pallas_call(
+        regrid_kernel,
+        out_shape=jax.ShapeDtypeStruct((flux_count, tile_rows, block_len), jnp.float32),
+        in_specs=[pl.BlockSpec(memory_space=pltpu.VMEM)] * 4,
+        out_specs=pl.BlockSpec(memory_space=pltpu.VMEM),
+        cost_estimate=pl.CostEstimate(
+            flops=2 * weight_count * flux_count * (tile_rows * entries * block_len + 2 * tile_rows * block_len * block_len),
+            transcendentals=0,
+            bytes_accessed=entries * width * 2 + weight_count * block_len * block_len * 2 + cells * 4,
+        ),
+    )(weight_ids, rows, fluxes, weights)
+
+
 def local(
     state, land_mask, intersection_list, mix_atm, mix_ocn, flux_map, ocean_map, regrid_weights
 ):
@@ -342,26 +394,22 @@
     top, bottom = edge_rows(state, lower_valid, upper_valid)
     west, east = edge_columns(state)
     mixing = jnp.where(ocean_side, mix_ocn, mix_atm)
-    first, first_planes = substep(state, top, bottom, west, east, mixing)
+    first, first_planes = substep(state, top, bottom, west, east, mixing, comp_count)
     first_top = first_planes[0].reshape(tile_rows, block_len)
     state_top = first_planes[1].reshape(tile_rows, block_len)
     top, bottom = edge_rows(first, lower_valid, upper_valid)
     west, east = edge_columns(first)
 
     def atmosphere_second(values, top, bottom, west, east):
-        moved, planes, total = substep(values, top, bottom, west, east, mix_atm, flux_map.T)
+        moved, total = substep(values, top, bottom, west, east, mix_atm, comp_count, flux_map.T)
         total = total.reshape(flux_count, tile_rows, block_len)
         sent = jnp.where(sea_cells[None], 0.5 * total, 0.0).astype(jnp.bfloat16)
-        return moved, planes[0].reshape(tile_rows, block_len), sent
+        return moved, sent
 
     def ocean_second(values, top, bottom, west, east):
-        return (
-            values,
-            jnp.zeros((tile_rows, block_len), jnp.float32),
-            jnp.zeros((flux_count, tile_rows, block_len), jnp.bfloat16),
-        )
-
-    second, second_top, flux_sent = lax.cond(
+        return values, jnp.zeros((flux_count, tile_rows, block_len), jnp.bfloat16)
+
+    second, flux_sent = lax.cond(
         ocean_side, ocean_second, atmosphere_second, first, top, bottom, west, east
     )
     entry_list = intersection_list.reshape(tile_rows * intersections, 3)
@@ -401,24 +449,16 @@
 
     def ocean_reply(values_top, arrived):
         flat = arrived.reshape(-1, width + 128)
-        fluxes = flat[:, :width]
         arrived_labels = flat[:, width].astype(jnp.int32) * tile_rows + flat[:, width + 1].astype(
             jnp.int32
         )
-        label_ids = jnp.arange(weight_count * tile_rows, dtype=jnp.int32)
-        selector = (arrived_labels[:, None] == label_ids[None, :]).astype(jnp.bfloat16)
-        binned = lax.dot_general(
-            selector, fluxes, (((0,), (0,)), ((), ())), preferred_element_type=jnp.float32
+        forcing = regrid_arrivals(
+            flat[:, width].astype(jnp.int32)[None],
+            flat[:, width + 1].astype(jnp.int32)[None],
+            flat,
+            weights_low,
+            flux_count,
         )
-        binned = binned.reshape(weight_count, tile_rows, flux_count, block_len)
-        binned_hi = lax.reduce_precision(binned, exponent_bits=8, mantissa_bits=7)
-        binned_lo = (binned - binned_hi).astype(jnp.bfloat16)
-        forcing = jnp.einsum(
-            "wdfa,wab->fdb",
-            binned_hi.astype(jnp.bfloat16),
-            weights_low,
-            preferred_element_type=jnp.float32,
-        ) + jnp.einsum("wdfa,wab->fdb", binned_lo, weights_low, preferred_element_type=jnp.float32)
         lifted = jnp.sum(forcing * ocean_map[:, 0][:, None, None], axis=0)
         top_level = jnp.where(sea_cells, values_top + lifted, state_top)
         table = jnp.einsum("db,wab->wda", top_level, weights_wide, precision=HIGHEST)
@@ -447,7 +487,9 @@
         return jnp.where(sea_cells[:, :, None], moved, state)
 
     final_state = lax.cond(ocean_side, ocean_final, lambda values, forcing: second, first, forcing)
-    surface_out = jnp.where(ocean_side, ocean_top, jnp.where(sea_cells, returned, second_top))
+    surface_out = jnp.where(
+        ocean_side, ocean_top, jnp.where(sea_cells, returned, final_state[:, :, 0])
+    )
     return (final_state, surface_out)
 
 

time: 208 us -> 211 us (1.014)
  Pallas kernels: 83.3 us -> 121 us
  matrix products: 47.5 us -> 22.9 us
  local copies, waits for them, and re-layouts: 36.7 us -> 29 us
  other arithmetic: 15.5 us -> 12.5 us
    pallas_call x1 -> x2, Pallas kernels: 23 us -> 72.7 us  [the longest x1 52.5 us: regrid_arrivals(): pl.pallas_call(regrid_kernel, out_shape=jax.ShapeDtypeStruct((flux_count,...]
    dot_general x3 -> x0, matrix products: 25.2 us -> none  [the longest x1 10.8 us: ocean_reply(): jnp.einsum('wdfa,wab->fdb', binned_hi.astype(jnp.bfloat16), weights_low,...]
    cond x9 -> x4, local copies, waits for them, and re-layouts: 22.6 us -> 11.3 us
    pallas_call x1, Pallas kernels: 54.2 us -> 42.8 us  [gather_to_ocean(): pl.pallas_call(functools.partial(gather_kernel, tuple(offsets), tuple(sha...]
    unnamed x22 -> x17, local copies, waits for them, and re-layouts: 2.19 us -> 7.41 us
  transfers between devices with their start and end apart: 8 -> 8, of which waited for: 1 -> 2; matrix products, arithmetic and copies ran while one was open for 7% -> 6% of each run, Pallas kernels for 0% -> 0%
where the time goes in v6:
time: 211 us; the launch traced here: 210 us
  Pallas kernels  121 us (57%)
  local copies, waits for them, and re-layouts  29 us (14%)
  matrix products  22.9 us (11%)
  starting transfers between devices  19.7 us (9%)
  other arithmetic  12.5 us (6%)
  waiting for transfers between devices  3.8 us (2%)
    pallas_call x1, Pallas kernels, regrid_arrivals(): pl.pallas_call(regrid_kernel, out_shape=jax.ShapeDtypeStruct((flux_count,...  52.5 us
    pallas_call x1, Pallas kernels, gather_to_ocean(): pl.pallas_call(functools.partial(gather_kernel, tuple(offsets), tuple(sha...  42.8 us
    pallas_call x1, Pallas kernels, substep(): pl.pallas_call(functools.partial(substep_kernel, with_flux, comp_total),...  20.2 us
    dot_general x1, matrix products, ocean_final(): jnp.einsum('frc,fk->rck', forcing, ocean_map, precision=HIGHEST)  18.3 us
    ppermute x2, starting transfers between devices, edge_rows(): after = lax.ppermute(values[:1], ('comp', 'lat'), down)  11.3 us
    cond x4, local copies, waits for them, and re-layouts  11.3 us
    unnamed x17, local copies, waits for them, and re-layouts  7.41 us
    pallas_call x1, Pallas kernels, spread_from_ocean(): pl.pallas_call(functools.partial(spread_kernel, tuple(offsets), tuple(sha...  5.28 us
  transfers between devices with their start and end apart: 8, of which 2 were waited for; matrix products, arithmetic and copies ran while one was open for 6% of the time, Pallas kernels for 0%

profile of v6, /device:TPU:25, one launch (start us, length us, event | category | flops | bytes accessed | tf_op | source)
XLA Modules:
  0.0 210.0 jit_solution(10222149662442316314)
XLA Ops:
  0.6 0.9 fusion.25
  1.5 5.8 %collective-permute-start.1 = (f32[1,128,128]{2,1,0:T(8,128)S(1)}, f32[1,128,128]{2,1,0:T(8,128)S(1)}, u32[]{:S(2)}, u32[]{:S(2)}) collective-permute-start(f32[1,128,128]{2,1,0:T(8,128)S(1)} %get-tuple-element.182), channel_id=1, source_target_pairs={{8,0},{16,8},{24,16},{32,24},{40,32},{48,40},{56,48},{64,56},{72,6... | collective-permute-start | bytes 196616 | tf_op jit(solution)/shard_map/ppermute | solution.py:160
  7.4 1.9 collective-permute-start
  9.3 1.3 fusion.23
  10.6 2.1 collective-permute-start.2
  12.7 1.6 fusion.24
  17.3 1.5 broadcast_select_fusion.3.mix_ref
  19.0 2.8 %convert_element_type.61 = f32[32,128,128]{2,1,0:T(8,128)} convert(bf16[32,128,128]{2,1,0:T(8,128)(2,1)} %param.22) | non-fusion elementwise | flops 524288 | bytes 3145728 | tf_op jit(solution)/shard_map/convert_element_type | solution.py:447
  21.8 1.1 pad_maximum_fusion.3.bottom_ref
  22.9 1.0 pad_maximum_fusion.2.top_ref
  25.2 20.2 %shard_map.106 = (f32[128,128,128]{2,1,0:T(8,128)}, f32[8,16384]{1,0:T(8,128)S(1)}) custom-call(f32[128,128,128]{2,1,0:T(8,128)} %x_ref.1, f32[16,128,128]{2,1,0:T(8,128)} %pad_maximum_fusion.2.top_ref, f32[16,128,128]{2,1,0:T(8,128)} %pad_maximum_fusion.3.bottom_ref, f32[128,1,128]{2,1,0:T(1,128)} %copy-done.4, f32[128,1,128]{2,1,0:T(1,128)} %copy-done.5, ...), custom_call_target="tpu_custom_call" | custom-call | flops 1610612736 | bytes 16777216 | tf_op jit(solution)/shard_map/pallas_call | solution.py:112
  46.3 1.3 fusion.22
  47.6 1.9 collective-permute-start.4
  49.5 5.5 %collective-permute-start.5 = (f32[1,128,128]{2,1,0:T(8,128)S(1)}, f32[1,128,128]{2,1,0:T(8,128)S(1)}, u32[]{:S(2)}, u32[]{:S(2)}) collective-permute-start(f32[1,128,128]{2,1,0:T(8,128)S(1)} %get-tuple-element.174), channel_id=1, source_target_pairs={{8,0},{16,8},{24,16},{32,24},{40,32},{48,40},{56,48},{64,56},{72,6... | collective-permute-start | bytes 196616 | tf_op jit(solution)/shard_map/ppermute | solution.py:160
  55.0 2.3 %collective-permute-start.6 = (f32[128,1,128]{2,1,0:T(1,128)S(1)}, f32[128,1,128]{2,1,0:T(1,128)S(1)}, u32[]{:S(2)}, u32[]{:S(2)}) collective-permute-start(f32[128,1,128]{2,1,0:T(1,128)S(1)} %get-tuple-element.177), channel_id=1, source_target_pairs={{0,1},{1,2},{2,3},{3,4},{4,5},{5,6},{6,7},{7,0},{8,9},{9,10},{10,1... | collective-permute-start | bytes 196616 | tf_op jit(solution)/shard_map/ppermute | solution.py:168
  57.5 1.1 collective-permute-done.6
  58.6 2.7 %collective-permute-done.7 = f32[128,1,128]{2,1,0:T(1,128)S(1)} collective-permute-done((f32[128,1,128]{2,1,0:T(1,128)S(1)}, f32[128,1,128]{2,1,0:T(1,128)S(1)}, u32[]{:S(2)}, u32[]{:S(2)}) %collective-permute-start.7) | collective-permute-done | bytes 65568 | tf_op jit(solution)/shard_map/ppermute | solution.py:169
  61.4 7.9 %conditional.3 = (f32[128,128,128]{2,1,0:T(8,128)}, bf16[8,128,128]{2,0,1:T(8,128)(2,1)S(1)}) conditional(s32[]{:T(128)} %convert_element_type.57, (f32[128,128,128]{2,1,0:T(8,128)}, pred[1,128,128]{2,1,0:T(8,128)(4,1)S(1)}, pred[1,128,128]{2,1,0:T(8,128)(4,1)S(1)}, f32[128,8]{0,1:T(8,128)S(1)}, f32[128,1,128]{2,1,0:T(1,128)S(1)}, ...), branch_computations={%region_0.1_spmd.clone, %region_1.2_spmd} | conditional | flops 1712226304 | bytes 26066960 | solution.py:412
  61.4 7.9 %copy.32 = f32[128,128,128]{2,1,0:T(8,128)} copy(f32[128,128,128]{2,1,0:T(8,128)} %param.1) | data formatting | bytes 16777216 | tf_op jit(solution)/shard_map/cond
  69.5 1.2 convolution_convert_fusion
  70.7 42.8 %shard_map.107 = bf16[24,32,1152]{2,1,0:T(8,128)(2,1)S(1)} custom-call(bf16[8,32,1152]{2,1,0:T(8,128)(2,1)} %bitcast.55), custom_call_target="tpu_custom_call" | custom-call | tf_op jit(solution)/shard_map/pallas_call | solution.py:238
  113.5 62.4 %conditional.4 = (f32[8,128,128]{2,1,0:T(8,128)}, f32[24,32,128]{2,1,0:T(8,128)S(1)}, f32[128,128]{1,0:T(8,128)S(1)}) conditional(s32[]{:T(128)} %convert_element_type.57, f32[128,128]{1,0:T(8,128)S(1)} %bitcast.52, (bf16[24,32,1152]{2,1,0:T(8,128)(2,1)S(1)}, bf16[32,128,128]{2,1,0:T(8,128)(2,1)}, f32[8,128]{1,0:T(8,128)S(1)}, ...), branch_computations={%region_4.5_spmd, %region_5.7_spmd} | conditional | flops 9395632128 | bytes 17301652 | solution.py:475
  115.3 52.5 %branch_1_fun.1 = f32[8,128,128]{2,1,0:T(8,128)} custom-call(s32[1,768]{1,0:T(1,128)} %reshape.125.weight_ids_ref, s32[1,768]{1,0:T(1,128)} %reshape.126.rows_ref, bf16[768,1152]{1,0:T(8,128)(2,1)S(1)} %bitcast.48, bf16[32,128,128]{2,1,0:T(8,128)(2,1)} %get-tuple-element.65.weights_ref), custom_call_target="tpu_custom_call" | custom-call | flops 8589934592 | bytes 3342336 | tf_op jit(solution)/shard_map/cond/branch_1_fun/pallas_call | solution.py:355
  167.9 1.2 multiply_reduce_fusion
  169.2 3.5 %fusion.4 = f32[128,32,128]{2,0,1:T(8,128)S(1)} fusion(f32[32,128,128]{2,1,0:T(8,128)} %get-tuple-element.70, f32[128,128]{1,0:T(8,128)S(1)} %add_select_fusion.1), kind=kOutput, calls=%fused_computation.18 | convolution fusion | flops 805306368 | bytes 4259840 | tf_op jit(solution)/shard_map/cond/branch_1_fun/db,wab->wda/dot_general | solution.py:464
  172.7 1.6 gather_fusion
  174.3 1.4 and_reduce_fusion
  175.9 5.3 %shard_map.108 = f32[8,32,128]{2,1,0:T(8,128)} custom-call(f32[24,32,128]{2,1,0:T(8,128)S(1)} %get-tuple-element.92.surface_ref), custom_call_target="tpu_custom_call" | custom-call | tf_op jit(solution)/shard_map/pallas_call | solution.py:309
  181.2 21.9 %conditional.5 = (f32[128,128,128]{2,1,0:T(8,128)}) conditional(s32[]{:T(128)} %convert_element_type.57, f32[128,128,128]{2,1,0:T(8,128)} %get-tuple-element.88, (pred[128,128]{1,0:T(8,128)(4,1)S(1)}, f32[8,128,128]{2,1,0:T(8,128)}, f32[8,128]{1,0:T(8,128)S(1)}, f32[128,128,128]{2,1,0:T(8,128)}, f32[128,128,128]{2,1,0:T(8,128)}) %tuple.76), branch_computations={%region_7.8_spmd, %region_8.9_spmd} | conditional | flops 205520896 | bytes 42487816 | solution.py:489
  181.4 18.3 %add_select_fusion = f32[128,128,128]{2,1,0:T(8,128)S(1)} fusion(f32[128,128,128]{2,1,0:T(8,128)} %get-tuple-element.75, f32[128,128,128]{2,1,0:T(8,128)} %get-tuple-element.72, pred[128,128]{1,0:T(8,128)(4,1)S(1)} %get-tuple-element.71, f32[8,128,128]{2,1,0:T(8,128)} %get-tuple-element.161, f32[8,128]{1,0:T(8,128)S(1)} %get-tuple-element.74), kind=kOutput, calls=%fused_computation.2 | convolution fusion | flops 205520896 | bytes 25710592 | tf_op jit(solution)/shard_map/cond/branch_1_fun/frc,fk->rck/dot_general | solution.py:486
  199.7 3.4 %copy.41 = f32[128,128,128]{2,1,0:T(8,128)} copy(f32[128,128,128]{2,1,0:T(8,128)S(1)} %add_select_fusion) | data formatting | bytes 16777216 | tf_op jit(solution)/shard_map/cond
  203.1 5.2 %copy.24 = f32[128,128,1]{1,0,2:T(8,128)S(1)} copy(f32[128,128,1]{2,1,0:T(8,128)} %bitcast.46) | data formatting | bytes 131072
  (60 shorter events, 9.5 us)
Async XLA Ops:
  1.5 20.3 %collective-permute-start.1 = (f32[1,128,128]{2,1,0:T(8,128)S(1)}, f32[1,128,128]{2,1,0:T(8,128)S(1)}, u32[]{:S(2)}, u32[]{:S(2)}) collective-permute-start(f32[1,128,128]{2,1,0:T(8,128)S(1)} %get-tuple-element.182), channel_id=1, source_target_pairs={{8,0},{16,8},{24,16},{32,24},{40,32},{48,40},{56,48},{64,56},{72,6... | collective-permute-start | bytes 196616 | tf_op jit(solution)/shard_map/ppermute | solution.py:160
  7.4 15.5 %collective-permute-start = (f32[1,128,128]{2,1,0:T(8,128)S(1)}, f32[1,128,128]{2,1,0:T(8,128)S(1)}, u32[]{:S(2)}, u32[]{:S(2)}) collective-permute-start(f32[1,128,128]{2,1,0:T(8,128)S(1)} %get-tuple-element.183), channel_id=1, source_target_pairs={{0,8},{8,16},{16,24},{24,32},{32,40},{40,48},{48,56},{56,64},{64,7... | collective-permute-start | bytes 196616 | tf_op jit(solution)/shard_map/ppermute | solution.py:159
  10.6 13.3 %collective-permute-start.2 = (f32[128,1,128]{2,1,0:T(1,128)S(1)}, f32[128,1,128]{2,1,0:T(1,128)S(1)}, u32[]{:S(2)}, u32[]{:S(2)}) collective-permute-start(f32[128,1,128]{2,1,0:T(1,128)S(1)} %get-tuple-element.179), channel_id=1, source_target_pairs={{0,1},{1,2},{2,3},{3,4},{4,5},{5,6},{6,7},{7,0},{8,9},{9,10},{10,1... | collective-permute-start | bytes 196616 | tf_op jit(solution)/shard_map/ppermute | solution.py:168
  12.7 11.3 %collective-permute-start.3 = (f32[128,1,128]{2,1,0:T(1,128)S(1)}, f32[128,1,128]{2,1,0:T(1,128)S(1)}, u32[]{:S(2)}, u32[]{:S(2)}) collective-permute-start(f32[128,1,128]{2,1,0:T(1,128)S(1)} %get-tuple-element.178), channel_id=1, source_target_pairs={{1,0},{2,1},{3,2},{4,3},{5,4},{6,5},{7,6},{0,7},{9,8},{10,9},{11,1... | collective-permute-start | bytes 196616 | tf_op jit(solution)/shard_map/ppermute | solution.py:169
  21.8 39.5 %copy-start.2 = (f32[128,128]{1,0:T(8,128)S(1)}, f32[128,128]{1,0:T(8,128)}, u32[]{:S(2)}) copy-start(f32[128,128]{1,0:T(8,128)} %param.18) | copy-start | bytes 196612
  21.8 39.6 %copy-start.7 = (f32[128,8]{0,1:T(8,128)S(1)}, f32[128,8]{0,1:T(8,128)}, u32[]{:S(2)}) copy-start(f32[128,8]{0,1:T(8,128)} %param.20) | copy-start | bytes 12292
  23.9 0.6 copy-start.4
  24.6 0.6 copy-start.5
  47.6 9.9 %collective-permute-start.4 = (f32[1,128,128]{2,1,0:T(8,128)S(1)}, f32[1,128,128]{2,1,0:T(8,128)S(1)}, u32[]{:S(2)}, u32[]{:S(2)}) collective-permute-start(f32[1,128,128]{2,1,0:T(8,128)S(1)} %get-tuple-element.175), channel_id=1, source_target_pairs={{0,8},{8,16},{16,24},{24,32},{32,40},{40,48},{48,56},{56,64},{64,7... | collective-permute-start | bytes 196616 | tf_op jit(solution)/shard_map/ppermute | solution.py:159
  49.5 8.0 %collective-permute-start.5 = (f32[1,128,128]{2,1,0:T(8,128)S(1)}, f32[1,128,128]{2,1,0:T(8,128)S(1)}, u32[]{:S(2)}, u32[]{:S(2)}) collective-permute-start(f32[1,128,128]{2,1,0:T(8,128)S(1)} %get-tuple-element.174), channel_id=1, source_target_pairs={{8,0},{16,8},{24,16},{32,24},{40,32},{48,40},{56,48},{64,56},{72,6... | collective-permute-start | bytes 196616 | tf_op jit(solution)/shard_map/ppermute | solution.py:160
  55.0 3.6 %collective-permute-start.6 = (f32[128,1,128]{2,1,0:T(1,128)S(1)}, f32[128,1,128]{2,1,0:T(1,128)S(1)}, u32[]{:S(2)}, u32[]{:S(2)}) collective-permute-start(f32[128,1,128]{2,1,0:T(1,128)S(1)} %get-tuple-element.177), channel_id=1, source_target_pairs={{0,1},{1,2},{2,3},{3,4},{4,5},{5,6},{6,7},{7,0},{8,9},{9,10},{10,1... | collective-permute-start | bytes 196616 | tf_op jit(solution)/shard_map/ppermute | solution.py:168
  57.3 4.0 %collective-permute-start.7 = (f32[128,1,128]{2,1,0:T(1,128)S(1)}, f32[128,1,128]{2,1,0:T(1,128)S(1)}, u32[]{:S(2)}, u32[]{:S(2)}) collective-permute-start(f32[128,1,128]{2,1,0:T(1,128)S(1)} %get-tuple-element.176), channel_id=1, source_target_pairs={{1,0},{2,1},{3,2},{4,3},{5,4},{6,5},{7,6},{0,7},{9,8},{10,9},{11,1... | collective-permute-start | bytes 196616 | tf_op jit(solution)/shard_map/ppermute | solution.py:169
  61.4 52.2 %copy-start.6 = (f32[8,128]{1,0:T(8,128)S(1)}, f32[8,128]{1,0:T(8,128)}, u32[]{:S(2)}) copy-start(f32[8,128]{1,0:T(8,128)} %param.21) | copy-start | bytes 12292
  113.5 54.3 %copy-start.1 = (bf16[24,32,1152]{2,1,0:T(8,128)(2,1)}, bf16[24,32,1152]{2,1,0:T(8,128)(2,1)S(1)}, u32[]{:S(2)}) copy-start(bf16[24,32,1152]{2,1,0:T(8,128)(2,1)S(1)} %get-tuple-element.64) | copy-start | bytes 5308420 | tf_op jit(solution)/shard_map/cond
  203.1 5.3 %copy-start = (f32[8,32,128]{2,1,0:T(8,128)S(1)}, f32[8,32,128]{2,1,0:T(8,128)}, u32[]{:S(2)}) copy-start(f32[8,32,128]{2,1,0:T(8,128)} %shard_map.108) | copy-start | bytes 393220
  203.1 6.2 %copy-start.3 = (s32[128,128]{1,0:T(8,128)S(1)}, s32[128,128]{1,0:T(8,128)}, u32[]{:S(2)}) copy-start(s32[128,128]{1,0:T(8,128)} %param.16) | copy-start | bytes 196612

commit v7 on v6

--- a/solution.py
+++ b/solution.py
@@ -320,49 +320,48 @@
     )(replies)
 
 
-def regrid_kernel(weight_ids_ref, rows_ref, fluxes_ref, weights_ref, out_ref):
-    flux_count, tile_rows, block_len = out_ref.shape
-    entries = fluxes_ref.shape[0]
-    weight_count = weights_ref.shape[0]
-    out_ref[...] = jnp.zeros_like(out_ref)
-    row_ids = lax.broadcasted_iota(jnp.int32, (tile_rows, entries), 0)
-    row_hits = row_ids == rows_ref[...]
-
-    def one_weight(w, carry):
-        picker = (row_hits & (weight_ids_ref[...] == w)).astype(jnp.bfloat16)
-        weight = weights_ref[w]
-        for f in range(flux_count):
-            binned = jnp.dot(
-                picker,
-                fluxes_ref[:, f * block_len : (f + 1) * block_len],
-                preferred_element_type=jnp.float32,
-            )
-            high = binned.astype(jnp.bfloat16)
-            low = (binned - high.astype(jnp.float32)).astype(jnp.bfloat16)
-            out_ref[f] += jnp.dot(high, weight, preferred_element_type=jnp.float32) + jnp.dot(
-                low, weight, preferred_element_type=jnp.float32
-            )
-        return carry
-
-    lax.fori_loop(0, weight_count, one_weight, 0)
-
-
-def regrid_arrivals(weight_ids, rows, fluxes, weights, flux_count):
-    entries, width = fluxes.shape
-    weight_count, block_len, _ = weights.shape
-    tile_rows = block_len
-    cells = flux_count * tile_rows * block_len
+def ocean_update_kernel(first_ref, state_ref, sea_ref, forcing_ref, spread_ref, out_ref):
+    rows, cols, levels = first_ref.shape
+    forcing = forcing_ref[...]
+    spread = spread_ref[...]
+    forcing_hi = forcing.astype(jnp.bfloat16)
+    forcing_lo = (forcing - forcing_hi.astype(jnp.float32)).astype(jnp.bfloat16)
+    spread_hi = spread.astype(jnp.bfloat16)
+    spread_lo = (spread - spread_hi.astype(jnp.float32)).astype(jnp.bfloat16)
+
+    def one(a, b):
+        return lax.dot_general(a, b, (((0,), (0,)), ((), ())), preferred_element_type=jnp.float32)
+
+    added = one(forcing_hi, spread_hi) + (one(forcing_hi, spread_lo) + one(forcing_lo, spread_hi))
+    lane_row = lax.broadcasted_iota(jnp.int32, (8, levels), 0)
+    ones = (lane_row == 0).astype(jnp.bfloat16)
+    picks = jnp.where(lax.broadcasted_iota(jnp.int32, sea_ref.shape, 0) == 0, sea_ref[...], 0)
+    mask = one(picks.astype(jnp.bfloat16), ones)
+    moved = first_ref[...].reshape(rows * cols, levels) + added
+    kept = jnp.where(mask > 0.5, moved, state_ref[...].reshape(rows * cols, levels))
+    out_ref[...] = kept.reshape(rows, cols, levels)
+
+
+def ocean_update(first, state, sea_rows, forcing, ocean_map):
+    rows, cols, levels = first.shape
+    flux_count = forcing.shape[0]
+    cells = rows * cols
     return pl.pallas_call(
-        regrid_kernel,
-        out_shape=jax.ShapeDtypeStruct((flux_count, tile_rows, block_len), jnp.float32),
-        in_specs=[pl.BlockSpec(memory_space=pltpu.VMEM)] * 4,
-        out_specs=pl.BlockSpec(memory_space=pltpu.VMEM),
+        ocean_update_kernel,
+        grid=(rows // ROW_BLOCK,),
+        in_specs=[
+            pl.BlockSpec((ROW_BLOCK, cols, levels), lambda i: (i, 0, 0)),
+            pl.BlockSpec((ROW_BLOCK, cols, levels), lambda i: (i, 0, 0)),
+            pl.BlockSpec((8, ROW_BLOCK * cols), lambda i: (0, i)),
+            pl.BlockSpec((flux_count, ROW_BLOCK * cols), lambda i: (0, i)),
+            pl.BlockSpec((flux_count, levels), lambda i: (0, 0)),
+        ],
+        out_specs=pl.BlockSpec((ROW_BLOCK, cols, levels), lambda i: (i, 0, 0)),
+        out_shape=jax.ShapeDtypeStruct(first.shape, jnp.float32),
         cost_estimate=pl.CostEstimate(
-            flops=2 * weight_count * flux_count * (tile_rows * entries * block_len + 2 * tile_rows * block_len * block_len),
-            transcendentals=0,
-            bytes_accessed=entries * width * 2 + weight_count * block_len * block_len * 2 + cells * 4,
+            flops=8 * cells * levels * flux_count, transcendentals=0, bytes_accessed=12 * cells * levels
         ),
-    )(weight_ids, rows, fluxes, weights)
+    )(first, state, sea_rows, forcing, ocean_map)
 
 
 def local(
@@ -452,13 +451,21 @@
         arrived_labels = flat[:, width].astype(jnp.int32) * tile_rows + flat[:, width + 1].astype(
             jnp.int32
         )
-        forcing = regrid_arrivals(
-            flat[:, width].astype(jnp.int32)[None],
-            flat[:, width + 1].astype(jnp.int32)[None],
-            flat,
+        fluxes = flat[:, :width]
+        label_ids = jnp.arange(weight_count * tile_rows, dtype=jnp.int32)
+        selector = (arrived_labels[:, None] == label_ids[None, :]).astype(jnp.bfloat16)
+        binned = lax.dot_general(
+            selector, fluxes, (((0,), (0,)), ((), ())), preferred_element_type=jnp.float32
+        )
+        binned = binned.reshape(weight_count, tile_rows, flux_count, block_len)
+        binned_hi = lax.reduce_precision(binned, exponent_bits=8, mantissa_bits=7)
+        binned_lo = (binned - binned_hi).astype(jnp.bfloat16)
+        forcing = jnp.einsum(
+            "wdfa,wab->fdb",
+            binned_hi.astype(jnp.bfloat16),
             weights_low,
-            flux_count,
-        )
+            preferred_element_type=jnp.float32,
+        ) + jnp.einsum("wdfa,wab->fdb", binned_lo, weights_low, preferred_element_type=jnp.float32)
         lifted = jnp.sum(forcing * ocean_map[:, 0][:, None, None], axis=0)
         top_level = jnp.where(sea_cells, values_top + lifted, state_top)
         table = jnp.einsum("db,wab->wda", top_level, weights_wide, precision=HIGHEST)
@@ -483,8 +490,13 @@
     first, forcing, answers = lax.optimization_barrier((first, forcing, answers))
 
     def ocean_final(values, forcing):
-        moved = values + jnp.einsum("frc,fk->rck", forcing, ocean_map, precision=HIGHEST)
-        return jnp.where(sea_cells[:, :, None], moved, state)
+        sea_rows = jnp.broadcast_to(
+            (land_mask == 1).astype(jnp.int32).reshape(1, tile_rows * block_len),
+            (8, tile_rows * block_len),
+        )
+        return ocean_update(
+            values, state, sea_rows, forcing.reshape(flux_count, tile_rows * block_len), ocean_map
+        )
 
     final_state = lax.cond(ocean_side, ocean_final, lambda values, forcing: second, first, forcing)
     surface_out = jnp.where(

time: 211 us -> 204 us (0.967)
  Pallas kernels: 121 us -> 85.3 us
  local copies, waits for them, and re-layouts: 29 us -> 48.5 us
  matrix products: 22.9 us -> 29.2 us
  other arithmetic: 12.5 us -> 15.6 us
    pallas_call x1, Pallas kernels: 52.5 us -> 17 us  [ocean_update(): pl.pallas_call(ocean_update_kernel, grid=(rows // ROW_BLOCK,), in_specs=[...]
    cond x4 -> x9, local copies, waits for them, and re-layouts: 11.3 us -> 27.1 us
    dot_general x1 -> x3, matrix products: 18.3 us -> 25.2 us  [the longest x1 10.8 us: ocean_reply(): jnp.einsum('wdfa,wab->fdb', binned_hi.astype(jnp.bfloat16), weights_low,...]
    another operation x2 -> x3, local copies, waits for them, and re-layouts: 0.14 us -> 2.3 us
    unnamed x17 -> x23, local copies, waits for them, and re-layouts: 7.41 us -> 7.43 us
  transfers between devices with their start and end apart: 8 -> 8, of which waited for: 2 -> 1; matrix products, arithmetic and copies ran while one was open for 6% -> 7% of each run, Pallas kernels for 0% -> 0%
where the time goes in v7:
time: 204 us; the launch traced here: 202 us
  Pallas kernels  85.3 us (42%)
  local copies, waits for them, and re-layouts  48.5 us (24%)
  matrix products  29.2 us (14%)
  starting transfers between devices  19.7 us (10%)
  other arithmetic  15.6 us (8%)
  waiting for transfers between devices  2.59 us (1%)
    pallas_call x1, Pallas kernels, gather_to_ocean(): pl.pallas_call(functools.partial(gather_kernel, tuple(offsets), tuple(sha...  42.8 us
    cond x9, local copies, waits for them, and re-layouts  27.1 us
    pallas_call x1, Pallas kernels, substep(): pl.pallas_call(functools.partial(substep_kernel, with_flux, comp_total),...  20.2 us
    pallas_call x1, Pallas kernels, ocean_update(): pl.pallas_call(ocean_update_kernel, grid=(rows // ROW_BLOCK,), in_specs=[...  17 us
    ppermute x2, starting transfers between devices, edge_rows(): after = lax.ppermute(values[:1], ('comp', 'lat'), down)  11.3 us
    dot_general x1, matrix products, ocean_reply(): jnp.einsum('wdfa,wab->fdb', binned_hi.astype(jnp.bfloat16), weights_low,...  10.8 us
    dot_general x1, matrix products, ocean_reply(): lax.dot_general(selector, fluxes, (((0,), (0,)), ((), ())), preferred_ele...  10.3 us
    unnamed x23, local copies, waits for them, and re-layouts  7.43 us
  transfers between devices with their start and end apart: 8, of which 1 were waited for; matrix products, arithmetic and copies ran while one was open for 7% of the time, Pallas kernels for 0%

profile of v7, /device:TPU:25, one launch (start us, length us, event | category | flops | bytes accessed | tf_op | source)
XLA Modules:
  0.0 202.2 jit_solution(13514183529791099335)
XLA Ops:
  1.5 5.8 %collective-permute-start.1 = (f32[1,128,128]{2,1,0:T(8,128)S(1)}, f32[1,128,128]{2,1,0:T(8,128)S(1)}, u32[]{:S(2)}, u32[]{:S(2)}) collective-permute-start(f32[1,128,128]{2,1,0:T(8,128)S(1)} %get-tuple-element.195), channel_id=1, source_target_pairs={{8,0},{16,8},{24,16},{32,24},{40,32},{48,40},{56,48},{64,56},{72,6... | collective-permute-start | bytes 196616 | tf_op jit(solution)/shard_map/ppermute | solution.py:160
  7.4 1.9 collective-permute-start
  9.3 1.3 fusion.38
  10.6 2.1 %collective-permute-start.2 = (f32[128,1,128]{2,1,0:T(1,128)S(1)}, f32[128,1,128]{2,1,0:T(1,128)S(1)}, u32[]{:S(2)}, u32[]{:S(2)}) collective-permute-start(f32[128,1,128]{2,1,0:T(1,128)S(1)} %get-tuple-element.192), channel_id=1, source_target_pairs={{0,1},{1,2},{2,3},{3,4},{4,5},{5,6},{6,7},{7,0},{8,9},{9,10},{10,1... | collective-permute-start | bytes 196616 | tf_op jit(solution)/shard_map/ppermute | solution.py:168
  12.7 1.6 fusion.39
  17.9 1.5 broadcast_select_fusion.3.mix_ref
  19.5 2.9 %convert_element_type.45 = f32[32,128,128]{2,1,0:T(8,128)} convert(bf16[32,128,128]{2,1,0:T(8,128)(2,1)} %param.22) | non-fusion elementwise | flops 524288 | bytes 3145728 | tf_op jit(solution)/shard_map/convert_element_type | solution.py:446
  25.8 20.2 %shard_map.106 = (f32[128,128,128]{2,1,0:T(8,128)}, f32[8,16384]{1,0:T(8,128)S(1)}) custom-call(f32[128,128,128]{2,1,0:T(8,128)} %x_ref.1, f32[16,128,128]{2,1,0:T(8,128)} %pad_maximum_fusion.2.top_ref, f32[16,128,128]{2,1,0:T(8,128)} %pad_maximum_fusion.3.bottom_ref, f32[128,1,128]{2,1,0:T(1,128)} %copy-done.7, f32[128,1,128]{2,1,0:T(1,128)} %copy-done.8, ...), custom_call_target="tpu_custom_call" | custom-call | flops 1610612736 | bytes 16777216 | tf_op jit(solution)/shard_map/pallas_call | solution.py:112
  48.3 1.9 collective-permute-start.4
  50.2 5.5 %collective-permute-start.5 = (f32[1,128,128]{2,1,0:T(8,128)S(1)}, f32[1,128,128]{2,1,0:T(8,128)S(1)}, u32[]{:S(2)}, u32[]{:S(2)}) collective-permute-start(f32[1,128,128]{2,1,0:T(8,128)S(1)} %get-tuple-element.187), channel_id=1, source_target_pairs={{8,0},{16,8},{24,16},{32,24},{40,32},{48,40},{56,48},{64,56},{72,6... | collective-permute-start | bytes 196616 | tf_op jit(solution)/shard_map/ppermute | solution.py:160
  55.7 2.3 %collective-permute-start.6 = (f32[128,1,128]{2,1,0:T(1,128)S(1)}, f32[128,1,128]{2,1,0:T(1,128)S(1)}, u32[]{:S(2)}, u32[]{:S(2)}) collective-permute-start(f32[128,1,128]{2,1,0:T(1,128)S(1)} %get-tuple-element.190), channel_id=1, source_target_pairs={{0,1},{1,2},{2,3},{3,4},{4,5},{5,6},{6,7},{7,0},{8,9},{9,10},{10,1... | collective-permute-start | bytes 196616 | tf_op jit(solution)/shard_map/ppermute | solution.py:168
  59.5 2.6 %collective-permute-done.7 = f32[128,1,128]{2,1,0:T(1,128)S(1)} collective-permute-done((f32[128,1,128]{2,1,0:T(1,128)S(1)}, f32[128,1,128]{2,1,0:T(1,128)S(1)}, u32[]{:S(2)}, u32[]{:S(2)}) %collective-permute-start.7) | collective-permute-done | bytes 65568 | tf_op jit(solution)/shard_map/ppermute | solution.py:169
  62.1 8.0 %conditional.3 = (f32[128,128,128]{2,1,0:T(8,128)}, bf16[8,128,128]{2,0,1:T(8,128)(2,1)S(1)}) conditional(s32[]{:T(128)} %convert_element_type.41, (f32[128,128,128]{2,1,0:T(8,128)}, pred[1,128,128]{2,1,0:T(8,128)(4,1)S(1)}, pred[1,128,128]{2,1,0:T(8,128)(4,1)S(1)}, f32[128,8]{0,1:T(8,128)S(1)}, f32[128,1,128]{2,1,0:T(1,128)S(1)}, ...), branch_computations={%region_0.1_spmd.clone, %region_1.2_spmd} | conditional | flops 1712226304 | bytes 26066960 | solution.py:411
  62.1 8.0 %copy.62 = f32[128,128,128]{2,1,0:T(8,128)} copy(f32[128,128,128]{2,1,0:T(8,128)} %param.1) | data formatting | bytes 16777216 | tf_op jit(solution)/shard_map/cond
  71.5 42.8 %shard_map.107 = bf16[24,32,1152]{2,1,0:T(8,128)(2,1)S(1)} custom-call(bf16[8,32,1152]{2,1,0:T(8,128)(2,1)} %bitcast.81), custom_call_target="tpu_custom_call" | custom-call | tf_op jit(solution)/shard_map/pallas_call | solution.py:238
  114.4 45.8 %conditional.4 = (f32[8,128,128]{2,1,0:T(8,128)}, f32[24,32,128]{2,1,0:T(8,128)S(1)}, f32[128,128]{1,0:T(8,128)}) conditional(s32[]{:T(128)} %convert_element_type.41, f32[128,128]{1,0:T(8,128)} %bitcast.15, (bf16[24,32,1152]{2,1,0:T(8,128)(2,1)S(1)}, bf16[32,128,128]{2,1,0:T(8,128)(2,1)S(1)}, f32[8,128]{1,0:T(8,128)S(1)}, f32[128,128]{1,0:T(8,128)}, ...), branch_computations={%region_4.5_spmd, %region_5.7_spmd} | conditional | flops 9419880448 | bytes 178050272 | solution.py:482
  114.8 10.3 %fusion.3 = f32[512,8,8,128]{3,1,2,0:T(8,128)} fusion(s32[768]{0:T(1024)S(1)} %get-tuple-element.178, bf16[768,1152]{1,0:T(8,128)(2,1)S(1)} %bitcast.75), kind=kOutput, calls=%fused_computation.13 | convolution fusion | flops 6445596672 | bytes 18354176 | tf_op jit(solution)/shard_map/cond/branch_1_fun/dot_general | solution.py:457
  125.1 9.6 %copy.40 = f32[512,8,8,128]{3,2,1,0:T(8,128)S(1)} copy(f32[512,8,8,128]{3,1,2,0:T(8,128)} %fusion.3) | data formatting | bytes 33554432 | tf_op jit(solution)/shard_map/cond
  134.7 4.1 %fusion.9 = f32[128,8,128]{2,0,1:T(8,128)S(1)} fusion(f32[32,128,8,128]{3,2,1,0:T(8,128)S(1)} %bitcast.69, bf16[32,128,128]{2,1,0:T(8,128)(2,1)S(1)} %get-tuple-element.65), kind=kOutput, calls=%fused_computation.18 | convolution fusion | flops 1086324736 | bytes 18350080 | tf_op jit(solution)/shard_map/cond/branch_1_fun/wdfa,wab->fdb/dot_general | solution.py:468
  138.8 1.6 copy-done
  140.6 10.8 %multiply_reduce_fusion = (f32[128,128]{1,0:T(8,128)S(1)}, f32[8,128,128]{2,1,0:T(8,128)}) fusion(f32[8]{0:T(128)S(1)} %slice_bitcast_fusion, f32[128,8,128]{2,0,1:T(8,128)S(1)} %fusion.9, bf16[32,128,128]{2,1,0:T(8,128)(2,1)S(1)} %get-tuple-element.65, f32[32,128,8,128]{3,2,1,0:T(8,128)} %bitcast.70), kind=kOutput, calls=%fused_computation.25 | convolution fusion | flops 1082507264 | bytes 18939936 | tf_op jit(solution)/shard_map/cond/branch_1_fun/wdfa,wab->fdb/dot_general | solution.py:463
  152.4 1.5 add_select_fusion
  153.9 2.8 %fusion.19 = f32[128,32,128]{2,0,1:T(8,128)S(1)} fusion(f32[32,128,128]{2,1,0:T(8,128)S(1)} %copy-done.3, f32[128,128]{1,0:T(8,128)} %add_select_fusion), kind=kOutput, calls=%fused_computation.31 | convolution fusion | flops 805306368 | bytes 4259840 | tf_op jit(solution)/shard_map/cond/branch_1_fun/db,wab->wda/dot_general | solution.py:471
  156.7 1.6 gather_fusion
  158.3 1.4 and_reduce_fusion
  160.2 5.3 %shard_map.108 = f32[8,32,128]{2,1,0:T(8,128)} custom-call(f32[24,32,128]{2,1,0:T(8,128)S(1)} %get-tuple-element.92.surface_ref), custom_call_target="tpu_custom_call" | custom-call | tf_op jit(solution)/shard_map/pallas_call | solution.py:309
  165.5 28.8 %conditional.5 = (f32[128,128,128]{2,1,0:T(8,128)}) conditional(s32[]{:T(128)} %convert_element_type.41, f32[128,128,128]{2,1,0:T(8,128)} %get-tuple-element.88, (s32[128,128]{1,0:T(8,128)}, f32[8,128,128]{2,1,0:T(8,128)}, f32[128,128,128]{2,1,0:T(8,128)}, f32[128,128,128]{2,1,0:T(8,128)}, f32[8,128]{1,0:T(8,128)}) %tuple.44), branch_computations={%region_7.8_spmd, %region_8.9_spmd} | conditional | flops 134250496 | bytes 43712520 | solution.py:501
  167.2 2.2 %copy.58 = f32[8,128,128]{2,0,1:T(8,128)} copy(f32[8,128,128]{2,1,0:T(8,128)} %get-tuple-element.173) | data formatting | bytes 1048576 | tf_op jit(solution)/shard_map
  169.4 17.0 %branch_1_fun.1 = f32[128,128,128]{2,1,0:T(8,128)} custom-call(f32[128,128,128]{2,1,0:T(8,128)} %get-tuple-element.71.first_ref, f32[128,128,128]{2,1,0:T(8,128)} %get-tuple-element.72.state_ref, s32[8,16384]{1,0:T(8,128)} %broadcast_in_dim.105.sea_ref, f32[8,16384]{1,0:T(8,128)} %bitcast.77, f32[8,128]{1,0:T(8,128)} %get-tuple-element.75.spread_ref), custom_call_target="tpu_custom_call" | custom-call | flops 134217728 | bytes 25165824 | tf_op jit(solution)/shard_map/cond/branch_1_fun/pallas_call | solution.py:349
  186.4 7.9 %copy.71 = f32[128,128,128]{2,1,0:T(8,128)} copy(f32[128,128,128]{2,1,0:T(8,128)} %branch_1_fun.1) | data formatting | bytes 16777216 | tf_op jit(solution)/shard_map/cond
  194.3 5.2 %copy.39 = f32[128,128,1]{1,0,2:T(8,128)S(1)} copy(f32[128,128,1]{2,1,0:T(8,128)} %bitcast.73) | data formatting | bytes 131072
  200.7 1.5 fusion.30
  (73 shorter events, 17.8 us)
Async XLA Ops:
  1.5 20.9 %collective-permute-start.1 = (f32[1,128,128]{2,1,0:T(8,128)S(1)}, f32[1,128,128]{2,1,0:T(8,128)S(1)}, u32[]{:S(2)}, u32[]{:S(2)}) collective-permute-start(f32[1,128,128]{2,1,0:T(8,128)S(1)} %get-tuple-element.195), channel_id=1, source_target_pairs={{8,0},{16,8},{24,16},{32,24},{40,32},{48,40},{56,48},{64,56},{72,6... | collective-permute-start | bytes 196616 | tf_op jit(solution)/shard_map/ppermute | solution.py:160
  7.4 16.1 %collective-permute-start = (f32[1,128,128]{2,1,0:T(8,128)S(1)}, f32[1,128,128]{2,1,0:T(8,128)S(1)}, u32[]{:S(2)}, u32[]{:S(2)}) collective-permute-start(f32[1,128,128]{2,1,0:T(8,128)S(1)} %get-tuple-element.196), channel_id=1, source_target_pairs={{0,8},{8,16},{16,24},{24,32},{32,40},{40,48},{48,56},{56,64},{64,7... | collective-permute-start | bytes 196616 | tf_op jit(solution)/shard_map/ppermute | solution.py:159
  10.6 13.9 %collective-permute-start.2 = (f32[128,1,128]{2,1,0:T(1,128)S(1)}, f32[128,1,128]{2,1,0:T(1,128)S(1)}, u32[]{:S(2)}, u32[]{:S(2)}) collective-permute-start(f32[128,1,128]{2,1,0:T(1,128)S(1)} %get-tuple-element.192), channel_id=1, source_target_pairs={{0,1},{1,2},{2,3},{3,4},{4,5},{5,6},{6,7},{7,0},{8,9},{9,10},{10,1... | collective-permute-start | bytes 196616 | tf_op jit(solution)/shard_map/ppermute | solution.py:168
  12.7 11.9 %collective-permute-start.3 = (f32[128,1,128]{2,1,0:T(1,128)S(1)}, f32[128,1,128]{2,1,0:T(1,128)S(1)}, u32[]{:S(2)}, u32[]{:S(2)}) collective-permute-start(f32[128,1,128]{2,1,0:T(1,128)S(1)} %get-tuple-element.191), channel_id=1, source_target_pairs={{1,0},{2,1},{3,2},{4,3},{5,4},{6,5},{7,6},{0,7},{9,8},{10,9},{11,1... | collective-permute-start | bytes 196616 | tf_op jit(solution)/shard_map/ppermute | solution.py:169
  22.4 39.7 %copy-start.6 = (f32[128,128]{1,0:T(8,128)S(1)}, f32[128,128]{1,0:T(8,128)}, u32[]{:S(2)}) copy-start(f32[128,128]{1,0:T(8,128)} %param.18) | copy-start | bytes 196612
  22.4 39.7 %copy-start.12 = (f32[128,8]{0,1:T(8,128)S(1)}, f32[128,8]{0,1:T(8,128)}, u32[]{:S(2)}) copy-start(f32[128,8]{0,1:T(8,128)} %param.20) | copy-start | bytes 12292
  24.5 0.6 copy-start.7
  25.2 0.6 copy-start.8
  46.0 16.1 %copy-start.10 = (f32[8,16384]{1,0:T(8,128)}, f32[8,16384]{1,0:T(8,128)S(1)}, u32[]{:S(2)}) copy-start(f32[8,16384]{1,0:T(8,128)S(1)} %get-tuple-element.89) | copy-start | bytes 1572868
  48.3 11.1 %collective-permute-start.4 = (f32[1,128,128]{2,1,0:T(8,128)S(1)}, f32[1,128,128]{2,1,0:T(8,128)S(1)}, u32[]{:S(2)}, u32[]{:S(2)}) collective-permute-start(f32[1,128,128]{2,1,0:T(8,128)S(1)} %get-tuple-element.188), channel_id=1, source_target_pairs={{0,8},{8,16},{16,24},{24,32},{32,40},{40,48},{48,56},{56,64},{64,7... | collective-permute-start | bytes 196616 | tf_op jit(solution)/shard_map/ppermute | solution.py:159
  50.2 9.2 %collective-permute-start.5 = (f32[1,128,128]{2,1,0:T(8,128)S(1)}, f32[1,128,128]{2,1,0:T(8,128)S(1)}, u32[]{:S(2)}, u32[]{:S(2)}) collective-permute-start(f32[1,128,128]{2,1,0:T(8,128)S(1)} %get-tuple-element.187), channel_id=1, source_target_pairs={{8,0},{16,8},{24,16},{32,24},{40,32},{48,40},{56,48},{64,56},{72,6... | collective-permute-start | bytes 196616 | tf_op jit(solution)/shard_map/ppermute | solution.py:160
  55.7 3.7 %collective-permute-start.6 = (f32[128,1,128]{2,1,0:T(1,128)S(1)}, f32[128,1,128]{2,1,0:T(1,128)S(1)}, u32[]{:S(2)}, u32[]{:S(2)}) collective-permute-start(f32[128,1,128]{2,1,0:T(1,128)S(1)} %get-tuple-element.190), channel_id=1, source_target_pairs={{0,1},{1,2},{2,3},{3,4},{4,5},{5,6},{6,7},{7,0},{8,9},{9,10},{10,1... | collective-permute-start | bytes 196616 | tf_op jit(solution)/shard_map/ppermute | solution.py:168
  58.0 4.0 %collective-permute-start.7 = (f32[128,1,128]{2,1,0:T(1,128)S(1)}, f32[128,1,128]{2,1,0:T(1,128)S(1)}, u32[]{:S(2)}, u32[]{:S(2)}) collective-permute-start(f32[128,1,128]{2,1,0:T(1,128)S(1)} %get-tuple-element.189), channel_id=1, source_target_pairs={{1,0},{2,1},{3,2},{4,3},{5,4},{6,5},{7,6},{0,7},{9,8},{10,9},{11,1... | collective-permute-start | bytes 196616 | tf_op jit(solution)/shard_map/ppermute | solution.py:169
  62.1 52.3 %copy-start.2 = (bf16[32,128,128]{2,1,0:T(8,128)(2,1)S(1)}, bf16[32,128,128]{2,1,0:T(8,128)(2,1)}, u32[]{:S(2)}) copy-start(bf16[32,128,128]{2,1,0:T(8,128)(2,1)} %param.22) | copy-start | bytes 3145732
  62.1 52.3 %copy-start.11 = (f32[8,128]{1,0:T(8,128)S(1)}, f32[8,128]{1,0:T(8,128)}, u32[]{:S(2)}) copy-start(f32[8,128]{1,0:T(8,128)} %param.21) | copy-start | bytes 12292
  114.4 10.7 %copy-start.4 = (bf16[24,32,1152]{2,1,0:T(8,128)(2,1)}, bf16[24,32,1152]{2,1,0:T(8,128)(2,1)S(1)}, u32[]{:S(2)}) copy-start(bf16[24,32,1152]{2,1,0:T(8,128)(2,1)S(1)} %get-tuple-element.64) | copy-start | bytes 5308420 | tf_op jit(solution)/shard_map/cond
  134.7 5.7 %copy-start = (f32[512,8,8,128]{3,2,1,0:T(8,128)}, f32[512,8,8,128]{3,2,1,0:T(8,128)S(1)}, u32[]{:S(2)}) copy-start(f32[512,8,8,128]{3,2,1,0:T(8,128)S(1)} %copy.40) | copy-start | bytes 50331652 | tf_op jit(solution)/shard_map/cond
  140.6 13.4 %copy-start.3 = (f32[32,128,128]{2,1,0:T(8,128)S(1)}, f32[32,128,128]{2,1,0:T(8,128)}, u32[]{:S(2)}) copy-start(f32[32,128,128]{2,1,0:T(8,128)} %get-tuple-element.70) | copy-start | bytes 6291460 | tf_op jit(solution)/shard_map/cond
  194.3 5.3 %copy-start.1 = (f32[8,32,128]{2,1,0:T(8,128)S(1)}, f32[8,32,128]{2,1,0:T(8,128)}, u32[]{:S(2)}) copy-start(f32[8,32,128]{2,1,0:T(8,128)} %shard_map.108) | copy-start | bytes 393220
  194.3 6.1 %copy-start.9 = (pred[128,2]{1,0:T(8,128)(4,1)S(1)}, pred[128,2]{1,0:T(8,128)(4,1)}, u32[]{:S(2)}) copy-start(pred[128,2]{1,0:T(8,128)(4,1)} %compare_and_fusion) | copy-start | bytes 772
  194.3 6.4 %copy-start.5 = (s32[128,128]{1,0:T(8,128)S(1)}, s32[128,128]{1,0:T(8,128)}, u32[]{:S(2)}) copy-start(s32[128,128]{1,0:T(8,128)} %param.16) | copy-start | bytes 196612

commit v8 on v7

--- a/solution.py
+++ b/solution.py
@@ -320,7 +320,19 @@
     )(replies)
 
 
-def ocean_update_kernel(first_ref, state_ref, sea_ref, forcing_ref, spread_ref, out_ref):
+def ocean_update_kernel(comp_total, first_ref, state_ref, sea_ref, forcing_ref, spread_ref, out_ref):
+    ocean = lax.axis_index("comp") == comp_total - 1
+
+    @pl.when(ocean)
+    def _():
+        ocean_block(first_ref, state_ref, sea_ref, forcing_ref, spread_ref, out_ref)
+
+    @pl.when(jnp.logical_not(ocean))
+    def _():
+        out_ref[...] = first_ref[...]
+
+
+def ocean_block(first_ref, state_ref, sea_ref, forcing_ref, spread_ref, out_ref):
     rows, cols, levels = first_ref.shape
     forcing = forcing_ref[...]
     spread = spread_ref[...]
@@ -342,12 +354,12 @@
     out_ref[...] = kept.reshape(rows, cols, levels)
 
 
-def ocean_update(first, state, sea_rows, forcing, ocean_map):
+def ocean_update(first, state, sea_rows, forcing, ocean_map, comp_total):
     rows, cols, levels = first.shape
     flux_count = forcing.shape[0]
     cells = rows * cols
     return pl.pallas_call(
-        ocean_update_kernel,
+        functools.partial(ocean_update_kernel, comp_total),
         grid=(rows // ROW_BLOCK,),
         in_specs=[
             pl.BlockSpec((ROW_BLOCK, cols, levels), lambda i: (i, 0, 0)),
@@ -487,21 +499,22 @@
         answers.reshape(neighbour_count * capacity, block_len), entry_slots, axis=0
     )
     returned = per_entry.reshape(tile_rows, intersections, block_len).sum(axis=1)
-    first, forcing, answers = lax.optimization_barrier((first, forcing, answers))
-
-    def ocean_final(values, forcing):
-        sea_rows = jnp.broadcast_to(
-            (land_mask == 1).astype(jnp.int32).reshape(1, tile_rows * block_len),
-            (8, tile_rows * block_len),
-        )
-        return ocean_update(
-            values, state, sea_rows, forcing.reshape(flux_count, tile_rows * block_len), ocean_map
-        )
-
-    final_state = lax.cond(ocean_side, ocean_final, lambda values, forcing: second, first, forcing)
-    surface_out = jnp.where(
-        ocean_side, ocean_top, jnp.where(sea_cells, returned, final_state[:, :, 0])
-    )
+    second, forcing, answers = lax.optimization_barrier((second, forcing, answers))
+    sea_rows = jnp.broadcast_to(
+        sea_cells.astype(jnp.int32).reshape(1, tile_rows * block_len), (8, tile_rows * block_len)
+    )
+    final_state = ocean_update(
+        second,
+        state,
+        sea_rows,
+        forcing.reshape(flux_count, tile_rows * block_len),
+        ocean_map,
+        comp_count,
+    )
+    top_plane = lax.cond(
+        ocean_side, lambda values: ocean_top, lambda values: values[:, :, 0], final_state
+    )
+    surface_out = jnp.where(ocean_side, ocean_top, jnp.where(sea_cells, returned, top_plane))
     return (final_state, surface_out)
 
 

time: 204 us -> 196 us (0.961)
  the two profiles are of different devices: /device:TPU:25 before, /device:TPU:1 now
where the time goes in v8:
time: 196 us; the launch traced here: 194 us
  Pallas kernels  135 us (69%)
  local copies, waits for them, and re-layouts  26.3 us (13%)
  starting transfers between devices  15.5 us (8%)
  other arithmetic  11.9 us (6%)
  waiting for transfers between devices  3.81 us (2%)
    pallas_call x1, Pallas kernels, spread_from_ocean(): pl.pallas_call(functools.partial(spread_kernel, tuple(offsets), tuple(sha...  54.2 us
    pallas_call x2, Pallas kernels, substep(): pl.pallas_call(functools.partial(substep_kernel, with_flux, comp_total),...  34.5 us
    pallas_call x1, Pallas kernels, gather_to_ocean(): pl.pallas_call(functools.partial(gather_kernel, tuple(offsets), tuple(sha...  31.6 us
    pallas_call x1, Pallas kernels, ocean_update(): pl.pallas_call(functools.partial(ocean_update_kernel, comp_total), grid=(...  14.4 us
    cond x4, local copies, waits for them, and re-layouts  12.1 us
    ppermute x2, starting transfers between devices, edge_rows(): before = lax.ppermute(values[-1:], ('comp', 'lat'), up)  8.55 us
    unnamed x19, local copies, waits for them, and re-layouts  4.33 us
    ppermute x2, starting transfers between devices, edge_columns(): before = lax.ppermute(values[:, -1:], 'lon', up)  4.19 us
  transfers between devices with their start and end apart: 8, of which 2 were waited for; matrix products, arithmetic and copies ran while one was open for 6% of the time, Pallas kernels for 0%

profile of v8, /device:TPU:1, one launch (start us, length us, event | category | flops | bytes accessed | tf_op | source)
XLA Modules:
  0.0 194.5 jit_solution(6012805606497735115)
XLA Ops:
  0.6 0.9 fusion.39
  1.5 1.3 collective-permute-start.1
  2.8 5.0 %collective-permute-start = (f32[1,128,128]{2,1,0:T(8,128)S(1)}, f32[1,128,128]{2,1,0:T(8,128)S(1)}, u32[]{:S(2)}, u32[]{:S(2)}) collective-permute-start(f32[1,128,128]{2,1,0:T(8,128)S(1)} %get-tuple-element.158), channel_id=1, source_target_pairs={{0,8},{8,16},{16,24},{24,32},{32,40},{40,48},{48,56},{56,64},{64,7... | collective-permute-start | bytes 196616 | tf_op jit(solution)/shard_map/ppermute | solution.py:159
  7.8 1.3 fusion.37
  9.1 2.2 %collective-permute-start.2 = (f32[128,1,128]{2,1,0:T(1,128)S(1)}, f32[128,1,128]{2,1,0:T(1,128)S(1)}, u32[]{:S(2)}, u32[]{:S(2)}) collective-permute-start(f32[128,1,128]{2,1,0:T(1,128)S(1)} %get-tuple-element.154), channel_id=1, source_target_pairs={{0,1},{1,2},{2,3},{3,4},{4,5},{5,6},{6,7},{7,0},{8,9},{9,10},{10,1... | collective-permute-start | bytes 196616 | tf_op jit(solution)/shard_map/ppermute | solution.py:168
  11.3 1.6 fusion.38
  15.9 1.5 broadcast_select_fusion.3.mix_ref
  17.6 2.9 %convert_element_type.45 = f32[32,128,128]{2,1,0:T(8,128)} convert(bf16[32,128,128]{2,1,0:T(8,128)(2,1)} %param.22) | non-fusion elementwise | flops 524288 | bytes 3145728 | tf_op jit(solution)/shard_map/convert_element_type | solution.py:458
  20.5 1.1 pad_maximum_fusion.3.bottom_ref
  21.5 1.0 pad_maximum_fusion.2.top_ref
  23.8 15.7 %shard_map.106 = (f32[128,128,128]{2,1,0:T(8,128)}, f32[8,16384]{1,0:T(8,128)S(1)}) custom-call(f32[128,128,128]{2,1,0:T(8,128)} %state_ref.1, f32[16,128,128]{2,1,0:T(8,128)} %pad_maximum_fusion.2.top_ref, f32[16,128,128]{2,1,0:T(8,128)} %pad_maximum_fusion.3.bottom_ref, f32[128,1,128]{2,1,0:T(1,128)} %copy-done.7, f32[128,1,128]{2,1,0:T(1,128)} %copy-done.8, ...), custom_call_target="tpu_custom_call" | custom-call | flops 1610612736 | bytes 16777216 | tf_op jit(solution)/shard_map/pallas_call | solution.py:112
  39.5 1.0 fusion.35
  40.5 1.3 fusion.36
  41.8 3.5 %collective-permute-start.4 = (f32[1,128,128]{2,1,0:T(8,128)S(1)}, f32[1,128,128]{2,1,0:T(8,128)S(1)}, u32[]{:S(2)}, u32[]{:S(2)}) collective-permute-start(f32[1,128,128]{2,1,0:T(8,128)S(1)} %get-tuple-element.150), channel_id=1, source_target_pairs={{0,8},{8,16},{16,24},{24,32},{32,40},{40,48},{48,56},{56,64},{64,7... | collective-permute-start | bytes 196616 | tf_op jit(solution)/shard_map/ppermute | solution.py:159
  45.4 1.3 collective-permute-start.5
  46.7 2.0 %collective-permute-start.6 = (f32[128,1,128]{2,1,0:T(1,128)S(1)}, f32[128,1,128]{2,1,0:T(1,128)S(1)}, u32[]{:S(2)}, u32[]{:S(2)}) collective-permute-start(f32[128,1,128]{2,1,0:T(1,128)S(1)} %get-tuple-element.152), channel_id=1, source_target_pairs={{0,1},{1,2},{2,3},{3,4},{4,5},{5,6},{6,7},{7,0},{8,9},{9,10},{10,1... | collective-permute-start | bytes 196616 | tf_op jit(solution)/shard_map/ppermute | solution.py:168
  48.9 1.7 collective-permute-done.5
  50.6 2.1 %collective-permute-done.7 = f32[128,1,128]{2,1,0:T(1,128)S(1)} collective-permute-done((f32[128,1,128]{2,1,0:T(1,128)S(1)}, f32[128,1,128]{2,1,0:T(1,128)S(1)}, u32[]{:S(2)}, u32[]{:S(2)}) %collective-permute-start.7) | collective-permute-done | bytes 65568 | tf_op jit(solution)/shard_map/ppermute | solution.py:169
  52.8 28.6 %conditional.3 = (f32[128,128,128]{2,1,0:T(8,128)}, bf16[8,128,128]{2,0,1:T(8,128)(2,1)S(1)}) conditional(s32[]{:T(128)} %convert_element_type.41, (f32[128,128,128]{2,1,0:T(8,128)}, pred[1,128,128]{2,1,0:T(8,128)(4,1)S(1)}, pred[1,128,128]{2,1,0:T(8,128)(4,1)S(1)}, f32[128,8]{0,1:T(8,128)S(1)}, f32[128,1,128]{2,1,0:T(1,128)S(1)}, ...), branch_computations={%region_0.1_spmd.clone, %region_1.2_spmd} | conditional | flops 1712226304 | bytes 76398640 | solution.py:423
  52.8 3.5 %copy.70.x_ref = f32[128,128,128]{2,1,0:T(8,128)S(1)} copy(f32[128,128,128]{2,1,0:T(8,128)} %get-tuple-element.84) | data formatting | bytes 16777216 | tf_op jit(solution)/shard_map/cond
  56.3 3.4 %copy-done.1 = f32[128,128,128]{2,1,0:T(8,128)} copy-done((f32[128,128,128]{2,1,0:T(8,128)}, f32[128,128,128]{2,1,0:T(8,128)S(1)}, u32[]{:S(2)}) %copy-start.1) | copy-done | bytes 8388632 | tf_op jit(solution)/shard_map/cond
  59.9 1.5 pad_maximum_fusion
  61.3 18.9 %branch_0_fun.1 = (f32[128,128,128]{2,1,0:T(8,128)}, f32[8,16384]{1,0:T(8,128)}) custom-call(f32[128,128,128]{2,1,0:T(8,128)} %copy-done.1, f32[16,128,128]{2,1,0:T(8,128)} %get-tuple-element.145.top_ref, f32[16,128,128]{2,1,0:T(8,128)} %get-tuple-element.146.bottom_ref, f32[128,1,128]{2,1,0:T(1,128)S(1)} %get-tuple-element.85.west_ref, ...), custom_call_target="tpu_custom_call" | custom-call | flops 1711276032 | bytes 16777216 | tf_op jit(solution)/shard_map/cond/branch_0_fun/pallas_call | solution.py:112
  80.2 1.1 fusion
  81.6 1.2 convolution_convert_fusion
  82.7 31.6 %shard_map.107 = bf16[24,32,1152]{2,1,0:T(8,128)(2,1)S(1)} custom-call(bf16[8,32,1152]{2,1,0:T(8,128)(2,1)} %bitcast.81), custom_call_target="tpu_custom_call" | custom-call | tf_op jit(solution)/shard_map/pallas_call | solution.py:238
  114.3 1.6 conditional.4
  116.0 54.2 %shard_map.108 = f32[8,32,128]{2,1,0:T(8,128)} custom-call(f32[24,32,128]{2,1,0:T(8,128)} %get-tuple-element.72.surface_ref), custom_call_target="tpu_custom_call" | custom-call | tf_op jit(solution)/shard_map/pallas_call | solution.py:309
  170.2 2.1 %copy.55 = f32[1,8,128,128]{3,1,2,0:T(8,128)} copy(f32[1,8,128,128]{3,2,1,0:T(8,128)} %bitcast.36) | data formatting | bytes 1048576
  173.1 14.4 %shard_map.109 = f32[128,128,128]{2,1,0:T(8,128)} custom-call(f32[128,128,128]{2,1,0:T(8,128)} %get-tuple-element.73.first_ref, f32[128,128,128]{2,1,0:T(8,128)} %state_ref.1, s32[8,16384]{1,0:T(8,128)} %broadcast_in_dim.132.sea_ref, f32[8,16384]{1,0:T(8,128)} %bitcast.75, f32[8,128]{1,0:T(8,128)S(1)} %copy-done.10), custom_call_target="tpu_custom_call" | custom-call | flops 134217728 | bytes 25165824 | tf_op jit(solution)/shard_map/pallas_call | solution.py:361
  187.6 5.2 %conditional.5 = (f32[128,128]{1,0:T(8,128)S(1)}) conditional(s32[]{:T(128)} %convert_element_type.41, f32[128,128,128]{2,1,0:T(8,128)} %shard_map.109, f32[128,128]{1,0:T(8,128)S(1)} %get-tuple-element.75), branch_computations={%region_8.9_spmd, %region_9.10_spmd} | conditional | bytes 131080 | solution.py:514
  187.6 5.2 %copy.35 = f32[128,128,1]{1,0,2:T(8,128)S(1)} copy(f32[128,128,1]{2,1,0:T(8,128)} %bitcast.69) | data formatting | bytes 131072 | tf_op jit(solution)/shard_map/cond
  (54 shorter events, 9.0 us)
Async XLA Ops:
  1.5 18.9 %collective-permute-start.1 = (f32[1,128,128]{2,1,0:T(8,128)S(1)}, f32[1,128,128]{2,1,0:T(8,128)S(1)}, u32[]{:S(2)}, u32[]{:S(2)}) collective-permute-start(f32[1,128,128]{2,1,0:T(8,128)S(1)} %get-tuple-element.157), channel_id=1, source_target_pairs={{8,0},{16,8},{24,16},{32,24},{40,32},{48,40},{56,48},{64,56},{72,6... | collective-permute-start | bytes 196616 | tf_op jit(solution)/shard_map/ppermute | solution.py:160
  2.8 18.7 %collective-permute-start = (f32[1,128,128]{2,1,0:T(8,128)S(1)}, f32[1,128,128]{2,1,0:T(8,128)S(1)}, u32[]{:S(2)}, u32[]{:S(2)}) collective-permute-start(f32[1,128,128]{2,1,0:T(8,128)S(1)} %get-tuple-element.158), channel_id=1, source_target_pairs={{0,8},{8,16},{16,24},{24,32},{32,40},{40,48},{48,56},{56,64},{64,7... | collective-permute-start | bytes 196616 | tf_op jit(solution)/shard_map/ppermute | solution.py:159
  9.1 13.4 %collective-permute-start.2 = (f32[128,1,128]{2,1,0:T(1,128)S(1)}, f32[128,1,128]{2,1,0:T(1,128)S(1)}, u32[]{:S(2)}, u32[]{:S(2)}) collective-permute-start(f32[128,1,128]{2,1,0:T(1,128)S(1)} %get-tuple-element.154), channel_id=1, source_target_pairs={{0,1},{1,2},{2,3},{3,4},{4,5},{5,6},{6,7},{7,0},{8,9},{9,10},{10,1... | collective-permute-start | bytes 196616 | tf_op jit(solution)/shard_map/ppermute | solution.py:168
  11.3 11.3 %collective-permute-start.3 = (f32[128,1,128]{2,1,0:T(1,128)S(1)}, f32[128,1,128]{2,1,0:T(1,128)S(1)}, u32[]{:S(2)}, u32[]{:S(2)}) collective-permute-start(f32[128,1,128]{2,1,0:T(1,128)S(1)} %get-tuple-element.153), channel_id=1, source_target_pairs={{1,0},{2,1},{3,2},{4,3},{5,4},{6,5},{7,6},{0,7},{9,8},{10,9},{11,1... | collective-permute-start | bytes 196616 | tf_op jit(solution)/shard_map/ppermute | solution.py:169
  20.4 32.3 %copy-start.6 = (f32[128,128]{1,0:T(8,128)S(1)}, f32[128,128]{1,0:T(8,128)}, u32[]{:S(2)}) copy-start(f32[128,128]{1,0:T(8,128)} %param.18) | copy-start | bytes 196612
  20.4 32.3 %copy-start.11 = (f32[128,8]{0,1:T(8,128)S(1)}, f32[128,8]{0,1:T(8,128)}, u32[]{:S(2)}) copy-start(f32[128,8]{0,1:T(8,128)} %param.20) | copy-start | bytes 12292
  22.6 0.6 copy-start.7
  23.2 0.6 copy-start.8
  39.5 13.2 %copy-start.9 = (f32[8,16384]{1,0:T(8,128)}, f32[8,16384]{1,0:T(8,128)S(1)}, u32[]{:S(2)}) copy-start(f32[8,16384]{1,0:T(8,128)S(1)} %get-tuple-element.69) | copy-start | bytes 1572868
  41.8 7.1 %collective-permute-start.4 = (f32[1,128,128]{2,1,0:T(8,128)S(1)}, f32[1,128,128]{2,1,0:T(8,128)S(1)}, u32[]{:S(2)}, u32[]{:S(2)}) collective-permute-start(f32[1,128,128]{2,1,0:T(8,128)S(1)} %get-tuple-element.150), channel_id=1, source_target_pairs={{0,8},{8,16},{16,24},{24,32},{32,40},{40,48},{48,56},{56,64},{64,7... | collective-permute-start | bytes 196616 | tf_op jit(solution)/shard_map/ppermute | solution.py:159
  45.4 5.2 %collective-permute-start.5 = (f32[1,128,128]{2,1,0:T(8,128)S(1)}, f32[1,128,128]{2,1,0:T(8,128)S(1)}, u32[]{:S(2)}, u32[]{:S(2)}) collective-permute-start(f32[1,128,128]{2,1,0:T(8,128)S(1)} %get-tuple-element.149), channel_id=1, source_target_pairs={{8,0},{16,8},{24,16},{32,24},{40,32},{48,40},{56,48},{64,56},{72,6... | collective-permute-start | bytes 196616 | tf_op jit(solution)/shard_map/ppermute | solution.py:160
  46.7 3.9 %collective-permute-start.6 = (f32[128,1,128]{2,1,0:T(1,128)S(1)}, f32[128,1,128]{2,1,0:T(1,128)S(1)}, u32[]{:S(2)}, u32[]{:S(2)}) collective-permute-start(f32[128,1,128]{2,1,0:T(1,128)S(1)} %get-tuple-element.152), channel_id=1, source_target_pairs={{0,1},{1,2},{2,3},{3,4},{4,5},{5,6},{6,7},{7,0},{8,9},{9,10},{10,1... | collective-permute-start | bytes 196616 | tf_op jit(solution)/shard_map/ppermute | solution.py:168
  48.7 4.0 %collective-permute-start.7 = (f32[128,1,128]{2,1,0:T(1,128)S(1)}, f32[128,1,128]{2,1,0:T(1,128)S(1)}, u32[]{:S(2)}, u32[]{:S(2)}) collective-permute-start(f32[128,1,128]{2,1,0:T(1,128)S(1)} %get-tuple-element.151), channel_id=1, source_target_pairs={{1,0},{2,1},{3,2},{4,3},{5,4},{6,5},{7,6},{0,7},{9,8},{10,9},{11,1... | collective-permute-start | bytes 196616 | tf_op jit(solution)/shard_map/ppermute | solution.py:169
  52.7 61.6 %copy-start.3 = (bf16[32,128,128]{2,1,0:T(8,128)(2,1)S(1)}, bf16[32,128,128]{2,1,0:T(8,128)(2,1)}, u32[]{:S(2)}) copy-start(bf16[32,128,128]{2,1,0:T(8,128)(2,1)} %param.22) | copy-start | bytes 3145732
  52.8 61.6 %copy-start.10 = (f32[8,128]{1,0:T(8,128)S(1)}, f32[8,128]{1,0:T(8,128)}, u32[]{:S(2)}) copy-start(f32[8,128]{1,0:T(8,128)} %spread_ref.1) | copy-start | bytes 12292
  56.3 3.4 %copy-start.1 = (f32[128,128,128]{2,1,0:T(8,128)}, f32[128,128,128]{2,1,0:T(8,128)S(1)}, u32[]{:S(2)}) copy-start(f32[128,128,128]{2,1,0:T(8,128)S(1)} %copy.70.x_ref) | copy-start | bytes 25165828 | tf_op jit(solution)/shard_map/cond
  187.6 5.2 %copy-start.2 = (f32[8,32,128]{2,1,0:T(8,128)S(1)}, f32[8,32,128]{2,1,0:T(8,128)}, u32[]{:S(2)}) copy-start(f32[8,32,128]{2,1,0:T(8,128)} %shard_map.108) | copy-start | bytes 393220

commit v9 on v8

--- a/solution.py
+++ b/solution.py
@@ -376,6 +376,56 @@
     )(first, state, sea_rows, forcing, ocean_map)
 
 
+def scatter_regrid_kernel(labels_ref, fluxes_ref, weights_ref, out_ref, binned_ref):
+    entries = fluxes_ref.shape[0]
+    weight_count, tile_rows, block_len = weights_ref.shape
+    flux_count = fluxes_ref.shape[1]
+    binned_ref[...] = jnp.zeros_like(binned_ref)
+
+    def add_one(e, carry):
+        label = labels_ref[e]
+        binned_ref[label] = binned_ref[label] + fluxes_ref[e]
+        return carry
+
+    lax.fori_loop(0, entries, add_one, 0, unroll=8)
+    out_ref[...] = jnp.zeros_like(out_ref)
+
+    def regrid_one(w, carry):
+        start = pl.multiple_of(w * tile_rows, tile_rows)
+        block = binned_ref[pl.ds(start, tile_rows)].reshape(tile_rows * flux_count, block_len)
+        high = block.astype(jnp.bfloat16)
+        low = (block - high.astype(jnp.float32)).astype(jnp.bfloat16)
+        weight = weights_ref[w]
+        out_ref[...] += jnp.dot(high, weight, preferred_element_type=jnp.float32) + jnp.dot(
+            low, weight, preferred_element_type=jnp.float32
+        )
+        return carry
+
+    lax.fori_loop(0, weight_count, regrid_one, 0)
+
+
+def scatter_regrid(labels, fluxes, weights):
+    entries, flux_count, block_len = fluxes.shape
+    weight_count, tile_rows, _ = weights.shape
+    return pl.pallas_call(
+        scatter_regrid_kernel,
+        out_shape=jax.ShapeDtypeStruct((tile_rows * flux_count, block_len), jnp.float32),
+        in_specs=[
+            pl.BlockSpec(memory_space=pltpu.SMEM),
+            pl.BlockSpec(memory_space=pltpu.VMEM),
+            pl.BlockSpec(memory_space=pltpu.VMEM),
+        ],
+        out_specs=pl.BlockSpec(memory_space=pltpu.VMEM),
+        scratch_shapes=[pltpu.VMEM((weight_count * tile_rows, flux_count, block_len), jnp.float32)],
+        compiler_params=pltpu.CompilerParams(vmem_limit_bytes=48 * 1024 * 1024),
+        cost_estimate=pl.CostEstimate(
+            flops=4 * weight_count * tile_rows * flux_count * block_len * block_len,
+            transcendentals=0,
+            bytes_accessed=entries * flux_count * block_len * 4 + weight_count * tile_rows * block_len * 2,
+        ),
+    )(labels, fluxes, weights)
+
+
 def local(
     state, land_mask, intersection_list, mix_atm, mix_ocn, flux_map, ocean_map, regrid_weights
 ):
@@ -463,21 +513,9 @@
         arrived_labels = flat[:, width].astype(jnp.int32) * tile_rows + flat[:, width + 1].astype(
             jnp.int32
         )
-        fluxes = flat[:, :width]
-        label_ids = jnp.arange(weight_count * tile_rows, dtype=jnp.int32)
-        selector = (arrived_labels[:, None] == label_ids[None, :]).astype(jnp.bfloat16)
-        binned = lax.dot_general(
-            selector, fluxes, (((0,), (0,)), ((), ())), preferred_element_type=jnp.float32
-        )
-        binned = binned.reshape(weight_count, tile_rows, flux_count, block_len)
-        binned_hi = lax.reduce_precision(binned, exponent_bits=8, mantissa_bits=7)
-        binned_lo = (binned - binned_hi).astype(jnp.bfloat16)
-        forcing = jnp.einsum(
-            "wdfa,wab->fdb",
-            binned_hi.astype(jnp.bfloat16),
-            weights_low,
-            preferred_element_type=jnp.float32,
-        ) + jnp.einsum("wdfa,wab->fdb", binned_lo, weights_low, preferred_element_type=jnp.float32)
+        fluxes = flat[:, :width].astype(jnp.float32).reshape(-1, flux_count, block_len)
+        forcing = scatter_regrid(arrived_labels, fluxes, weights_low)
+        forcing = forcing.reshape(tile_rows, flux_count, block_len).transpose(1, 0, 2)
         lifted = jnp.sum(forcing * ocean_map[:, 0][:, None, None], axis=0)
         top_level = jnp.where(sea_cells, values_top + lifted, state_top)
         table = jnp.einsum("db,wab->wda", top_level, weights_wide, precision=HIGHEST)

time: 196 us -> 180 us (0.918)
  Pallas kernels: 135 us -> 118 us
    pallas_call x1, Pallas kernels: 54.2 us -> 37.3 us  [spread_from_ocean(): pl.pallas_call(functools.partial(spread_kernel, tuple(offsets), tuple(sha...]
    unnamed x19 -> x30, local copies, waits for them, and re-layouts: 4.33 us -> 2.19 us
  transfers between devices with their start and end apart: 8 -> 8, of which waited for: 2 -> 2; matrix products, arithmetic and copies ran while one was open for 6% -> 9% of each run, Pallas kernels for 0% -> 0%
where the time goes in v9:
time: 180 us; the launch traced here: 178 us
  Pallas kernels  118 us (66%)
  local copies, waits for them, and re-layouts  24.8 us (14%)
  starting transfers between devices  16.4 us (9%)
  other arithmetic  13.7 us (8%)
  waiting for transfers between devices  3.21 us (2%)
    pallas_call x1, Pallas kernels, spread_from_ocean(): pl.pallas_call(functools.partial(spread_kernel, tuple(offsets), tuple(sha...  37.3 us
    pallas_call x2, Pallas kernels, substep(): pl.pallas_call(functools.partial(substep_kernel, with_flux, comp_total),...  34.5 us
    pallas_call x1, Pallas kernels, gather_to_ocean(): pl.pallas_call(functools.partial(gather_kernel, tuple(offsets), tuple(sha...  31.5 us
    pallas_call x1, Pallas kernels, ocean_update(): pl.pallas_call(functools.partial(ocean_update_kernel, comp_total), grid=(...  14.2 us
    cond x4, local copies, waits for them, and re-layouts  12 us
    ppermute x2, starting transfers between devices, edge_rows(): before = lax.ppermute(values[-1:], ('comp', 'lat'), up)  9.53 us
    ppermute x2, starting transfers between devices, edge_columns(): before = lax.ppermute(values[:, -1:], 'lon', up)  4.17 us
  transfers between devices with their start and end apart: 8, of which 2 were waited for; matrix products, arithmetic and copies ran while one was open for 9% of the time, Pallas kernels for 0%

profile of v9, /device:TPU:1, one launch (start us, length us, event | category | flops | bytes accessed | tf_op | source)
XLA Modules:
  0.0 177.8 jit_solution(14422911991818343637)
XLA Ops:
  0.6 1.5 fusion.23
  2.2 1.3 collective-permute-start.1
  3.5 5.8 %collective-permute-start = (f32[1,128,128]{2,1,0:T(8,128)}, f32[1,128,128]{2,1,0:T(8,128)}, u32[]{:S(2)}, u32[]{:S(2)}) collective-permute-start(f32[1,128,128]{2,1,0:T(8,128)} %get-tuple-element.156), channel_id=1, source_target_pairs={{0,8},{8,16},{16,24},{24,32},{32,40},{40,48},{48,56},{56,64},{64,7... | collective-permute-start | bytes 196616 | tf_op jit(solution)/shard_map/ppermute | solution.py:159
  9.2 1.9 %fusion.21 = (f32[128,1,128]{2,1,0:T(1,128)}, f32[128,1,128]{2,1,0:T(1,128)}) fusion(f32[128,128,128]{2,1,0:T(8,128)} %state_ref.1), kind=kLoop, calls=%fused_computation.61 | loop fusion | bytes 262144 | tf_op jit(solution)/shard_map/slice | solution.py:169
  11.2 2.1 %collective-permute-start.2 = (f32[128,1,128]{2,1,0:T(1,128)}, f32[128,1,128]{2,1,0:T(1,128)S(1)}, u32[]{:S(2)}, u32[]{:S(2)}) collective-permute-start(f32[128,1,128]{2,1,0:T(1,128)} %get-tuple-element.152), channel_id=1, source_target_pairs={{0,1},{1,2},{2,3},{3,4},{4,5},{5,6},{6,7},{7,0},{8,9},{9,10},{10,1... | collective-permute-start | bytes 196616 | tf_op jit(solution)/shard_map/ppermute | solution.py:168
  13.3 1.7 fusion.22
  21.7 1.6 convert_element_type.39
  23.4 0.8 broadcast_select_fusion.1
  24.2 1.1 pad_maximum_fusion.3.bottom_ref
  25.3 1.0 pad_maximum_fusion.2.top_ref
  27.6 15.7 %shard_map.106 = (f32[128,128,128]{2,1,0:T(8,128)}, f32[8,16384]{1,0:T(8,128)S(1)}) custom-call(f32[128,128,128]{2,1,0:T(8,128)} %state_ref.1, f32[16,128,128]{2,1,0:T(8,128)} %pad_maximum_fusion.2.top_ref, f32[16,128,128]{2,1,0:T(8,128)} %pad_maximum_fusion.3.bottom_ref, f32[128,1,128]{2,1,0:T(1,128)} %copy-done.8, f32[128,1,128]{2,1,0:T(1,128)} %copy-done.9, ...), custom_call_target="tpu_custom_call" | custom-call | flops 1610612736 | bytes 16777216 | tf_op jit(solution)/shard_map/pallas_call | solution.py:112
  43.3 1.0 fusion.19
  44.3 1.3 fusion.20
  45.6 3.8 %collective-permute-start.4 = (f32[1,128,128]{2,1,0:T(8,128)S(1)}, f32[1,128,128]{2,1,0:T(8,128)S(1)}, u32[]{:S(2)}, u32[]{:S(2)}) collective-permute-start(f32[1,128,128]{2,1,0:T(8,128)S(1)} %get-tuple-element.148), channel_id=1, source_target_pairs={{0,8},{8,16},{16,24},{24,32},{32,40},{40,48},{48,56},{56,64},{64,7... | collective-permute-start | bytes 196616 | tf_op jit(solution)/shard_map/ppermute | solution.py:159
  49.4 1.3 collective-permute-start.5
  50.7 2.0 %collective-permute-start.6 = (f32[128,1,128]{2,1,0:T(1,128)S(1)}, f32[128,1,128]{2,1,0:T(1,128)S(1)}, u32[]{:S(2)}, u32[]{:S(2)}) collective-permute-start(f32[128,1,128]{2,1,0:T(1,128)S(1)} %get-tuple-element.150), channel_id=1, source_target_pairs={{0,1},{1,2},{2,3},{3,4},{4,5},{5,6},{6,7},{7,0},{8,9},{9,10},{10,1... | collective-permute-start | bytes 196616 | tf_op jit(solution)/shard_map/ppermute | solution.py:168
  53.5 1.1 collective-permute-done.5
  54.6 2.1 %collective-permute-done.7 = f32[128,1,128]{2,1,0:T(1,128)S(1)} collective-permute-done((f32[128,1,128]{2,1,0:T(1,128)S(1)}, f32[128,1,128]{2,1,0:T(1,128)S(1)}, u32[]{:S(2)}, u32[]{:S(2)}) %collective-permute-start.7) | collective-permute-done | bytes 65568 | tf_op jit(solution)/shard_map/ppermute | solution.py:169
  56.8 28.5 %conditional.3 = (f32[128,128,128]{2,1,0:T(8,128)}, bf16[8,128,128]{2,0,1:T(8,128)(2,1)S(1)}) conditional(s32[]{:T(128)} %convert_element_type.35, (f32[128,128,128]{2,1,0:T(8,128)}, pred[1,128,128]{2,1,0:T(8,128)(4,1)S(1)}, pred[1,128,128]{2,1,0:T(8,128)(4,1)S(1)}, f32[128,8]{0,1:T(8,128)S(1)}, f32[128,1,128]{2,1,0:T(1,128)S(1)}, ...), branch_computations={%region_0.1_spmd.clone, %region_1.2_spmd} | conditional | flops 1712226304 | bytes 76398640 | solution.py:473
  56.8 3.4 %copy.44.x_ref = f32[128,128,128]{2,1,0:T(8,128)S(1)} copy(f32[128,128,128]{2,1,0:T(8,128)} %get-tuple-element.84) | data formatting | bytes 16777216 | tf_op jit(solution)/shard_map/cond
  60.2 3.4 %copy-done = f32[128,128,128]{2,1,0:T(8,128)} copy-done((f32[128,128,128]{2,1,0:T(8,128)}, f32[128,128,128]{2,1,0:T(8,128)S(1)}, u32[]{:S(2)}) %copy-start) | copy-done | bytes 8388632 | tf_op jit(solution)/shard_map/cond
  63.8 1.5 pad_maximum_fusion
  65.3 18.9 %branch_0_fun.1 = (f32[128,128,128]{2,1,0:T(8,128)}, f32[8,16384]{1,0:T(8,128)}) custom-call(f32[128,128,128]{2,1,0:T(8,128)} %copy-done, f32[16,128,128]{2,1,0:T(8,128)} %get-tuple-element.145.top_ref, f32[16,128,128]{2,1,0:T(8,128)} %get-tuple-element.146.bottom_ref, f32[128,1,128]{2,1,0:T(1,128)S(1)} %get-tuple-element.85.west_ref, ...), custom_call_target="tpu_custom_call" | custom-call | flops 1711276032 | bytes 16777216 | tf_op jit(solution)/shard_map/cond/branch_0_fun/pallas_call | solution.py:112
  84.1 1.1 fusion
  85.5 1.2 convolution_convert_fusion
  86.7 31.5 %shard_map.107 = bf16[24,32,1152]{2,1,0:T(8,128)(2,1)S(1)} custom-call(bf16[8,32,1152]{2,1,0:T(8,128)(2,1)} %bitcast.62), custom_call_target="tpu_custom_call" | custom-call | tf_op jit(solution)/shard_map/pallas_call | solution.py:238
  118.3 37.3 %shard_map.108 = f32[8,32,128]{2,1,0:T(8,128)} custom-call(f32[24,32,128]{2,1,0:T(8,128)S(1)} %get-tuple-element.72.surface_ref), custom_call_target="tpu_custom_call" | custom-call | tf_op jit(solution)/shard_map/pallas_call | solution.py:309
  155.6 0.9 broadcast_in_dim.130.sea_ref
  156.5 14.2 %shard_map.109 = f32[128,128,128]{2,1,0:T(8,128)} custom-call(f32[128,128,128]{2,1,0:T(8,128)} %get-tuple-element.73.first_ref, f32[128,128,128]{2,1,0:T(8,128)} %state_ref.1, s32[8,16384]{1,0:T(8,128)} %broadcast_in_dim.130.sea_ref, f32[8,16384]{1,0:T(8,128)S(1)} %bitcast.56, f32[8,128]{1,0:T(8,128)} %spread_ref.1), custom_call_target="tpu_custom_call" | custom-call | flops 134217728 | bytes 25165824 | tf_op jit(solution)/shard_map/pallas_call | solution.py:361
  170.7 5.2 %conditional.5 = (f32[128,128]{1,0:T(8,128)S(1)}) conditional(s32[]{:T(128)} %convert_element_type.35, f32[128,128,128]{2,1,0:T(8,128)} %shard_map.109, f32[128,128]{1,0:T(8,128)S(1)} %get-tuple-element.75), branch_computations={%region_8.9_spmd, %region_9.10_spmd} | conditional | bytes 131080 | solution.py:552
  170.7 5.2 %copy.26 = f32[128,128,1]{1,0,2:T(8,128)S(1)} copy(f32[128,128,1]{2,1,0:T(8,128)} %bitcast.49) | data formatting | bytes 131072 | tf_op jit(solution)/shard_map/cond
  176.0 0.9 gather_fusion.1
  (65 shorter events, 10.2 us)
Async XLA Ops:
  2.2 21.2 %collective-permute-start.1 = (f32[1,128,128]{2,1,0:T(8,128)}, f32[1,128,128]{2,1,0:T(8,128)}, u32[]{:S(2)}, u32[]{:S(2)}) collective-permute-start(f32[1,128,128]{2,1,0:T(8,128)} %get-tuple-element.155), channel_id=1, source_target_pairs={{8,0},{16,8},{24,16},{32,24},{40,32},{48,40},{56,48},{64,56},{72,6... | collective-permute-start | bytes 196616 | tf_op jit(solution)/shard_map/ppermute | solution.py:160
  3.4 12.2 %copy-start.11 = (s32[128,128]{1,0:T(8,128)S(1)}, s32[128,128]{1,0:T(8,128)}, u32[]{:S(2)}) copy-start(s32[128,128]{1,0:T(8,128)} %param.16) | copy-start | bytes 196612
  3.5 21.8 %collective-permute-start = (f32[1,128,128]{2,1,0:T(8,128)}, f32[1,128,128]{2,1,0:T(8,128)}, u32[]{:S(2)}, u32[]{:S(2)}) collective-permute-start(f32[1,128,128]{2,1,0:T(8,128)} %get-tuple-element.156), channel_id=1, source_target_pairs={{0,8},{8,16},{16,24},{24,32},{32,40},{40,48},{48,56},{56,64},{64,7... | collective-permute-start | bytes 196616 | tf_op jit(solution)/shard_map/ppermute | solution.py:159
  11.2 15.2 %collective-permute-start.2 = (f32[128,1,128]{2,1,0:T(1,128)}, f32[128,1,128]{2,1,0:T(1,128)S(1)}, u32[]{:S(2)}, u32[]{:S(2)}) collective-permute-start(f32[128,1,128]{2,1,0:T(1,128)} %get-tuple-element.152), channel_id=1, source_target_pairs={{0,1},{1,2},{2,3},{3,4},{4,5},{5,6},{6,7},{7,0},{8,9},{9,10},{10,1... | collective-permute-start | bytes 196616 | tf_op jit(solution)/shard_map/ppermute | solution.py:168
  13.3 13.1 %collective-permute-start.3 = (f32[128,1,128]{2,1,0:T(1,128)}, f32[128,1,128]{2,1,0:T(1,128)S(1)}, u32[]{:S(2)}, u32[]{:S(2)}) collective-permute-start(f32[128,1,128]{2,1,0:T(1,128)} %get-tuple-element.151), channel_id=1, source_target_pairs={{1,0},{2,1},{3,2},{4,3},{5,4},{6,5},{7,6},{0,7},{9,8},{10,9},{11,1... | collective-permute-start | bytes 196616 | tf_op jit(solution)/shard_map/ppermute | solution.py:169
  13.3 6.4 %copy-start.7 = (f32[128,128]{1,0:T(8,128)S(1)}, f32[128,128]{1,0:T(8,128)}, u32[]{:S(2)}) copy-start(f32[128,128]{1,0:T(8,128)} %param.18) | copy-start | bytes 196612
  13.3 6.4 %copy-start.10 = (f32[128,128]{1,0:T(8,128)S(1)}, f32[128,128]{1,0:T(8,128)}, u32[]{:S(2)}) copy-start(f32[128,128]{1,0:T(8,128)} %param.19) | copy-start | bytes 196612
  13.3 8.4 %copy-start.5 = (bf16[32,128,128]{2,1,0:T(8,128)(2,1)S(1)}, bf16[32,128,128]{2,1,0:T(8,128)(2,1)}, u32[]{:S(2)}) copy-start(bf16[32,128,128]{2,1,0:T(8,128)(2,1)} %param.22) | copy-start | bytes 3145732
  19.0 6.3 %copy-start.15 = (s32[256]{0:T(256)}, s32[256]{0:T(256)S(1)}, u32[]{:S(2)}) copy-start(s32[256]{0:T(256)S(1)} %multiply_add_fusion) | copy-start | bytes 3076
  26.4 26.5 %copy-start.18 = (s32[256,1]{0,1:T(1,128)S(1)}, s32[256,1]{0,1:T(1,128)}, u32[]{:S(2)}) copy-start(s32[256,1]{0,1:T(1,128)} %compare_select_fusion.2) | copy-start | bytes 3076
  26.4 30.4 %copy-start.17 = (f32[128,8]{0,1:T(8,128)S(1)}, f32[128,8]{0,1:T(8,128)}, u32[]{:S(2)}) copy-start(f32[128,8]{0,1:T(8,128)} %param.20) | copy-start | bytes 12292
  26.4 0.6 copy-start.8
  27.0 0.6 copy-start.9
  43.3 13.5 %copy-start.13 = (f32[8,16384]{1,0:T(8,128)}, f32[8,16384]{1,0:T(8,128)S(1)}, u32[]{:S(2)}) copy-start(f32[8,16384]{1,0:T(8,128)S(1)} %get-tuple-element.69) | copy-start | bytes 1572868
  45.6 7.9 %collective-permute-start.4 = (f32[1,128,128]{2,1,0:T(8,128)S(1)}, f32[1,128,128]{2,1,0:T(8,128)S(1)}, u32[]{:S(2)}, u32[]{:S(2)}) collective-permute-start(f32[1,128,128]{2,1,0:T(8,128)S(1)} %get-tuple-element.148), channel_id=1, source_target_pairs={{0,8},{8,16},{16,24},{24,32},{32,40},{40,48},{48,56},{56,64},{64,7... | collective-permute-start | bytes 196616 | tf_op jit(solution)/shard_map/ppermute | solution.py:159
  49.4 5.2 %collective-permute-start.5 = (f32[1,128,128]{2,1,0:T(8,128)S(1)}, f32[1,128,128]{2,1,0:T(8,128)S(1)}, u32[]{:S(2)}, u32[]{:S(2)}) collective-permute-start(f32[1,128,128]{2,1,0:T(8,128)S(1)} %get-tuple-element.147), channel_id=1, source_target_pairs={{8,0},{16,8},{24,16},{32,24},{40,32},{48,40},{56,48},{64,56},{72,6... | collective-permute-start | bytes 196616 | tf_op jit(solution)/shard_map/ppermute | solution.py:160
  50.7 3.9 %collective-permute-start.6 = (f32[128,1,128]{2,1,0:T(1,128)S(1)}, f32[128,1,128]{2,1,0:T(1,128)S(1)}, u32[]{:S(2)}, u32[]{:S(2)}) collective-permute-start(f32[128,1,128]{2,1,0:T(1,128)S(1)} %get-tuple-element.150), channel_id=1, source_target_pairs={{0,1},{1,2},{2,3},{3,4},{4,5},{5,6},{6,7},{7,0},{8,9},{9,10},{10,1... | collective-permute-start | bytes 196616 | tf_op jit(solution)/shard_map/ppermute | solution.py:168
  52.7 4.0 %collective-permute-start.7 = (f32[128,1,128]{2,1,0:T(1,128)S(1)}, f32[128,1,128]{2,1,0:T(1,128)S(1)}, u32[]{:S(2)}, u32[]{:S(2)}) collective-permute-start(f32[128,1,128]{2,1,0:T(1,128)S(1)} %get-tuple-element.149), channel_id=1, source_target_pairs={{1,0},{2,1},{3,2},{4,3},{5,4},{6,5},{7,6},{0,7},{9,8},{10,9},{11,1... | collective-permute-start | bytes 196616 | tf_op jit(solution)/shard_map/ppermute | solution.py:169
  56.7 28.7 %copy-start.16 = (s32[256]{0:T(256)S(1)}, s32[256]{0:T(256)}, u32[]{:S(2)}) copy-start(s32[256]{0:T(256)} %copy-done.15) | copy-start | bytes 3076
  60.2 3.4 %copy-start = (f32[128,128,128]{2,1,0:T(8,128)}, f32[128,128,128]{2,1,0:T(8,128)S(1)}, u32[]{:S(2)}) copy-start(f32[128,128,128]{2,1,0:T(8,128)S(1)} %copy.44.x_ref) | copy-start | bytes 25165828 | tf_op jit(solution)/shard_map/cond
  85.5 32.7 %copy-start.14 = (f32[8,128]{1,0:T(8,128)S(1)}, f32[8,128]{1,0:T(8,128)}, u32[]{:S(2)}) copy-start(f32[8,128]{1,0:T(8,128)} %spread_ref.1) | copy-start | bytes 12292
  170.7 5.3 %copy-start.1 = (f32[8,32,128]{2,1,0:T(8,128)S(1)}, f32[8,32,128]{2,1,0:T(8,128)}, u32[]{:S(2)}) copy-start(f32[8,32,128]{2,1,0:T(8,128)} %shard_map.108) | copy-start | bytes 393220
  170.7 6.1 %copy-start.12 = (pred[128,2]{1,0:T(8,128)(4,1)S(1)}, pred[128,2]{1,0:T(8,128)(4,1)}, u32[]{:S(2)}) copy-start(pred[128,2]{1,0:T(8,128)(4,1)} %compare_and_fusion) | copy-start | bytes 772

commit v10 on v9

--- a/solution.py
+++ b/solution.py
@@ -320,8 +320,8 @@
     )(replies)
 
 
-def ocean_update_kernel(comp_total, first_ref, state_ref, sea_ref, forcing_ref, spread_ref, out_ref):
-    ocean = lax.axis_index("comp") == comp_total - 1
+def ocean_update_kernel(flag_ref, first_ref, state_ref, sea_ref, forcing_ref, spread_ref, out_ref):
+    ocean = flag_ref[0] == 1
 
     @pl.when(ocean)
     def _():
@@ -358,22 +358,26 @@
     rows, cols, levels = first.shape
     flux_count = forcing.shape[0]
     cells = rows * cols
+    flag = (lax.axis_index("comp") == comp_total - 1).astype(jnp.int32).reshape(1)
     return pl.pallas_call(
-        functools.partial(ocean_update_kernel, comp_total),
-        grid=(rows // ROW_BLOCK,),
-        in_specs=[
-            pl.BlockSpec((ROW_BLOCK, cols, levels), lambda i: (i, 0, 0)),
-            pl.BlockSpec((ROW_BLOCK, cols, levels), lambda i: (i, 0, 0)),
-            pl.BlockSpec((8, ROW_BLOCK * cols), lambda i: (0, i)),
-            pl.BlockSpec((flux_count, ROW_BLOCK * cols), lambda i: (0, i)),
-            pl.BlockSpec((flux_count, levels), lambda i: (0, 0)),
-        ],
-        out_specs=pl.BlockSpec((ROW_BLOCK, cols, levels), lambda i: (i, 0, 0)),
+        ocean_update_kernel,
+        grid_spec=pltpu.PrefetchScalarGridSpec(
+            num_scalar_prefetch=1,
+            grid=(rows // ROW_BLOCK,),
+            in_specs=[
+                pl.BlockSpec((ROW_BLOCK, cols, levels), lambda i, f: (i, 0, 0)),
+                pl.BlockSpec((ROW_BLOCK, cols, levels), lambda i, f: (i * f[0], 0, 0)),
+                pl.BlockSpec((8, ROW_BLOCK * cols), lambda i, f: (0, i * f[0])),
+                pl.BlockSpec((flux_count, ROW_BLOCK * cols), lambda i, f: (0, i * f[0])),
+                pl.BlockSpec((flux_count, levels), lambda i, f: (0, 0)),
+            ],
+            out_specs=pl.BlockSpec((ROW_BLOCK, cols, levels), lambda i, f: (i, 0, 0)),
+        ),
         out_shape=jax.ShapeDtypeStruct(first.shape, jnp.float32),
         cost_estimate=pl.CostEstimate(
             flops=8 * cells * levels * flux_count, transcendentals=0, bytes_accessed=12 * cells * levels
         ),
-    )(first, state, sea_rows, forcing, ocean_map)
+    )(flag, first, state, sea_rows, forcing, ocean_map)
 
 
 def scatter_regrid_kernel(labels_ref, fluxes_ref, weights_ref, out_ref, binned_ref):

time: 180 us -> 177 us (0.983)
  the two profiles are of different devices: /device:TPU:1 before, /device:TPU:25 now
where the time goes in v10:
time: 177 us; the launch traced here: 175 us
  Pallas kernels  114 us (64%)
  starting transfers between devices  19.8 us (11%)
  local copies, waits for them, and re-layouts  18.2 us (10%)
  other arithmetic  13.6 us (8%)
  matrix products  4.65 us (3%)
  waiting for transfers between devices  3.2 us (2%)
    pallas_call x1, Pallas kernels, gather_to_ocean(): pl.pallas_call(functools.partial(gather_kernel, tuple(offsets), tuple(sha...  56.5 us
    pallas_call x1, Pallas kernels, substep(): pl.pallas_call(functools.partial(substep_kernel, with_flux, comp_total),...  20.2 us
    pallas_call x1, Pallas kernels, ocean_update(): pl.pallas_call(ocean_update_kernel, grid_spec=pltpu.PrefetchScalarGridSpe...  16.8 us
    pallas_call x1, Pallas kernels, scatter_regrid(): pl.pallas_call(scatter_regrid_kernel, out_shape=jax.ShapeDtypeStruct((til...  15.6 us
    ppermute x2, starting transfers between devices, edge_rows(): after = lax.ppermute(values[:1], ('comp', 'lat'), down)  11.1 us
    pallas_call x1, Pallas kernels, spread_from_ocean(): pl.pallas_call(functools.partial(spread_kernel, tuple(offsets), tuple(sha...  5.33 us
    ppermute x2, starting transfers between devices, edge_columns(): before = lax.ppermute(values[:, -1:], 'lon', up)  4.35 us
    ppermute x2, starting transfers between devices, edge_rows(): before = lax.ppermute(values[-1:], ('comp', 'lat'), up)  4.23 us
  transfers between devices with their start and end apart: 8, of which 2 were waited for; matrix products, arithmetic and copies ran while one was open for 9% of the time, Pallas kernels for 0%

profile of v10, /device:TPU:25, one launch (start us, length us, event | category | flops | bytes accessed | tf_op | source)
XLA Modules:
  0.0 174.9 jit_solution(16635785056212238720)
XLA Ops:
  0.6 1.5 fusion.23
  2.2 5.8 %collective-permute-start.1 = (f32[1,128,128]{2,1,0:T(8,128)}, f32[1,128,128]{2,1,0:T(8,128)}, u32[]{:S(2)}, u32[]{:S(2)}) collective-permute-start(f32[1,128,128]{2,1,0:T(8,128)} %get-tuple-element.155), channel_id=1, source_target_pairs={{8,0},{16,8},{24,16},{32,24},{40,32},{48,40},{56,48},{64,56},{72,6... | collective-permute-start | bytes 196616 | tf_op jit(solution)/shard_map/ppermute | solution.py:160
  8.0 2.1 %collective-permute-start = (f32[1,128,128]{2,1,0:T(8,128)}, f32[1,128,128]{2,1,0:T(8,128)}, u32[]{:S(2)}, u32[]{:S(2)}) collective-permute-start(f32[1,128,128]{2,1,0:T(8,128)} %get-tuple-element.156), channel_id=1, source_target_pairs={{0,8},{8,16},{16,24},{24,32},{32,40},{40,48},{48,56},{56,64},{64,7... | collective-permute-start | bytes 196616 | tf_op jit(solution)/shard_map/ppermute | solution.py:159
  10.1 2.0 %fusion.21 = (f32[128,1,128]{2,1,0:T(1,128)}, f32[128,1,128]{2,1,0:T(1,128)}) fusion(f32[128,128,128]{2,1,0:T(8,128)} %state_ref.1), kind=kLoop, calls=%fused_computation.61 | loop fusion | bytes 262144 | tf_op jit(solution)/shard_map/slice | solution.py:169
  12.0 2.1 %collective-permute-start.2 = (f32[128,1,128]{2,1,0:T(1,128)}, f32[128,1,128]{2,1,0:T(1,128)S(1)}, u32[]{:S(2)}, u32[]{:S(2)}) collective-permute-start(f32[128,1,128]{2,1,0:T(1,128)} %get-tuple-element.152), channel_id=1, source_target_pairs={{0,1},{1,2},{2,3},{3,4},{4,5},{5,6},{6,7},{7,0},{8,9},{9,10},{10,1... | collective-permute-start | bytes 196616 | tf_op jit(solution)/shard_map/ppermute | solution.py:168
  14.1 1.7 fusion.22
  16.4 0.8 copy.24
  21.1 0.8 select_convert_fusion
  22.5 1.6 convert_element_type.40
  24.2 0.8 broadcast_select_fusion.1
  25.0 1.1 pad_maximum_fusion.3.bottom_ref
  26.1 1.0 pad_maximum_fusion.2.top_ref
  28.4 20.2 %shard_map.106 = (f32[128,128,128]{2,1,0:T(8,128)}, f32[8,16384]{1,0:T(8,128)S(1)}) custom-call(f32[128,128,128]{2,1,0:T(8,128)} %state_ref.1, f32[16,128,128]{2,1,0:T(8,128)} %pad_maximum_fusion.2.top_ref, f32[16,128,128]{2,1,0:T(8,128)} %pad_maximum_fusion.3.bottom_ref, f32[128,1,128]{2,1,0:T(1,128)} %copy-done.8, f32[128,1,128]{2,1,0:T(1,128)} %copy-done.9, ...), custom_call_target="tpu_custom_call" | custom-call | flops 1610612736 | bytes 16777216 | tf_op jit(solution)/shard_map/pallas_call | solution.py:112
  48.6 1.0 fusion.19
  49.6 1.3 fusion.20
  50.9 2.2 %collective-permute-start.4 = (f32[1,128,128]{2,1,0:T(8,128)S(1)}, f32[1,128,128]{2,1,0:T(8,128)S(1)}, u32[]{:S(2)}, u32[]{:S(2)}) collective-permute-start(f32[1,128,128]{2,1,0:T(8,128)S(1)} %get-tuple-element.148), channel_id=1, source_target_pairs={{0,8},{8,16},{16,24},{24,32},{32,40},{40,48},{48,56},{56,64},{64,7... | collective-permute-start | bytes 196616 | tf_op jit(solution)/shard_map/ppermute | solution.py:159
  53.1 5.2 %collective-permute-start.5 = (f32[1,128,128]{2,1,0:T(8,128)S(1)}, f32[1,128,128]{2,1,0:T(8,128)S(1)}, u32[]{:S(2)}, u32[]{:S(2)}) collective-permute-start(f32[1,128,128]{2,1,0:T(8,128)S(1)} %get-tuple-element.147), channel_id=1, source_target_pairs={{8,0},{16,8},{24,16},{32,24},{40,32},{48,40},{56,48},{64,56},{72,6... | collective-permute-start | bytes 196616 | tf_op jit(solution)/shard_map/ppermute | solution.py:160
  58.3 2.3 %collective-permute-start.6 = (f32[128,1,128]{2,1,0:T(1,128)S(1)}, f32[128,1,128]{2,1,0:T(1,128)S(1)}, u32[]{:S(2)}, u32[]{:S(2)}) collective-permute-start(f32[128,1,128]{2,1,0:T(1,128)S(1)} %get-tuple-element.150), channel_id=1, source_target_pairs={{0,1},{1,2},{2,3},{3,4},{4,5},{5,6},{6,7},{7,0},{8,9},{9,10},{10,1... | collective-permute-start | bytes 196616 | tf_op jit(solution)/shard_map/ppermute | solution.py:168
  62.0 2.7 %collective-permute-done.7 = f32[128,1,128]{2,1,0:T(1,128)S(1)} collective-permute-done((f32[128,1,128]{2,1,0:T(1,128)S(1)}, f32[128,1,128]{2,1,0:T(1,128)S(1)}, u32[]{:S(2)}, u32[]{:S(2)}) %collective-permute-start.7) | collective-permute-done | bytes 65568 | tf_op jit(solution)/shard_map/ppermute | solution.py:169
  65.3 1.2 convolution_convert_fusion
  66.5 56.5 %shard_map.107 = bf16[24,32,1152]{2,1,0:T(8,128)(2,1)S(1)} custom-call(bf16[8,32,1152]{2,1,0:T(8,128)(2,1)} %bitcast.63), custom_call_target="tpu_custom_call" | custom-call | tf_op jit(solution)/shard_map/pallas_call | solution.py:238
  123.0 26.2 %conditional.4 = (f32[8,128,128]{2,0,1:T(8,128)S(1)}, f32[24,32,128]{2,1,0:T(8,128)S(1)}, f32[128,128]{1,0:T(8,128)S(1)}) conditional(s32[]{:T(128)} %convert_element_type.36, f32[128,128]{1,0:T(8,128)S(1)} %bitcast.59, (bf16[24,32,1152]{2,1,0:T(8,128)(2,1)S(1)}, bf16[32,128,128]{2,1,0:T(8,128)(2,1)}, f32[8,128]{1,0:T(8,128)S(1)}, ...), branch_computations={%region_4.5_spmd, %region_5.7_spmd} | conditional | flops 2953967360 | bytes 37537000 | solution.py:536
  125.4 15.6 %branch_1_fun.1 = f32[1024,128]{1,0:T(8,128)S(1)} custom-call(s32[768]{0:T(1024)S(1)} %get-tuple-element.138.labels_ref, f32[768,8,128]{2,1,0:T(8,128)S(1)} %bitcast.49, bf16[32,128,128]{2,1,0:T(8,128)(2,1)S(1)} %copy-done.6), custom_call_target="tpu_custom_call" | custom-call | flops 2147483648 | bytes 4194304 | tf_op jit(solution)/shard_map/cond/branch_1_fun/pallas_call | solution.py:414
  141.3 1.1 slice.51
  142.4 3.5 %fusion.3 = f32[128,32,128]{2,0,1:T(8,128)S(1)} fusion(f32[32,128,128]{2,1,0:T(8,128)} %get-tuple-element.55, f32[128,128]{1,0:T(8,128)S(1)} %add_select_fusion), kind=kOutput, calls=%fused_computation.14 | convolution fusion | flops 805306368 | bytes 4259840 | tf_op jit(solution)/shard_map/cond/branch_1_fun/db,wab->wda/dot_general | solution.py:525
  146.0 1.6 gather_fusion
  147.6 1.4 and_reduce_fusion
  149.2 5.3 %shard_map.108 = f32[8,32,128]{2,1,0:T(8,128)} custom-call(f32[24,32,128]{2,1,0:T(8,128)S(1)} %get-tuple-element.72.surface_ref), custom_call_target="tpu_custom_call" | custom-call | tf_op jit(solution)/shard_map/pallas_call | solution.py:309
  154.5 0.9 broadcast_in_dim.130.sea_ref
  155.4 16.8 %shard_map.109 = f32[128,128,128]{2,1,0:T(8,128)} custom-call(s32[1]{0:T(128)} %bitcast.11.flag_ref, f32[128,128,128]{2,1,0:T(8,128)} %get-tuple-element.73.first_ref, f32[128,128,128]{2,1,0:T(8,128)} %state_ref.1, s32[8,16384]{1,0:T(8,128)} %broadcast_in_dim.130.sea_ref, f32[8,16384]{1,0:T(8,128)S(1)} %bitcast.57, f32[8,128]{1,0:T(8,128)} %spread_ref.1), custom_call_target="tpu_custom_call" | custom-call | flops 134217728 | bytes 25165824 | tf_op jit(solution)/shard_map/pallas_call | solution.py:362
  172.3 0.9 copy-done.1
  173.2 0.9 gather_fusion.1
  (79 shorter events, 12.2 us)
Async XLA Ops:
  2.2 22.0 %collective-permute-start.1 = (f32[1,128,128]{2,1,0:T(8,128)}, f32[1,128,128]{2,1,0:T(8,128)}, u32[]{:S(2)}, u32[]{:S(2)}) collective-permute-start(f32[1,128,128]{2,1,0:T(8,128)} %get-tuple-element.155), channel_id=1, source_target_pairs={{8,0},{16,8},{24,16},{32,24},{40,32},{48,40},{56,48},{64,56},{72,6... | collective-permute-start | bytes 196616 | tf_op jit(solution)/shard_map/ppermute | solution.py:160
  8.0 8.4 %copy-start.11 = (s32[128,128]{1,0:T(8,128)S(1)}, s32[128,128]{1,0:T(8,128)}, u32[]{:S(2)}) copy-start(s32[128,128]{1,0:T(8,128)} %param.16) | copy-start | bytes 196612
  8.0 18.1 %collective-permute-start = (f32[1,128,128]{2,1,0:T(8,128)}, f32[1,128,128]{2,1,0:T(8,128)}, u32[]{:S(2)}, u32[]{:S(2)}) collective-permute-start(f32[1,128,128]{2,1,0:T(8,128)} %get-tuple-element.156), channel_id=1, source_target_pairs={{0,8},{8,16},{16,24},{24,32},{32,40},{40,48},{48,56},{56,64},{64,7... | collective-permute-start | bytes 196616 | tf_op jit(solution)/shard_map/ppermute | solution.py:159
  12.0 15.1 %collective-permute-start.2 = (f32[128,1,128]{2,1,0:T(1,128)}, f32[128,1,128]{2,1,0:T(1,128)S(1)}, u32[]{:S(2)}, u32[]{:S(2)}) collective-permute-start(f32[128,1,128]{2,1,0:T(1,128)} %get-tuple-element.152), channel_id=1, source_target_pairs={{0,1},{1,2},{2,3},{3,4},{4,5},{5,6},{6,7},{7,0},{8,9},{9,10},{10,1... | collective-permute-start | bytes 196616 | tf_op jit(solution)/shard_map/ppermute | solution.py:168
  14.1 13.1 %collective-permute-start.3 = (f32[128,1,128]{2,1,0:T(1,128)}, f32[128,1,128]{2,1,0:T(1,128)S(1)}, u32[]{:S(2)}, u32[]{:S(2)}) collective-permute-start(f32[128,1,128]{2,1,0:T(1,128)} %get-tuple-element.151), channel_id=1, source_target_pairs={{1,0},{2,1},{3,2},{4,3},{5,4},{6,5},{7,6},{0,7},{9,8},{10,9},{11,1... | collective-permute-start | bytes 196616 | tf_op jit(solution)/shard_map/ppermute | solution.py:169
  14.1 6.4 %copy-start.7 = (f32[128,128]{1,0:T(8,128)S(1)}, f32[128,128]{1,0:T(8,128)}, u32[]{:S(2)}) copy-start(f32[128,128]{1,0:T(8,128)} %param.18) | copy-start | bytes 196612
  14.1 6.4 %copy-start.10 = (f32[128,128]{1,0:T(8,128)S(1)}, f32[128,128]{1,0:T(8,128)}, u32[]{:S(2)}) copy-start(f32[128,128]{1,0:T(8,128)} %param.19) | copy-start | bytes 196612
  14.1 8.4 %copy-start.5 = (bf16[32,128,128]{2,1,0:T(8,128)(2,1)S(1)}, bf16[32,128,128]{2,1,0:T(8,128)(2,1)}, u32[]{:S(2)}) copy-start(bf16[32,128,128]{2,1,0:T(8,128)(2,1)} %param.22) | copy-start | bytes 3145732
  19.7 6.3 %copy-start.15 = (s32[256]{0:T(256)}, s32[256]{0:T(256)S(1)}, u32[]{:S(2)}) copy-start(s32[256]{0:T(256)S(1)} %multiply_add_fusion) | copy-start | bytes 3076
  27.1 33.6 %copy-start.18 = (s32[256,1]{0,1:T(1,128)S(1)}, s32[256,1]{0,1:T(1,128)}, u32[]{:S(2)}) copy-start(s32[256,1]{0,1:T(1,128)} %compare_select_fusion.2) | copy-start | bytes 3076
  27.1 37.5 %copy-start.17 = (f32[128,8]{0,1:T(8,128)S(1)}, f32[128,8]{0,1:T(8,128)}, u32[]{:S(2)}) copy-start(f32[128,8]{0,1:T(8,128)} %param.20) | copy-start | bytes 12292
  27.1 0.6 copy-start.8
  27.8 0.6 copy-start.9
  48.6 16.1 %copy-start.13 = (f32[8,16384]{1,0:T(8,128)}, f32[8,16384]{1,0:T(8,128)S(1)}, u32[]{:S(2)}) copy-start(f32[8,16384]{1,0:T(8,128)S(1)} %get-tuple-element.69) | copy-start | bytes 1572868
  50.9 10.5 %collective-permute-start.4 = (f32[1,128,128]{2,1,0:T(8,128)S(1)}, f32[1,128,128]{2,1,0:T(8,128)S(1)}, u32[]{:S(2)}, u32[]{:S(2)}) collective-permute-start(f32[1,128,128]{2,1,0:T(8,128)S(1)} %get-tuple-element.148), channel_id=1, source_target_pairs={{0,8},{8,16},{16,24},{24,32},{32,40},{40,48},{48,56},{56,64},{64,7... | collective-permute-start | bytes 196616 | tf_op jit(solution)/shard_map/ppermute | solution.py:159
  53.1 8.3 %collective-permute-start.5 = (f32[1,128,128]{2,1,0:T(8,128)S(1)}, f32[1,128,128]{2,1,0:T(8,128)S(1)}, u32[]{:S(2)}, u32[]{:S(2)}) collective-permute-start(f32[1,128,128]{2,1,0:T(8,128)S(1)} %get-tuple-element.147), channel_id=1, source_target_pairs={{8,0},{16,8},{24,16},{32,24},{40,32},{48,40},{56,48},{64,56},{72,6... | collective-permute-start | bytes 196616 | tf_op jit(solution)/shard_map/ppermute | solution.py:160
  58.3 3.6 %collective-permute-start.6 = (f32[128,1,128]{2,1,0:T(1,128)S(1)}, f32[128,1,128]{2,1,0:T(1,128)S(1)}, u32[]{:S(2)}, u32[]{:S(2)}) collective-permute-start(f32[128,1,128]{2,1,0:T(1,128)S(1)} %get-tuple-element.150), channel_id=1, source_target_pairs={{0,1},{1,2},{2,3},{3,4},{4,5},{5,6},{6,7},{7,0},{8,9},{9,10},{10,1... | collective-permute-start | bytes 196616 | tf_op jit(solution)/shard_map/ppermute | solution.py:168
  60.6 4.0 %collective-permute-start.7 = (f32[128,1,128]{2,1,0:T(1,128)S(1)}, f32[128,1,128]{2,1,0:T(1,128)S(1)}, u32[]{:S(2)}, u32[]{:S(2)}) collective-permute-start(f32[128,1,128]{2,1,0:T(1,128)S(1)} %get-tuple-element.149), channel_id=1, source_target_pairs={{1,0},{2,1},{3,2},{4,3},{5,4},{6,5},{7,6},{0,7},{9,8},{10,9},{11,1... | collective-permute-start | bytes 196616 | tf_op jit(solution)/shard_map/ppermute | solution.py:169
  64.7 0.6 copy-start.16
  64.9 58.0 %copy-start.14 = (f32[8,128]{1,0:T(8,128)S(1)}, f32[8,128]{1,0:T(8,128)}, u32[]{:S(2)}) copy-start(f32[8,128]{1,0:T(8,128)} %spread_ref.1) | copy-start | bytes 12292
  123.0 1.2 copy-start.2
  124.2 1.2 copy-start.6
  141.0 5.0 %copy-start.3 = (f32[1024,128]{1,0:T(8,128)}, f32[1024,128]{1,0:T(8,128)S(1)}, u32[]{:S(2)}) copy-start(f32[1024,128]{1,0:T(8,128)S(1)} %branch_1_fun.1) | copy-start | bytes 1572868 | tf_op jit(solution)/shard_map/cond
  146.0 3.2 %copy-start.4 = (f32[1024,128]{1,0:T(8,128)S(1)}, f32[1024,128]{1,0:T(8,128)}, u32[]{:S(2)}) copy-start(f32[1024,128]{1,0:T(8,128)} %copy-done.3) | copy-start | bytes 1572868 | tf_op jit(solution)/shard_map/cond
  172.3 0.9 copy-start.1
  172.3 1.8 %copy-start.12 = (pred[128,2]{1,0:T(8,128)(4,1)S(1)}, pred[128,2]{1,0:T(8,128)(4,1)}, u32[]{:S(2)}) copy-start(pred[128,2]{1,0:T(8,128)(4,1)} %compare_and_fusion) | copy-start | bytes 772

commit v11 on v10

--- a/solution.py
+++ b/solution.py
@@ -152,24 +152,6 @@
     )
 
 
-def edge_rows(values, lower_valid, upper_valid):
-    bands = lax.axis_size("comp") * lax.axis_size("lat")
-    up = [(i, i + 1) for i in range(bands - 1)]
-    down = [(j, i) for i, j in up]
-    before = lax.ppermute(values[-1:], ("comp", "lat"), up)
-    after = lax.ppermute(values[:1], ("comp", "lat"), down)
-    return (jnp.where(lower_valid, before, 0.0), jnp.where(upper_valid, after, 0.0))
-
-
-def edge_columns(values):
-    size = lax.axis_size("lon")
-    up = [(i, (i + 1) % size) for i in range(size)]
-    down = [(j, i) for i, j in up]
-    before = lax.ppermute(values[:, -1:], "lon", up)
-    after = lax.ppermute(values[:, :1], "lon", down)
-    return before, after
-
-
 MESH_IDS = pl.DeviceIdType.MESH
 
 
@@ -430,6 +412,71 @@
     )(labels, fluxes, weights)
 
 
+def halo_kernel(shape, values_ref, rows_out, cols_out, rows_land, cols_land, send_sems, recv_sems):
+    comp_total, lat_total, lon_total = shape
+    bands = comp_total * lat_total
+    band = lax.axis_index("comp") * lat_total + lax.axis_index("lat")
+    lon = lax.axis_index("lon")
+    rows, cols, _ = values_ref.shape
+    up = (band + 1) % bands
+    down = (band + bands - 1) % bands
+    up_device = (up // lat_total, up % lat_total, lon)
+    down_device = (down // lat_total, down % lat_total, lon)
+    east_device = (band // lat_total, band % lat_total, (lon + 1) % lon_total)
+    west_device = (band // lat_total, band % lat_total, (lon + lon_total - 1) % lon_total)
+    barrier = pltpu.get_barrier_semaphore()
+    for device in (up_device, down_device, east_device, west_device):
+        pl.semaphore_signal(barrier, 1, device_id=device, device_id_type=MESH_IDS)
+    pl.semaphore_wait(barrier, 4)
+    plan = [
+        (values_ref.at[pl.ds(rows - 1, 1)], rows_land.at[0], up_device),
+        (values_ref.at[pl.ds(0, 1)], rows_land.at[1], down_device),
+        (values_ref.at[:, pl.ds(cols - 1, 1)], cols_land.at[0], east_device),
+        (values_ref.at[:, pl.ds(0, 1)], cols_land.at[1], west_device),
+    ]
+    copies = []
+    for slot, (source, target, device) in enumerate(plan):
+        copy = pltpu.make_async_remote_copy(
+            src_ref=source,
+            dst_ref=target,
+            send_sem=send_sems.at[slot],
+            recv_sem=recv_sems.at[slot],
+            device_id=device,
+            device_id_type=MESH_IDS,
+        )
+        copy.start()
+        copies.append(copy)
+    for copy in copies:
+        copy.wait_send()
+    for copy in copies:
+        copy.wait_recv()
+    rows_out[...] = rows_land[...]
+    cols_out[...] = cols_land[...]
+
+
+def halo_edges(values, shape, collective):
+    rows, cols, levels = values.shape
+    return pl.pallas_call(
+        functools.partial(halo_kernel, tuple(shape)),
+        out_shape=(
+            jax.ShapeDtypeStruct((2, 1, cols, levels), values.dtype),
+            jax.ShapeDtypeStruct((2, rows, 1, levels), values.dtype),
+        ),
+        in_specs=[pl.BlockSpec(memory_space=pl.ANY)],
+        out_specs=(
+            pl.BlockSpec(memory_space=pltpu.VMEM),
+            pl.BlockSpec(memory_space=pltpu.VMEM),
+        ),
+        scratch_shapes=[
+            pltpu.VMEM((2, 1, cols, levels), values.dtype),
+            pltpu.VMEM((2, rows, 1, levels), values.dtype),
+            pltpu.SemaphoreType.DMA((4,)),
+            pltpu.SemaphoreType.DMA((4,)),
+        ],
+        compiler_params=pltpu.CompilerParams(collective_id=collective, has_side_effects=True),
+    )(values)
+
+
 def local(
     state, land_mask, intersection_list, mix_atm, mix_ocn, flux_map, ocean_map, regrid_weights
 ):
@@ -456,14 +503,20 @@
     )
     sea_cells = land_mask == 1
 
-    top, bottom = edge_rows(state, lower_valid, upper_valid)
-    west, east = edge_columns(state)
+    mesh_shape = (comp_count, lat_count, lon_count)
+
+    def halos(values, collective):
+        rows, cols = halo_edges(values, mesh_shape, collective)
+        top = jnp.where(lower_valid, rows[0], 0.0)
+        bottom = jnp.where(upper_valid, rows[1], 0.0)
+        return top, bottom, cols[0], cols[1]
+
+    top, bottom, west, east = halos(state, 2)
     mixing = jnp.where(ocean_side, mix_ocn, mix_atm)
     first, first_planes = substep(state, top, bottom, west, east, mixing, comp_count)
     first_top = first_planes[0].reshape(tile_rows, block_len)
     state_top = first_planes[1].reshape(tile_rows, block_len)
-    top, bottom = edge_rows(first, lower_valid, upper_valid)
-    west, east = edge_columns(first)
+    top, bottom, west, east = halos(first, 3)
 
     def atmosphere_second(values, top, bottom, west, east):
         moved, total = substep(values, top, bottom, west, east, mix_atm, comp_count, flux_map.T)
@@ -506,7 +559,6 @@
         axis=1,
     )
     packed, _, entry_slots = pack_rows(entry_blocks, neighbour_ids, labels, sending, capacity, neighbour_count)
-    mesh_shape = (comp_count, lat_count, lon_count)
     arrived = gather_to_ocean(packed, offsets, mesh_shape)
     weights_low = regrid_weights
     weights_wide = regrid_weights.astype(jnp.float32)

time: 177 us -> 161 us (0.910)
  the two profiles are of different devices: /device:TPU:25 before, /device:TPU:1 now
where the time goes in v11:
time: 161 us; the launch traced here: 160 us
  Pallas kernels  129 us (80%)
  local copies, waits for them, and re-layouts  19.4 us (12%)
  other arithmetic  9.85 us (6%)
    pallas_call x2, Pallas kernels, substep(): pl.pallas_call(functools.partial(substep_kernel, with_flux, comp_total),...  34.7 us
    pallas_call x1, Pallas kernels, spread_from_ocean(): pl.pallas_call(functools.partial(spread_kernel, tuple(offsets), tuple(sha...  32.8 us
    pallas_call x2, Pallas kernels, halo_edges(): pl.pallas_call(functools.partial(halo_kernel, tuple(shape)), out_shape=(j...  25 us
    pallas_call x1, Pallas kernels, gather_to_ocean(): pl.pallas_call(functools.partial(gather_kernel, tuple(offsets), tuple(sha...  24 us
    pallas_call x1, Pallas kernels, ocean_update(): pl.pallas_call(ocean_update_kernel, grid_spec=pltpu.PrefetchScalarGridSpe...  12 us
    cond x4, local copies, waits for them, and re-layouts  12 us

profile of v11, /device:TPU:1, one launch (start us, length us, event | category | flops | bytes accessed | tf_op | source)
XLA Modules:
  0.0 160.0 jit_solution(13591199336886164431)
XLA Ops:
  0.7 12.5 %shard_map.106 = (f32[2,1,128,128]{3,2,1,0:T(8,128)}, f32[2,128,1,128]{3,2,1,0:T(1,128)}) custom-call(f32[128,128,128]{2,1,0:T(8,128)} %state_ref.1), custom_call_target="tpu_custom_call" | custom-call | tf_op jit(solution)/shard_map/pallas_call | solution.py:459
  13.1 0.9 select_bitcast_fusion
  14.0 1.6 %fusion.20 = (f32[15,128,128]{2,1,0:T(8,128)S(1)}, f32[15,128,128]{2,1,0:T(8,128)S(1)}) fusion(f32[128,128,128]{2,1,0:T(8,128)} %state_ref.1), kind=kLoop, calls=%fused_computation.62 | loop fusion | bytes 3932160 | tf_op jit(solution)/shard_map/slice | solution.py:88
  15.7 1.5 pad_maximum_fusion.2
  17.2 0.6 broadcast_select_fusion.1.mix_ref
  17.8 0.6 fusion.21
  18.4 15.7 %shard_map.107 = (f32[128,128,128]{2,1,0:T(8,128)}, f32[8,16384]{1,0:T(8,128)}) custom-call(f32[128,128,128]{2,1,0:T(8,128)} %state_ref.1, f32[16,128,128]{2,1,0:T(8,128)} %get-tuple-element.216.top_ref, f32[16,128,128]{2,1,0:T(8,128)} %get-tuple-element.217.bottom_ref, f32[128,1,128]{2,1,0:T(1,128)} %bitcast.86, f32[128,1,128]{2,1,0:T(1,128)} %bitcast.85, ...), custom_call_target="tpu_custom_call" | custom-call | flops 1610612736 | bytes 16777216 | tf_op jit(solution)/shard_map/pallas_call | solution.py:112
  34.1 12.5 %shard_map.108 = (f32[2,1,128,128]{3,2,1,0:T(8,128)S(1)}, f32[2,128,1,128]{3,2,1,0:T(1,128)S(1)}) custom-call(f32[128,128,128]{2,1,0:T(8,128)} %get-tuple-element.114.values_ref), custom_call_target="tpu_custom_call" | custom-call | tf_op jit(solution)/shard_map/pallas_call | solution.py:459
  46.8 30.0 %conditional.3 = (f32[128,128,128]{2,1,0:T(8,128)}, bf16[8,128,128]{2,0,1:T(8,128)(2,1)S(1)}) conditional(s32[]{:T(128)} %convert_element_type.36, (f32[128,128,128]{2,1,0:T(8,128)}, pred[1,1,128,128]{3,2,1,0:T(8,128)(4,1)S(1)}, pred[1,1,128,128]{3,2,1,0:T(8,128)(4,1)S(1)}, f32[128,8]{0,1:T(8,128)S(1)}, f32[2,128,1,128]{3,2,1,0:T(1,128)S(1)}, ...), branch_computations={%region_0.1_spmd.clone, %region_1.2_spmd} | conditional | flops 1712226304 | bytes 76660784 | solution.py:530
  46.8 3.4 %copy.60.x_ref = f32[128,128,128]{2,1,0:T(8,128)S(1)} copy(f32[128,128,128]{2,1,0:T(8,128)} %get-tuple-element.100) | data formatting | bytes 16777216 | tf_op jit(solution)/shard_map/cond
  50.2 3.4 %copy-done = f32[128,128,128]{2,1,0:T(8,128)} copy-done((f32[128,128,128]{2,1,0:T(8,128)}, f32[128,128,128]{2,1,0:T(8,128)S(1)}, u32[]{:S(2)}) %copy-start) | copy-done | bytes 8388632 | tf_op jit(solution)/shard_map/cond
  53.6 0.2 fusion.19
  53.8 1.5 pad_maximum_fusion
  55.3 0.6 slice.95
  56.0 0.6 slice.96
  56.6 19.0 %branch_0_fun.1 = (f32[128,128,128]{2,1,0:T(8,128)}, f32[8,16384]{1,0:T(8,128)}) custom-call(f32[128,128,128]{2,1,0:T(8,128)} %copy-done, f32[16,128,128]{2,1,0:T(8,128)} %get-tuple-element.205.top_ref, f32[16,128,128]{2,1,0:T(8,128)} %get-tuple-element.206.bottom_ref, f32[128,1,128]{2,1,0:T(1,128)} %bitcast.83, f32[128,1,128]{2,1,0:T(1,128)} %bitcast.84, ...), custom_call_target="tpu_custom_call" | custom-call | flops 1711276032 | bytes 16777216 | tf_op jit(solution)/shard_map/cond/branch_0_fun/pallas_call | solution.py:112
  75.6 1.1 fusion
  77.0 0.1 copy.40
  77.1 0.2 reshape.179
  77.5 0.2 convert_reduce_fusion
  77.8 1.2 convolution_convert_fusion
  79.0 24.0 %shard_map.109 = bf16[24,32,1152]{2,1,0:T(8,128)(2,1)S(1)} custom-call(bf16[8,32,1152]{2,1,0:T(8,128)(2,1)} %bitcast.79), custom_call_target="tpu_custom_call" | custom-call | tf_op jit(solution)/shard_map/pallas_call | solution.py:220
  103.1 1.2 slice.77
  104.3 2.8 %convert_element_type.40 = f32[32,128,128]{2,1,0:T(8,128)} convert(bf16[32,128,128]{2,1,0:T(8,128)(2,1)} %param.22) | non-fusion elementwise | flops 524288 | bytes 3145728 | tf_op jit(solution)/shard_map/convert_element_type | solution.py:564
  107.1 32.8 %shard_map.110 = f32[8,32,128]{2,1,0:T(8,128)} custom-call(f32[24,32,128]{2,1,0:T(8,128)S(1)} %get-tuple-element.80.surface_ref), custom_call_target="tpu_custom_call" | custom-call | tf_op jit(solution)/shard_map/pallas_call | solution.py:291
  139.9 0.9 broadcast_in_dim.130.sea_ref
  140.8 12.0 %shard_map.111 = f32[128,128,128]{2,1,0:T(8,128)} custom-call(s32[1]{0:T(128)} %bitcast.11.flag_ref, f32[128,128,128]{2,1,0:T(8,128)} %get-tuple-element.81.first_ref, f32[128,128,128]{2,1,0:T(8,128)} %state_ref.1, s32[8,16384]{1,0:T(8,128)} %broadcast_in_dim.130.sea_ref, f32[8,16384]{1,0:T(8,128)S(1)} %bitcast.73, f32[8,128]{1,0:T(8,128)} %spread_ref.1), custom_call_target="tpu_custom_call" | custom-call | flops 134217728 | bytes 25165824 | tf_op jit(solution)/shard_map/pallas_call | solution.py:344
  152.9 5.3 %conditional.5 = (f32[128,128]{1,0:T(8,128)S(1)}) conditional(s32[]{:T(128)} %convert_element_type.36, f32[128,128,128]{2,1,0:T(8,128)} %shard_map.111, f32[128,128]{1,0:T(8,128)S(1)} %get-tuple-element.83), branch_computations={%region_8.9_spmd, %region_9.10_spmd} | conditional | bytes 131080 | solution.py:608
  152.9 5.3 %copy.42 = f32[128,128,1]{1,0,2:T(8,128)S(1)} copy(f32[128,128,1]{2,1,0:T(8,128)} %bitcast.66) | data formatting | bytes 131072 | tf_op jit(solution)/shard_map/cond
  158.2 0.7 gather_fusion.1
  159.1 0.2 select_reduce_fusion
  159.3 0.6 select_select_fusion
  (44 shorter events, 1.0 us)
Async XLA Ops:
  15.7 1.5 copy-start.6
  15.7 1.5 copy-start.8
  15.7 2.1 %copy-start.7 = (f32[2,128,1,128]{3,2,1,0:T(1,128)S(1)}, f32[2,128,1,128]{3,2,1,0:T(1,128)}, u32[]{:S(2)}) copy-start(f32[2,128,1,128]{3,2,1,0:T(1,128)} %get-tuple-element.72) | copy-start | bytes 393220
  34.1 12.6 %copy-start.9 = (s32[128,128]{1,0:T(8,128)S(1)}, s32[128,128]{1,0:T(8,128)}, u32[]{:S(2)}) copy-start(s32[128,128]{1,0:T(8,128)} %param.16) | copy-start | bytes 196612
  34.1 12.6 %copy-start.13 = (f32[128,8]{0,1:T(8,128)S(1)}, f32[128,8]{0,1:T(8,128)}, u32[]{:S(2)}) copy-start(f32[128,8]{0,1:T(8,128)} %param.20) | copy-start | bytes 12292
  46.8 30.2 %copy-start.14 = (s32[128,1,2,3]{0,2,3,1:T(2,128)S(1)}, s32[128,1,2,3]{0,2,3,1:T(2,128)}, u32[]{:S(2)}) copy-start(s32[128,1,2,3]{0,2,3,1:T(2,128)} %param.17) | copy-start | bytes 9220
  50.2 3.4 %copy-start = (f32[128,128,128]{2,1,0:T(8,128)}, f32[128,128,128]{2,1,0:T(8,128)S(1)}, u32[]{:S(2)}) copy-start(f32[128,128,128]{2,1,0:T(8,128)S(1)} %copy.60.x_ref) | copy-start | bytes 25165828 | tf_op jit(solution)/shard_map/cond
  76.7 0.7 copy-start.15
  77.7 1.3 copy-start.11
  103.1 4.0 %copy-start.5 = (bf16[32,128,128]{2,1,0:T(8,128)(2,1)S(1)}, bf16[32,128,128]{2,1,0:T(8,128)(2,1)}, u32[]{:S(2)}) copy-start(bf16[32,128,128]{2,1,0:T(8,128)(2,1)} %param.22) | copy-start | bytes 3145732
  103.1 4.0 %copy-start.10 = (f32[8,128]{1,0:T(8,128)S(1)}, f32[8,128]{1,0:T(8,128)}, u32[]{:S(2)}) copy-start(f32[8,128]{1,0:T(8,128)} %spread_ref.1) | copy-start | bytes 12292
  152.9 5.3 %copy-start.12 = (s32[256]{0:T(256)S(1)}, s32[256]{0:T(256)}, u32[]{:S(2)}) copy-start(s32[256]{0:T(256)} %copy-done.11) | copy-start | bytes 3076
  152.9 5.3 %copy-start.1 = (f32[8,32,128]{2,1,0:T(8,128)S(1)}, f32[8,32,128]{2,1,0:T(8,128)}, u32[]{:S(2)}) copy-start(f32[8,32,128]{2,1,0:T(8,128)} %shard_map.110) | copy-start | bytes 393220

commit v12 on v11

--- a/solution.py
+++ b/solution.py
@@ -302,7 +302,9 @@
     )(replies)
 
 
-def ocean_update_kernel(flag_ref, first_ref, state_ref, sea_ref, forcing_ref, spread_ref, out_ref):
+def ocean_update_kernel(
+    flag_ref, first_ref, moved_ref, state_ref, sea_ref, forcing_ref, spread_ref, out_ref
+):
     ocean = flag_ref[0] == 1
 
     @pl.when(ocean)
@@ -311,7 +313,7 @@
 
     @pl.when(jnp.logical_not(ocean))
     def _():
-        out_ref[...] = first_ref[...]
+        out_ref[...] = moved_ref[...]
 
 
 def ocean_block(first_ref, state_ref, sea_ref, forcing_ref, spread_ref, out_ref):
@@ -336,7 +338,7 @@
     out_ref[...] = kept.reshape(rows, cols, levels)
 
 
-def ocean_update(first, state, sea_rows, forcing, ocean_map, comp_total):
+def ocean_update(first, moved, state, sea_rows, forcing, ocean_map, comp_total):
     rows, cols, levels = first.shape
     flux_count = forcing.shape[0]
     cells = rows * cols
@@ -347,7 +349,8 @@
             num_scalar_prefetch=1,
             grid=(rows // ROW_BLOCK,),
             in_specs=[
-                pl.BlockSpec((ROW_BLOCK, cols, levels), lambda i, f: (i, 0, 0)),
+                pl.BlockSpec((ROW_BLOCK, cols, levels), lambda i, f: (i * f[0], 0, 0)),
+                pl.BlockSpec((ROW_BLOCK, cols, levels), lambda i, f: (i * (1 - f[0]), 0, 0)),
                 pl.BlockSpec((ROW_BLOCK, cols, levels), lambda i, f: (i * f[0], 0, 0)),
                 pl.BlockSpec((8, ROW_BLOCK * cols), lambda i, f: (0, i * f[0])),
                 pl.BlockSpec((flux_count, ROW_BLOCK * cols), lambda i, f: (0, i * f[0])),
@@ -359,7 +362,7 @@
         cost_estimate=pl.CostEstimate(
             flops=8 * cells * levels * flux_count, transcendentals=0, bytes_accessed=12 * cells * levels
         ),
-    )(flag, first, state, sea_rows, forcing, ocean_map)
+    )(flag, first, moved, state, sea_rows, forcing, ocean_map)
 
 
 def scatter_regrid_kernel(labels_ref, fluxes_ref, weights_ref, out_ref, binned_ref):
@@ -518,18 +521,9 @@
     state_top = first_planes[1].reshape(tile_rows, block_len)
     top, bottom, west, east = halos(first, 3)
 
-    def atmosphere_second(values, top, bottom, west, east):
-        moved, total = substep(values, top, bottom, west, east, mix_atm, comp_count, flux_map.T)
-        total = total.reshape(flux_count, tile_rows, block_len)
-        sent = jnp.where(sea_cells[None], 0.5 * total, 0.0).astype(jnp.bfloat16)
-        return moved, sent
-
-    def ocean_second(values, top, bottom, west, east):
-        return values, jnp.zeros((flux_count, tile_rows, block_len), jnp.bfloat16)
-
-    second, flux_sent = lax.cond(
-        ocean_side, ocean_second, atmosphere_second, first, top, bottom, west, east
-    )
+    second, total = substep(first, top, bottom, west, east, mix_atm, comp_count, flux_map.T)
+    total = total.reshape(flux_count, tile_rows, block_len)
+    flux_sent = jnp.where(sea_cells[None], 0.5 * total, 0.0).astype(jnp.bfloat16)
     entry_list = intersection_list.reshape(tile_rows * intersections, 3)
     owners = entry_list[:, 0]
     targets = entry_list[:, 1]
@@ -593,11 +587,12 @@
         answers.reshape(neighbour_count * capacity, block_len), entry_slots, axis=0
     )
     returned = per_entry.reshape(tile_rows, intersections, block_len).sum(axis=1)
-    second, forcing, answers = lax.optimization_barrier((second, forcing, answers))
+    first, second, forcing, answers = lax.optimization_barrier((first, second, forcing, answers))
     sea_rows = jnp.broadcast_to(
         sea_cells.astype(jnp.int32).reshape(1, tile_rows * block_len), (8, tile_rows * block_len)
     )
     final_state = ocean_update(
+        first,
         second,
         state,
         sea_rows,

time: 161 us -> 168 us (1.043)
  the two profiles are of different devices: /device:TPU:1 before, /device:TPU:25 now
where the time goes in v12:
time: 168 us; the launch traced here: 165 us
  Pallas kernels  133 us (79%)
  other arithmetic  13.9 us (8%)
  local copies, waits for them, and re-layouts  12.1 us (7%)
  matrix products  4.65 us (3%)
    pallas_call x2, Pallas kernels, substep(): pl.pallas_call(functools.partial(substep_kernel, with_flux, comp_total),...  39.2 us
    pallas_call x1, Pallas kernels, gather_to_ocean(): pl.pallas_call(functools.partial(gather_kernel, tuple(offsets), tuple(sha...  38.5 us
    pallas_call x1, Pallas kernels, ocean_update(): pl.pallas_call(ocean_update_kernel, grid_spec=pltpu.PrefetchScalarGridSpe...  17 us
    pallas_call x2, Pallas kernels, halo_edges(): pl.pallas_call(functools.partial(halo_kernel, tuple(shape)), out_shape=(j...  15.7 us
    pallas_call x1, Pallas kernels, scatter_regrid(): pl.pallas_call(scatter_regrid_kernel, out_shape=jax.ShapeDtypeStruct((til...  15.6 us
    pallas_call x1, Pallas kernels, spread_from_ocean(): pl.pallas_call(functools.partial(spread_kernel, tuple(offsets), tuple(sha...  7.11 us
    dot_general x1, matrix products, ocean_reply(): jnp.einsum('db,wab->wda', top_level, weights_wide, precision=HIGHEST)  3.49 us

profile of v12, /device:TPU:25, one launch (start us, length us, event | category | flops | bytes accessed | tf_op | source)
XLA Modules:
  0.0 164.9 jit_solution(1969370728215778346)
XLA Ops:
  0.6 1.6 fusion.19
  2.3 9.4 %shard_map.104 = (f32[2,1,128,128]{3,2,1,0:T(8,128)}, f32[2,128,1,128]{3,2,1,0:T(1,128)}) custom-call(f32[128,128,128]{2,1,0:T(8,128)} %state_ref.1), custom_call_target="tpu_custom_call" | custom-call | tf_op jit(solution)/shard_map/pallas_call | solution.py:462
  11.7 0.9 select_bitcast_fusion.2
  12.6 1.5 pad_maximum_fusion
  14.1 0.6 fusion.21
  14.7 0.6 broadcast_select_fusion.1.mix_ref
  15.4 20.2 %shard_map.105 = (f32[128,128,128]{2,1,0:T(8,128)}, f32[8,16384]{1,0:T(8,128)}) custom-call(f32[128,128,128]{2,1,0:T(8,128)} %state_ref.1, f32[16,128,128]{2,1,0:T(8,128)} %get-tuple-element.106.top_ref, f32[16,128,128]{2,1,0:T(8,128)} %get-tuple-element.107.bottom_ref, f32[128,1,128]{2,1,0:T(1,128)} %bitcast.86, f32[128,1,128]{2,1,0:T(1,128)} %bitcast.85, ...), custom_call_target="tpu_custom_call" | custom-call | flops 1610612736 | bytes 16777216 | tf_op jit(solution)/shard_map/pallas_call | solution.py:112
  35.6 1.6 fusion.18
  37.2 6.3 %shard_map.106 = (f32[2,1,128,128]{3,2,1,0:T(8,128)}, f32[2,128,1,128]{3,2,1,0:T(1,128)}) custom-call(f32[128,128,128]{2,1,0:T(8,128)} %get-tuple-element.55.values_ref.x_ref.first_ref), custom_call_target="tpu_custom_call" | custom-call | tf_op jit(solution)/shard_map/pallas_call | solution.py:462
  43.6 0.9 select_bitcast_fusion
  44.5 1.0 pad_maximum_fusion.2.top_ref
  45.5 1.0 pad_maximum_fusion.3.bottom_ref
  46.6 0.7 fusion.20
  47.3 19.0 %shard_map.107 = (f32[128,128,128]{2,1,0:T(8,128)}, f32[8,16384]{1,0:T(8,128)}) custom-call(f32[128,128,128]{2,1,0:T(8,128)} %get-tuple-element.55.values_ref.x_ref.first_ref, f32[16,128,128]{2,1,0:T(8,128)} %pad_maximum_fusion.2.top_ref, f32[16,128,128]{2,1,0:T(8,128)} %pad_maximum_fusion.3.bottom_ref, f32[128,1,128]{2,1,0:T(1,128)} %bitcast.88, ...), custom_call_target="tpu_custom_call" | custom-call | flops 1711276032 | bytes 16777216 | tf_op jit(solution)/shard_map/pallas_call | solution.py:112
  66.2 1.1 slice.79
  67.8 1.1 fusion.8
  69.5 1.2 convolution_convert_fusion
  70.6 38.5 %shard_map.108 = bf16[24,32,1152]{2,1,0:T(8,128)(2,1)S(1)} custom-call(bf16[8,32,1152]{2,1,0:T(8,128)(2,1)} %bitcast.81), custom_call_target="tpu_custom_call" | custom-call | tf_op jit(solution)/shard_map/pallas_call | solution.py:220
  109.2 2.9 %convert_element_type.40 = f32[32,128,128]{2,1,0:T(8,128)} convert(bf16[32,128,128]{2,1,0:T(8,128)(2,1)} %param.20) | non-fusion elementwise | flops 524288 | bytes 3145728 | tf_op jit(solution)/shard_map/convert_element_type | solution.py:558
  112.0 26.0 %conditional.2 = (f32[8,128,128]{2,0,1:T(8,128)S(1)}, f32[24,32,128]{2,1,0:T(8,128)S(1)}, f32[128,128]{1,0:T(8,128)S(1)}) conditional(s32[]{:T(128)} %convert_element_type.35, f32[128,128]{1,0:T(8,128)S(1)} %bitcast.78, (bf16[24,32,1152]{2,1,0:T(8,128)(2,1)S(1)}, bf16[32,128,128]{2,1,0:T(8,128)(2,1)S(1)}, f32[8,128]{1,0:T(8,128)S(1)}, ...), branch_computations={%region_2.3_spmd, %region_3.5_spmd} | conditional | flops 2953967360 | bytes 33342668 | solution.py:582
  112.9 0.4 copy-done.1
  113.3 0.7 copy.41
  114.0 15.6 %branch_1_fun.1 = f32[1024,128]{1,0:T(8,128)S(1)} custom-call(s32[768]{0:T(1024)S(1)} %get-tuple-element.88.labels_ref, f32[768,8,128]{2,1,0:T(8,128)S(1)} %bitcast.68, bf16[32,128,128]{2,1,0:T(8,128)(2,1)S(1)} %get-tuple-element.23.weights_ref), custom_call_target="tpu_custom_call" | custom-call | flops 2147483648 | bytes 4194304 | tf_op jit(solution)/shard_map/cond/branch_1_fun/pallas_call | solution.py:399
  129.6 1.3 slice.49
  131.2 3.5 %fusion.2 = f32[128,32,128]{2,0,1:T(8,128)S(1)} fusion(f32[32,128,128]{2,1,0:T(8,128)} %get-tuple-element.28, f32[128,128]{1,0:T(8,128)S(1)} %add_select_fusion), kind=kOutput, calls=%fused_computation.10 | convolution fusion | flops 805306368 | bytes 4259840 | tf_op jit(solution)/shard_map/cond/branch_1_fun/db,wab->wda/dot_general | solution.py:571
  134.8 1.6 gather_fusion
  136.3 1.4 and_reduce_fusion
  138.0 7.1 %shard_map.109 = f32[8,32,128]{2,1,0:T(8,128)} custom-call(f32[24,32,128]{2,1,0:T(8,128)S(1)} %get-tuple-element.54.surface_ref), custom_call_target="tpu_custom_call" | custom-call | tf_op jit(solution)/shard_map/pallas_call | solution.py:291
  145.1 0.8 broadcast_in_dim.132.sea_ref
  146.0 17.0 %shard_map.110 = f32[128,128,128]{2,1,0:T(8,128)} custom-call(s32[1]{0:T(128)} %bitcast.11.flag_ref, f32[128,128,128]{2,1,0:T(8,128)} %get-tuple-element.55.values_ref.x_ref.first_ref, f32[128,128,128]{2,1,0:T(8,128)} %get-tuple-element.56.moved_ref, f32[128,128,128]{2,1,0:T(8,128)} %state_ref.1, s32[8,16384]{1,0:T(8,128)} %broadcast_in_dim.132.sea_ref, ...), custom_call_target="tpu_custom_call" | custom-call | flops 134217728 | bytes 25165824 | tf_op jit(solution)/shard_map/pallas_call | solution.py:346
  163.0 0.7 gather_fusion.1
  164.2 0.6 select_select_fusion
  (56 shorter events, 2.8 us)
Async XLA Ops:
  12.6 1.5 copy-start.6
  12.6 2.1 %copy-start.5 = (f32[128,128]{1,0:T(8,128)S(1)}, f32[128,128]{1,0:T(8,128)}, u32[]{:S(2)}) copy-start(f32[128,128]{1,0:T(8,128)} %mix_ref.1) | copy-start | bytes 196612
  12.6 2.1 %copy-start.8 = (f32[128,128]{1,0:T(8,128)S(1)}, f32[128,128]{1,0:T(8,128)}, u32[]{:S(2)}) copy-start(f32[128,128]{1,0:T(8,128)} %param.17) | copy-start | bytes 196612
  44.5 2.1 %copy-start.7 = (f32[2,128,1,128]{3,2,1,0:T(1,128)S(1)}, f32[2,128,1,128]{3,2,1,0:T(1,128)}, u32[]{:S(2)}) copy-start(f32[2,128,1,128]{3,2,1,0:T(1,128)} %get-tuple-element.49) | copy-start | bytes 393220
  47.3 20.1 %copy-start.13 = (s32[128,1,2,3]{0,2,3,1:T(2,128)S(1)}, s32[128,1,2,3]{0,2,3,1:T(2,128)}, u32[]{:S(2)}) copy-start(s32[128,1,2,3]{0,2,3,1:T(2,128)} %param.15) | copy-start | bytes 9220
  47.3 20.6 %copy-start.9 = (s32[128,128]{1,0:T(8,128)S(1)}, s32[128,128]{1,0:T(8,128)}, u32[]{:S(2)}) copy-start(s32[128,128]{1,0:T(8,128)} %param.14) | copy-start | bytes 196612
  66.2 2.9 %copy-start.14 = (s32[8]{0:T(128)S(1)}, s32[8]{0:T(128)}, u32[]{:S(2)}) copy-start(s32[8]{0:T(128)} %constant.90.clone) | copy-start | bytes 100
  69.5 42.6 %copy-start.11 = (s32[256]{0:T(256)}, s32[256]{0:T(256)S(1)}, u32[]{:S(2)}) copy-start(s32[256]{0:T(256)S(1)} %multiply_add_fusion) | copy-start | bytes 3076
  109.1 2.9 %copy-start.4 = (bf16[32,128,128]{2,1,0:T(8,128)(2,1)S(1)}, bf16[32,128,128]{2,1,0:T(8,128)(2,1)}, u32[]{:S(2)}) copy-start(bf16[32,128,128]{2,1,0:T(8,128)(2,1)} %param.20) | copy-start | bytes 3145732
  109.1 2.9 %copy-start.10 = (f32[8,128]{1,0:T(8,128)S(1)}, f32[8,128]{1,0:T(8,128)}, u32[]{:S(2)}) copy-start(f32[8,128]{1,0:T(8,128)} %spread_ref.1) | copy-start | bytes 12292
  112.1 1.2 copy-start.1
  129.6 5.2 %copy-start.2 = (f32[1024,128]{1,0:T(8,128)}, f32[1024,128]{1,0:T(8,128)S(1)}, u32[]{:S(2)}) copy-start(f32[1024,128]{1,0:T(8,128)S(1)} %branch_1_fun.1) | copy-start | bytes 1572868 | tf_op jit(solution)/shard_map/cond
  134.8 3.2 %copy-start.3 = (f32[1024,128]{1,0:T(8,128)S(1)}, f32[1024,128]{1,0:T(8,128)}, u32[]{:S(2)}) copy-start(f32[1024,128]{1,0:T(8,128)} %copy-done.2) | copy-start | bytes 1572868 | tf_op jit(solution)/shard_map/cond
  146.0 17.0 %copy-start.12 = (s32[256]{0:T(256)S(1)}, s32[256]{0:T(256)}, u32[]{:S(2)}) copy-start(s32[256]{0:T(256)} %copy-done.11) | copy-start | bytes 3076
  146.0 17.0 %copy-start = (f32[8,32,128]{2,1,0:T(8,128)S(1)}, f32[8,32,128]{2,1,0:T(8,128)}, u32[]{:S(2)}) copy-start(f32[8,32,128]{2,1,0:T(8,128)} %shard_map.109) | copy-start | bytes 393220

commit v13 on v11

--- a/solution.py
+++ b/solution.py
@@ -302,16 +302,26 @@
     )(replies)
 
 
-def ocean_update_kernel(flag_ref, first_ref, state_ref, sea_ref, forcing_ref, spread_ref, out_ref):
-    ocean = flag_ref[0] == 1
-
-    @pl.when(ocean)
+def ocean_update_kernel(flag_ref, base_ref, state_ref, sea_ref, forcing_ref, spread_ref, out_ref):
+    rows, cols, levels = base_ref.shape
+    flux_count = forcing_ref.shape[0]
+
+    def block(base_block, state_block, sea_block, forcing_block, out_block):
+        ocean_block(base_block, state_block, sea_block, forcing_block, spread_ref, out_block)
+
+    @pl.when(flag_ref[0] == 1)
     def _():
-        ocean_block(first_ref, state_ref, sea_ref, forcing_ref, spread_ref, out_ref)
-
-    @pl.when(jnp.logical_not(ocean))
-    def _():
-        out_ref[...] = first_ref[...]
+        pltpu.emit_pipeline(
+            block,
+            grid=(rows // ROW_BLOCK,),
+            in_specs=[
+                pl.BlockSpec((ROW_BLOCK, cols, levels), lambda i: (i, 0, 0)),
+                pl.BlockSpec((ROW_BLOCK, cols, levels), lambda i: (i, 0, 0)),
+                pl.BlockSpec((8, ROW_BLOCK * cols), lambda i: (0, i)),
+                pl.BlockSpec((flux_count, ROW_BLOCK * cols), lambda i: (0, i)),
+            ],
+            out_specs=[pl.BlockSpec((ROW_BLOCK, cols, levels), lambda i: (i, 0, 0))],
+        )(base_ref, state_ref, sea_ref, forcing_ref, out_ref)
 
 
 def ocean_block(first_ref, state_ref, sea_ref, forcing_ref, spread_ref, out_ref):
@@ -343,19 +353,17 @@
     flag = (lax.axis_index("comp") == comp_total - 1).astype(jnp.int32).reshape(1)
     return pl.pallas_call(
         ocean_update_kernel,
-        grid_spec=pltpu.PrefetchScalarGridSpec(
-            num_scalar_prefetch=1,
-            grid=(rows // ROW_BLOCK,),
-            in_specs=[
-                pl.BlockSpec((ROW_BLOCK, cols, levels), lambda i, f: (i, 0, 0)),
-                pl.BlockSpec((ROW_BLOCK, cols, levels), lambda i, f: (i * f[0], 0, 0)),
-                pl.BlockSpec((8, ROW_BLOCK * cols), lambda i, f: (0, i * f[0])),
-                pl.BlockSpec((flux_count, ROW_BLOCK * cols), lambda i, f: (0, i * f[0])),
-                pl.BlockSpec((flux_count, levels), lambda i, f: (0, 0)),
-            ],
-            out_specs=pl.BlockSpec((ROW_BLOCK, cols, levels), lambda i, f: (i, 0, 0)),
-        ),
         out_shape=jax.ShapeDtypeStruct(first.shape, jnp.float32),
+        in_specs=[
+            pl.BlockSpec(memory_space=pltpu.SMEM),
+            pl.BlockSpec(memory_space=pl.ANY),
+            pl.BlockSpec(memory_space=pl.ANY),
+            pl.BlockSpec(memory_space=pl.ANY),
+            pl.BlockSpec(memory_space=pl.ANY),
+            pl.BlockSpec(memory_space=pltpu.VMEM),
+        ],
+        out_specs=pl.BlockSpec(memory_space=pl.ANY),
+        input_output_aliases={1: 0},
         cost_estimate=pl.CostEstimate(
             flops=8 * cells * levels * flux_count, transcendentals=0, bytes_accessed=12 * cells * levels
         ),

time: 161 us -> 159 us (0.988)
  the two profiles are of different devices: /device:TPU:1 before, /device:TPU:25 now
where the time goes in v13:
time: 159 us; the launch traced here: 158 us
  Pallas kernels  131 us (82%)
  local copies, waits for them, and re-layouts  11 us (7%)
  other arithmetic  9.73 us (6%)
  matrix products  4.66 us (3%)
    pallas_call x1, Pallas kernels, gather_to_ocean(): pl.pallas_call(functools.partial(gather_kernel, tuple(offsets), tuple(sha...  58.5 us
    pallas_call x1, Pallas kernels, substep(): pl.pallas_call(functools.partial(substep_kernel, with_flux, comp_total),...  20.2 us
    pallas_call x1, Pallas kernels, ocean_update(): pl.pallas_call(ocean_update_kernel, out_shape=jax.ShapeDtypeStruct(first....  17.5 us
    pallas_call x1, Pallas kernels, scatter_regrid(): pl.pallas_call(scatter_regrid_kernel, out_shape=jax.ShapeDtypeStruct((til...  15.6 us
    pallas_call x2, Pallas kernels, halo_edges(): pl.pallas_call(functools.partial(halo_kernel, tuple(shape)), out_shape=(j...  15 us
    pallas_call x1, Pallas kernels, spread_from_ocean(): pl.pallas_call(functools.partial(spread_kernel, tuple(offsets), tuple(sha...  4.71 us
    dot_general x1, matrix products, ocean_reply(): jnp.einsum('db,wab->wda', top_level, weights_wide, precision=HIGHEST)  3.48 us

profile of v13, /device:TPU:25, one launch (start us, length us, event | category | flops | bytes accessed | tf_op | source)
XLA Modules:
  0.0 157.8 jit_solution(10662782219074966860)
XLA Ops:
  0.7 9.4 %shard_map.106 = (f32[2,1,128,128]{3,2,1,0:T(8,128)}, f32[2,128,1,128]{3,2,1,0:T(1,128)}) custom-call(f32[128,128,128]{2,1,0:T(8,128)} %state_ref.1), custom_call_target="tpu_custom_call" | custom-call | tf_op jit(solution)/shard_map/pallas_call | solution.py:467
  10.0 0.9 select_bitcast_fusion
  10.9 1.6 %fusion.20 = (f32[15,128,128]{2,1,0:T(8,128)S(1)}, f32[15,128,128]{2,1,0:T(8,128)S(1)}) fusion(f32[128,128,128]{2,1,0:T(8,128)} %state_ref.1), kind=kLoop, calls=%fused_computation.62 | loop fusion | bytes 3932160 | tf_op jit(solution)/shard_map/slice | solution.py:88
  12.6 1.5 pad_maximum_fusion.2
  14.1 0.6 broadcast_select_fusion.1.mix_ref
  14.7 0.6 fusion.21
  15.4 20.2 %shard_map.107 = (f32[128,128,128]{2,1,0:T(8,128)}, f32[8,16384]{1,0:T(8,128)}) custom-call(f32[128,128,128]{2,1,0:T(8,128)} %state_ref.1, f32[16,128,128]{2,1,0:T(8,128)} %get-tuple-element.216.top_ref, f32[16,128,128]{2,1,0:T(8,128)} %get-tuple-element.217.bottom_ref, f32[128,1,128]{2,1,0:T(1,128)} %bitcast.86, f32[128,1,128]{2,1,0:T(1,128)} %bitcast.85, ...), custom_call_target="tpu_custom_call" | custom-call | flops 1610612736 | bytes 16777216 | tf_op jit(solution)/shard_map/pallas_call | solution.py:112
  35.5 5.6 %shard_map.108 = (f32[2,1,128,128]{3,2,1,0:T(8,128)S(1)}, f32[2,128,1,128]{3,2,1,0:T(1,128)S(1)}) custom-call(f32[128,128,128]{2,1,0:T(8,128)} %get-tuple-element.114.values_ref), custom_call_target="tpu_custom_call" | custom-call | tf_op jit(solution)/shard_map/pallas_call | solution.py:467
  41.6 0.4 copy-done.14
  42.7 1.2 convolution_convert_fusion
  43.9 58.5 %shard_map.109 = bf16[24,32,1152]{2,1,0:T(8,128)(2,1)S(1)} custom-call(bf16[8,32,1152]{2,1,0:T(8,128)(2,1)} %bitcast.79), custom_call_target="tpu_custom_call" | custom-call | tf_op jit(solution)/shard_map/pallas_call | solution.py:220
  102.4 1.2 slice.77
  103.6 2.8 %convert_element_type.40 = f32[32,128,128]{2,1,0:T(8,128)} convert(bf16[32,128,128]{2,1,0:T(8,128)(2,1)} %param.22) | non-fusion elementwise | flops 524288 | bytes 3145728 | tf_op jit(solution)/shard_map/convert_element_type | solution.py:572
  106.4 25.7 %conditional.4 = (f32[8,128,128]{2,0,1:T(8,128)S(1)}, f32[24,32,128]{2,1,0:T(8,128)S(1)}, f32[128,128]{1,0:T(8,128)S(1)}) conditional(s32[]{:T(128)} %convert_element_type.36, f32[128,128]{1,0:T(8,128)S(1)} %bitcast.75, (bf16[24,32,1152]{2,1,0:T(8,128)(2,1)S(1)}, bf16[32,128,128]{2,1,0:T(8,128)(2,1)S(1)}, f32[8,128]{1,0:T(8,128)S(1)}, ...), branch_computations={%region_4.5_spmd, %region_5.7_spmd} | conditional | flops 2953967360 | bytes 33342668 | solution.py:596
  106.4 0.4 fusion.4
  106.8 0.4 convert_bitcast_fusion
  107.2 0.4 copy-done.2
  107.6 0.7 copy.44
  108.3 15.6 %branch_1_fun.1 = f32[1024,128]{1,0:T(8,128)S(1)} custom-call(s32[768]{0:T(1024)S(1)} %get-tuple-element.198.labels_ref, f32[768,8,128]{2,1,0:T(8,128)S(1)} %bitcast.65, bf16[32,128,128]{2,1,0:T(8,128)(2,1)S(1)} %get-tuple-element.50.weights_ref), custom_call_target="tpu_custom_call" | custom-call | flops 2147483648 | bytes 4194304 | tf_op jit(solution)/shard_map/cond/branch_1_fun/pallas_call | solution.py:404
  124.0 0.2 multiply_reduce_fusion
  124.2 1.1 slice.51
  125.4 3.5 %fusion.5 = f32[128,32,128]{2,0,1:T(8,128)S(1)} fusion(f32[32,128,128]{2,1,0:T(8,128)} %get-tuple-element.55, f32[128,128]{1,0:T(8,128)S(1)} %add_select_fusion), kind=kOutput, calls=%fused_computation.18 | convolution fusion | flops 805306368 | bytes 4259840 | tf_op jit(solution)/shard_map/cond/branch_1_fun/db,wab->wda/dot_general | solution.py:585
  128.9 1.6 gather_fusion
  130.5 1.4 and_reduce_fusion
  132.1 4.7 %shard_map.110 = f32[8,32,128]{2,1,0:T(8,128)} custom-call(f32[24,32,128]{2,1,0:T(8,128)S(1)} %get-tuple-element.80.surface_ref), custom_call_target="tpu_custom_call" | custom-call | tf_op jit(solution)/shard_map/pallas_call | solution.py:291
  136.8 0.8 broadcast_in_dim.130.sea_ref
  137.7 17.5 %shard_map.111 = f32[128,128,128]{2,1,0:T(8,128)} custom-call(s32[1]{0:T(128)} %bitcast.11.flag_ref, f32[128,128,128]{2,1,0:T(8,128)} %get-tuple-element.81.base_ref, f32[128,128,128]{2,1,0:T(8,128)} %state_ref.1, s32[8,16384]{1,0:T(8,128)} %broadcast_in_dim.130.sea_ref, f32[8,16384]{1,0:T(8,128)S(1)} %bitcast.73, ...), custom_call_target="tpu_custom_call", output_to_operand_aliasing={{}: (1, {})} | custom-call | flops 134217728 | bytes 25165824 | tf_op jit(solution)/shard_map/pallas_call | solution.py:354
  155.1 0.7 copy-done.12
  155.8 0.2 copy-done.1
  156.0 0.7 gather_fusion.1
  156.9 0.2 select_reduce_fusion
  157.2 0.6 select_select_fusion
  (54 shorter events, 1.7 us)
Async XLA Ops:
  12.6 1.5 copy-start.6
  12.6 1.5 copy-start.8
  12.6 2.1 %copy-start.7 = (f32[2,128,1,128]{3,2,1,0:T(1,128)S(1)}, f32[2,128,1,128]{3,2,1,0:T(1,128)}, u32[]{:S(2)}) copy-start(f32[2,128,1,128]{3,2,1,0:T(1,128)} %get-tuple-element.72) | copy-start | bytes 393220
  35.5 5.7 %copy-start.9 = (s32[128,128]{1,0:T(8,128)S(1)}, s32[128,128]{1,0:T(8,128)}, u32[]{:S(2)}) copy-start(s32[128,128]{1,0:T(8,128)} %param.16) | copy-start | bytes 196612
  35.5 5.8 %copy-start.13 = (f32[128,8]{0,1:T(8,128)S(1)}, f32[128,8]{0,1:T(8,128)}, u32[]{:S(2)}) copy-start(f32[128,8]{0,1:T(8,128)} %param.20) | copy-start | bytes 12292
  41.3 0.7 copy-start.14
  41.4 0.9 copy-start.15
  42.6 1.3 copy-start.11
  102.4 4.0 %copy-start.5 = (bf16[32,128,128]{2,1,0:T(8,128)(2,1)S(1)}, bf16[32,128,128]{2,1,0:T(8,128)(2,1)}, u32[]{:S(2)}) copy-start(bf16[32,128,128]{2,1,0:T(8,128)(2,1)} %param.22) | copy-start | bytes 3145732
  102.4 4.0 %copy-start.10 = (f32[8,128]{1,0:T(8,128)S(1)}, f32[8,128]{1,0:T(8,128)}, u32[]{:S(2)}) copy-start(f32[8,128]{1,0:T(8,128)} %spread_ref.1) | copy-start | bytes 12292
  106.4 1.2 copy-start.2
  123.9 5.0 %copy-start.3 = (f32[1024,128]{1,0:T(8,128)}, f32[1024,128]{1,0:T(8,128)S(1)}, u32[]{:S(2)}) copy-start(f32[1024,128]{1,0:T(8,128)S(1)} %branch_1_fun.1) | copy-start | bytes 1572868 | tf_op jit(solution)/shard_map/cond
  128.9 3.2 %copy-start.4 = (f32[1024,128]{1,0:T(8,128)S(1)}, f32[1024,128]{1,0:T(8,128)}, u32[]{:S(2)}) copy-start(f32[1024,128]{1,0:T(8,128)} %copy-done.3) | copy-start | bytes 1572868 | tf_op jit(solution)/shard_map/cond
  155.1 0.7 copy-start.12
  155.1 0.9 copy-start.1

commit v14 on v13

--- a/solution.py
+++ b/solution.py
@@ -336,7 +336,15 @@
     def one(a, b):
         return lax.dot_general(a, b, (((0,), (0,)), ((), ())), preferred_element_type=jnp.float32)
 
-    added = one(forcing_hi, spread_hi) + (one(forcing_hi, spread_lo) + one(forcing_lo, spread_hi))
+    stacked = jnp.concatenate(
+        [forcing_hi.astype(jnp.float32), forcing_hi.astype(jnp.float32), forcing_lo.astype(jnp.float32)],
+        axis=0,
+    ).astype(jnp.bfloat16)
+    spread_stack = jnp.concatenate(
+        [spread_hi.astype(jnp.float32), spread_lo.astype(jnp.float32), spread_hi.astype(jnp.float32)],
+        axis=0,
+    ).astype(jnp.bfloat16)
+    added = one(stacked, spread_stack)
     lane_row = lax.broadcasted_iota(jnp.int32, (8, levels), 0)
     ones = (lane_row == 0).astype(jnp.bfloat16)
     picks = jnp.where(lax.broadcasted_iota(jnp.int32, sea_ref.shape, 0) == 0, sea_ref[...], 0)

time: 159 us -> 158 us (level)
  no operation moved by 1% of the time
where the time goes in v14:
time: 158 us; the launch traced here: 157 us
  Pallas kernels  130 us (82%)
  local copies, waits for them, and re-layouts  11 us (7%)
  other arithmetic  9.73 us (6%)
  matrix products  4.66 us (3%)
    pallas_call x1, Pallas kernels, gather_to_ocean(): pl.pallas_call(functools.partial(gather_kernel, tuple(offsets), tuple(sha...  58.5 us
    pallas_call x1, Pallas kernels, substep(): pl.pallas_call(functools.partial(substep_kernel, with_flux, comp_total),...  20.2 us
    pallas_call x1, Pallas kernels, ocean_update(): pl.pallas_call(ocean_update_kernel, out_shape=jax.ShapeDtypeStruct(first....  16.4 us
    pallas_call x1, Pallas kernels, scatter_regrid(): pl.pallas_call(scatter_regrid_kernel, out_shape=jax.ShapeDtypeStruct((til...  15.6 us
    pallas_call x2, Pallas kernels, halo_edges(): pl.pallas_call(functools.partial(halo_kernel, tuple(shape)), out_shape=(j...  15 us
    pallas_call x1, Pallas kernels, spread_from_ocean(): pl.pallas_call(functools.partial(spread_kernel, tuple(offsets), tuple(sha...  4.71 us
    dot_general x1, matrix products, ocean_reply(): jnp.einsum('db,wab->wda', top_level, weights_wide, precision=HIGHEST)  3.48 us

profile of v14, /device:TPU:25, one launch (start us, length us, event | category | flops | bytes accessed | tf_op | source)
XLA Modules:
  0.0 156.8 jit_solution(16149279094450041115)
XLA Ops:
  0.7 9.4 %shard_map.106 = (f32[2,1,128,128]{3,2,1,0:T(8,128)}, f32[2,128,1,128]{3,2,1,0:T(1,128)}) custom-call(f32[128,128,128]{2,1,0:T(8,128)} %state_ref.1), custom_call_target="tpu_custom_call" | custom-call | tf_op jit(solution)/shard_map/pallas_call | solution.py:475
  10.0 0.9 select_bitcast_fusion
  10.9 1.6 %fusion.20 = (f32[15,128,128]{2,1,0:T(8,128)S(1)}, f32[15,128,128]{2,1,0:T(8,128)S(1)}) fusion(f32[128,128,128]{2,1,0:T(8,128)} %state_ref.1), kind=kLoop, calls=%fused_computation.62 | loop fusion | bytes 3932160 | tf_op jit(solution)/shard_map/slice | solution.py:88
  12.6 1.5 pad_maximum_fusion.2
  14.1 0.6 broadcast_select_fusion.1.mix_ref
  14.7 0.6 fusion.21
  15.4 20.2 %shard_map.107 = (f32[128,128,128]{2,1,0:T(8,128)}, f32[8,16384]{1,0:T(8,128)}) custom-call(f32[128,128,128]{2,1,0:T(8,128)} %state_ref.1, f32[16,128,128]{2,1,0:T(8,128)} %get-tuple-element.216.top_ref, f32[16,128,128]{2,1,0:T(8,128)} %get-tuple-element.217.bottom_ref, f32[128,1,128]{2,1,0:T(1,128)} %bitcast.86, f32[128,1,128]{2,1,0:T(1,128)} %bitcast.85, ...), custom_call_target="tpu_custom_call" | custom-call | flops 1610612736 | bytes 16777216 | tf_op jit(solution)/shard_map/pallas_call | solution.py:112
  35.5 5.6 %shard_map.108 = (f32[2,1,128,128]{3,2,1,0:T(8,128)S(1)}, f32[2,128,1,128]{3,2,1,0:T(1,128)S(1)}) custom-call(f32[128,128,128]{2,1,0:T(8,128)} %get-tuple-element.114.values_ref), custom_call_target="tpu_custom_call" | custom-call | tf_op jit(solution)/shard_map/pallas_call | solution.py:475
  41.6 0.4 copy-done.14
  42.7 1.2 convolution_convert_fusion
  43.9 58.5 %shard_map.109 = bf16[24,32,1152]{2,1,0:T(8,128)(2,1)S(1)} custom-call(bf16[8,32,1152]{2,1,0:T(8,128)(2,1)} %bitcast.79), custom_call_target="tpu_custom_call" | custom-call | tf_op jit(solution)/shard_map/pallas_call | solution.py:220
  102.4 1.2 slice.77
  103.6 2.8 %convert_element_type.40 = f32[32,128,128]{2,1,0:T(8,128)} convert(bf16[32,128,128]{2,1,0:T(8,128)(2,1)} %param.22) | non-fusion elementwise | flops 524288 | bytes 3145728 | tf_op jit(solution)/shard_map/convert_element_type | solution.py:580
  106.4 25.7 %conditional.4 = (f32[8,128,128]{2,0,1:T(8,128)S(1)}, f32[24,32,128]{2,1,0:T(8,128)S(1)}, f32[128,128]{1,0:T(8,128)S(1)}) conditional(s32[]{:T(128)} %convert_element_type.36, f32[128,128]{1,0:T(8,128)S(1)} %bitcast.75, (bf16[24,32,1152]{2,1,0:T(8,128)(2,1)S(1)}, bf16[32,128,128]{2,1,0:T(8,128)(2,1)S(1)}, f32[8,128]{1,0:T(8,128)S(1)}, ...), branch_computations={%region_4.5_spmd, %region_5.7_spmd} | conditional | flops 2953967360 | bytes 33342668 | solution.py:604
  106.4 0.4 fusion.4
  106.8 0.4 convert_bitcast_fusion
  107.2 0.4 copy-done.2
  107.6 0.7 copy.44
  108.3 15.6 %branch_1_fun.1 = f32[1024,128]{1,0:T(8,128)S(1)} custom-call(s32[768]{0:T(1024)S(1)} %get-tuple-element.198.labels_ref, f32[768,8,128]{2,1,0:T(8,128)S(1)} %bitcast.65, bf16[32,128,128]{2,1,0:T(8,128)(2,1)S(1)} %get-tuple-element.50.weights_ref), custom_call_target="tpu_custom_call" | custom-call | flops 2147483648 | bytes 4194304 | tf_op jit(solution)/shard_map/cond/branch_1_fun/pallas_call | solution.py:412
  124.0 0.2 multiply_reduce_fusion
  124.2 1.1 slice.51
  125.4 3.5 %fusion.5 = f32[128,32,128]{2,0,1:T(8,128)S(1)} fusion(f32[32,128,128]{2,1,0:T(8,128)} %get-tuple-element.55, f32[128,128]{1,0:T(8,128)S(1)} %add_select_fusion), kind=kOutput, calls=%fused_computation.18 | convolution fusion | flops 805306368 | bytes 4259840 | tf_op jit(solution)/shard_map/cond/branch_1_fun/db,wab->wda/dot_general | solution.py:593
  128.9 1.6 %gather_fusion = f32[768,128]{1,0:T(8,128)S(1)} fusion(f32[4096,128]{1,0:T(8,128)S(1)} %bitcast.67, s32[1024]{0:T(1024)S(1)} %pad_clamp_fusion), kind=kCustom, calls=%fused_computation | custom fusion | bytes 789504 | tf_op jit(solution)/shard_map/cond/branch_1_fun/jit(_take)/gather | solution.py:594
  130.5 1.4 and_reduce_fusion
  132.1 4.7 %shard_map.110 = f32[8,32,128]{2,1,0:T(8,128)} custom-call(f32[24,32,128]{2,1,0:T(8,128)S(1)} %get-tuple-element.80.surface_ref), custom_call_target="tpu_custom_call" | custom-call | tf_op jit(solution)/shard_map/pallas_call | solution.py:291
  136.8 0.8 broadcast_in_dim.130.sea_ref
  137.7 16.4 %shard_map.111 = f32[128,128,128]{2,1,0:T(8,128)} custom-call(s32[1]{0:T(128)} %bitcast.11.flag_ref, f32[128,128,128]{2,1,0:T(8,128)} %get-tuple-element.81.base_ref, f32[128,128,128]{2,1,0:T(8,128)} %state_ref.1, s32[8,16384]{1,0:T(8,128)} %broadcast_in_dim.130.sea_ref, f32[8,16384]{1,0:T(8,128)S(1)} %bitcast.73, ...), custom_call_target="tpu_custom_call", output_to_operand_aliasing={{}: (1, {})} | custom-call | flops 134217728 | bytes 25165824 | tf_op jit(solution)/shard_map/pallas_call | solution.py:362
  154.1 0.7 copy-done.12
  154.7 0.2 copy-done.1
  155.0 0.7 gather_fusion.1
  155.9 0.2 select_reduce_fusion
  156.1 0.6 select_select_fusion
  (54 shorter events, 1.7 us)
Async XLA Ops:
  12.6 1.5 copy-start.6
  12.6 1.5 copy-start.8
  12.6 2.1 %copy-start.7 = (f32[2,128,1,128]{3,2,1,0:T(1,128)S(1)}, f32[2,128,1,128]{3,2,1,0:T(1,128)}, u32[]{:S(2)}) copy-start(f32[2,128,1,128]{3,2,1,0:T(1,128)} %get-tuple-element.72) | copy-start | bytes 393220
  35.5 5.7 %copy-start.9 = (s32[128,128]{1,0:T(8,128)S(1)}, s32[128,128]{1,0:T(8,128)}, u32[]{:S(2)}) copy-start(s32[128,128]{1,0:T(8,128)} %param.16) | copy-start | bytes 196612
  35.5 5.8 %copy-start.13 = (f32[128,8]{0,1:T(8,128)S(1)}, f32[128,8]{0,1:T(8,128)}, u32[]{:S(2)}) copy-start(f32[128,8]{0,1:T(8,128)} %param.20) | copy-start | bytes 12292
  41.3 0.7 copy-start.14
  41.4 0.9 copy-start.15
  42.6 1.3 copy-start.11
  102.4 4.0 %copy-start.5 = (bf16[32,128,128]{2,1,0:T(8,128)(2,1)S(1)}, bf16[32,128,128]{2,1,0:T(8,128)(2,1)}, u32[]{:S(2)}) copy-start(bf16[32,128,128]{2,1,0:T(8,128)(2,1)} %param.22) | copy-start | bytes 3145732
  102.4 4.0 %copy-start.10 = (f32[8,128]{1,0:T(8,128)S(1)}, f32[8,128]{1,0:T(8,128)}, u32[]{:S(2)}) copy-start(f32[8,128]{1,0:T(8,128)} %spread_ref.1) | copy-start | bytes 12292
  106.4 1.2 copy-start.2
  123.9 5.0 %copy-start.3 = (f32[1024,128]{1,0:T(8,128)}, f32[1024,128]{1,0:T(8,128)S(1)}, u32[]{:S(2)}) copy-start(f32[1024,128]{1,0:T(8,128)S(1)} %branch_1_fun.1) | copy-start | bytes 1572868 | tf_op jit(solution)/shard_map/cond
  128.9 3.2 %copy-start.4 = (f32[1024,128]{1,0:T(8,128)S(1)}, f32[1024,128]{1,0:T(8,128)}, u32[]{:S(2)}) copy-start(f32[1024,128]{1,0:T(8,128)} %copy-done.3) | copy-start | bytes 1572868 | tf_op jit(solution)/shard_map/cond
  154.1 0.7 copy-start.12
  154.1 0.9 copy-start.1

commit v15 on v14

--- a/solution.py
+++ b/solution.py
@@ -10,6 +10,7 @@
 PHYSICS = 0.5
 HIGHEST = lax.Precision.HIGHEST
 ROW_BLOCK = 8
+UPDATE_BLOCK = 16
 
 
 def split_bf16(values):
@@ -313,14 +314,14 @@
     def _():
         pltpu.emit_pipeline(
             block,
-            grid=(rows // ROW_BLOCK,),
+            grid=(rows // UPDATE_BLOCK,),
             in_specs=[
-                pl.BlockSpec((ROW_BLOCK, cols, levels), lambda i: (i, 0, 0)),
-                pl.BlockSpec((ROW_BLOCK, cols, levels), lambda i: (i, 0, 0)),
-                pl.BlockSpec((8, ROW_BLOCK * cols), lambda i: (0, i)),
-                pl.BlockSpec((flux_count, ROW_BLOCK * cols), lambda i: (0, i)),
+                pl.BlockSpec((UPDATE_BLOCK, cols, levels), lambda i: (i, 0, 0)),
+                pl.BlockSpec((UPDATE_BLOCK, cols, levels), lambda i: (i, 0, 0)),
+                pl.BlockSpec((8, UPDATE_BLOCK * cols), lambda i: (0, i)),
+                pl.BlockSpec((flux_count, UPDATE_BLOCK * cols), lambda i: (0, i)),
             ],
-            out_specs=[pl.BlockSpec((ROW_BLOCK, cols, levels), lambda i: (i, 0, 0))],
+            out_specs=[pl.BlockSpec((UPDATE_BLOCK, cols, levels), lambda i: (i, 0, 0))],
         )(base_ref, state_ref, sea_ref, forcing_ref, out_ref)
 
 
@@ -604,6 +605,13 @@
     forcing, replies, ocean_top = lax.cond(
         ocean_side, ocean_reply, atmosphere_reply, first_top, arrived
     )
+    atmosphere_top = lax.cond(
+        ocean_side,
+        lambda values: jnp.zeros((tile_rows, block_len), jnp.float32),
+        lambda values: values[:, :, 0],
+        second,
+    )
+    replies, atmosphere_top = lax.optimization_barrier((replies, atmosphere_top))
     answers = spread_from_ocean(replies, offsets, mesh_shape)
     per_entry = jnp.take(
         answers.reshape(neighbour_count * capacity, block_len), entry_slots, axis=0
@@ -621,10 +629,9 @@
         ocean_map,
         comp_count,
     )
-    top_plane = lax.cond(
-        ocean_side, lambda values: ocean_top, lambda values: values[:, :, 0], final_state
-    )
-    surface_out = jnp.where(ocean_side, ocean_top, jnp.where(sea_cells, returned, top_plane))
+    surface_out = jnp.where(
+        ocean_side, ocean_top, jnp.where(sea_cells, returned, atmosphere_top)
+    )
     return (final_state, surface_out)
 
 

time: 158 us -> 151 us (0.956)
  Pallas kernels: 130 us -> 127 us
  local copies, waits for them, and re-layouts: 11 us -> 9.25 us
    pallas_call x1, Pallas kernels: 16.4 us -> 12.2 us  [ocean_update(): pl.pallas_call(ocean_update_kernel, out_shape=jax.ShapeDtypeStruct(first....]
where the time goes in v15:
time: 151 us; the launch traced here: 150 us
  Pallas kernels  127 us (84%)
  local copies, waits for them, and re-layouts  9.25 us (6%)
  other arithmetic  8.52 us (6%)
  matrix products  4.65 us (3%)
    pallas_call x1, Pallas kernels, gather_to_ocean(): pl.pallas_call(functools.partial(gather_kernel, tuple(offsets), tuple(sha...  58.5 us
    pallas_call x1, Pallas kernels, substep(): pl.pallas_call(functools.partial(substep_kernel, with_flux, comp_total),...  20.1 us
    pallas_call x1, Pallas kernels, scatter_regrid(): pl.pallas_call(scatter_regrid_kernel, out_shape=jax.ShapeDtypeStruct((til...  16.1 us
    pallas_call x2, Pallas kernels, halo_edges(): pl.pallas_call(functools.partial(halo_kernel, tuple(shape)), out_shape=(j...  15 us
    pallas_call x1, Pallas kernels, ocean_update(): pl.pallas_call(ocean_update_kernel, out_shape=jax.ShapeDtypeStruct(first....  12.2 us
    pallas_call x1, Pallas kernels, spread_from_ocean(): pl.pallas_call(functools.partial(spread_kernel, tuple(offsets), tuple(sha...  4.71 us
    dot_general x1, matrix products, ocean_reply(): jnp.einsum('db,wab->wda', top_level, weights_wide, precision=HIGHEST)  3.48 us

profile of v15, /device:TPU:25, one launch (start us, length us, event | category | flops | bytes accessed | tf_op | source)
XLA Modules:
  0.0 150.2 jit_solution(1002388210348269146)
XLA Ops:
  0.7 9.4 %shard_map.106 = (f32[2,1,128,128]{3,2,1,0:T(8,128)}, f32[2,128,1,128]{3,2,1,0:T(1,128)}) custom-call(f32[128,128,128]{2,1,0:T(8,128)} %state_ref.1), custom_call_target="tpu_custom_call" | custom-call | tf_op jit(solution)/shard_map/pallas_call | solution.py:476
  10.0 0.9 select_bitcast_fusion
  10.9 1.6 %fusion.20 = (f32[15,128,128]{2,1,0:T(8,128)S(1)}, f32[15,128,128]{2,1,0:T(8,128)S(1)}) fusion(f32[128,128,128]{2,1,0:T(8,128)} %state_ref.1), kind=kLoop, calls=%fused_computation.62 | loop fusion | bytes 3932160 | tf_op jit(solution)/shard_map/slice | solution.py:89
  12.6 1.5 pad_maximum_fusion.2
  14.1 0.6 broadcast_select_fusion.1.mix_ref
  14.7 0.6 fusion.21
  15.4 20.1 %shard_map.107 = (f32[128,128,128]{2,1,0:T(8,128)}, f32[8,16384]{1,0:T(8,128)S(1)}) custom-call(f32[128,128,128]{2,1,0:T(8,128)} %state_ref.1, f32[16,128,128]{2,1,0:T(8,128)} %get-tuple-element.219.top_ref, f32[16,128,128]{2,1,0:T(8,128)} %get-tuple-element.220.bottom_ref, f32[128,1,128]{2,1,0:T(1,128)} %bitcast.86, f32[128,1,128]{2,1,0:T(1,128)} %bitcast.85, ...), custom_call_target="tpu_custom_call" | custom-call | flops 1610612736 | bytes 16777216 | tf_op jit(solution)/shard_map/pallas_call | solution.py:113
  35.5 5.6 %shard_map.108 = (f32[2,1,128,128]{3,2,1,0:T(8,128)S(1)}, f32[2,128,1,128]{3,2,1,0:T(1,128)S(1)}) custom-call(f32[128,128,128]{2,1,0:T(8,128)} %get-tuple-element.117.values_ref), custom_call_target="tpu_custom_call" | custom-call | tf_op jit(solution)/shard_map/pallas_call | solution.py:476
  41.5 0.4 copy-done.15
  42.1 0.1 reshape.179
  42.3 0.2 convert_reduce_fusion
  42.7 1.2 convolution_convert_fusion
  43.8 58.5 %shard_map.109 = bf16[24,32,1152]{2,1,0:T(8,128)(2,1)S(1)} custom-call(bf16[8,32,1152]{2,1,0:T(8,128)(2,1)} %bitcast.79), custom_call_target="tpu_custom_call" | custom-call | tf_op jit(solution)/shard_map/pallas_call | solution.py:221
  102.4 1.6 %convert_element_type.40 = f32[32,128,128]{2,1,0:T(8,128)} convert(bf16[32,128,128]{2,1,0:T(8,128)(2,1)S(1)} %copy-done.4) | non-fusion elementwise | flops 524288 | bytes 3145728 | tf_op jit(solution)/shard_map/convert_element_type | solution.py:581
  104.0 25.7 %conditional.4 = (f32[8,128,128]{2,0,1:T(8,128)S(1)}, f32[24,32,128]{2,1,0:T(8,128)S(1)}, f32[128,128]{1,0:T(8,128)S(1)}) conditional(s32[]{:T(128)} %convert_element_type.36, f32[128,128]{1,0:T(8,128)S(1)} %bitcast.76, (bf16[24,32,1152]{2,1,0:T(8,128)(2,1)S(1)}, bf16[32,128,128]{2,1,0:T(8,128)(2,1)S(1)}, f32[8,128]{1,0:T(8,128)}, ...), branch_computations={%region_4.5_spmd, %region_5.7_spmd} | conditional | flops 2953967360 | bytes 37553412 | solution.py:605
  104.0 0.4 fusion.4
  104.4 0.4 convert_bitcast_fusion
  104.8 0.4 copy-done.1
  105.2 0.4 copy-done.5
  105.6 0.7 copy.44
  106.3 16.1 %branch_1_fun.1 = f32[1024,128]{1,0:T(8,128)S(1)} custom-call(s32[768]{0:T(1024)S(1)} %get-tuple-element.201.labels_ref, f32[768,8,128]{2,1,0:T(8,128)S(1)} %bitcast.65, bf16[32,128,128]{2,1,0:T(8,128)(2,1)} %copy-done.5), custom_call_target="tpu_custom_call" | custom-call | flops 2147483648 | bytes 4194304 | tf_op jit(solution)/shard_map/cond/branch_1_fun/pallas_call | solution.py:413
  122.6 0.2 multiply_reduce_fusion
  122.9 3.5 %fusion.5 = f32[128,32,128]{2,0,1:T(8,128)S(1)} fusion(f32[32,128,128]{2,1,0:T(8,128)} %get-tuple-element.54, f32[128,128]{1,0:T(8,128)S(1)} %add_select_fusion), kind=kOutput, calls=%fused_computation.18 | convolution fusion | flops 805306368 | bytes 4259840 | tf_op jit(solution)/shard_map/cond/branch_1_fun/db,wab->wda/dot_general | solution.py:594
  126.4 1.6 %gather_fusion = f32[768,128]{1,0:T(8,128)S(1)} fusion(f32[4096,128]{1,0:T(8,128)S(1)} %bitcast.67, s32[1024]{0:T(1024)S(1)} %pad_clamp_fusion), kind=kCustom, calls=%fused_computation | custom fusion | bytes 789504 | tf_op jit(solution)/shard_map/cond/branch_1_fun/jit(_take)/gather | solution.py:595
  128.0 1.4 and_reduce_fusion
  129.5 0.2 broadcast_select_fusion
  129.7 4.7 %shard_map.110 = f32[8,32,128]{2,1,0:T(8,128)} custom-call(f32[24,32,128]{2,1,0:T(8,128)S(1)} %get-tuple-element.82.surface_ref), custom_call_target="tpu_custom_call" | custom-call | tf_op jit(solution)/shard_map/pallas_call | solution.py:292
  134.5 1.6 %gather_fusion.1 = f32[256,128]{1,0:T(8,128)S(1)} fusion(f32[256,128]{1,0:T(8,128)} %bitcast.68, s32[1024]{0:T(1024)S(1)} %pad_clamp_fusion.1), kind=kCustom, calls=%fused_computation.1 | custom fusion | bytes 263168 | tf_op jit(solution)/shard_map/jit(_take)/gather | solution.py:616
  136.3 0.2 select_reduce_fusion
  136.5 0.6 select_select_fusion
  137.2 0.8 broadcast_in_dim.130.sea_ref
  138.0 12.2 %shard_map.111 = f32[128,128,128]{2,1,0:T(8,128)} custom-call(s32[1]{0:T(128)} %bitcast.11.flag_ref, f32[128,128,128]{2,1,0:T(8,128)} %get-tuple-element.83.base_ref, f32[128,128,128]{2,1,0:T(8,128)} %state_ref.1, s32[8,16384]{1,0:T(8,128)} %broadcast_in_dim.130.sea_ref, f32[8,16384]{1,0:T(8,128)S(1)} %bitcast.73, ...), custom_call_target="tpu_custom_call", output_to_operand_aliasing={{}: (1, {})} | custom-call | flops 134217728 | bytes 25165824 | tf_op jit(solution)/shard_map/pallas_call | solution.py:363
  (56 shorter events, 1.3 us)
Async XLA Ops:
  12.6 1.5 %copy-start.6 = (f32[128,128]{1,0:T(8,128)S(1)}, f32[128,128]{1,0:T(8,128)}, u32[]{:S(2)}) copy-start(f32[128,128]{1,0:T(8,128)} %param.18) | copy-start | bytes 196612
  12.6 1.5 %copy-start.8 = (f32[128,128]{1,0:T(8,128)S(1)}, f32[128,128]{1,0:T(8,128)}, u32[]{:S(2)}) copy-start(f32[128,128]{1,0:T(8,128)} %param.19) | copy-start | bytes 196612
  12.6 2.1 %copy-start.7 = (f32[2,128,1,128]{3,2,1,0:T(1,128)S(1)}, f32[2,128,1,128]{3,2,1,0:T(1,128)}, u32[]{:S(2)}) copy-start(f32[2,128,1,128]{3,2,1,0:T(1,128)} %get-tuple-element.73) | copy-start | bytes 393220
  35.5 5.7 %copy-start.9 = (s32[128,128]{1,0:T(8,128)S(1)}, s32[128,128]{1,0:T(8,128)}, u32[]{:S(2)}) copy-start(s32[128,128]{1,0:T(8,128)} %param.16) | copy-start | bytes 196612
  35.5 5.7 %copy-start.14 = (f32[128,8]{0,1:T(8,128)S(1)}, f32[128,8]{0,1:T(8,128)}, u32[]{:S(2)}) copy-start(f32[128,8]{0,1:T(8,128)} %param.20) | copy-start | bytes 12292
  41.2 0.7 copy-start.15
  41.3 0.9 copy-start.16
  42.0 60.4 %copy-start.4 = (bf16[32,128,128]{2,1,0:T(8,128)(2,1)S(1)}, bf16[32,128,128]{2,1,0:T(8,128)(2,1)}, u32[]{:S(2)}) copy-start(bf16[32,128,128]{2,1,0:T(8,128)(2,1)} %param.22) | copy-start | bytes 3145732
  42.5 59.9 %copy-start.12 = (s32[256]{0:T(256)}, s32[256]{0:T(256)S(1)}, u32[]{:S(2)}) copy-start(s32[256]{0:T(256)S(1)} %multiply_add_fusion) | copy-start | bytes 3076
  104.0 1.2 copy-start.1
  104.0 1.6 %copy-start.5 = (bf16[32,128,128]{2,1,0:T(8,128)(2,1)}, bf16[32,128,128]{2,1,0:T(8,128)(2,1)S(1)}, u32[]{:S(2)}) copy-start(bf16[32,128,128]{2,1,0:T(8,128)(2,1)S(1)} %get-tuple-element.49.weights_ref) | copy-start | bytes 3145732 | tf_op jit(solution)/shard_map/cond
  106.3 16.2 %copy-start.11 = (f32[8,128]{1,0:T(8,128)S(1)}, f32[8,128]{1,0:T(8,128)}, u32[]{:S(2)}) copy-start(f32[8,128]{1,0:T(8,128)} %get-tuple-element.195) | copy-start | bytes 12292 | tf_op jit(solution)/shard_map/cond
  122.5 3.9 %copy-start.2 = (f32[1024,128]{1,0:T(8,128)}, f32[1024,128]{1,0:T(8,128)S(1)}, u32[]{:S(2)}) copy-start(f32[1024,128]{1,0:T(8,128)S(1)} %branch_1_fun.1) | copy-start | bytes 1572868 | tf_op jit(solution)/shard_map/cond
  126.4 3.2 %copy-start.3 = (f32[1024,128]{1,0:T(8,128)S(1)}, f32[1024,128]{1,0:T(8,128)}, u32[]{:S(2)}) copy-start(f32[1024,128]{1,0:T(8,128)} %copy-done.2) | copy-start | bytes 1572868 | tf_op jit(solution)/shard_map/cond
  129.7 4.8 %copy-start.13 = (s32[256]{0:T(256)S(1)}, s32[256]{0:T(256)}, u32[]{:S(2)}) copy-start(s32[256]{0:T(256)} %copy-done.12) | copy-start | bytes 3076
  129.7 8.3 %copy-start.10 = (f32[8,128]{1,0:T(8,128)S(1)}, f32[8,128]{1,0:T(8,128)}, u32[]{:S(2)}) copy-start(f32[8,128]{1,0:T(8,128)} %spread_ref.1) | copy-start | bytes 12292

commit v16 on v15

--- a/solution.py
+++ b/solution.py
@@ -9,8 +9,8 @@
 SMOOTHING = 0.2
 PHYSICS = 0.5
 HIGHEST = lax.Precision.HIGHEST
-ROW_BLOCK = 8
-UPDATE_BLOCK = 16
+ROW_BLOCK = 16
+UPDATE_BLOCK = 32
 
 
 def split_bf16(values):

time: 151 us -> 141 us (0.934)
  Pallas kernels: 127 us -> 118 us
    pallas_call x1, Pallas kernels: 20.1 us -> 16.4 us  [substep(): pl.pallas_call(functools.partial(substep_kernel, with_flux, comp_total),...]
    pallas_call x1, Pallas kernels: 58.5 us -> 55.6 us  [gather_to_ocean(): pl.pallas_call(functools.partial(gather_kernel, tuple(offsets), tuple(sha...]
    pallas_call x1, Pallas kernels: 12.2 us -> 10.1 us  [ocean_update(): pl.pallas_call(ocean_update_kernel, out_shape=jax.ShapeDtypeStruct(first....]
where the time goes in v16:
time: 141 us
  Pallas kernels  118 us (84%)
  local copies, waits for them, and re-layouts  8.89 us (6%)
  other arithmetic  8.16 us (6%)
  matrix products  4.66 us (3%)
    pallas_call x1, Pallas kernels, gather_to_ocean(): pl.pallas_call(functools.partial(gather_kernel, tuple(offsets), tuple(sha...  55.6 us
    pallas_call x1, Pallas kernels, substep(): pl.pallas_call(functools.partial(substep_kernel, with_flux, comp_total),...  16.4 us
    pallas_call x1, Pallas kernels, scatter_regrid(): pl.pallas_call(scatter_regrid_kernel, out_shape=jax.ShapeDtypeStruct((til...  16.1 us
    pallas_call x2, Pallas kernels, halo_edges(): pl.pallas_call(functools.partial(halo_kernel, tuple(shape)), out_shape=(j...  15 us
    pallas_call x1, Pallas kernels, ocean_update(): pl.pallas_call(ocean_update_kernel, out_shape=jax.ShapeDtypeStruct(first....  10.1 us
    pallas_call x1, Pallas kernels, spread_from_ocean(): pl.pallas_call(functools.partial(spread_kernel, tuple(offsets), tuple(sha...  4.71 us
    dot_general x1, matrix products, ocean_reply(): jnp.einsum('db,wab->wda', top_level, weights_wide, precision=HIGHEST)  3.49 us

profile of v16, /device:TPU:25, one launch (start us, length us, event | category | flops | bytes accessed | tf_op | source)
XLA Modules:
  0.0 140.8 jit_solution(5621751813339017394)
XLA Ops:
  0.7 9.4 %shard_map.106 = (f32[2,1,128,128]{3,2,1,0:T(8,128)}, f32[2,128,1,128]{3,2,1,0:T(1,128)}) custom-call(f32[128,128,128]{2,1,0:T(8,128)} %state_ref.1), custom_call_target="tpu_custom_call" | custom-call | tf_op jit(solution)/shard_map/pallas_call | solution.py:476
  10.1 0.9 select_bitcast_fusion
  11.0 1.3 fusion.20
  12.3 1.1 pad_maximum_fusion.2
  13.4 0.6 broadcast_select_fusion.1.mix_ref
  14.0 0.6 fusion.21
  14.6 16.4 %shard_map.107 = (f32[128,128,128]{2,1,0:T(8,128)}, f32[8,16384]{1,0:T(8,128)S(1)}) custom-call(f32[128,128,128]{2,1,0:T(8,128)} %state_ref.1, f32[8,128,128]{2,1,0:T(8,128)} %get-tuple-element.219.top_ref, f32[8,128,128]{2,1,0:T(8,128)} %get-tuple-element.220.bottom_ref, f32[128,1,128]{2,1,0:T(1,128)} %bitcast.86, f32[128,1,128]{2,1,0:T(1,128)} %bitcast.85, ...), custom_call_target="tpu_custom_call" | custom-call | flops 1610612736 | bytes 16777216 | tf_op jit(solution)/shard_map/pallas_call | solution.py:113
  31.0 5.6 %shard_map.108 = (f32[2,1,128,128]{3,2,1,0:T(8,128)S(1)}, f32[2,128,1,128]{3,2,1,0:T(1,128)S(1)}) custom-call(f32[128,128,128]{2,1,0:T(8,128)} %get-tuple-element.117.values_ref), custom_call_target="tpu_custom_call" | custom-call | tf_op jit(solution)/shard_map/pallas_call | solution.py:476
  37.0 0.4 copy-done.15
  37.6 0.1 reshape.179
  37.9 0.2 convert_reduce_fusion
  38.2 1.2 convolution_convert_fusion
  39.4 55.6 %shard_map.109 = bf16[24,32,1152]{2,1,0:T(8,128)(2,1)S(1)} custom-call(bf16[8,32,1152]{2,1,0:T(8,128)(2,1)} %bitcast.79), custom_call_target="tpu_custom_call" | custom-call | tf_op jit(solution)/shard_map/pallas_call | solution.py:221
  95.1 1.6 %convert_element_type.40 = f32[32,128,128]{2,1,0:T(8,128)} convert(bf16[32,128,128]{2,1,0:T(8,128)(2,1)S(1)} %copy-done.4) | non-fusion elementwise | flops 524288 | bytes 3145728 | tf_op jit(solution)/shard_map/convert_element_type | solution.py:581
  96.7 25.7 %conditional.4 = (f32[8,128,128]{2,0,1:T(8,128)S(1)}, f32[24,32,128]{2,1,0:T(8,128)S(1)}, f32[128,128]{1,0:T(8,128)S(1)}) conditional(s32[]{:T(128)} %convert_element_type.36, f32[128,128]{1,0:T(8,128)S(1)} %bitcast.76, (bf16[24,32,1152]{2,1,0:T(8,128)(2,1)S(1)}, bf16[32,128,128]{2,1,0:T(8,128)(2,1)S(1)}, f32[8,128]{1,0:T(8,128)}, ...), branch_computations={%region_4.5_spmd, %region_5.7_spmd} | conditional | flops 2953967360 | bytes 37553412 | solution.py:605
  96.7 0.4 fusion.4
  97.1 0.4 convert_bitcast_fusion
  97.5 0.4 copy-done.1
  97.9 0.4 copy-done.5
  98.3 0.7 copy.44
  99.0 16.1 %branch_1_fun.1 = f32[1024,128]{1,0:T(8,128)S(1)} custom-call(s32[768]{0:T(1024)S(1)} %get-tuple-element.201.labels_ref, f32[768,8,128]{2,1,0:T(8,128)S(1)} %bitcast.65, bf16[32,128,128]{2,1,0:T(8,128)(2,1)} %copy-done.5), custom_call_target="tpu_custom_call" | custom-call | flops 2147483648 | bytes 4194304 | tf_op jit(solution)/shard_map/cond/branch_1_fun/pallas_call | solution.py:413
  115.3 0.2 multiply_reduce_fusion
  115.6 3.5 %fusion.5 = f32[128,32,128]{2,0,1:T(8,128)S(1)} fusion(f32[32,128,128]{2,1,0:T(8,128)} %get-tuple-element.54, f32[128,128]{1,0:T(8,128)S(1)} %add_select_fusion), kind=kOutput, calls=%fused_computation.18 | convolution fusion | flops 805306368 | bytes 4259840 | tf_op jit(solution)/shard_map/cond/branch_1_fun/db,wab->wda/dot_general | solution.py:594
  119.1 1.6 %gather_fusion = f32[768,128]{1,0:T(8,128)S(1)} fusion(f32[4096,128]{1,0:T(8,128)S(1)} %bitcast.67, s32[1024]{0:T(1024)S(1)} %pad_clamp_fusion), kind=kCustom, calls=%fused_computation | custom fusion | bytes 789504 | tf_op jit(solution)/shard_map/cond/branch_1_fun/jit(_take)/gather | solution.py:595
  120.7 1.4 and_reduce_fusion
  122.2 0.2 broadcast_select_fusion
  122.4 4.7 %shard_map.110 = f32[8,32,128]{2,1,0:T(8,128)} custom-call(f32[24,32,128]{2,1,0:T(8,128)S(1)} %get-tuple-element.82.surface_ref), custom_call_target="tpu_custom_call" | custom-call | tf_op jit(solution)/shard_map/pallas_call | solution.py:292
  127.2 1.6 %gather_fusion.1 = f32[256,128]{1,0:T(8,128)S(1)} fusion(f32[256,128]{1,0:T(8,128)} %bitcast.68, s32[1024]{0:T(1024)S(1)} %pad_clamp_fusion.1), kind=kCustom, calls=%fused_computation.1 | custom fusion | bytes 263168 | tf_op jit(solution)/shard_map/jit(_take)/gather | solution.py:616
  129.0 0.2 select_reduce_fusion
  129.2 0.6 select_select_fusion
  129.9 0.8 broadcast_in_dim.130.sea_ref
  130.7 10.1 %shard_map.111 = f32[128,128,128]{2,1,0:T(8,128)} custom-call(s32[1]{0:T(128)} %bitcast.11.flag_ref, f32[128,128,128]{2,1,0:T(8,128)} %get-tuple-element.83.base_ref, f32[128,128,128]{2,1,0:T(8,128)} %state_ref.1, s32[8,16384]{1,0:T(8,128)} %broadcast_in_dim.130.sea_ref, f32[8,16384]{1,0:T(8,128)S(1)} %bitcast.73, ...), custom_call_target="tpu_custom_call", output_to_operand_aliasing={{}: (1, {})} | custom-call | flops 134217728 | bytes 25165824 | tf_op jit(solution)/shard_map/pallas_call | solution.py:363
  (56 shorter events, 1.3 us)
Async XLA Ops:
  10.0 3.3 %copy-start.6 = (f32[128,128]{1,0:T(8,128)S(1)}, f32[128,128]{1,0:T(8,128)}, u32[]{:S(2)}) copy-start(f32[128,128]{1,0:T(8,128)} %param.18) | copy-start | bytes 196612
  10.0 3.3 %copy-start.8 = (f32[128,128]{1,0:T(8,128)S(1)}, f32[128,128]{1,0:T(8,128)}, u32[]{:S(2)}) copy-start(f32[128,128]{1,0:T(8,128)} %param.19) | copy-start | bytes 196612
  11.0 3.0 %copy-start.7 = (f32[2,128,1,128]{3,2,1,0:T(1,128)S(1)}, f32[2,128,1,128]{3,2,1,0:T(1,128)}, u32[]{:S(2)}) copy-start(f32[2,128,1,128]{3,2,1,0:T(1,128)} %get-tuple-element.73) | copy-start | bytes 393220
  31.0 5.7 %copy-start.9 = (s32[128,128]{1,0:T(8,128)S(1)}, s32[128,128]{1,0:T(8,128)}, u32[]{:S(2)}) copy-start(s32[128,128]{1,0:T(8,128)} %param.16) | copy-start | bytes 196612
  31.0 5.7 %copy-start.14 = (f32[128,8]{0,1:T(8,128)S(1)}, f32[128,8]{0,1:T(8,128)}, u32[]{:S(2)}) copy-start(f32[128,8]{0,1:T(8,128)} %param.20) | copy-start | bytes 12292
  36.8 0.7 copy-start.15
  36.8 0.9 copy-start.16
  37.6 57.5 %copy-start.4 = (bf16[32,128,128]{2,1,0:T(8,128)(2,1)S(1)}, bf16[32,128,128]{2,1,0:T(8,128)(2,1)}, u32[]{:S(2)}) copy-start(bf16[32,128,128]{2,1,0:T(8,128)(2,1)} %param.22) | copy-start | bytes 3145732
  38.1 57.0 %copy-start.12 = (s32[256]{0:T(256)}, s32[256]{0:T(256)S(1)}, u32[]{:S(2)}) copy-start(s32[256]{0:T(256)S(1)} %multiply_add_fusion) | copy-start | bytes 3076
  96.7 1.2 copy-start.1
  96.7 1.6 %copy-start.5 = (bf16[32,128,128]{2,1,0:T(8,128)(2,1)}, bf16[32,128,128]{2,1,0:T(8,128)(2,1)S(1)}, u32[]{:S(2)}) copy-start(bf16[32,128,128]{2,1,0:T(8,128)(2,1)S(1)} %get-tuple-element.49.weights_ref) | copy-start | bytes 3145732 | tf_op jit(solution)/shard_map/cond
  99.0 16.2 %copy-start.11 = (f32[8,128]{1,0:T(8,128)S(1)}, f32[8,128]{1,0:T(8,128)}, u32[]{:S(2)}) copy-start(f32[8,128]{1,0:T(8,128)} %get-tuple-element.195) | copy-start | bytes 12292 | tf_op jit(solution)/shard_map/cond
  115.2 3.9 %copy-start.2 = (f32[1024,128]{1,0:T(8,128)}, f32[1024,128]{1,0:T(8,128)S(1)}, u32[]{:S(2)}) copy-start(f32[1024,128]{1,0:T(8,128)S(1)} %branch_1_fun.1) | copy-start | bytes 1572868 | tf_op jit(solution)/shard_map/cond
  119.1 3.2 %copy-start.3 = (f32[1024,128]{1,0:T(8,128)S(1)}, f32[1024,128]{1,0:T(8,128)}, u32[]{:S(2)}) copy-start(f32[1024,128]{1,0:T(8,128)} %copy-done.2) | copy-start | bytes 1572868 | tf_op jit(solution)/shard_map/cond
  122.4 4.8 %copy-start.13 = (s32[256]{0:T(256)S(1)}, s32[256]{0:T(256)}, u32[]{:S(2)}) copy-start(s32[256]{0:T(256)} %copy-done.12) | copy-start | bytes 3076
  122.4 8.3 %copy-start.10 = (f32[8,128]{1,0:T(8,128)S(1)}, f32[8,128]{1,0:T(8,128)}, u32[]{:S(2)}) copy-start(f32[8,128]{1,0:T(8,128)} %spread_ref.1) | copy-start | bytes 12292

commit v17 on v16

--- a/solution.py
+++ b/solution.py
@@ -9,7 +9,7 @@
 SMOOTHING = 0.2
 PHYSICS = 0.5
 HIGHEST = lax.Precision.HIGHEST
-ROW_BLOCK = 16
+ROW_BLOCK = 32
 UPDATE_BLOCK = 32
 
 

time: 141 us -> 139 us (0.986)
  Pallas kernels: 118 us -> 116 us
    pallas_call x1, Pallas kernels: 55.6 us -> 53.7 us  [gather_to_ocean(): pl.pallas_call(functools.partial(gather_kernel, tuple(offsets), tuple(sha...]
where the time goes in v17:
time: 139 us; the launch traced here: 138 us
  Pallas kernels  116 us (83%)
  local copies, waits for them, and re-layouts  8.69 us (6%)
  other arithmetic  7.93 us (6%)
  matrix products  4.66 us (3%)
    pallas_call x1, Pallas kernels, gather_to_ocean(): pl.pallas_call(functools.partial(gather_kernel, tuple(offsets), tuple(sha...  53.7 us
    pallas_call x1, Pallas kernels, substep(): pl.pallas_call(functools.partial(substep_kernel, with_flux, comp_total),...  16.5 us
    pallas_call x1, Pallas kernels, scatter_regrid(): pl.pallas_call(scatter_regrid_kernel, out_shape=jax.ShapeDtypeStruct((til...  16.1 us
    pallas_call x2, Pallas kernels, halo_edges(): pl.pallas_call(functools.partial(halo_kernel, tuple(shape)), out_shape=(j...  15 us
    pallas_call x1, Pallas kernels, ocean_update(): pl.pallas_call(ocean_update_kernel, out_shape=jax.ShapeDtypeStruct(first....  10.1 us
    pallas_call x1, Pallas kernels, spread_from_ocean(): pl.pallas_call(functools.partial(spread_kernel, tuple(offsets), tuple(sha...  4.22 us
    dot_general x1, matrix products, ocean_reply(): jnp.einsum('db,wab->wda', top_level, weights_wide, precision=HIGHEST)  3.49 us

profile of v17, /device:TPU:25, one launch (start us, length us, event | category | flops | bytes accessed | tf_op | source)
XLA Modules:
  0.0 138.1 jit_solution(5345815937398406107)
XLA Ops:
  0.7 9.4 %shard_map.106 = (f32[2,1,128,128]{3,2,1,0:T(8,128)}, f32[2,128,1,128]{3,2,1,0:T(1,128)}) custom-call(f32[128,128,128]{2,1,0:T(8,128)} %state_ref.1), custom_call_target="tpu_custom_call" | custom-call | tf_op jit(solution)/shard_map/pallas_call | solution.py:476
  10.1 0.9 select_bitcast_fusion
  11.0 1.1 fusion.20
  12.1 0.8 pad_maximum_fusion.2
  12.9 0.6 broadcast_select_fusion.1.mix_ref
  13.6 0.7 fusion.21
  14.2 16.5 %shard_map.107 = (f32[128,128,128]{2,1,0:T(8,128)}, f32[8,16384]{1,0:T(8,128)S(1)}) custom-call(f32[128,128,128]{2,1,0:T(8,128)} %state_ref.1, f32[4,128,128]{2,1,0:T(8,128)} %get-tuple-element.219.top_ref, f32[4,128,128]{2,1,0:T(8,128)} %get-tuple-element.220.bottom_ref, f32[128,1,128]{2,1,0:T(1,128)} %bitcast.86, f32[128,1,128]{2,1,0:T(1,128)} %bitcast.85, ...), custom_call_target="tpu_custom_call" | custom-call | flops 1610612736 | bytes 16777216 | tf_op jit(solution)/shard_map/pallas_call | solution.py:113
  30.7 5.6 %shard_map.108 = (f32[2,1,128,128]{3,2,1,0:T(8,128)S(1)}, f32[2,128,1,128]{3,2,1,0:T(1,128)S(1)}) custom-call(f32[128,128,128]{2,1,0:T(8,128)} %get-tuple-element.117.values_ref), custom_call_target="tpu_custom_call" | custom-call | tf_op jit(solution)/shard_map/pallas_call | solution.py:476
  36.8 0.4 copy-done.15
  37.3 0.1 reshape.179
  37.6 0.2 convert_reduce_fusion
  38.0 1.2 convolution_convert_fusion
  39.1 53.7 %shard_map.109 = bf16[24,32,1152]{2,1,0:T(8,128)(2,1)S(1)} custom-call(bf16[8,32,1152]{2,1,0:T(8,128)(2,1)} %bitcast.79), custom_call_target="tpu_custom_call" | custom-call | tf_op jit(solution)/shard_map/pallas_call | solution.py:221
  92.9 1.6 %convert_element_type.40 = f32[32,128,128]{2,1,0:T(8,128)} convert(bf16[32,128,128]{2,1,0:T(8,128)(2,1)S(1)} %copy-done.4) | non-fusion elementwise | flops 524288 | bytes 3145728 | tf_op jit(solution)/shard_map/convert_element_type | solution.py:581
  94.5 25.7 %conditional.4 = (f32[8,128,128]{2,0,1:T(8,128)S(1)}, f32[24,32,128]{2,1,0:T(8,128)S(1)}, f32[128,128]{1,0:T(8,128)S(1)}) conditional(s32[]{:T(128)} %convert_element_type.36, f32[128,128]{1,0:T(8,128)S(1)} %bitcast.76, (bf16[24,32,1152]{2,1,0:T(8,128)(2,1)S(1)}, bf16[32,128,128]{2,1,0:T(8,128)(2,1)S(1)}, f32[8,128]{1,0:T(8,128)}, ...), branch_computations={%region_4.5_spmd, %region_5.7_spmd} | conditional | flops 2953967360 | bytes 37553412 | solution.py:605
  94.5 0.4 fusion.4
  94.8 0.4 convert_bitcast_fusion
  95.3 0.4 copy-done.1
  95.6 0.4 copy-done.5
  96.0 0.7 copy.44
  96.8 16.1 %branch_1_fun.1 = f32[1024,128]{1,0:T(8,128)S(1)} custom-call(s32[768]{0:T(1024)S(1)} %get-tuple-element.201.labels_ref, f32[768,8,128]{2,1,0:T(8,128)S(1)} %bitcast.65, bf16[32,128,128]{2,1,0:T(8,128)(2,1)} %copy-done.5), custom_call_target="tpu_custom_call" | custom-call | flops 2147483648 | bytes 4194304 | tf_op jit(solution)/shard_map/cond/branch_1_fun/pallas_call | solution.py:413
  113.0 0.2 multiply_reduce_fusion
  113.4 3.5 %fusion.5 = f32[128,32,128]{2,0,1:T(8,128)S(1)} fusion(f32[32,128,128]{2,1,0:T(8,128)} %get-tuple-element.54, f32[128,128]{1,0:T(8,128)S(1)} %add_select_fusion), kind=kOutput, calls=%fused_computation.18 | convolution fusion | flops 805306368 | bytes 4259840 | tf_op jit(solution)/shard_map/cond/branch_1_fun/db,wab->wda/dot_general | solution.py:594
  116.9 1.6 %gather_fusion = f32[768,128]{1,0:T(8,128)S(1)} fusion(f32[4096,128]{1,0:T(8,128)S(1)} %bitcast.67, s32[1024]{0:T(1024)S(1)} %pad_clamp_fusion), kind=kCustom, calls=%fused_computation | custom fusion | bytes 789504 | tf_op jit(solution)/shard_map/cond/branch_1_fun/jit(_take)/gather | solution.py:595
  118.5 1.4 and_reduce_fusion
  119.9 0.2 broadcast_select_fusion
  120.2 4.2 %shard_map.110 = f32[8,32,128]{2,1,0:T(8,128)} custom-call(f32[24,32,128]{2,1,0:T(8,128)S(1)} %get-tuple-element.82.surface_ref), custom_call_target="tpu_custom_call" | custom-call | tf_op jit(solution)/shard_map/pallas_call | solution.py:292
  124.4 1.6 %gather_fusion.1 = f32[256,128]{1,0:T(8,128)S(1)} fusion(f32[256,128]{1,0:T(8,128)} %bitcast.68, s32[1024]{0:T(1024)S(1)} %pad_clamp_fusion.1), kind=kCustom, calls=%fused_computation.1 | custom fusion | bytes 263168 | tf_op jit(solution)/shard_map/jit(_take)/gather | solution.py:616
  126.2 0.2 select_reduce_fusion
  126.5 0.6 select_select_fusion
  127.1 0.8 broadcast_in_dim.130.sea_ref
  128.0 10.1 %shard_map.111 = f32[128,128,128]{2,1,0:T(8,128)} custom-call(s32[1]{0:T(128)} %bitcast.11.flag_ref, f32[128,128,128]{2,1,0:T(8,128)} %get-tuple-element.83.base_ref, f32[128,128,128]{2,1,0:T(8,128)} %state_ref.1, s32[8,16384]{1,0:T(8,128)} %broadcast_in_dim.130.sea_ref, f32[8,16384]{1,0:T(8,128)S(1)} %bitcast.73, ...), custom_call_target="tpu_custom_call", output_to_operand_aliasing={{}: (1, {})} | custom-call | flops 134217728 | bytes 25165824 | tf_op jit(solution)/shard_map/pallas_call | solution.py:363
  (56 shorter events, 1.3 us)
Async XLA Ops:
  10.0 2.9 %copy-start.6 = (f32[128,128]{1,0:T(8,128)S(1)}, f32[128,128]{1,0:T(8,128)}, u32[]{:S(2)}) copy-start(f32[128,128]{1,0:T(8,128)} %param.18) | copy-start | bytes 196612
  10.1 2.9 %copy-start.8 = (f32[128,128]{1,0:T(8,128)S(1)}, f32[128,128]{1,0:T(8,128)}, u32[]{:S(2)}) copy-start(f32[128,128]{1,0:T(8,128)} %param.19) | copy-start | bytes 196612
  10.1 3.5 %copy-start.7 = (f32[2,128,1,128]{3,2,1,0:T(1,128)S(1)}, f32[2,128,1,128]{3,2,1,0:T(1,128)}, u32[]{:S(2)}) copy-start(f32[2,128,1,128]{3,2,1,0:T(1,128)} %get-tuple-element.73) | copy-start | bytes 393220
  30.7 5.7 %copy-start.9 = (s32[128,128]{1,0:T(8,128)S(1)}, s32[128,128]{1,0:T(8,128)}, u32[]{:S(2)}) copy-start(s32[128,128]{1,0:T(8,128)} %param.16) | copy-start | bytes 196612
  30.7 5.7 %copy-start.14 = (f32[128,8]{0,1:T(8,128)S(1)}, f32[128,8]{0,1:T(8,128)}, u32[]{:S(2)}) copy-start(f32[128,8]{0,1:T(8,128)} %param.20) | copy-start | bytes 12292
  36.5 0.7 copy-start.15
  36.6 0.9 copy-start.16
  37.3 55.6 %copy-start.4 = (bf16[32,128,128]{2,1,0:T(8,128)(2,1)S(1)}, bf16[32,128,128]{2,1,0:T(8,128)(2,1)}, u32[]{:S(2)}) copy-start(bf16[32,128,128]{2,1,0:T(8,128)(2,1)} %param.22) | copy-start | bytes 3145732
  37.8 55.0 %copy-start.12 = (s32[256]{0:T(256)}, s32[256]{0:T(256)S(1)}, u32[]{:S(2)}) copy-start(s32[256]{0:T(256)S(1)} %multiply_add_fusion) | copy-start | bytes 3076
  94.5 1.2 copy-start.1
  94.5 1.6 %copy-start.5 = (bf16[32,128,128]{2,1,0:T(8,128)(2,1)}, bf16[32,128,128]{2,1,0:T(8,128)(2,1)S(1)}, u32[]{:S(2)}) copy-start(bf16[32,128,128]{2,1,0:T(8,128)(2,1)S(1)} %get-tuple-element.49.weights_ref) | copy-start | bytes 3145732 | tf_op jit(solution)/shard_map/cond
  96.8 16.2 %copy-start.11 = (f32[8,128]{1,0:T(8,128)S(1)}, f32[8,128]{1,0:T(8,128)}, u32[]{:S(2)}) copy-start(f32[8,128]{1,0:T(8,128)} %get-tuple-element.195) | copy-start | bytes 12292 | tf_op jit(solution)/shard_map/cond
  112.9 3.9 %copy-start.2 = (f32[1024,128]{1,0:T(8,128)}, f32[1024,128]{1,0:T(8,128)S(1)}, u32[]{:S(2)}) copy-start(f32[1024,128]{1,0:T(8,128)S(1)} %branch_1_fun.1) | copy-start | bytes 1572868 | tf_op jit(solution)/shard_map/cond
  116.9 3.2 %copy-start.3 = (f32[1024,128]{1,0:T(8,128)S(1)}, f32[1024,128]{1,0:T(8,128)}, u32[]{:S(2)}) copy-start(f32[1024,128]{1,0:T(8,128)} %copy-done.2) | copy-start | bytes 1572868 | tf_op jit(solution)/shard_map/cond
  120.1 4.3 %copy-start.13 = (s32[256]{0:T(256)S(1)}, s32[256]{0:T(256)}, u32[]{:S(2)}) copy-start(s32[256]{0:T(256)} %copy-done.12) | copy-start | bytes 3076
  120.2 7.8 %copy-start.10 = (f32[8,128]{1,0:T(8,128)S(1)}, f32[8,128]{1,0:T(8,128)}, u32[]{:S(2)}) copy-start(f32[8,128]{1,0:T(8,128)} %spread_ref.1) | copy-start | bytes 12292

commit v18 on v17

--- a/solution.py
+++ b/solution.py
@@ -9,7 +9,7 @@
 SMOOTHING = 0.2
 PHYSICS = 0.5
 HIGHEST = lax.Precision.HIGHEST
-ROW_BLOCK = 32
+ROW_BLOCK = 64
 UPDATE_BLOCK = 32
 
 

time: 139 us -> 140 us (level)
    pallas_call x1, Pallas kernels: 16.5 us -> 18.1 us  [substep(): pl.pallas_call(functools.partial(substep_kernel, with_flux, comp_total),...]
where the time goes in v18:
time: 140 us; the launch traced here: 139 us
  Pallas kernels  117 us (84%)
  local copies, waits for them, and re-layouts  9.17 us (7%)
  other arithmetic  7.76 us (6%)
  matrix products  4.66 us (3%)
    pallas_call x1, Pallas kernels, gather_to_ocean(): pl.pallas_call(functools.partial(gather_kernel, tuple(offsets), tuple(sha...  53.1 us
    pallas_call x1, Pallas kernels, substep(): pl.pallas_call(functools.partial(substep_kernel, with_flux, comp_total),...  18.1 us
    pallas_call x1, Pallas kernels, scatter_regrid(): pl.pallas_call(scatter_regrid_kernel, out_shape=jax.ShapeDtypeStruct((til...  16.1 us
    pallas_call x2, Pallas kernels, halo_edges(): pl.pallas_call(functools.partial(halo_kernel, tuple(shape)), out_shape=(j...  15 us
    pallas_call x1, Pallas kernels, ocean_update(): pl.pallas_call(ocean_update_kernel, out_shape=jax.ShapeDtypeStruct(first....  10.1 us
    pallas_call x1, Pallas kernels, spread_from_ocean(): pl.pallas_call(functools.partial(spread_kernel, tuple(offsets), tuple(sha...  4.08 us
    dot_general x1, matrix products, ocean_reply(): jnp.einsum('db,wab->wda', top_level, weights_wide, precision=HIGHEST)  3.49 us

profile of v18, /device:TPU:25, one launch (start us, length us, event | category | flops | bytes accessed | tf_op | source)
XLA Modules:
  0.0 139.4 jit_solution(3090588274132249081)
XLA Ops:
  0.7 9.4 %shard_map.106 = (f32[2,1,128,128]{3,2,1,0:T(8,128)}, f32[2,128,1,128]{3,2,1,0:T(1,128)}) custom-call(f32[128,128,128]{2,1,0:T(8,128)} %state_ref.1), custom_call_target="tpu_custom_call" | custom-call | tf_op jit(solution)/shard_map/pallas_call | solution.py:476
  10.0 0.9 select_bitcast_fusion
  10.9 0.9 fusion.20
  11.8 0.7 pad_maximum_fusion.2
  12.6 0.6 broadcast_select_fusion.1.mix_ref
  13.2 1.5 %fusion.21 = (f32[1,128,1,128]{3,1,2,0:T(8,128)}, f32[1,128,1,128]{3,1,2,0:T(8,128)}) fusion(f32[2,128,1,128]{3,1,2,0:T(8,128)} %bitcast.90), kind=kLoop, calls=%fused_computation.63 | loop fusion | bytes 262144 | tf_op jit(solution)/shard_map/slice | solution.py:529
  14.7 18.1 %shard_map.107 = (f32[128,128,128]{2,1,0:T(8,128)}, f32[8,16384]{1,0:T(8,128)S(1)}) custom-call(f32[128,128,128]{2,1,0:T(8,128)} %state_ref.1, f32[2,128,128]{2,1,0:T(8,128)} %get-tuple-element.219.top_ref, f32[2,128,128]{2,1,0:T(8,128)} %get-tuple-element.220.bottom_ref, f32[128,1,128]{2,1,0:T(1,128)} %bitcast.86, f32[128,1,128]{2,1,0:T(1,128)} %bitcast.85, ...), custom_call_target="tpu_custom_call" | custom-call | flops 1610612736 | bytes 16777216 | tf_op jit(solution)/shard_map/pallas_call | solution.py:113
  32.8 5.6 %shard_map.108 = (f32[2,1,128,128]{3,2,1,0:T(8,128)S(1)}, f32[2,128,1,128]{3,2,1,0:T(1,128)S(1)}) custom-call(f32[128,128,128]{2,1,0:T(8,128)} %get-tuple-element.117.values_ref), custom_call_target="tpu_custom_call" | custom-call | tf_op jit(solution)/shard_map/pallas_call | solution.py:476
  38.5 0.2 conditional.3
  39.0 0.2 copy-done.14
  39.6 0.2 convert_reduce_fusion
  40.0 1.2 convolution_convert_fusion
  41.2 53.1 %shard_map.109 = bf16[24,32,1152]{2,1,0:T(8,128)(2,1)S(1)} custom-call(bf16[8,32,1152]{2,1,0:T(8,128)(2,1)} %bitcast.79), custom_call_target="tpu_custom_call" | custom-call | tf_op jit(solution)/shard_map/pallas_call | solution.py:221
  94.3 1.6 %convert_element_type.40 = f32[32,128,128]{2,1,0:T(8,128)} convert(bf16[32,128,128]{2,1,0:T(8,128)(2,1)S(1)} %copy-done.4) | non-fusion elementwise | flops 524288 | bytes 3145728 | tf_op jit(solution)/shard_map/convert_element_type | solution.py:581
  95.9 25.6 %conditional.4 = (f32[8,128,128]{2,0,1:T(8,128)S(1)}, f32[24,32,128]{2,1,0:T(8,128)S(1)}, f32[128,128]{1,0:T(8,128)S(1)}) conditional(s32[]{:T(128)} %convert_element_type.36, f32[128,128]{1,0:T(8,128)S(1)} %bitcast.76, (bf16[24,32,1152]{2,1,0:T(8,128)(2,1)S(1)}, bf16[32,128,128]{2,1,0:T(8,128)(2,1)S(1)}, f32[8,128]{1,0:T(8,128)}, ...), branch_computations={%region_4.5_spmd, %region_5.7_spmd} | conditional | flops 2953967360 | bytes 37553412 | solution.py:605
  95.9 0.4 fusion.4
  96.3 0.4 convert_bitcast_fusion
  96.7 0.4 copy-done.1
  97.1 0.4 copy-done.5
  97.5 0.7 copy.44
  98.2 16.1 %branch_1_fun.1 = f32[1024,128]{1,0:T(8,128)S(1)} custom-call(s32[768]{0:T(1024)S(1)} %get-tuple-element.201.labels_ref, f32[768,8,128]{2,1,0:T(8,128)S(1)} %bitcast.65, bf16[32,128,128]{2,1,0:T(8,128)(2,1)} %copy-done.5), custom_call_target="tpu_custom_call" | custom-call | flops 2147483648 | bytes 4194304 | tf_op jit(solution)/shard_map/cond/branch_1_fun/pallas_call | solution.py:413
  114.5 0.2 multiply_reduce_fusion
  114.8 3.5 %fusion.5 = f32[128,32,128]{2,0,1:T(8,128)S(1)} fusion(f32[32,128,128]{2,1,0:T(8,128)} %get-tuple-element.54, f32[128,128]{1,0:T(8,128)S(1)} %add_select_fusion), kind=kOutput, calls=%fused_computation.18 | convolution fusion | flops 805306368 | bytes 4259840 | tf_op jit(solution)/shard_map/cond/branch_1_fun/db,wab->wda/dot_general | solution.py:594
  118.3 1.6 %gather_fusion = f32[768,128]{1,0:T(8,128)S(1)} fusion(f32[4096,128]{1,0:T(8,128)S(1)} %bitcast.67, s32[1024]{0:T(1024)S(1)} %pad_clamp_fusion), kind=kCustom, calls=%fused_computation | custom fusion | bytes 789504 | tf_op jit(solution)/shard_map/cond/branch_1_fun/jit(_take)/gather | solution.py:595
  119.9 1.4 and_reduce_fusion
  121.4 0.2 broadcast_select_fusion
  121.6 4.1 %shard_map.110 = f32[8,32,128]{2,1,0:T(8,128)} custom-call(f32[24,32,128]{2,1,0:T(8,128)S(1)} %get-tuple-element.82.surface_ref), custom_call_target="tpu_custom_call" | custom-call | tf_op jit(solution)/shard_map/pallas_call | solution.py:292
  125.8 1.6 %gather_fusion.1 = f32[256,128]{1,0:T(8,128)S(1)} fusion(f32[256,128]{1,0:T(8,128)} %bitcast.68, s32[1024]{0:T(1024)S(1)} %pad_clamp_fusion.1), kind=kCustom, calls=%fused_computation.1 | custom fusion | bytes 263168 | tf_op jit(solution)/shard_map/jit(_take)/gather | solution.py:616
  127.5 0.2 select_reduce_fusion
  127.8 0.6 select_select_fusion
  128.4 0.8 broadcast_in_dim.130.sea_ref
  129.3 10.1 %shard_map.111 = f32[128,128,128]{2,1,0:T(8,128)} custom-call(s32[1]{0:T(128)} %bitcast.11.flag_ref, f32[128,128,128]{2,1,0:T(8,128)} %get-tuple-element.83.base_ref, f32[128,128,128]{2,1,0:T(8,128)} %state_ref.1, s32[8,16384]{1,0:T(8,128)} %broadcast_in_dim.130.sea_ref, f32[8,16384]{1,0:T(8,128)S(1)} %bitcast.73, ...), custom_call_target="tpu_custom_call", output_to_operand_aliasing={{}: (1, {})} | custom-call | flops 134217728 | bytes 25165824 | tf_op jit(solution)/shard_map/pallas_call | solution.py:363
  (54 shorter events, 1.4 us)
Async XLA Ops:
  0.7 11.9 %copy-start.6 = (f32[128,128]{1,0:T(8,128)S(1)}, f32[128,128]{1,0:T(8,128)}, u32[]{:S(2)}) copy-start(f32[128,128]{1,0:T(8,128)} %param.18) | copy-start | bytes 196612
  0.7 11.9 %copy-start.7 = (f32[128,128]{1,0:T(8,128)S(1)}, f32[128,128]{1,0:T(8,128)}, u32[]{:S(2)}) copy-start(f32[128,128]{1,0:T(8,128)} %param.19) | copy-start | bytes 196612
  32.8 5.7 %copy-start.8 = (s32[128,128]{1,0:T(8,128)S(1)}, s32[128,128]{1,0:T(8,128)}, u32[]{:S(2)}) copy-start(s32[128,128]{1,0:T(8,128)} %param.16) | copy-start | bytes 196612
  32.8 5.7 %copy-start.13 = (f32[128,8]{0,1:T(8,128)S(1)}, f32[128,8]{0,1:T(8,128)}, u32[]{:S(2)}) copy-start(f32[128,8]{0,1:T(8,128)} %param.20) | copy-start | bytes 12292
  38.5 0.7 copy-start.14
  38.8 0.8 copy-start.15
  39.4 55.0 %copy-start.4 = (bf16[32,128,128]{2,1,0:T(8,128)(2,1)S(1)}, bf16[32,128,128]{2,1,0:T(8,128)(2,1)}, u32[]{:S(2)}) copy-start(bf16[32,128,128]{2,1,0:T(8,128)(2,1)} %param.22) | copy-start | bytes 3145732
  39.8 54.4 %copy-start.11 = (s32[256]{0:T(256)}, s32[256]{0:T(256)S(1)}, u32[]{:S(2)}) copy-start(s32[256]{0:T(256)S(1)} %multiply_add_fusion) | copy-start | bytes 3076
  95.9 1.2 copy-start.1
  95.9 1.6 %copy-start.5 = (bf16[32,128,128]{2,1,0:T(8,128)(2,1)}, bf16[32,128,128]{2,1,0:T(8,128)(2,1)S(1)}, u32[]{:S(2)}) copy-start(bf16[32,128,128]{2,1,0:T(8,128)(2,1)S(1)} %get-tuple-element.49.weights_ref) | copy-start | bytes 3145732 | tf_op jit(solution)/shard_map/cond
  98.2 16.2 %copy-start.10 = (f32[8,128]{1,0:T(8,128)S(1)}, f32[8,128]{1,0:T(8,128)}, u32[]{:S(2)}) copy-start(f32[8,128]{1,0:T(8,128)} %get-tuple-element.195) | copy-start | bytes 12292 | tf_op jit(solution)/shard_map/cond
  114.4 3.9 %copy-start.2 = (f32[1024,128]{1,0:T(8,128)}, f32[1024,128]{1,0:T(8,128)S(1)}, u32[]{:S(2)}) copy-start(f32[1024,128]{1,0:T(8,128)S(1)} %branch_1_fun.1) | copy-start | bytes 1572868 | tf_op jit(solution)/shard_map/cond
  118.3 3.2 %copy-start.3 = (f32[1024,128]{1,0:T(8,128)S(1)}, f32[1024,128]{1,0:T(8,128)}, u32[]{:S(2)}) copy-start(f32[1024,128]{1,0:T(8,128)} %copy-done.2) | copy-start | bytes 1572868 | tf_op jit(solution)/shard_map/cond
  121.6 4.1 %copy-start.12 = (s32[256]{0:T(256)S(1)}, s32[256]{0:T(256)}, u32[]{:S(2)}) copy-start(s32[256]{0:T(256)} %copy-done.11) | copy-start | bytes 3076
  121.6 7.7 %copy-start.9 = (f32[8,128]{1,0:T(8,128)S(1)}, f32[8,128]{1,0:T(8,128)}, u32[]{:S(2)}) copy-start(f32[8,128]{1,0:T(8,128)} %spread_ref.1) | copy-start | bytes 12292

commit v19 on v17

--- a/solution.py
+++ b/solution.py
@@ -10,7 +10,7 @@
 PHYSICS = 0.5
 HIGHEST = lax.Precision.HIGHEST
 ROW_BLOCK = 32
-UPDATE_BLOCK = 32
+UPDATE_BLOCK = 64
 
 
 def split_bf16(values):

time: 139 us -> 138 us (level)
  no operation moved by 1% of the time
where the time goes in v19:
time: 138 us
  Pallas kernels  115 us (83%)
  local copies, waits for them, and re-layouts  8.69 us (6%)
  other arithmetic  7.93 us (6%)
  matrix products  4.66 us (3%)
    pallas_call x1, Pallas kernels, gather_to_ocean(): pl.pallas_call(functools.partial(gather_kernel, tuple(offsets), tuple(sha...  53.7 us
    pallas_call x1, Pallas kernels, substep(): pl.pallas_call(functools.partial(substep_kernel, with_flux, comp_total),...  16.5 us
    pallas_call x1, Pallas kernels, scatter_regrid(): pl.pallas_call(scatter_regrid_kernel, out_shape=jax.ShapeDtypeStruct((til...  16.1 us
    pallas_call x2, Pallas kernels, halo_edges(): pl.pallas_call(functools.partial(halo_kernel, tuple(shape)), out_shape=(j...  15 us
    pallas_call x1, Pallas kernels, ocean_update(): pl.pallas_call(ocean_update_kernel, out_shape=jax.ShapeDtypeStruct(first....  9.68 us
    pallas_call x1, Pallas kernels, spread_from_ocean(): pl.pallas_call(functools.partial(spread_kernel, tuple(offsets), tuple(sha...  4.22 us
    dot_general x1, matrix products, ocean_reply(): jnp.einsum('db,wab->wda', top_level, weights_wide, precision=HIGHEST)  3.49 us

profile of v19, /device:TPU:25, one launch (start us, length us, event | category | flops | bytes accessed | tf_op | source)
XLA Modules:
  0.0 137.7 jit_solution(16845651202472757253)
XLA Ops:
  0.7 9.4 %shard_map.106 = (f32[2,1,128,128]{3,2,1,0:T(8,128)}, f32[2,128,1,128]{3,2,1,0:T(1,128)}) custom-call(f32[128,128,128]{2,1,0:T(8,128)} %state_ref.1), custom_call_target="tpu_custom_call" | custom-call | tf_op jit(solution)/shard_map/pallas_call | solution.py:476
  10.1 0.9 select_bitcast_fusion
  11.0 1.1 fusion.20
  12.1 0.8 pad_maximum_fusion.2
  12.9 0.6 broadcast_select_fusion.1.mix_ref
  13.6 0.7 fusion.21
  14.2 16.5 %shard_map.107 = (f32[128,128,128]{2,1,0:T(8,128)}, f32[8,16384]{1,0:T(8,128)S(1)}) custom-call(f32[128,128,128]{2,1,0:T(8,128)} %state_ref.1, f32[4,128,128]{2,1,0:T(8,128)} %get-tuple-element.219.top_ref, f32[4,128,128]{2,1,0:T(8,128)} %get-tuple-element.220.bottom_ref, f32[128,1,128]{2,1,0:T(1,128)} %bitcast.86, f32[128,1,128]{2,1,0:T(1,128)} %bitcast.85, ...), custom_call_target="tpu_custom_call" | custom-call | flops 1610612736 | bytes 16777216 | tf_op jit(solution)/shard_map/pallas_call | solution.py:113
  30.7 5.6 %shard_map.108 = (f32[2,1,128,128]{3,2,1,0:T(8,128)S(1)}, f32[2,128,1,128]{3,2,1,0:T(1,128)S(1)}) custom-call(f32[128,128,128]{2,1,0:T(8,128)} %get-tuple-element.117.values_ref), custom_call_target="tpu_custom_call" | custom-call | tf_op jit(solution)/shard_map/pallas_call | solution.py:476
  36.8 0.4 copy-done.15
  37.3 0.1 reshape.179
  37.6 0.2 convert_reduce_fusion
  38.0 1.2 convolution_convert_fusion
  39.1 53.7 %shard_map.109 = bf16[24,32,1152]{2,1,0:T(8,128)(2,1)S(1)} custom-call(bf16[8,32,1152]{2,1,0:T(8,128)(2,1)} %bitcast.79), custom_call_target="tpu_custom_call" | custom-call | tf_op jit(solution)/shard_map/pallas_call | solution.py:221
  92.9 1.6 %convert_element_type.40 = f32[32,128,128]{2,1,0:T(8,128)} convert(bf16[32,128,128]{2,1,0:T(8,128)(2,1)S(1)} %copy-done.4) | non-fusion elementwise | flops 524288 | bytes 3145728 | tf_op jit(solution)/shard_map/convert_element_type | solution.py:581
  94.5 25.7 %conditional.4 = (f32[8,128,128]{2,0,1:T(8,128)S(1)}, f32[24,32,128]{2,1,0:T(8,128)S(1)}, f32[128,128]{1,0:T(8,128)S(1)}) conditional(s32[]{:T(128)} %convert_element_type.36, f32[128,128]{1,0:T(8,128)S(1)} %bitcast.76, (bf16[24,32,1152]{2,1,0:T(8,128)(2,1)S(1)}, bf16[32,128,128]{2,1,0:T(8,128)(2,1)S(1)}, f32[8,128]{1,0:T(8,128)}, ...), branch_computations={%region_4.5_spmd, %region_5.7_spmd} | conditional | flops 2953967360 | bytes 37553412 | solution.py:605
  94.5 0.4 fusion.4
  94.8 0.4 convert_bitcast_fusion
  95.3 0.4 copy-done.1
  95.6 0.4 copy-done.5
  96.0 0.7 copy.44
  96.8 16.1 %branch_1_fun.1 = f32[1024,128]{1,0:T(8,128)S(1)} custom-call(s32[768]{0:T(1024)S(1)} %get-tuple-element.201.labels_ref, f32[768,8,128]{2,1,0:T(8,128)S(1)} %bitcast.65, bf16[32,128,128]{2,1,0:T(8,128)(2,1)} %copy-done.5), custom_call_target="tpu_custom_call" | custom-call | flops 2147483648 | bytes 4194304 | tf_op jit(solution)/shard_map/cond/branch_1_fun/pallas_call | solution.py:413
  113.0 0.2 multiply_reduce_fusion
  113.4 3.5 %fusion.5 = f32[128,32,128]{2,0,1:T(8,128)S(1)} fusion(f32[32,128,128]{2,1,0:T(8,128)} %get-tuple-element.54, f32[128,128]{1,0:T(8,128)S(1)} %add_select_fusion), kind=kOutput, calls=%fused_computation.18 | convolution fusion | flops 805306368 | bytes 4259840 | tf_op jit(solution)/shard_map/cond/branch_1_fun/db,wab->wda/dot_general | solution.py:594
  116.9 1.6 %gather_fusion = f32[768,128]{1,0:T(8,128)S(1)} fusion(f32[4096,128]{1,0:T(8,128)S(1)} %bitcast.67, s32[1024]{0:T(1024)S(1)} %pad_clamp_fusion), kind=kCustom, calls=%fused_computation | custom fusion | bytes 789504 | tf_op jit(solution)/shard_map/cond/branch_1_fun/jit(_take)/gather | solution.py:595
  118.5 1.4 and_reduce_fusion
  119.9 0.2 broadcast_select_fusion
  120.2 4.2 %shard_map.110 = f32[8,32,128]{2,1,0:T(8,128)} custom-call(f32[24,32,128]{2,1,0:T(8,128)S(1)} %get-tuple-element.82.surface_ref), custom_call_target="tpu_custom_call" | custom-call | tf_op jit(solution)/shard_map/pallas_call | solution.py:292
  124.4 1.6 %gather_fusion.1 = f32[256,128]{1,0:T(8,128)S(1)} fusion(f32[256,128]{1,0:T(8,128)} %bitcast.68, s32[1024]{0:T(1024)S(1)} %pad_clamp_fusion.1), kind=kCustom, calls=%fused_computation.1 | custom fusion | bytes 263168 | tf_op jit(solution)/shard_map/jit(_take)/gather | solution.py:616
  126.2 0.2 select_reduce_fusion
  126.5 0.6 select_select_fusion
  127.1 0.8 broadcast_in_dim.130.sea_ref
  128.0 9.7 %shard_map.111 = f32[128,128,128]{2,1,0:T(8,128)} custom-call(s32[1]{0:T(128)} %bitcast.11.flag_ref, f32[128,128,128]{2,1,0:T(8,128)} %get-tuple-element.83.base_ref, f32[128,128,128]{2,1,0:T(8,128)} %state_ref.1, s32[8,16384]{1,0:T(8,128)} %broadcast_in_dim.130.sea_ref, f32[8,16384]{1,0:T(8,128)S(1)} %bitcast.73, ...), custom_call_target="tpu_custom_call", output_to_operand_aliasing={{}: (1, {})} | custom-call | flops 134217728 | bytes 25165824 | tf_op jit(solution)/shard_map/pallas_call | solution.py:363
  (56 shorter events, 1.3 us)
Async XLA Ops:
  10.0 2.9 %copy-start.6 = (f32[128,128]{1,0:T(8,128)S(1)}, f32[128,128]{1,0:T(8,128)}, u32[]{:S(2)}) copy-start(f32[128,128]{1,0:T(8,128)} %param.18) | copy-start | bytes 196612
  10.1 2.9 %copy-start.8 = (f32[128,128]{1,0:T(8,128)S(1)}, f32[128,128]{1,0:T(8,128)}, u32[]{:S(2)}) copy-start(f32[128,128]{1,0:T(8,128)} %param.19) | copy-start | bytes 196612
  10.1 3.5 %copy-start.7 = (f32[2,128,1,128]{3,2,1,0:T(1,128)S(1)}, f32[2,128,1,128]{3,2,1,0:T(1,128)}, u32[]{:S(2)}) copy-start(f32[2,128,1,128]{3,2,1,0:T(1,128)} %get-tuple-element.73) | copy-start | bytes 393220
  30.7 5.7 %copy-start.9 = (s32[128,128]{1,0:T(8,128)S(1)}, s32[128,128]{1,0:T(8,128)}, u32[]{:S(2)}) copy-start(s32[128,128]{1,0:T(8,128)} %param.16) | copy-start | bytes 196612
  30.7 5.7 %copy-start.14 = (f32[128,8]{0,1:T(8,128)S(1)}, f32[128,8]{0,1:T(8,128)}, u32[]{:S(2)}) copy-start(f32[128,8]{0,1:T(8,128)} %param.20) | copy-start | bytes 12292
  36.5 0.7 copy-start.15
  36.6 0.9 copy-start.16
  37.3 55.6 %copy-start.4 = (bf16[32,128,128]{2,1,0:T(8,128)(2,1)S(1)}, bf16[32,128,128]{2,1,0:T(8,128)(2,1)}, u32[]{:S(2)}) copy-start(bf16[32,128,128]{2,1,0:T(8,128)(2,1)} %param.22) | copy-start | bytes 3145732
  37.8 55.0 %copy-start.12 = (s32[256]{0:T(256)}, s32[256]{0:T(256)S(1)}, u32[]{:S(2)}) copy-start(s32[256]{0:T(256)S(1)} %multiply_add_fusion) | copy-start | bytes 3076
  94.5 1.2 copy-start.1
  94.5 1.6 %copy-start.5 = (bf16[32,128,128]{2,1,0:T(8,128)(2,1)}, bf16[32,128,128]{2,1,0:T(8,128)(2,1)S(1)}, u32[]{:S(2)}) copy-start(bf16[32,128,128]{2,1,0:T(8,128)(2,1)S(1)} %get-tuple-element.49.weights_ref) | copy-start | bytes 3145732 | tf_op jit(solution)/shard_map/cond
  96.8 16.2 %copy-start.11 = (f32[8,128]{1,0:T(8,128)S(1)}, f32[8,128]{1,0:T(8,128)}, u32[]{:S(2)}) copy-start(f32[8,128]{1,0:T(8,128)} %get-tuple-element.195) | copy-start | bytes 12292 | tf_op jit(solution)/shard_map/cond
  112.9 3.9 %copy-start.2 = (f32[1024,128]{1,0:T(8,128)}, f32[1024,128]{1,0:T(8,128)S(1)}, u32[]{:S(2)}) copy-start(f32[1024,128]{1,0:T(8,128)S(1)} %branch_1_fun.1) | copy-start | bytes 1572868 | tf_op jit(solution)/shard_map/cond
  116.9 3.2 %copy-start.3 = (f32[1024,128]{1,0:T(8,128)S(1)}, f32[1024,128]{1,0:T(8,128)}, u32[]{:S(2)}) copy-start(f32[1024,128]{1,0:T(8,128)} %copy-done.2) | copy-start | bytes 1572868 | tf_op jit(solution)/shard_map/cond
  120.1 4.3 %copy-start.13 = (s32[256]{0:T(256)S(1)}, s32[256]{0:T(256)}, u32[]{:S(2)}) copy-start(s32[256]{0:T(256)} %copy-done.12) | copy-start | bytes 3076
  120.2 7.8 %copy-start.10 = (f32[8,128]{1,0:T(8,128)S(1)}, f32[8,128]{1,0:T(8,128)}, u32[]{:S(2)}) copy-start(f32[8,128]{1,0:T(8,128)} %spread_ref.1) | copy-start | bytes 12292

commit v20 on v19

--- a/solution.py
+++ b/solution.py
@@ -404,7 +404,7 @@
         )
         return carry
 
-    lax.fori_loop(0, weight_count, regrid_one, 0)
+    lax.fori_loop(0, weight_count, regrid_one, 0, unroll=4)
 
 
 def scatter_regrid(labels, fluxes, weights):

time: 138 us -> 134 us (0.971)
  Pallas kernels: 115 us -> 111 us
    pallas_call x1, Pallas kernels: 16.1 us -> 12.1 us  [scatter_regrid(): pl.pallas_call(scatter_regrid_kernel, out_shape=jax.ShapeDtypeStruct((til...]
where the time goes in v20:
time: 134 us
  Pallas kernels  111 us (83%)
  local copies, waits for them, and re-layouts  8.69 us (6%)
  other arithmetic  7.93 us (6%)
  matrix products  4.66 us (3%)
    pallas_call x1, Pallas kernels, gather_to_ocean(): pl.pallas_call(functools.partial(gather_kernel, tuple(offsets), tuple(sha...  53.7 us
    pallas_call x1, Pallas kernels, substep(): pl.pallas_call(functools.partial(substep_kernel, with_flux, comp_total),...  16.5 us
    pallas_call x2, Pallas kernels, halo_edges(): pl.pallas_call(functools.partial(halo_kernel, tuple(shape)), out_shape=(j...  15 us
    pallas_call x1, Pallas kernels, scatter_regrid(): pl.pallas_call(scatter_regrid_kernel, out_shape=jax.ShapeDtypeStruct((til...  12.1 us
    pallas_call x1, Pallas kernels, ocean_update(): pl.pallas_call(ocean_update_kernel, out_shape=jax.ShapeDtypeStruct(first....  9.68 us
    pallas_call x1, Pallas kernels, spread_from_ocean(): pl.pallas_call(functools.partial(spread_kernel, tuple(offsets), tuple(sha...  4.22 us
    dot_general x1, matrix products, ocean_reply(): jnp.einsum('db,wab->wda', top_level, weights_wide, precision=HIGHEST)  3.49 us

profile of v20, /device:TPU:25, one launch (start us, length us, event | category | flops | bytes accessed | tf_op | source)
XLA Modules:
  0.0 133.6 jit_solution(14472095908151612392)
XLA Ops:
  0.7 9.4 %shard_map.106 = (f32[2,1,128,128]{3,2,1,0:T(8,128)}, f32[2,128,1,128]{3,2,1,0:T(1,128)}) custom-call(f32[128,128,128]{2,1,0:T(8,128)} %state_ref.1), custom_call_target="tpu_custom_call" | custom-call | tf_op jit(solution)/shard_map/pallas_call | solution.py:476
  10.1 0.9 select_bitcast_fusion
  11.0 1.1 fusion.20
  12.1 0.8 pad_maximum_fusion.2
  12.9 0.6 broadcast_select_fusion.1.mix_ref
  13.6 0.7 fusion.21
  14.2 16.5 %shard_map.107 = (f32[128,128,128]{2,1,0:T(8,128)}, f32[8,16384]{1,0:T(8,128)S(1)}) custom-call(f32[128,128,128]{2,1,0:T(8,128)} %state_ref.1, f32[4,128,128]{2,1,0:T(8,128)} %get-tuple-element.219.top_ref, f32[4,128,128]{2,1,0:T(8,128)} %get-tuple-element.220.bottom_ref, f32[128,1,128]{2,1,0:T(1,128)} %bitcast.86, f32[128,1,128]{2,1,0:T(1,128)} %bitcast.85, ...), custom_call_target="tpu_custom_call" | custom-call | flops 1610612736 | bytes 16777216 | tf_op jit(solution)/shard_map/pallas_call | solution.py:113
  30.7 5.6 %shard_map.108 = (f32[2,1,128,128]{3,2,1,0:T(8,128)S(1)}, f32[2,128,1,128]{3,2,1,0:T(1,128)S(1)}) custom-call(f32[128,128,128]{2,1,0:T(8,128)} %get-tuple-element.117.values_ref), custom_call_target="tpu_custom_call" | custom-call | tf_op jit(solution)/shard_map/pallas_call | solution.py:476
  36.8 0.4 copy-done.15
  37.3 0.1 reshape.179
  37.6 0.2 convert_reduce_fusion
  38.0 1.2 convolution_convert_fusion
  39.1 53.7 %shard_map.109 = bf16[24,32,1152]{2,1,0:T(8,128)(2,1)S(1)} custom-call(bf16[8,32,1152]{2,1,0:T(8,128)(2,1)} %bitcast.79), custom_call_target="tpu_custom_call" | custom-call | tf_op jit(solution)/shard_map/pallas_call | solution.py:221
  92.9 1.6 %convert_element_type.40 = f32[32,128,128]{2,1,0:T(8,128)} convert(bf16[32,128,128]{2,1,0:T(8,128)(2,1)S(1)} %copy-done.4) | non-fusion elementwise | flops 524288 | bytes 3145728 | tf_op jit(solution)/shard_map/convert_element_type | solution.py:581
  94.5 21.6 %conditional.4 = (f32[8,128,128]{2,0,1:T(8,128)S(1)}, f32[24,32,128]{2,1,0:T(8,128)S(1)}, f32[128,128]{1,0:T(8,128)S(1)}) conditional(s32[]{:T(128)} %convert_element_type.36, f32[128,128]{1,0:T(8,128)S(1)} %bitcast.76, (bf16[24,32,1152]{2,1,0:T(8,128)(2,1)S(1)}, bf16[32,128,128]{2,1,0:T(8,128)(2,1)S(1)}, f32[8,128]{1,0:T(8,128)}, ...), branch_computations={%region_4.5_spmd, %region_5.7_spmd} | conditional | flops 2953967360 | bytes 37553412 | solution.py:605
  94.5 0.4 fusion.4
  94.8 0.4 convert_bitcast_fusion
  95.3 0.4 copy-done.1
  95.6 0.4 copy-done.5
  96.0 0.7 copy.44
  96.8 12.1 %branch_1_fun.1 = f32[1024,128]{1,0:T(8,128)S(1)} custom-call(s32[768]{0:T(1024)S(1)} %get-tuple-element.201.labels_ref, f32[768,8,128]{2,1,0:T(8,128)S(1)} %bitcast.65, bf16[32,128,128]{2,1,0:T(8,128)(2,1)} %copy-done.5), custom_call_target="tpu_custom_call" | custom-call | flops 2147483648 | bytes 4194304 | tf_op jit(solution)/shard_map/cond/branch_1_fun/pallas_call | solution.py:413
  109.0 0.2 multiply_reduce_fusion
  109.3 3.5 %fusion.5 = f32[128,32,128]{2,0,1:T(8,128)S(1)} fusion(f32[32,128,128]{2,1,0:T(8,128)} %get-tuple-element.54, f32[128,128]{1,0:T(8,128)S(1)} %add_select_fusion), kind=kOutput, calls=%fused_computation.18 | convolution fusion | flops 805306368 | bytes 4259840 | tf_op jit(solution)/shard_map/cond/branch_1_fun/db,wab->wda/dot_general | solution.py:594
  112.9 1.6 %gather_fusion = f32[768,128]{1,0:T(8,128)S(1)} fusion(f32[4096,128]{1,0:T(8,128)S(1)} %bitcast.67, s32[1024]{0:T(1024)S(1)} %pad_clamp_fusion), kind=kCustom, calls=%fused_computation | custom fusion | bytes 789504 | tf_op jit(solution)/shard_map/cond/branch_1_fun/jit(_take)/gather | solution.py:595
  114.5 1.4 %and_reduce_fusion = pred[768]{0:T(1024)(128)(4,1)S(1)} fusion(bf16[768,1152]{1,0:T(8,128)(2,1)} %bitcast.71), kind=kLoop, calls=%fused_computation.14 | loop fusion | flops 7680 | bytes 3840 | tf_op jit(solution)/shard_map/cond/branch_1_fun/jit(_take)/and | solution.py:595
  115.9 0.2 broadcast_select_fusion
  116.2 4.2 %shard_map.110 = f32[8,32,128]{2,1,0:T(8,128)} custom-call(f32[24,32,128]{2,1,0:T(8,128)S(1)} %get-tuple-element.82.surface_ref), custom_call_target="tpu_custom_call" | custom-call | tf_op jit(solution)/shard_map/pallas_call | solution.py:292
  120.4 1.6 %gather_fusion.1 = f32[256,128]{1,0:T(8,128)S(1)} fusion(f32[256,128]{1,0:T(8,128)} %bitcast.68, s32[1024]{0:T(1024)S(1)} %pad_clamp_fusion.1), kind=kCustom, calls=%fused_computation.1 | custom fusion | bytes 263168 | tf_op jit(solution)/shard_map/jit(_take)/gather | solution.py:616
  122.2 0.2 select_reduce_fusion
  122.5 0.6 select_select_fusion
  123.1 0.8 broadcast_in_dim.130.sea_ref
  124.0 9.7 %shard_map.111 = f32[128,128,128]{2,1,0:T(8,128)} custom-call(s32[1]{0:T(128)} %bitcast.11.flag_ref, f32[128,128,128]{2,1,0:T(8,128)} %get-tuple-element.83.base_ref, f32[128,128,128]{2,1,0:T(8,128)} %state_ref.1, s32[8,16384]{1,0:T(8,128)} %broadcast_in_dim.130.sea_ref, f32[8,16384]{1,0:T(8,128)S(1)} %bitcast.73, ...), custom_call_target="tpu_custom_call", output_to_operand_aliasing={{}: (1, {})} | custom-call | flops 134217728 | bytes 25165824 | tf_op jit(solution)/shard_map/pallas_call | solution.py:363
  (56 shorter events, 1.3 us)
Async XLA Ops:
  10.0 2.9 %copy-start.6 = (f32[128,128]{1,0:T(8,128)S(1)}, f32[128,128]{1,0:T(8,128)}, u32[]{:S(2)}) copy-start(f32[128,128]{1,0:T(8,128)} %param.18) | copy-start | bytes 196612
  10.1 2.9 %copy-start.8 = (f32[128,128]{1,0:T(8,128)S(1)}, f32[128,128]{1,0:T(8,128)}, u32[]{:S(2)}) copy-start(f32[128,128]{1,0:T(8,128)} %param.19) | copy-start | bytes 196612
  10.1 3.5 %copy-start.7 = (f32[2,128,1,128]{3,2,1,0:T(1,128)S(1)}, f32[2,128,1,128]{3,2,1,0:T(1,128)}, u32[]{:S(2)}) copy-start(f32[2,128,1,128]{3,2,1,0:T(1,128)} %get-tuple-element.73) | copy-start | bytes 393220
  30.7 5.7 %copy-start.9 = (s32[128,128]{1,0:T(8,128)S(1)}, s32[128,128]{1,0:T(8,128)}, u32[]{:S(2)}) copy-start(s32[128,128]{1,0:T(8,128)} %param.16) | copy-start | bytes 196612
  30.7 5.7 %copy-start.14 = (f32[128,8]{0,1:T(8,128)S(1)}, f32[128,8]{0,1:T(8,128)}, u32[]{:S(2)}) copy-start(f32[128,8]{0,1:T(8,128)} %param.20) | copy-start | bytes 12292
  36.5 0.7 copy-start.15
  36.6 0.9 copy-start.16
  37.3 55.6 %copy-start.4 = (bf16[32,128,128]{2,1,0:T(8,128)(2,1)S(1)}, bf16[32,128,128]{2,1,0:T(8,128)(2,1)}, u32[]{:S(2)}) copy-start(bf16[32,128,128]{2,1,0:T(8,128)(2,1)} %param.22) | copy-start | bytes 3145732
  37.8 55.0 %copy-start.12 = (s32[256]{0:T(256)}, s32[256]{0:T(256)S(1)}, u32[]{:S(2)}) copy-start(s32[256]{0:T(256)S(1)} %multiply_add_fusion) | copy-start | bytes 3076
  94.5 1.2 copy-start.1
  94.5 1.6 %copy-start.5 = (bf16[32,128,128]{2,1,0:T(8,128)(2,1)}, bf16[32,128,128]{2,1,0:T(8,128)(2,1)S(1)}, u32[]{:S(2)}) copy-start(bf16[32,128,128]{2,1,0:T(8,128)(2,1)S(1)} %get-tuple-element.49.weights_ref) | copy-start | bytes 3145732 | tf_op jit(solution)/shard_map/cond
  96.8 12.1 %copy-start.11 = (f32[8,128]{1,0:T(8,128)S(1)}, f32[8,128]{1,0:T(8,128)}, u32[]{:S(2)}) copy-start(f32[8,128]{1,0:T(8,128)} %get-tuple-element.195) | copy-start | bytes 12292 | tf_op jit(solution)/shard_map/cond
  108.9 3.9 %copy-start.2 = (f32[1024,128]{1,0:T(8,128)}, f32[1024,128]{1,0:T(8,128)S(1)}, u32[]{:S(2)}) copy-start(f32[1024,128]{1,0:T(8,128)S(1)} %branch_1_fun.1) | copy-start | bytes 1572868 | tf_op jit(solution)/shard_map/cond
  112.9 3.2 %copy-start.3 = (f32[1024,128]{1,0:T(8,128)S(1)}, f32[1024,128]{1,0:T(8,128)}, u32[]{:S(2)}) copy-start(f32[1024,128]{1,0:T(8,128)} %copy-done.2) | copy-start | bytes 1572868 | tf_op jit(solution)/shard_map/cond
  116.1 4.3 %copy-start.13 = (s32[256]{0:T(256)S(1)}, s32[256]{0:T(256)}, u32[]{:S(2)}) copy-start(s32[256]{0:T(256)} %copy-done.12) | copy-start | bytes 3076
  116.1 7.8 %copy-start.10 = (f32[8,128]{1,0:T(8,128)S(1)}, f32[8,128]{1,0:T(8,128)}, u32[]{:S(2)}) copy-start(f32[8,128]{1,0:T(8,128)} %spread_ref.1) | copy-start | bytes 12292
